TPU v7x, 32 devices: a whole 2x2x4 slice. The times are simulated.
32 devices in a mesh: dp: 16 (over z, x, core), tensor: 2 (over y).
Axes of the slice: x: 2, y: 2, z: 4, core: 2. Of those that a mesh axis runs over, the one named last changes fastest.
Arguments:
- tokens: bfloat16 [8192, 2048], P(('dp', 'tensor')), may hold values from -6 to 6
- layer_input: bfloat16 [8192, 256], P(('dp', 'tensor')), may hold values from -6 to 6
- block_ids: int32 [1, 8192], replicated, may hold values from 0 to 63, never falling along the last dimension, each value on 1 to 256 neighbouring positions
- block_table: int32 [1, 64, 64], replicated, may hold values from 0 to 1, as said below
- w_query: bfloat16 [2048, 2048], P('dp', 'tensor'), may hold values from -0.125 to 0.125
- w_key: bfloat16 [2048, 512], P('dp', 'tensor'), may hold values from -0.125 to 0.125
- w_value: bfloat16 [2048, 512], P('dp', 'tensor'), may hold values from -0.125 to 0.125
- w_output: bfloat16 [2048, 2048], P('tensor', 'dp'), may hold values from -0.125 to 0.125
- w_left: bfloat16 [2048, 64], P('dp'), may hold values from -0.125 to 0.125
- w_right: bfloat16 [64, 2048], P(None, 'dp'), may hold values from -0.75 to 0.75
- w_gate: bfloat16 [2048, 8192], P('dp', 'tensor'), may hold values from -0.125 to 0.125
- w_up: bfloat16 [2048, 8192], P('dp', 'tensor'), may hold values from -0.125 to 0.125
- w_down: bfloat16 [8192, 2048], P('tensor', 'dp'), may hold values from -0.0625 to 0.0625
- w_layer_gate: bfloat16 [2048, 256], P('dp'), may hold values from -0.125 to 0.125
- w_layer_proj: bfloat16 [256, 2048], P(None, 'dp'), may hold values from -0.375 to 0.375
- query_gain: bfloat16 [256], P('dp'), may hold values from 0.19921875 to 0.5
- key_gain: bfloat16 [256], P('dp'), may hold values from 0.19921875 to 0.5
- gain_input: bfloat16 [2048], P('dp'), may hold values from 0.5 to 1.5
- gain_attn_out: bfloat16 [2048], P('dp'), may hold values from 0.5 to 1.5
- gain_laurel: bfloat16 [2048], P('dp'), may hold values from 0.5 to 1.5
- gain_ffw_in: bfloat16 [2048], P('dp'), may hold values from 0.5 to 1.5
- gain_ffw_out: bfloat16 [2048], P('dp'), may hold values from 0.5 to 1.5
- gain_layer_out: bfloat16 [2048], P('dp'), may hold values from 0.5 to 1.5
- out_grad: bfloat16 [8192, 2048], P(('dp', 'tensor')), may hold values from -6 to 6
Outputs:
- output: bfloat16 [8192, 2048], P(('dp', 'tensor'))
- grad_tokens: float32 [8192, 2048], P(('dp', 'tensor'))
- grad_layer_input: float32 [8192, 256], P(('dp', 'tensor'))
- grad_w_query: float32 [2048, 2048], P('dp', 'tensor')
- grad_w_key: float32 [2048, 512], P('dp', 'tensor')
- grad_w_value: float32 [2048, 512], P('dp', 'tensor')
- grad_w_output: float32 [2048, 2048], P('tensor', 'dp')
- grad_w_left: float32 [2048, 64], P('dp')
- grad_w_right: float32 [64, 2048], P(None, 'dp')
- grad_w_gate: float32 [2048, 8192], P('dp', 'tensor')
- grad_w_up: float32 [2048, 8192], P('dp', 'tensor')
- grad_w_down: float32 [8192, 2048], P('tensor', 'dp')
- grad_w_layer_gate: float32 [2048, 256], P('dp')
- grad_w_layer_proj: float32 [256, 2048], P(None, 'dp')
- grad_query_gain: float32 [256], P('dp')
- grad_key_gain: float32 [256], P('dp')
- grad_gain_input: float32 [2048], P('dp')
- grad_gain_attn_out: float32 [2048], P('dp')
- grad_gain_laurel: float32 [2048], P('dp')
- grad_gain_ffw_in: float32 [2048], P('dp')
- grad_gain_ffw_out: float32 [2048], P('dp')
- grad_gain_layer_out: float32 [2048], P('dp')
Inputs may be any that keep to these rules, and one draw needn't show every extreme that they name: `block_ids`: in each sequence the block numbers never fall, every number below 64 occurs, a block holds 1 to 256 tokens and one holds exactly 256. `block_table`: entry (r, i, j) is 1 where j == i, and 0 where j > i or j <= i - 2; the others are 0 or 1.
All inputs are finite; a program needn't handle non-finite values.
Results may differ from a plain program's by a relative error of at most 0.02.
Values may be sent and summed in bfloat16 or wider, within the bound.
A program may use at most 256 MiB of HBM per device.

v0:
```python
import jax
import jax.numpy as jnp
from jax import lax
from jax.sharding import PartitionSpec as P

HD = 256


EPS = 1e-06
ROOT_HALF = 0.7071067811865476
NEGATIVE = -1e30


def from_behind(x, axis, by):
    length = lax.axis_size(axis)
    pairs = [(i, i + by) for i in range(length) if 0 <= i + by < length]
    return lax.ppermute(x, axis, pairs)


def norm_gain(values, gains):
    return values * lax.rsqrt(jnp.mean(values * values, axis=-1, keepdims=True) + EPS) * gains


def norm_plain(values):
    return values * lax.rsqrt(jnp.mean(values * values, axis=-1, keepdims=True) + EPS)


def gelu_tanh(values):
    return jax.nn.gelu(values, approximate=True)


def rope_tables(row_count, head_width, first):
    positions = (first + jnp.arange(row_count, dtype=jnp.int32)).astype(jnp.float32)[:, None]
    frequency = 10000.0 ** (-2.0 * jnp.arange(head_width // 2, dtype=jnp.float32) / head_width)
    angles = positions * frequency[None, :]
    return (jnp.cos(angles), jnp.sin(angles))


def rotate(values, cosines, sines):
    half_width = values.shape[-1] // 2
    front_half = values[..., :half_width]
    back_half = values[..., half_width:]
    cos_wide = cosines[:, None, :]
    sin_wide = sines[:, None, :]
    return jnp.concatenate(
        [
            front_half * cos_wide - back_half * sin_wide,
            back_half * cos_wide + front_half * sin_wide,
        ],
        axis=-1,
    )


def to_float(values):
    return values.astype(jnp.float32)


def product(left_in, right_in):
    return jnp.dot(left_in, right_in, preferred_element_type=jnp.float32)


def neighbour(values, step):
    return (
        from_behind(values[0].astype(jnp.bfloat16), "dp", step).astype(jnp.float32),
        from_behind(values[1].astype(jnp.bfloat16), "dp", step).astype(jnp.float32),
    )


def local(
    tokens,
    layer_input,
    block_ids,
    block_table,
    w_query,
    w_key,
    w_value,
    w_output,
    w_left,
    w_right,
    w_gate,
    w_up,
    w_down,
    w_layer_gate,
    w_layer_proj,
    query_gain,
    key_gain,
    gain_input,
    gain_attn_out,
    gain_laurel,
    gain_ffw_in,
    gain_ffw_out,
    gain_layer_out,
    out_grad,
):
    (
        query_full,
        key_full,
        value_full,
        output_full,
        left_full,
        right_full,
        gate_full,
        up_full,
        down_full,
        lgate_full,
        lproj_full,
        query_scale,
        key_scale,
        input_scale,
        attn_scale,
        laurel_scale,
        ffw_in_scale,
        ffw_out_scale,
        layer_scale,
    ) = (
        lax.all_gather(w_query, "dp", axis=0, tiled=True),
        lax.all_gather(w_key, "dp", axis=0, tiled=True),
        lax.all_gather(w_value, "dp", axis=0, tiled=True),
        lax.all_gather(w_output, "dp", axis=1, tiled=True),
        lax.all_gather(w_left, "dp", axis=0, tiled=True),
        lax.all_gather(w_right, "dp", axis=1, tiled=True),
        lax.all_gather(w_gate, "dp", axis=0, tiled=True),
        lax.all_gather(w_up, "dp", axis=0, tiled=True),
        lax.all_gather(w_down, "dp", axis=1, tiled=True),
        lax.all_gather(w_layer_gate, "dp", axis=0, tiled=True),
        lax.all_gather(w_layer_proj, "dp", axis=1, tiled=True),
        lax.all_gather(query_gain, "dp", axis=0, tiled=True),
        lax.all_gather(key_gain, "dp", axis=0, tiled=True),
        lax.all_gather(gain_input, "dp", axis=0, tiled=True),
        lax.all_gather(gain_attn_out, "dp", axis=0, tiled=True),
        lax.all_gather(gain_laurel, "dp", axis=0, tiled=True),
        lax.all_gather(gain_ffw_in, "dp", axis=0, tiled=True),
        lax.all_gather(gain_ffw_out, "dp", axis=0, tiled=True),
        lax.all_gather(gain_layer_out, "dp", axis=0, tiled=True),
    )
    inputs = to_float(tokens)
    normed, input_norm_back = jax.vjp(norm_gain, inputs, to_float(input_scale))
    normed_low = normed.astype(jnp.bfloat16)
    seq_rows = lax.all_gather(normed_low, "tensor", axis=0, tiled=True)
    piece_len = seq_rows.shape[0]
    seq_total = block_ids.shape[1]
    per_seq = seq_total // piece_len
    dp_index = lax.axis_index("dp")
    row_index = dp_index // per_seq
    slot = dp_index % per_seq
    first = slot * piece_len
    has_before = slot > 0
    has_after = slot < per_seq - 1
    query_raw = product(seq_rows, query_full)
    key_raw = product(seq_rows, key_full)
    value_raw = product(seq_rows, value_full)
    cosines, sines = rope_tables(piece_len, HD, first)

    def prepare(query_in, key_in, value_in, query_gains, key_gains):
        query_out = rotate(
            norm_gain(query_in.reshape(piece_len, -1, HD), query_gains), cosines, sines
        )
        key_out = rotate(norm_gain(key_in.reshape(piece_len, -1, HD), key_gains), cosines, sines)
        return (query_out, key_out, norm_plain(value_in.reshape(piece_len, -1, HD)))

    prepared, prepare_backward_pass = jax.vjp(
        prepare, query_raw, key_raw, value_raw, to_float(query_scale), to_float(key_scale)
    )
    query_rot, key_rot, value_nrm = prepared
    heads_local = query_rot.shape[1]
    kv_local = key_rot.shape[1]
    group = heads_local // kv_local
    query_low = query_rot.astype(jnp.bfloat16).reshape(piece_len, kv_local, group, HD)
    key_low = key_rot.astype(jnp.bfloat16)
    value_low = value_nrm.astype(jnp.bfloat16)
    before_key, before_value = neighbour((to_float(key_low), to_float(value_low)), 1)
    after_key, after_value = neighbour((to_float(key_low), to_float(value_low)), -1)
    keys_all = jnp.concatenate(
        [before_key.astype(jnp.bfloat16), key_low, after_key.astype(jnp.bfloat16)], axis=0
    )
    values_all = jnp.concatenate(
        [before_value.astype(jnp.bfloat16), value_low, after_value.astype(jnp.bfloat16)], axis=0
    )
    block_count = block_table.shape[-1]
    ids_row = lax.dynamic_index_in_dim(block_ids, row_index, 0, keepdims=False)
    table_row = lax.dynamic_index_in_dim(block_table, row_index, 0, keepdims=False)
    own_ids = lax.dynamic_slice_in_dim(ids_row, first, piece_len, 0)
    before_ids = lax.dynamic_slice_in_dim(ids_row, jnp.maximum(first - piece_len, 0), piece_len, 0)
    before_ids = jnp.where(has_before, before_ids, -1)
    after_ids = lax.dynamic_slice_in_dim(
        ids_row, jnp.minimum(first + piece_len, seq_total - piece_len), piece_len, 0
    )
    after_ids = jnp.where(has_after, after_ids, -1)
    key_ids = jnp.concatenate([before_ids, own_ids, after_ids], axis=0)
    numbers = jnp.arange(block_count, dtype=jnp.int32)
    query_member = (own_ids[:, None] == numbers[None, :]).astype(jnp.float32)
    key_member = (key_ids[:, None] == numbers[None, :]).astype(jnp.float32)
    reach = product(query_member, table_row.astype(jnp.float32))
    query_block = min(512, piece_len)
    block_total = piece_len // query_block
    offsets = jnp.arange(block_total, dtype=jnp.int32) * query_block

    def scores_for():
        allowed = product(reach, key_member.T) > 0.5
        scores = jnp.einsum(
            "qkgd,ckd->kgqc", query_low, keys_all, preferred_element_type=jnp.float32
        )
        return (query_low, jnp.where(allowed[None, None], scores, NEGATIVE))

    def attend(offset):
        query_part, scores = scores_for()
        highest = jnp.max(scores, axis=-1, keepdims=True)
        weights_exp = jnp.exp(scores - highest)
        totals = jnp.sum(weights_exp, axis=-1, keepdims=True)
        probs_low = (weights_exp / totals).astype(jnp.bfloat16)
        attended = jnp.einsum(
            "kgqc,ckd->qkgd", probs_low, values_all, preferred_element_type=jnp.float32
        )
        return (attended, highest + jnp.log(totals))

    attended, log_totals = lax.map(attend, offsets)
    heads_low = attended.reshape(piece_len, heads_local * HD).astype(jnp.bfloat16)
    attn_out = lax.psum_scatter(
        product(heads_low, output_full), "tensor", scatter_dimension=0, tiled=True
    )
    attn_normed, attn_norm_back = jax.vjp(norm_gain, attn_out, to_float(attn_scale))
    left_low = product(normed_low, left_full).astype(jnp.bfloat16)
    right_out = product(left_low, right_full)
    laurel_normed, laurel_back = jax.vjp(norm_gain, right_out, to_float(laurel_scale))
    mixed = (inputs + attn_normed + (normed + laurel_normed)) * ROOT_HALF
    ffw_normed, ffw_norm_back = jax.vjp(norm_gain, mixed, to_float(ffw_in_scale))
    ffw_low = ffw_normed.astype(jnp.bfloat16)
    ffw_rows = lax.all_gather(ffw_low, "tensor", axis=0, tiled=True)
    gate_raw = product(ffw_rows, gate_full)
    up_raw = product(ffw_rows, up_full)

    def activate(gate_in, up_in):
        return gelu_tanh(gate_in) * up_in

    hidden, activate_back = jax.vjp(activate, gate_raw, up_raw)
    hidden_low = hidden.astype(jnp.bfloat16)
    ffw_out = lax.psum_scatter(
        product(hidden_low, down_full), "tensor", scatter_dimension=0, tiled=True
    )
    ffw_out_normed, ffw_out_back = jax.vjp(norm_gain, ffw_out, to_float(ffw_out_scale))
    block_mid = mixed + ffw_out_normed
    mid_low = block_mid.astype(jnp.bfloat16)
    layer_pre = product(mid_low, lgate_full)

    def layer_gate_fn(pre_values, per_layer):
        return gelu_tanh(pre_values) * per_layer

    gated, gated_back = jax.vjp(layer_gate_fn, layer_pre, to_float(layer_input))
    gated_low = gated.astype(jnp.bfloat16)
    layer_proj = product(gated_low, lproj_full)
    proj_normed, proj_back = jax.vjp(norm_gain, layer_proj, to_float(layer_scale))
    result = block_mid + proj_normed
    grad_out = to_float(out_grad)
    d_proj, d_layer_scale = proj_back(grad_out)
    d_proj_low = d_proj.astype(jnp.bfloat16)
    d_gated = product(d_proj_low, lproj_full.T)
    grad_lproj = product(gated_low.T, d_proj_low)
    d_pre, grad_layer_input = gated_back(d_gated)
    d_pre_low = d_pre.astype(jnp.bfloat16)
    d_mid = grad_out + product(d_pre_low, lgate_full.T)
    grad_lgate = product(mid_low.T, d_pre_low)
    d_ffw_out, d_ffw_out_scale = ffw_out_back(d_mid)
    d_ffw_low = d_ffw_out.astype(jnp.bfloat16)
    d_ffw_rows = lax.all_gather(d_ffw_low, "tensor", axis=0, tiled=True)
    d_hidden = product(d_ffw_rows, down_full.T)
    d_gate, d_up = activate_back(d_hidden)
    d_gate_low = d_gate.astype(jnp.bfloat16)
    d_up_low = d_up.astype(jnp.bfloat16)
    d_ffw_normed = lax.psum_scatter(
        (product(d_gate_low, gate_full.T) + product(d_up_low, up_full.T)).astype(jnp.bfloat16),
        "tensor",
        scatter_dimension=0,
        tiled=True,
    ).astype(jnp.float32)
    d_mixed_extra, d_ffw_in_scale = ffw_norm_back(d_ffw_normed)
    d_branch = (d_mid + d_mixed_extra) * ROOT_HALF
    d_right, d_laurel_scale = laurel_back(d_branch)
    d_right_low = d_right.astype(jnp.bfloat16)
    grad_right = product(left_low.T, d_right_low)
    d_left_low = product(d_right_low, right_full.T).astype(jnp.bfloat16)
    grad_left = product(normed_low.T, d_left_low)
    d_normed = d_branch + product(d_left_low, left_full.T)
    d_attn, d_attn_scale = attn_norm_back(d_branch)
    d_attn_low = d_attn.astype(jnp.bfloat16)
    d_attn_rows = lax.all_gather(d_attn_low, "tensor", axis=0, tiled=True)
    grad_output_w = product(heads_low.T, d_attn_rows)
    d_heads = (
        product(d_attn_rows, output_full.T)
        .astype(jnp.bfloat16)
        .reshape(piece_len, kv_local, group, HD)
    )

    def attn_back(carry, items):
        key_acc, value_acc = carry
        offset, log_part = items
        query_part, scores = scores_for()
        probs = jnp.exp(scores - log_part)
        probs_low = probs.astype(jnp.bfloat16)
        value_acc = value_acc + jnp.einsum(
            "kgqc,qkgd->ckd", probs_low, d_heads, preferred_element_type=jnp.float32
        )
        d_probs = jnp.einsum(
            "qkgd,ckd->kgqc", d_heads, values_all, preferred_element_type=jnp.float32
        )
        deltas = jnp.sum(probs * d_probs, axis=-1, keepdims=True)
        d_scores = (probs * (d_probs - deltas)).astype(jnp.bfloat16)
        key_acc = key_acc + jnp.einsum(
            "kgqc,qkgd->ckd", d_scores, query_part, preferred_element_type=jnp.float32
        )
        d_query_part = jnp.einsum(
            "kgqc,ckd->qkgd", d_scores, keys_all, preferred_element_type=jnp.float32
        )
        return ((key_acc, value_acc), d_query_part)

    zero_kv = jnp.zeros((3 * piece_len, kv_local, HD), jnp.float32)
    (d_keys_all, d_values_all), d_query_blocks = lax.scan(
        attn_back, (zero_kv, zero_kv), (offsets, log_totals)
    )
    from_after_key, from_after_value = neighbour(
        (d_keys_all[:piece_len], d_values_all[:piece_len]), -1
    )
    from_before_key, from_before_value = neighbour(
        (d_keys_all[2 * piece_len :], d_values_all[2 * piece_len :]), 1
    )
    d_key_rot = d_keys_all[piece_len : 2 * piece_len] + from_after_key + from_before_key
    d_value_nrm = d_values_all[piece_len : 2 * piece_len] + from_after_value + from_before_value
    d_query_rot = d_query_blocks.reshape(piece_len, heads_local, HD)
    (
        query_unnormed_gradient,
        key_unnormed_gradient,
        value_unnormed_gradient,
        query_scale_gradient,
        key_scale_gradient,
    ) = prepare_backward_pass((d_query_rot, d_key_rot, d_value_nrm))
    d_query_low = query_unnormed_gradient.astype(jnp.bfloat16)
    d_key_low = key_unnormed_gradient.astype(jnp.bfloat16)
    d_value_low = value_unnormed_gradient.astype(jnp.bfloat16)
    grad_query = product(seq_rows.T, d_query_low)
    grad_key = product(seq_rows.T, d_key_low)
    grad_value = product(seq_rows.T, d_value_low)
    query_part = d_query_low
    d_normed = d_normed + lax.psum_scatter(
        (
            product(query_part, query_full.T)
            + product(d_key_low, key_full.T)
            + product(d_value_low, value_full.T)
        ).astype(jnp.bfloat16),
        "tensor",
        scatter_dimension=0,
        tiled=True,
    ).astype(jnp.float32)
    d_inputs_extra, d_input_scale = input_norm_back(d_normed)
    grad_tokens = d_branch + d_inputs_extra
    (
        sum_left,
        sum_right,
        sum_lgate,
        sum_lproj,
        sum_qscale,
        key_scale_gradient_sum,
        sum_input,
        sum_attn,
        sum_laurel,
        sum_ffw_in,
        sum_ffw_out,
        sum_layer,
    ) = (
        lax.psum(grad_left.astype(jnp.bfloat16), "tensor").astype(jnp.float32),
        lax.psum(grad_right.astype(jnp.bfloat16), "tensor").astype(jnp.float32),
        lax.psum(grad_lgate.astype(jnp.bfloat16), "tensor").astype(jnp.float32),
        lax.psum(grad_lproj.astype(jnp.bfloat16), "tensor").astype(jnp.float32),
        lax.psum(query_scale_gradient.astype(jnp.bfloat16), "tensor").astype(jnp.float32),
        lax.psum(key_scale_gradient.astype(jnp.bfloat16), "tensor").astype(jnp.float32),
        lax.psum(d_input_scale.astype(jnp.bfloat16), "tensor").astype(jnp.float32),
        lax.psum(d_attn_scale.astype(jnp.bfloat16), "tensor").astype(jnp.float32),
        lax.psum(d_laurel_scale.astype(jnp.bfloat16), "tensor").astype(jnp.float32),
        lax.psum(d_ffw_in_scale.astype(jnp.bfloat16), "tensor").astype(jnp.float32),
        lax.psum(d_ffw_out_scale.astype(jnp.bfloat16), "tensor").astype(jnp.float32),
        lax.psum(d_layer_scale.astype(jnp.bfloat16), "tensor").astype(jnp.float32),
    )
    (
        out_query,
        out_key,
        out_value,
        out_output,
        out_left,
        out_right,
        out_lgate,
        out_lproj,
        out_qscale,
        key_scale_output,
        out_input,
        out_attn,
        out_laurel,
        out_ffw_in,
        out_ffw_out,
        out_layer,
    ) = (
        lax.psum_scatter(grad_query, "dp", scatter_dimension=0, tiled=True),
        lax.psum_scatter(grad_key, "dp", scatter_dimension=0, tiled=True),
        lax.psum_scatter(grad_value, "dp", scatter_dimension=0, tiled=True),
        lax.psum_scatter(grad_output_w, "dp", scatter_dimension=1, tiled=True),
        lax.psum_scatter(sum_left, "dp", scatter_dimension=0, tiled=True),
        lax.psum_scatter(sum_right, "dp", scatter_dimension=1, tiled=True),
        lax.psum_scatter(sum_lgate, "dp", scatter_dimension=0, tiled=True),
        lax.psum_scatter(sum_lproj, "dp", scatter_dimension=1, tiled=True),
        lax.psum_scatter(sum_qscale, "dp", scatter_dimension=0, tiled=True),
        lax.psum_scatter(key_scale_gradient_sum, "dp", scatter_dimension=0, tiled=True),
        lax.psum_scatter(sum_input, "dp", scatter_dimension=0, tiled=True),
        lax.psum_scatter(sum_attn, "dp", scatter_dimension=0, tiled=True),
        lax.psum_scatter(sum_laurel, "dp", scatter_dimension=0, tiled=True),
        lax.psum_scatter(sum_ffw_in, "dp", scatter_dimension=0, tiled=True),
        lax.psum_scatter(sum_ffw_out, "dp", scatter_dimension=0, tiled=True),
        lax.psum_scatter(sum_layer, "dp", scatter_dimension=0, tiled=True),
    )
    grad_gate = product(ffw_rows.T, d_gate_low)
    grad_up = product(ffw_rows.T, d_up_low)
    grad_down = product(hidden_low.T, d_ffw_rows)
    out_gate, out_up, out_down = (
        lax.psum_scatter(grad_gate, "dp", scatter_dimension=0, tiled=True),
        lax.psum_scatter(grad_up, "dp", scatter_dimension=0, tiled=True),
        lax.psum_scatter(grad_down, "dp", scatter_dimension=1, tiled=True),
    )
    return (
        result.astype(jnp.bfloat16),
        grad_tokens,
        grad_layer_input,
        out_query,
        out_key,
        out_value,
        out_output,
        out_left,
        out_right,
        out_gate,
        out_up,
        out_down,
        out_lgate,
        out_lproj,
        out_qscale,
        key_scale_output,
        out_input,
        out_attn,
        out_laurel,
        out_ffw_in,
        out_ffw_out,
        out_layer,
    )


def solution(mesh):
    placed = (
        P(("dp", "tensor"), None),
        P(("dp", "tensor"), None),
        P(),
        P(),
        P("dp", "tensor"),
        P("dp", "tensor"),
        P("dp", "tensor"),
        P("tensor", "dp"),
        P("dp", None),
        P(None, "dp"),
        P("dp", "tensor"),
        P("dp", "tensor"),
        P("tensor", "dp"),
        P("dp", None),
        P(None, "dp"),
        P("dp"),
        P("dp"),
        P("dp"),
        P("dp"),
        P("dp"),
        P("dp"),
        P("dp"),
        P("dp"),
        P(("dp", "tensor"), None),
    )
    return jax.shard_map(
        local,
        mesh=mesh,
        in_specs=placed,
        out_specs=(
            P(("dp", "tensor"), None),
            P(("dp", "tensor"), None),
            P(("dp", "tensor"), None),
            P("dp", "tensor"),
            P("dp", "tensor"),
            P("dp", "tensor"),
            P("tensor", "dp"),
            P("dp", None),
            P(None, "dp"),
            P("dp", "tensor"),
            P("dp", "tensor"),
            P("tensor", "dp"),
            P("dp", None),
            P(None, "dp"),
            P("dp"),
            P("dp"),
            P("dp"),
            P("dp"),
            P("dp"),
            P("dp"),
            P("dp"),
            P("dp"),
        ),
        check_vma=False,
    )
```

profile of v0, /device:TPU:0, one launch (start us, length us, event | category | flops | bytes accessed | tf_op | source)
XLA Modules:
  0.0 2809.4 jit_solution(7324540838034577584)
XLA Ops:
  8.0 23.1 all-gather
  41.0 29.8 %all-reduce.15 = (bf16[256]{0:T(256)(128)(2,1)S(1)}, bf16[256]{0:T(256)(128)(2,1)S(1)}) all-reduce(bf16[256]{0:T(256)(128)(2,1)S(1)} %dynamic-update-slice.1, bf16[256]{0:T(256)(128)(2,1)S(1)} %dynamic-update-slice), channel_id=1, replica_groups=mesh['dp'=16,'tensor'=2] {'dp'}, use_global_device_ids=true, to_apply=%add.5 | all-reduce | flops 512 | bytes 2048
  74.8 9.8 all-gather.20.cloned.1.call-done
  90.2 3.7 collective-permute-start
  94.0 30.8 %all-gather.24.cloned.1.call-done = bf16[2048,256]{1,0:T(8,128)(2,1)} async-done(((bf16[128,256]{1,0:T(8,128)(2,1)}), bf16[2048,256]{1,0:T(8,128)(2,1)}) %all-gather.24.cloned.1.call-update) | async-done | bytes 1048592 | tf_op jit(solution)/shard_map/all_gather | solution.py:117
  131.6 3.8 collective-permute-start.2
  135.3 44.3 %all-gather.26.cloned.1.call-done = bf16[2048,1024]{1,0:T(8,128)(2,1)} async-done(((bf16[128,1024]{1,0:T(8,128)(2,1)}), bf16[2048,1024]{1,0:T(8,128)(2,1)}) %all-gather.26.cloned.1.call-update) | async-done | bytes 4194320 | tf_op jit(solution)/shard_map/all_gather | solution.py:116
  179.6 5.2 fusion.127
  193.0 3.3 fusion.4
  201.0 5.8 fusion.51
  206.9 26.5 all-gather.28.cloned.1.call-done
  233.3 6.9 fusion.128
  240.9 18.9 all-gather.1
  259.9 17.4 all-gather.2
  277.4 18.6 all-gather.3
  296.0 18.3 all_gather.78
  314.2 19.3 all_gather.79
  345.4 28.4 %all-gather.30.cloned.1.call-done = bf16[512,2048]{1,0:T(8,128)(2,1)} async-done(((bf16[256,2048]{1,0:T(8,128)(2,1)}), bf16[512,2048]{1,0:T(8,128)(2,1)}) %all-gather.30.cloned.1.call-update) | async-done | bytes 2097168 | tf_op jit(solution)/shard_map/all_gather | solution.py:228
  373.7 129.3 %all-gather.32.cloned.1.call-done = bf16[2048,4096]{1,0:T(8,128)(2,1)} async-done(((bf16[128,4096]{1,0:T(8,128)(2,1)}), bf16[2048,4096]{1,0:T(8,128)(2,1)}) %all-gather.32.cloned.1.call-update) | async-done | bytes 16777232 | tf_op jit(solution)/shard_map/all_gather | solution.py:122
  503.0 15.0 fusion.129
  518.1 112.5 %all-gather.34.cloned.1.call-done = bf16[2048,4096]{1,0:T(8,128)(2,1)} async-done(((bf16[128,4096]{1,0:T(8,128)(2,1)}), bf16[2048,4096]{1,0:T(8,128)(2,1)}) %all-gather.34.cloned.1.call-update) | async-done | bytes 16777232 | tf_op jit(solution)/shard_map/all_gather | solution.py:123
  630.5 20.0 multiply_convert_fusion.1
  650.5 110.8 %all-gather.36.cloned.1.call-done = bf16[4096,2048]{1,0:T(8,128)(2,1)} async-done(((bf16[4096,128]{1,0:T(8,128)(2,1)}), bf16[4096,2048]{1,0:T(8,128)(2,1)}) %all-gather.36.cloned.1.call-update) | async-done | bytes 16777232 | tf_op jit(solution)/shard_map/all_gather | solution.py:124
  761.3 15.0 fusion.130
  777.8 19.1 all-gather.4
  796.9 17.5 all-gather.5
  815.0 14.0 reduce-scatter.18.cloned.1.call-done
  832.9 36.1 %all-gather.38.cloned.1.call-done = bf16[2048,256]{1,0:T(8,128)(2,1)} async-done(((bf16[128,256]{1,0:T(8,128)(2,1)}), bf16[2048,256]{1,0:T(8,128)(2,1)}) %all-gather.38.cloned.1.call-update) | async-done | bytes 1048592 | tf_op jit(solution)/shard_map/all_gather | solution.py:125
  871.3 35.6 %all-gather.40.cloned.1.call-done = bf16[256,2048]{1,0:T(8,128)(2,1)} async-done(((bf16[256,128]{1,0:T(8,128)(2,1)}), bf16[256,2048]{1,0:T(8,128)(2,1)}) %all-gather.40.cloned.1.call-update) | async-done | bytes 1048592 | tf_op jit(solution)/shard_map/all_gather | solution.py:126
  918.9 32.7 %all-gather.42.cloned.1.call-done = bf16[512,2048]{1,0:T(8,128)(2,1)} async-done(((bf16[256,2048]{1,0:T(8,128)(2,1)}), bf16[512,2048]{1,0:T(8,128)(2,1)}) %all-gather.42.cloned.1.call-update) | async-done | bytes 2097168 | tf_op jit(solution)/shard_map/all_gather | solution.py:264
  951.6 21.7 multiply_convert_fusion
  973.3 15.4 fusion.131
  988.7 16.1 add_convert_fusion.1
  1005.5 31.3 %reduce-scatter.20.cloned.1.call-done = bf16[256,2048]{1,0:T(8,128)(2,1)} async-done(((bf16[512,2048]{1,0:T(8,128)(2,1)}), bf16[256,2048]{1,0:T(8,128)(2,1)}) %reduce-scatter.20.cloned.1.call-update) | async-done | bytes 1048592 | tf_op jit(solution)/shard_map/reduce_scatter | solution.py:269
  1039.7 4.7 multiply_reduce_fusion.1
  1054.8 25.5 all-gather.44.cloned.1.call-done
  1080.3 5.2 convolution_convert_fusion.4
  1086.6 9.8 fusion.126
  1098.0 3.3 collective-permute-start.7
  1101.3 9.5 fusion
  1110.8 7.0 fusion.16
  1117.9 3.1 fusion.125
  1121.0 3.9 convolution_bitcast_fusion.1
  1130.1 3.8 collective-permute-start.5
  1134.0 4.6 fusion.132
  1146.2 11.5 all-reduce.20.cloned.1.call-done
  1171.8 7.3 fusion.137
  1180.3 5.7 fusion.134
  1187.7 18.2 fusion.140
  1207.4 17.6 fusion.139
  1225.1 17.8 fusion.138
  1244.9 3.5 fusion.35
  1248.5 6.9 all-reduce.16
  1255.4 59.8 %all-reduce.14 = (f32[256]{0:T(256)S(1)}, f32[256]{0:T(256)S(1)}, f32[2048]{0:T(1024)S(1)}, f32[2048]{0:T(1024)S(1)}, f32[2048]{0:T(1024)S(1)}, /*index=5*/f32[2...) all-reduce(bf16[256]{0:T(256)(128)(2,1)S(1)} %get-tuple-element.107, ...), channel_id=17, replica_groups=mesh['dp'=16,'tensor'=2] {'dp'}, use_global_device_ids=true, to_apply=%region_42.43.clone | all-reduce | flops 12800 | bytes 76800
  1319.8 3.6 fusion.46
  1323.4 53.4 %reduce-scatter.28.cloned.1.call-done = f32[128,256]{1,0:T(8,128)} async-done(((f32[2048,256]{1,0:T(8,128)}), f32[128,256]{1,0:T(8,128)}) %reduce-scatter.28.cloned.1.call-update) | async-done | bytes 131088 | tf_op jit(solution)/shard_map/reduce_scatter | solution.py:401
  1376.9 64.9 %reduce-scatter.26.cloned.1.call-done = f32[128,256]{1,0:T(8,128)} async-done(((f32[2048,256]{1,0:T(8,128)}), f32[128,256]{1,0:T(8,128)}) %reduce-scatter.26.cloned.1.call-update) | async-done | bytes 131088 | tf_op jit(solution)/shard_map/reduce_scatter | solution.py:400
  1441.7 65.4 %reduce-scatter.42.cloned.1.call-done = f32[128,256]{1,0:T(8,128)} async-done(((f32[2048,256]{1,0:T(8,128)}), f32[128,256]{1,0:T(8,128)}) %reduce-scatter.42.cloned.1.call-update) | async-done | bytes 131088 | tf_op jit(solution)/shard_map/reduce_scatter | solution.py:405
  1507.1 64.8 %reduce-scatter.44.cloned.1.call-done = f32[256,128]{1,0:T(8,128)} async-done(((f32[256,2048]{1,0:T(8,128)}), f32[256,128]{1,0:T(8,128)}) %reduce-scatter.44.cloned.1.call-update) | async-done | bytes 131088 | tf_op jit(solution)/shard_map/reduce_scatter | solution.py:406
  1571.9 109.1 %reduce-scatter.30.cloned.1.call-done = f32[1024,128]{1,0:T(8,128)} async-done(((f32[1024,2048]{1,0:T(8,128)}), f32[1024,128]{1,0:T(8,128)}) %reduce-scatter.30.cloned.1.call-update) | async-done | bytes 524304 | tf_op jit(solution)/shard_map/reduce_scatter | solution.py:402
  1681.0 109.5 %reduce-scatter.24.cloned.1.call-done = f32[128,1024]{1,0:T(8,128)} async-done(((f32[2048,1024]{1,0:T(8,128)}), f32[128,1024]{1,0:T(8,128)}) %reduce-scatter.24.cloned.1.call-update) | async-done | bytes 524304 | tf_op jit(solution)/shard_map/reduce_scatter | solution.py:399
  1790.5 337.9 %reduce-scatter.40.cloned.1.call-done = f32[4096,128]{1,0:T(8,128)} async-done(((f32[4096,2048]{1,0:T(8,128)}), f32[4096,128]{1,0:T(8,128)}) %reduce-scatter.40.cloned.1.call-update) | async-done | bytes 2097168 | tf_op jit(solution)/shard_map/reduce_scatter | solution.py:422
  2128.4 337.0 %reduce-scatter.38.cloned.1.call-done = f32[128,4096]{1,0:T(8,128)} async-done(((f32[2048,4096]{1,0:T(8,128)}), f32[128,4096]{1,0:T(8,128)}) %reduce-scatter.38.cloned.1.call-update) | async-done | bytes 2097168 | tf_op jit(solution)/shard_map/reduce_scatter | solution.py:421
  2465.4 337.2 %reduce-scatter.36.cloned.1.call-done = f32[128,4096]{1,0:T(8,128)} async-done(((f32[2048,4096]{1,0:T(8,128)}), f32[128,4096]{1,0:T(8,128)}) %reduce-scatter.36.cloned.1.call-update) | async-done | bytes 2097168 | tf_op jit(solution)/shard_map/reduce_scatter | solution.py:420
  (450 shorter events, 123.5 us)
Async XLA Ops:
  7.2 67.6 %all-gather.22.cloned.1.call-start = ((), (), s32[]{:S(2)}) async-start(), calls=%async_computation.16 | async-start | bytes 1114112 | tf_op jit(solution)/shard_map/all_gather | solution.py:118
  7.9 76.7 %all-gather.20.cloned.1.call-start = ((), (), s32[]{:S(2)}) async-start(), calls=%async_computation.15 | async-start | bytes 3145728 | tf_op jit(solution)/shard_map/all_gather | solution.py:139
  31.1 307.3 %copy-start.59 = (f32[16,1,128]{2,1,0:T(1,128)}, f32[16,1,128]{2,1,0:T(1,128)S(1)}, u32[]{:S(2)}) copy-start(f32[16,1,128]{2,1,0:T(1,128)S(1)} %convert_element_type.350) | copy-start | bytes 24580
  33.2 38.2 %copy-start.128 = (s32[1,64,64]{2,1,0:T(8,128)S(1)}, s32[1,64,64]{2,1,0:T(8,128)}, u32[]{:S(2)}) copy-start(s32[1,64,64]{2,1,0:T(8,128)} %param.27) | copy-start | bytes 49156
  36.4 88.4 %all-gather.24.cloned.1.call-start = ((), (), s32[]{:S(2)}) async-start(), calls=%async_computation.17 | async-start | bytes 1114112 | tf_op jit(solution)/shard_map/all_gather | solution.py:117
  37.1 142.5 %all-gather.26.cloned.1.call-start = ((), (), s32[]{:S(2)}) async-start(), calls=%async_computation.18 | async-start | bytes 4456448 | tf_op jit(solution)/shard_map/all_gather | solution.py:116
  37.7 195.7 %all-gather.28.cloned.1.call-start = ((), (), s32[]{:S(2)}) async-start(), calls=%async_computation.19 | async-start | bytes 4456448 | tf_op jit(solution)/shard_map/all_gather | solution.py:119
  38.3 297.6 %reduce-scatter.16.cloned.1.call-start = ((), (), s32[]{:S(2)}) async-start(), calls=%async_computation.20 | async-start | bytes 6291456 | tf_op jit(solution)/shard_map/reduce_scatter | solution.py:218
  71.4 55.4 %copy-start.108 = (f32[256]{0:T(256)}, f32[256]{0:T(256)S(1)}, u32[]{:S(2)}) copy-start(f32[256]{0:T(256)S(1)} %convert_element_type.280) | copy-start | bytes 3076
  73.7 124.9 %copy-start.16 = (pred[512,1536]{0,1:T(8,128)(4,1)}, pred[512,1536]{0,1:T(8,128)(4,1)S(1)}, u32[]{:S(2)}) copy-start(pred[512,1536]{0,1:T(8,128)(4,1)S(1)} %copy.111) | copy-start | bytes 2359300
  73.7 54.0 %copy-start.117 = (f32[128]{0:T(128)}, f32[128]{0:T(128)S(1)}, u32[]{:S(2)}) copy-start(f32[128]{0:T(128)S(1)} %multiply_power_fusion) | copy-start | bytes 1540
  73.8 53.9 %copy-start.71 = (f32[512]{0:T(512)}, f32[512]{0:T(512)S(1)}, u32[]{:S(2)}) copy-start(f32[512]{0:T(512)S(1)} %add_convert_fusion.4) | copy-start | bytes 6148
  74.8 117.3 %copy-start.29 = (f32[512,128]{1,0:T(8,128)}, f32[512,128]{1,0:T(8,128)S(1)}, u32[]{:S(2)}) copy-start(f32[512,128]{1,0:T(8,128)S(1)} %get-tuple-element.145) | copy-start | bytes 786436
  74.8 117.3 %copy-start.31 = (f32[512,128]{1,0:T(8,128)}, f32[512,128]{1,0:T(8,128)S(1)}, u32[]{:S(2)}) copy-start(f32[512,128]{1,0:T(8,128)S(1)} %get-tuple-element.146) | copy-start | bytes 786436
  84.6 40.2 %copy-start.14 = (bf16[512,2048]{1,0:T(8,128)(2,1)S(1)}, bf16[512,2048]{1,0:T(8,128)(2,1)}, u32[]{:S(2)}) copy-start(bf16[512,2048]{1,0:T(8,128)(2,1)} %all-gather.20.cloned.1.call-done) | copy-start | bytes 6291460
  87.4 39.4 %copy-start.113 = (f32[512]{0:T(512)}, f32[512]{0:T(512)S(1)}, u32[]{:S(2)}) copy-start(f32[512]{0:T(512)S(1)} %get-tuple-element.157) | copy-start | bytes 6148
  87.4 39.4 %copy-start.81 = (f32[512]{0:T(512)}, f32[512]{0:T(512)S(1)}, u32[]{:S(2)}) copy-start(f32[512]{0:T(512)S(1)} %fusion.102) | copy-start | bytes 6148
  88.9 109.7 %collective-permute-start.1 = (bf16[512,1,256]{0,2,1:T(8,128)(2,1)}, bf16[512,1,256]{0,2,1:T(8,128)(2,1)}, u32[]{:S(2)}, u32[]{:S(2)}) collective-permute-start(bf16[512,1,256]{0,2,1:T(8,128)(2,1)} %fusion.91), channel_id=1, source_target_pairs={{2,0},{4,2},{6,4},{8,6},{10,8},{12,10},{14,12},{16,14},{18,16},{20... | collective-permute-start | bytes 786440 | tf_op jit(solution)/shard_map/ppermute | solution.py:17
  90.2 108.4 %collective-permute-start = (bf16[512,1,256]{0,2,1:T(8,128)(2,1)}, bf16[512,1,256]{0,2,1:T(8,128)(2,1)}, u32[]{:S(2)}, u32[]{:S(2)}) collective-permute-start(bf16[512,1,256]{0,2,1:T(8,128)(2,1)} %fusion.91), channel_id=1, source_target_pairs={{0,2},{2,4},{4,6},{6,8},{8,10},{10,12},{12,14},{14,16},{16,18},{18... | collective-permute-start | bytes 786440 | tf_op jit(solution)/shard_map/ppermute | solution.py:17
  128.9 63.6 %copy-start.49 = (bf16[512,1,128]{0,2,1:T(8,128)(2,1)}, bf16[512,1,128]{0,2,1:T(8,128)(2,1)S(1)}, u32[]{:S(2)}) copy-start(bf16[512,1,128]{0,2,1:T(8,128)(2,1)S(1)} %get-tuple-element.138) | copy-start | bytes 393220
  130.3 62.2 %collective-permute-start.3 = (bf16[512,1,256]{0,2,1:T(8,128)(2,1)}, bf16[512,1,256]{0,2,1:T(8,128)(2,1)}, u32[]{:S(2)}, u32[]{:S(2)}) collective-permute-start(bf16[512,1,256]{0,2,1:T(8,128)(2,1)} %pad_maximum_fusion.3), channel_id=1, source_target_pairs={{2,0},{4,2},{6,4},{8,6},{10,8},{12,10},{14,12},{16,14},{18,16},{20... | collective-permute-start | bytes 786440 | tf_op jit(solution)/shard_map/ppermute | solution.py:17
  131.6 60.9 %collective-permute-start.2 = (bf16[512,1,256]{0,2,1:T(8,128)(2,1)}, bf16[512,1,256]{0,2,1:T(8,128)(2,1)}, u32[]{:S(2)}, u32[]{:S(2)}) collective-permute-start(bf16[512,1,256]{0,2,1:T(8,128)(2,1)} %pad_maximum_fusion.3), channel_id=1, source_target_pairs={{0,2},{2,4},{4,6},{6,8},{8,10},{10,12},{12,14},{14,16},{16,18},{18... | collective-permute-start | bytes 786440 | tf_op jit(solution)/shard_map/ppermute | solution.py:17
  240.3 37.1 %copy-start.123 = (bf16[128]{0:T(256)(128)(2,1)S(1)}, bf16[128]{0:T(256)(128)(2,1)}, u32[]{:S(2)}) copy-start(bf16[128]{0:T(256)(128)(2,1)} %param.44) | copy-start | bytes 772
  240.3 55.7 %copy-start.87 = (bf16[128,64]{0,1:T(8,128)(2,1)S(1)}, bf16[128,64]{0,1:T(8,128)(2,1)}, u32[]{:S(2)}) copy-start(bf16[128,64]{0,1:T(8,128)(2,1)} %param.32) | copy-start | bytes 49156
  240.3 74.0 %copy-start.88 = (bf16[64,128]{1,0:T(8,128)(2,1)S(1)}, bf16[64,128]{1,0:T(8,128)(2,1)}, u32[]{:S(2)}) copy-start(bf16[64,128]{1,0:T(8,128)(2,1)} %param.33) | copy-start | bytes 49156
  240.3 93.3 %copy-start.19 = (bf16[256,2048]{1,0:T(8,128)(2,1)S(1)}, bf16[256,2048]{1,0:T(8,128)(2,1)}, u32[]{:S(2)}) copy-start(bf16[256,2048]{1,0:T(8,128)(2,1)} %fusion.33) | copy-start | bytes 3145732
  240.3 133.4 %all-gather.30.cloned.1.call-start = ((), (), s32[]{:S(2)}) async-start(), calls=%async_computation.21 | async-start | bytes 3145728 | tf_op jit(solution)/shard_map/all_gather | solution.py:228
  259.9 78.6 %copy-start.66 = (f32[16,1,128]{2,1,0:T(1,128)}, f32[16,1,128]{2,1,0:T(1,128)S(1)}, u32[]{:S(2)}) copy-start(f32[16,1,128]{2,1,0:T(1,128)S(1)} %convert_element_type.351) | copy-start | bytes 24580
  277.4 61.1 %copy-start.68 = (f32[16,1,128]{2,1,0:T(1,128)}, f32[16,1,128]{2,1,0:T(1,128)S(1)}, u32[]{:S(2)}) copy-start(f32[16,1,128]{2,1,0:T(1,128)S(1)} %convert_element_type.352) | copy-start | bytes 24580
  343.3 159.8 %all-gather.32.cloned.1.call-start = ((), (), s32[]{:S(2)}) async-start(), calls=%async_computation.22 | async-start | bytes 17825792 | tf_op jit(solution)/shard_map/all_gather | solution.py:122
  344.0 286.5 %all-gather.34.cloned.1.call-start = ((), (), s32[]{:S(2)}) async-start(), calls=%async_computation.23 | async-start | bytes 17825792 | tf_op jit(solution)/shard_map/all_gather | solution.py:123
  344.7 416.6 %all-gather.36.cloned.1.call-start = ((), (), s32[]{:S(2)}) async-start(), calls=%async_computation.24 | async-start | bytes 17825792 | tf_op jit(solution)/shard_map/all_gather | solution.py:124
  345.3 483.7 %reduce-scatter.18.cloned.1.call-start = ((), (), s32[]{:S(2)}) async-start(), calls=%async_computation.25 | async-start | bytes 6291456 | tf_op jit(solution)/shard_map/reduce_scatter | solution.py:237
  776.4 92.6 %all-gather.38.cloned.1.call-start = ((), (), s32[]{:S(2)}) async-start(), calls=%async_computation.26 | async-start | bytes 1114112 | tf_op jit(solution)/shard_map/all_gather | solution.py:125
  777.0 130.0 %all-gather.40.cloned.1.call-start = ((), (), s32[]{:S(2)}) async-start(), calls=%async_computation.27 | async-start | bytes 1114112 | tf_op jit(solution)/shard_map/all_gather | solution.py:126
  777.7 173.9 %all-gather.42.cloned.1.call-start = ((), (), s32[]{:S(2)}) async-start(), calls=%async_computation.28 | async-start | bytes 3145728 | tf_op jit(solution)/shard_map/all_gather | solution.py:264
  832.9 74.0 %copy-start.54 = (bf16[256,256]{1,0:T(8,128)(2,1)S(1)}, bf16[256,256]{1,0:T(8,128)(2,1)}, u32[]{:S(2)}) copy-start(bf16[256,256]{1,0:T(8,128)(2,1)} %param.25) | copy-start | bytes 393220
  871.3 37.4 %copy-start.21 = (bf16[256,2048]{1,0:T(8,128)(2,1)S(1)}, bf16[256,2048]{1,0:T(8,128)(2,1)}, u32[]{:S(2)}) copy-start(bf16[256,2048]{1,0:T(8,128)(2,1)} %param.47) | copy-start | bytes 3145732
  918.9 118.0 %reduce-scatter.20.cloned.1.call-start = ((), (), s32[]{:S(2)}) async-start(), calls=%async_computation.29 | async-start | bytes 3145728 | tf_op jit(solution)/shard_map/reduce_scatter | solution.py:269
  1004.8 32.0 %copy-start.99 = (f32[256]{0:T(256)S(1)}, f32[256]{0:T(256)}, u32[]{:S(2)}) copy-start(f32[256]{0:T(256)} %copy-done.98) | copy-start | bytes 3076
  1004.8 34.8 %copy-start.112 = (f32[256]{0:T(256)S(1)}, f32[256]{0:T(256)}, u32[]{:S(2)}) copy-start(f32[256]{0:T(256)} %copy-done.111) | copy-start | bytes 3076
  1004.9 34.8 %copy-start.93 = (f32[256]{0:T(256)S(1)}, f32[256]{0:T(256)}, u32[]{:S(2)}) copy-start(f32[256]{0:T(256)} %copy-done.92) | copy-start | bytes 3076
  1004.9 34.8 %copy-start.96 = (f32[256]{0:T(256)S(1)}, f32[256]{0:T(256)}, u32[]{:S(2)}) copy-start(f32[256]{0:T(256)} %copy-done.95) | copy-start | bytes 3076
  1004.9 34.8 %copy-start.119 = (f32[256]{0:T(256)S(1)}, f32[256]{0:T(256)}, u32[]{:S(2)}) copy-start(f32[256]{0:T(256)} %get-tuple-element.147) | copy-start | bytes 3076
  1004.9 75.4 %all-gather.44.cloned.1.call-start = ((), (), s32[]{:S(2)}) async-start(), calls=%async_computation.30 | async-start | bytes 3145728 | tf_op jit(solution)/shard_map/all_gather | solution.py:285
  1005.5 38.9 %copy-start.70 = (f32[2048]{0:T(1024)}, f32[2048]{0:T(1024)S(1)}, u32[]{:S(2)}) copy-start(f32[2048]{0:T(1024)S(1)} %broadcast_multiply_fusion) | copy-start | bytes 24580
  1047.1 110.7 %all-reduce.20.cloned.1.call-start = ((), (), s32[]{:S(2)}) async-start(), calls=%async_computation.43 | async-start | bytes 5242880 | tf_op jit(solution)/shard_map/psum | solution.py:368
  1054.7 190.0 %reduce-scatter.22.cloned.1.call-start = ((), (), s32[]{:S(2)}) async-start(), calls=%async_computation.31 | async-start | bytes 3145728 | tf_op jit(solution)/shard_map/reduce_scatter | solution.py:342
  1096.5 45.1 %collective-permute-start.6 = (bf16[512,1,256]{0,2,1:T(8,128)(2,1)S(1)}, bf16[512,1,256]{0,2,1:T(8,128)(2,1)S(1)}, u32[]{:S(2)}, u32[]{:S(2)}) collective-permute-start(bf16[512,1,256]{0,2,1:T(8,128)(2,1)S(1)} %get-tuple-element.132), channel_id=1, source_target_pairs={{2,0},{4,2},{6,4},{8,6},{10,8},{12,10},{14,12},{16,14},{18,16},{20... | collective-permute-start | bytes 786440 | tf_op jit(solution)/shard_map/ppermute | solution.py:17
  1098.0 43.6 %collective-permute-start.7 = (bf16[512,1,256]{0,2,1:T(8,128)(2,1)S(1)}, bf16[512,1,256]{0,2,1:T(8,128)(2,1)S(1)}, u32[]{:S(2)}, u32[]{:S(2)}) collective-permute-start(bf16[512,1,256]{0,2,1:T(8,128)(2,1)S(1)} %get-tuple-element.133), channel_id=1, source_target_pairs={{0,2},{2,4},{4,6},{6,8},{8,10},{10,12},{12,14},{14,16},{16,18},{18... | collective-permute-start | bytes 786440 | tf_op jit(solution)/shard_map/ppermute | solution.py:17
  1128.8 9.8 collective-permute-start.4
  1130.1 8.5 collective-permute-start.5
  1146.2 177.3 %reduce-scatter.32.cloned.1.call-start = ((), (), s32[]{:S(2)}) async-start(), calls=%async_computation.36 | async-start | bytes 557056 | tf_op jit(solution)/shard_map/reduce_scatter | solution.py:403
  1159.5 163.9 %reduce-scatter.34.cloned.1.call-start = ((), (), s32[]{:S(2)}) async-start(), calls=%async_computation.37 | async-start | bytes 557056 | tf_op jit(solution)/shard_map/reduce_scatter | solution.py:404
  1161.4 215.5 %reduce-scatter.28.cloned.1.call-start = ((), (), s32[]{:S(2)}) async-start(), calls=%async_computation.34 | async-start | bytes 2228224 | tf_op jit(solution)/shard_map/reduce_scatter | solution.py:401
  1163.6 278.1 %reduce-scatter.26.cloned.1.call-start = ((), (), s32[]{:S(2)}) async-start(), calls=%async_computation.33 | async-start | bytes 2228224 | tf_op jit(solution)/shard_map/reduce_scatter | solution.py:400
  1165.8 341.4 %reduce-scatter.42.cloned.1.call-start = ((), (), s32[]{:S(2)}) async-start(), calls=%async_computation.41 | async-start | bytes 2228224 | tf_op jit(solution)/shard_map/reduce_scatter | solution.py:405
  1168.7 403.2 %reduce-scatter.44.cloned.1.call-start = ((), (), s32[]{:S(2)}) async-start(), calls=%async_computation.42 | async-start | bytes 2228224 | tf_op jit(solution)/shard_map/reduce_scatter | solution.py:406
  1171.7 509.3 %reduce-scatter.30.cloned.1.call-start = ((), (), s32[]{:S(2)}) async-start(), calls=%async_computation.35 | async-start | bytes 8912896 | tf_op jit(solution)/shard_map/reduce_scatter | solution.py:402
  1179.1 611.4 %reduce-scatter.24.cloned.1.call-start = ((), (), s32[]{:S(2)}) async-start(), calls=%async_computation.32 | async-start | bytes 8912896 | tf_op jit(solution)/shard_map/reduce_scatter | solution.py:399
  1186.0 942.4 %reduce-scatter.40.cloned.1.call-start = ((), (), s32[]{:S(2)}) async-start(), calls=%async_computation.40 | async-start | bytes 35651584 | tf_op jit(solution)/shard_map/reduce_scatter | solution.py:422
  1205.8 1259.6 %reduce-scatter.38.cloned.1.call-start = ((), (), s32[]{:S(2)}) async-start(), calls=%async_computation.39 | async-start | bytes 35651584 | tf_op jit(solution)/shard_map/reduce_scatter | solution.py:421
  1225.1 1577.6 %reduce-scatter.36.cloned.1.call-start = ((), (), s32[]{:S(2)}) async-start(), calls=%async_computation.38 | async-start | bytes 35651584 | tf_op jit(solution)/shard_map/reduce_scatter | solution.py:420
  1244.7 75.1 %copy-start.101 = (f32[256]{0:T(256)S(1)}, f32[256]{0:T(256)}, u32[]{:S(2)}) copy-start(f32[256]{0:T(256)} %copy-done.100) | copy-start | bytes 3076
  (108 other events, 431.2 us)
Sparse Core Ops, SparseCore 0:
  10.2 40.6 all-gather.21
  52.4 32.1 all-gather.19
  86.8 37.9 all-gather.23
  126.8 52.7 all-gather.25
  181.6 51.7 all-gather.27
  240.5 52.4 reduce-scatter.15
  343.4 30.3 all-gather.29
  376.1 126.8 all-gather.31
  505.4 125.0 all-gather.33
  632.8 128.5 all-gather.35
  776.5 52.4 reduce-scatter.17
  831.0 37.9 all-gather.37
  871.2 35.7 all-gather.39
  919.0 32.6 all-gather.41
  1005.0 31.8 reduce-scatter.19
  1047.2 33.1 all-gather.43
  1082.8 74.8 all-reduce.19
  1160.4 31.8 reduce-scatter.21
  1196.8 55.7 reduce-scatter.31
  1256.5 54.8 reduce-scatter.33
  1316.2 60.6 reduce-scatter.27
  1381.2 60.5 reduce-scatter.25
  1446.5 60.5 reduce-scatter.41
  1511.3 60.5 reduce-scatter.43
  1577.1 103.8 reduce-scatter.29
  1686.0 104.4 reduce-scatter.23
  1795.8 332.5 reduce-scatter.39
  2133.8 331.5 reduce-scatter.37
  2470.9 331.7 reduce-scatter.35
where the time goes:
time: 2820 us; the launch traced here: 2810 us
  waiting for transfers between devices  2160 us (77%)
  matrix products  259 us (9%)
  blocking collectives  249 us (9%)
  other arithmetic  65.9 us (2%)
  local copies, waits for them, and re-layouts  31.9 us (1%)
    reduce_scatter x1, waiting for transfers between devices, local(): lax.psum_scatter(grad_down, 'dp', scatter_dimension=1, tiled=True)  338 us
    reduce_scatter x1, waiting for transfers between devices, local(): lax.psum_scatter(grad_gate, 'dp', scatter_dimension=0, tiled=True)  337 us
    reduce_scatter x1, waiting for transfers between devices, local(): lax.psum_scatter(grad_up, 'dp', scatter_dimension=0, tiled=True)  337 us
    dot_general x34, matrix products, product(): return jnp.dot(left_in, right_in, preferred_element_type=jnp.float32)  224 us
    all_gather x1, waiting for transfers between devices, local(): lax.all_gather(w_gate, 'dp', axis=0, tiled=True)  129 us
    all_gather x1, waiting for transfers between devices, local(): lax.all_gather(w_up, 'dp', axis=0, tiled=True)  112 us
    all_gather x1, waiting for transfers between devices, local(): lax.all_gather(w_down, 'dp', axis=1, tiled=True)  111 us
    reduce_scatter x1, waiting for transfers between devices, local(): lax.psum_scatter(grad_query, 'dp', scatter_dimension=0, tiled=True)  110 us
  transfers between devices with their start and end apart: 37, of which 24 were waited for; matrix products, arithmetic and copies ran while one was open for 8% of the time, Pallas kernels for 0%

commit v1 on v0

v1 whole, which is shorter than its diff:
```python
import jax
import jax.numpy as jnp
from jax import lax
from jax.sharding import PartitionSpec as P

HD = 256
EPS = 1e-06
ROOT_HALF = 0.7071067811865476
NEGATIVE = -1e30
F32 = jnp.float32
BF16 = jnp.bfloat16


def norm_gain(values, gains):
    return values * lax.rsqrt(jnp.mean(values * values, axis=-1, keepdims=True) + EPS) * gains


def norm_plain(values):
    return values * lax.rsqrt(jnp.mean(values * values, axis=-1, keepdims=True) + EPS)


def gelu_tanh(values):
    return jax.nn.gelu(values, approximate=True)


def rope_tables(positions, head_width):
    positions = positions.astype(F32)[:, None]
    frequency = 10000.0 ** (-2.0 * jnp.arange(head_width // 2, dtype=F32) / head_width)
    angles = positions * frequency[None, :]
    return (jnp.cos(angles), jnp.sin(angles))


def rotate(values, cosines, sines):
    half_width = values.shape[-1] // 2
    front_half = values[..., :half_width]
    back_half = values[..., half_width:]
    cos_wide = cosines[:, None, :]
    sin_wide = sines[:, None, :]
    return jnp.concatenate(
        [
            front_half * cos_wide - back_half * sin_wide,
            back_half * cos_wide + front_half * sin_wide,
        ],
        axis=-1,
    )


def to_float(values):
    return values.astype(F32)


def low(values):
    return values.astype(BF16)


def product(left_in, right_in):
    return jnp.dot(left_in, right_in, preferred_element_type=F32)


def product_t(left_in, right_in):
    return lax.dot_general(left_in, right_in, (((1,), (1,)), ((), ())), preferred_element_type=F32)


def product_l(left_in, right_in):
    return lax.dot_general(left_in, right_in, (((0,), (0,)), ((), ())), preferred_element_type=F32)


def tie(*values):
    return lax.optimization_barrier(values)


class Ring:
    def __init__(self):
        self.devices = lax.axis_size("dp")
        self.chips = self.devices // 2
        order = list(range(0, self.chips, 2)) + list(range(self.chips - 1, 0, -2))
        self.cw = [
            (2 * order[p] + c, 2 * order[(p + 1) % self.chips] + c)
            for p in range(self.chips)
            for c in range(2)
        ]
        self.ccw = [(b, a) for a, b in self.cw]
        self.core_pairs = [(d, d ^ 1) for d in range(self.devices)]
        me = lax.axis_index("dp")
        self.core = lax.rem(me, 2)
        self.chip = me // 2
        self.place = jnp.where(
            lax.rem(self.chip, 2) == 0, self.chip // 2, self.chips - 1 - self.chip // 2
        )

    def chip_at(self, offset):
        place = lax.rem(self.place + offset + self.chips, self.chips)
        return jnp.where(place < self.chips // 2, 2 * place, 2 * (self.chips - 1 - place) + 1)

    def up(self, values):
        return lax.ppermute(values, "dp", self.cw)

    def down(self, values):
        return lax.ppermute(values, "dp", self.ccw)

    def swap(self, values):
        return lax.ppermute(values, "dp", self.core_pairs)


def across(values):
    return lax.ppermute(values, "tensor", [(0, 1), (1, 0)])


class Gather:
    def __init__(self, ring, block):
        self.ring = ring
        self.rows = block.shape[0]
        self.going_up = block
        self.going_down = block
        self.parts = [(0, 0, block)]
        self.step_count = 0

    def step(self):
        ring, half = self.ring, self.ring.chips // 2
        self.step_count += 1
        k = self.step_count
        if k < half:
            self.going_up = ring.up(self.going_up)
            self.going_down = ring.down(self.going_down)
            self.parts += [(-k, 0, self.going_up), (k, 0, self.going_down)]
        else:
            cut = self.rows // 2
            self.going_up = ring.up(self.going_up[:cut])
            self.going_down = ring.down(self.going_down[cut:])
            self.parts += [(half, 0, self.going_up), (half, cut, self.going_down)]

    def after(self, other):
        self.going_up, self.going_down, _ = tie(
            self.going_up, self.going_down, (other.going_up, other.going_down)
        )

    def assemble(self):
        whole = jnp.zeros((self.ring.chips * self.rows,) + self.parts[0][2].shape[1:], BF16)
        for offset, row, part in self.parts:
            start = self.ring.chip_at(offset) * self.rows + row
            whole = lax.dynamic_update_slice_in_dim(whole, part, start, 0)
        return whole


class Reduce:
    def __init__(self, ring, part):
        self.ring = ring
        self.part = part
        self.step_count = 0

    def step(self):
        ring, half = self.ring, self.ring.chips // 2
        self.step_count += 1
        k = self.step_count
        if k == 1:
            term = low(self.part(half))
            self.cut = term.shape[0] // 2
            up, down = term[: self.cut], term[self.cut :]
        else:
            d = half + 1 - k
            up_term, down_term = self.part(d), self.part(-d)
            if k == 2:
                rest = jnp.zeros(self.got_up.shape, F32)
                up = low(up_term + jnp.concatenate([to_float(self.got_up), rest], axis=0))
                down = low(down_term + jnp.concatenate([rest, to_float(self.got_down)], axis=0))
            else:
                up = low(up_term + to_float(self.got_up))
                down = low(down_term + to_float(self.got_down))
        self.got_up = ring.up(up)
        self.got_down = ring.down(down)

    def result(self):
        return self.part(0) + to_float(self.got_up) + to_float(self.got_down)

    def after(self, other):
        pass


def local(
    tokens,
    layer_input,
    block_ids,
    block_table,
    w_query,
    w_key,
    w_value,
    w_output,
    w_left,
    w_right,
    w_gate,
    w_up,
    w_down,
    w_layer_gate,
    w_layer_proj,
    query_gain,
    key_gain,
    gain_input,
    gain_attn_out,
    gain_laurel,
    gain_ffw_in,
    gain_ffw_out,
    gain_layer_out,
    out_grad,
):
    ring = Ring()
    side = lax.axis_index("tensor")
    core = ring.core
    rows = w_query.shape[0]
    own = tokens.shape[0]
    width = tokens.shape[1]
    q_cols = w_query.shape[1]
    kv_cols = w_key.shape[1]
    rank = w_left.shape[1]
    small = w_layer_gate.shape[1]
    ff_cols = w_gate.shape[1] // 2
    chips = ring.chips

    def gain_block(query_part, key_part, parts):
        count = query_part.shape[0]
        columns = parts + [
            jnp.pad(query_part, (0, rows - count)),
            jnp.pad(key_part, (0, rows - count)),
        ]
        block = jnp.stack(columns, axis=1)
        return jnp.pad(block, ((0, 0), (0, 128 - block.shape[1])))

    gains = gain_block(
        query_gain,
        key_gain,
        [gain_input, gain_attn_out, gain_laurel, gain_ffw_in, gain_ffw_out, gain_layer_out],
    )
    other_tokens = across(tokens)

    def core_split(matrix):
        mine = lax.dynamic_slice_in_dim(matrix, core * ff_cols, ff_cols, 1)
        theirs = lax.dynamic_slice_in_dim(matrix, (1 - core) * ff_cols, ff_cols, 1)
        got = ring.swap(theirs)
        return jnp.where(
            core == 0,
            jnp.concatenate([mine, got], axis=0),
            jnp.concatenate([got, mine], axis=0),
        )

    first_pack = jnp.concatenate([w_query, w_key, w_value, gains], axis=1)
    second_pack = jnp.concatenate(
        [w_output.T, w_left, w_right.T, w_layer_gate, w_layer_proj.T], axis=1
    )
    gate_block = core_split(w_gate)
    up_block = core_split(w_up)
    down_block = core_split(w_down.T)

    half = chips // 2
    ga = Gather(ring, first_pack)
    gb = Gather(ring, second_pack)
    for _ in range(half):
        ga.step()
        gb.step()
    gg = Gather(ring, gate_block)
    gu = Gather(ring, up_block)
    gg.after(ga)
    gu.after(gb)
    for _ in range(half):
        gg.step()
        gu.step()
    gd0 = Gather(ring, down_block[:rows])
    gd1 = Gather(ring, down_block[rows:])
    gd0.after(gg)
    gd1.after(gu)
    for _ in range(half):
        gd0.step()
        gd1.step()

    def by_core(gather):
        mine = gather.assemble()
        theirs = ring.swap(mine)
        mine = mine.reshape(chips, 1, rows, -1)
        theirs = theirs.reshape(chips, 1, rows, -1)
        both = jnp.where(
            core == 0,
            jnp.concatenate([mine, theirs], axis=1),
            jnp.concatenate([theirs, mine], axis=1),
        )
        return both.reshape(width, -1)

    first_all = by_core(ga)
    second_all = by_core(gb)
    query_full = first_all[:, :q_cols]
    key_full = first_all[:, q_cols : q_cols + kv_cols]
    value_full = first_all[:, q_cols + kv_cols : q_cols + 2 * kv_cols]
    gains_full = first_all[:, q_cols + 2 * kv_cols :]
    output_t = second_all[:, :q_cols]
    left_full = second_all[:, q_cols : q_cols + rank]
    right_t = second_all[:, q_cols + rank : q_cols + 2 * rank]
    lgate_full = second_all[:, q_cols + 2 * rank : q_cols + 2 * rank + small]
    lproj_t = second_all[:, q_cols + 2 * rank + small :]
    gate_full = gg.assemble()
    up_full = gu.assemble()

    def down_whole():
        top = gd0.assemble().reshape(chips, 1, rows, ff_cols)
        bottom = gd1.assemble().reshape(chips, 1, rows, ff_cols)
        return jnp.concatenate([top, bottom], axis=1).reshape(width, ff_cols)

    down_t = down_whole()

    gain_columns = to_float(gains_full[:, :8])
    (
        input_scale,
        attn_scale,
        laurel_scale,
        ffw_in_scale,
        ffw_out_scale,
        layer_scale,
    ) = (gain_columns[:, i] for i in range(6))
    head_part = query_gain.shape[0]

    def head_gain(column):
        return column.reshape(ring.devices, rows)[:, :head_part].reshape(HD)

    query_scale = head_gain(gain_columns[:, 6])
    key_scale = head_gain(gain_columns[:, 7])

    inputs = to_float(tokens)
    normed, input_norm_back = jax.vjp(norm_gain, inputs, input_scale)
    normed_low = low(normed)
    seq_rows = jnp.concatenate(
        [normed_low, low(norm_gain(to_float(other_tokens), input_scale))], axis=0
    )
    piece_len = 2 * own
    seq_total = block_ids.shape[1]
    per_seq = seq_total // piece_len
    dp_index = lax.axis_index("dp")
    row_index = dp_index // per_seq
    slot = lax.rem(dp_index, per_seq)
    first = slot * piece_len
    has_before = slot > 0
    has_after = slot < per_seq - 1
    query_raw = product(seq_rows, query_full)
    key_raw = product(seq_rows, key_full)
    value_raw = product(seq_rows, value_full)
    natural = jnp.arange(piece_len, dtype=jnp.int32)
    here = first + lax.rem(natural + side * own, piece_len)
    cosines, sines = rope_tables(here, HD)

    def prepare(query_in, key_in, value_in, query_gains, key_gains):
        query_out = rotate(
            norm_gain(query_in.reshape(piece_len, -1, HD), query_gains), cosines, sines
        )
        key_out = rotate(norm_gain(key_in.reshape(piece_len, -1, HD), key_gains), cosines, sines)
        return (query_out, key_out, norm_plain(value_in.reshape(piece_len, -1, HD)))

    prepared, prepare_back = jax.vjp(
        prepare, query_raw, key_raw, value_raw, query_scale, key_scale
    )
    query_rot, key_rot, value_nrm = prepared
    heads_local = query_rot.shape[1]
    kv_local = key_rot.shape[1]
    group = heads_local // kv_local
    query_low = low(query_rot).reshape(piece_len, kv_local, group, HD)

    def in_order(values):
        return jnp.where(
            side == 0, values, jnp.concatenate([values[own:], values[:own]], axis=0)
        )

    kv_own = in_order(jnp.concatenate([low(key_rot), low(value_nrm)], axis=1))
    reach_after = min(256, piece_len)
    forward_pairs = [(i, i + 1) for i in range(ring.devices - 1)]
    backward_pairs = [(i + 1, i) for i in range(ring.devices - 1)]
    kv_before = lax.ppermute(kv_own, "dp", forward_pairs)
    kv_after = lax.ppermute(kv_own[:reach_after], "dp", backward_pairs)
    kv_all = jnp.concatenate([kv_before, kv_own, kv_after], axis=0)
    keys_all = kv_all[:, :kv_local]
    values_all = kv_all[:, kv_local:]

    ids_row = lax.dynamic_index_in_dim(block_ids, row_index, 0, keepdims=False)
    table_row = lax.dynamic_index_in_dim(block_table, row_index, 0, keepdims=False)
    own_ids = lax.dynamic_slice_in_dim(ids_row, first, piece_len, 0)
    before_ids = lax.dynamic_slice_in_dim(ids_row, jnp.maximum(first - piece_len, 0), piece_len, 0)
    before_ids = jnp.where(has_before, before_ids, -2)
    after_ids = lax.dynamic_slice_in_dim(
        ids_row, jnp.minimum(first + piece_len, seq_total - reach_after), reach_after, 0
    )
    after_ids = jnp.where(has_after, after_ids, -2)
    key_ids = jnp.concatenate([before_ids, own_ids, after_ids], axis=0)
    query_ids = in_order(own_ids)
    block_count = block_table.shape[-1]
    number_rows = jnp.arange(block_count, dtype=jnp.int32)
    sees_last = jnp.sum(
        jnp.where(number_rows[None, :] == number_rows[:, None] - 1, table_row, 0), axis=1
    )
    query_sees = jnp.sum(
        jnp.where(query_ids[:, None] == number_rows[None, :], sees_last[None, :], 0), axis=1
    )
    previous_ids = jnp.where(query_sees == 1, query_ids - 1, query_ids)

    def scores_for():
        allowed = (query_ids[:, None] == key_ids[None, :]) | (
            previous_ids[:, None] == key_ids[None, :]
        )
        scores = jnp.einsum("qkgd,ckd->kgqc", query_low, keys_all, preferred_element_type=F32)
        return jnp.where(allowed[None, None], scores, NEGATIVE)

    scores = scores_for()
    highest = jnp.max(scores, axis=-1, keepdims=True)
    weights_exp = jnp.exp(scores - highest)
    totals = jnp.sum(weights_exp, axis=-1, keepdims=True)
    probs_low = low(weights_exp / totals)
    attended = jnp.einsum("kgqc,ckd->qkgd", probs_low, values_all, preferred_element_type=F32)
    log_totals = highest + jnp.log(totals)
    heads_low = low(attended.reshape(piece_len, heads_local * HD))

    def sum_sides(partial):
        return partial[:own] + to_float(across(low(partial[own:])))

    def both_sides(values):
        return jnp.concatenate([values, across(values)], axis=0)

    def four_ways(values):
        pair = both_sides(values)
        return jnp.concatenate([pair, ring.swap(pair)], axis=0)

    def sum_four(partial):
        pair = partial[: 2 * own] + to_float(ring.swap(low(partial[2 * own :])))
        return sum_sides(pair)

    attn_out = sum_sides(product_t(heads_low, output_t))
    attn_normed, attn_norm_back = jax.vjp(norm_gain, attn_out, attn_scale)
    left_low = low(product(normed_low, left_full))
    right_out = product_t(left_low, right_t)
    laurel_normed, laurel_back = jax.vjp(norm_gain, right_out, laurel_scale)
    mixed = (inputs + attn_normed + (normed + laurel_normed)) * ROOT_HALF
    ffw_normed, ffw_norm_back = jax.vjp(norm_gain, mixed, ffw_in_scale)
    ffw_rows = four_ways(low(ffw_normed))

    gate_raw = product(ffw_rows, gate_full)
    up_raw = product(ffw_rows, up_full)

    def activate(gate_in, up_in):
        return gelu_tanh(gate_in) * up_in

    hidden, activate_back = jax.vjp(activate, gate_raw, up_raw)
    hidden_low = low(hidden)
    ffw_out = sum_four(product_t(hidden_low, down_t))
    ffw_out_normed, ffw_out_back = jax.vjp(norm_gain, ffw_out, ffw_out_scale)
    block_mid = mixed + ffw_out_normed
    mid_low = low(block_mid)
    layer_pre = product(mid_low, lgate_full)

    def layer_gate_fn(pre_values, per_layer):
        return gelu_tanh(pre_values) * per_layer

    gated, gated_back = jax.vjp(layer_gate_fn, layer_pre, to_float(layer_input))
    gated_low = low(gated)
    layer_proj = product_t(gated_low, lproj_t)
    proj_normed, proj_back = jax.vjp(norm_gain, layer_proj, layer_scale)
    result = block_mid + proj_normed

    grad_out = to_float(out_grad)
    d_proj, d_layer_scale = proj_back(grad_out)
    d_proj_low = low(d_proj)
    d_gated = product(d_proj_low, lproj_t)
    grad_lproj_t = product_l(d_proj_low, gated_low)
    d_pre, grad_layer_input = gated_back(d_gated)
    d_pre_low = low(d_pre)
    d_mid = grad_out + product_t(d_pre_low, lgate_full)
    grad_lgate = product_l(mid_low, d_pre_low)
    d_ffw_out, d_ffw_out_scale = ffw_out_back(d_mid)
    d_ffw_rows = four_ways(low(d_ffw_out))
    d_hidden = product(d_ffw_rows, down_t)
    d_gate, d_up = activate_back(d_hidden)
    d_gate_low = low(d_gate)
    d_up_low = low(d_up)

    def columns_at(values, offset, start, count):
        return lax.dynamic_slice_in_dim(
            values, ring.chip_at(offset) * (2 * rows) + start, count, 1
        )

    rd0 = Reduce(
        ring, lambda o: product_l(columns_at(d_ffw_rows, o, 0, rows), hidden_low)
    )
    rd1 = Reduce(
        ring, lambda o: product_l(columns_at(d_ffw_rows, o, rows, rows), hidden_low)
    )
    rg = Reduce(ring, lambda o: product_l(columns_at(ffw_rows, o, 0, 2 * rows), d_gate_low))
    ru = Reduce(ring, lambda o: product_l(columns_at(ffw_rows, o, 0, 2 * rows), d_up_low))
    for _ in range(half):
        rd0.step()
        rd1.step()
    d_gate_ring, d_up_ring, _ = tie(
        d_gate_low, d_up_low, (rd0.got_up, rd0.got_down, rd1.got_up, rd1.got_down)
    )
    rg.part = lambda o: product_l(columns_at(ffw_rows, o, 0, 2 * rows), d_gate_ring)
    ru.part = lambda o: product_l(columns_at(ffw_rows, o, 0, 2 * rows), d_up_ring)
    for _ in range(half):
        rg.step()
        ru.step()

    d_ffw_normed = sum_four(product_t(d_gate_low, gate_full) + product_t(d_up_low, up_full))
    d_mixed_extra, d_ffw_in_scale = ffw_norm_back(d_ffw_normed)
    d_branch = (d_mid + d_mixed_extra) * ROOT_HALF
    d_attn, d_attn_scale = attn_norm_back(d_branch)
    d_attn_rows = both_sides(low(d_attn))
    d_right, d_laurel_scale = laurel_back(d_branch)
    d_right_low = low(d_right)
    grad_right_t = product_l(d_right_low, left_low)
    d_left_low = low(product(d_right_low, right_t))
    grad_left = product_l(normed_low, d_left_low)
    d_normed = d_branch + product_t(d_left_low, left_full)
    d_heads = low(product(d_attn_rows, output_t)).reshape(piece_len, kv_local, group, HD)

    probs = jnp.exp(scores_for() - log_totals)
    probs_low = low(probs)
    d_values_all = jnp.einsum("kgqc,qkgd->ckd", probs_low, d_heads, preferred_element_type=F32)
    d_probs = jnp.einsum("qkgd,ckd->kgqc", d_heads, values_all, preferred_element_type=F32)
    deltas = jnp.sum(probs * d_probs, axis=-1, keepdims=True)
    d_scores = low(probs * (d_probs - deltas))
    d_keys_all = jnp.einsum("kgqc,qkgd->ckd", d_scores, query_low, preferred_element_type=F32)
    d_query_rot = jnp.einsum("kgqc,ckd->qkgd", d_scores, keys_all, preferred_element_type=F32)
    d_kv_all = jnp.concatenate([d_keys_all, d_values_all], axis=1)
    to_before = low(d_kv_all[:piece_len])
    to_after = low(d_kv_all[2 * piece_len :])
    from_after = to_float(lax.ppermute(to_before, "dp", backward_pairs))
    from_before = to_float(lax.ppermute(to_after, "dp", forward_pairs))
    d_kv = d_kv_all[piece_len : 2 * piece_len] + from_after
    d_kv = d_kv + jnp.pad(from_before, ((0, piece_len - reach_after), (0, 0), (0, 0)))
    d_kv = in_order(d_kv)
    d_query, d_key, d_value, query_scale_grad, key_scale_grad = prepare_back(
        (d_query_rot.reshape(piece_len, heads_local, HD), d_kv[:, :kv_local], d_kv[:, kv_local:])
    )
    d_query_low = low(d_query)
    d_key_low = low(d_key)
    d_value_low = low(d_value)
    d_normed = d_normed + sum_sides(
        product_t(d_query_low, query_full)
        + product_t(d_key_low, key_full)
        + product_t(d_value_low, value_full)
    )
    d_inputs_extra, d_input_scale = input_norm_back(d_normed)
    grad_tokens = d_branch + d_inputs_extra

    def over_cores(grad):
        blocks = grad.reshape(chips, 2, rows, -1)
        mine = lax.dynamic_index_in_dim(blocks, core, 1, keepdims=False)
        theirs = lax.dynamic_index_in_dim(blocks, 1 - core, 1, keepdims=False)
        return mine + to_float(ring.swap(low(theirs)))

    def ring_of(blocks):
        return Reduce(
            ring, lambda o: lax.dynamic_index_in_dim(blocks, ring.chip_at(o), 0, keepdims=False)
        )

    d_qkv = jnp.concatenate([d_query_low, d_key_low, d_value_low], axis=1)
    grad_output_t = product_l(d_attn_rows, heads_low)
    grad_qkv = product_l(seq_rows, d_qkv)

    def head_gain_back(grads):
        padded = jnp.pad(grads.reshape(ring.devices, head_part), ((0, 0), (0, rows - head_part)))
        return padded.reshape(width)

    gain_grads = jnp.stack(
        [
            d_input_scale,
            d_attn_scale,
            d_laurel_scale,
            d_ffw_in_scale,
            d_ffw_out_scale,
            d_layer_scale,
            head_gain_back(query_scale_grad),
            head_gain_back(key_scale_grad),
        ],
        axis=1,
    )
    gain_grads = jnp.pad(gain_grads, ((0, 0), (0, 128 - gain_grads.shape[1])))
    small_grads = jnp.concatenate(
        [grad_left, grad_right_t, grad_lgate, grad_lproj_t, gain_grads], axis=1
    )
    small_blocks = over_cores(small_grads)
    part_rows = rows // 2
    small_halves = small_blocks.reshape(chips, 2, part_rows, -1)
    small_mine = lax.dynamic_index_in_dim(small_halves, side, 1, keepdims=False)
    small_theirs = lax.dynamic_index_in_dim(small_halves, 1 - side, 1, keepdims=False)
    small_mine = small_mine + to_float(across(low(small_theirs)))

    ro = ring_of(over_cores(grad_output_t))
    rq = ring_of(over_cores(grad_qkv))
    rs = ring_of(small_mine)
    for _ in range(half):
        ro.step()
        rq.step()
        rs.step()

    def back_to_rows(block):
        mine = lax.dynamic_slice_in_dim(block, core * rows, rows, 0)
        theirs = lax.dynamic_slice_in_dim(block, (1 - core) * rows, rows, 0)
        got = ring.swap(theirs)
        return jnp.where(
            core == 0,
            jnp.concatenate([mine, got], axis=1),
            jnp.concatenate([got, mine], axis=1),
        )

    out_down_t = back_to_rows(jnp.concatenate([rd0.result(), rd1.result()], axis=0))
    out_gate = back_to_rows(rg.result())
    out_up = back_to_rows(ru.result())
    out_output = ro.result().T
    out_qkv = rq.result()
    small_half = rs.result()
    small_other = across(small_half)
    out_small = jnp.where(
        side == 0,
        jnp.concatenate([small_half, small_other], axis=0),
        jnp.concatenate([small_other, small_half], axis=0),
    )
    out_gains = out_small[:, 2 * rank + 2 * small :]
    return (
        low(result),
        grad_tokens,
        grad_layer_input,
        out_qkv[:, :q_cols],
        out_qkv[:, q_cols : q_cols + kv_cols],
        out_qkv[:, q_cols + kv_cols :],
        out_output,
        out_small[:, :rank],
        out_small[:, rank : 2 * rank].T,
        out_gate,
        out_up,
        out_down_t.T,
        out_small[:, 2 * rank : 2 * rank + small],
        out_small[:, 2 * rank + small : 2 * rank + 2 * small].T,
        out_gains[:head_part, 6],
        out_gains[:head_part, 7],
        out_gains[:, 0],
        out_gains[:, 1],
        out_gains[:, 2],
        out_gains[:, 3],
        out_gains[:, 4],
        out_gains[:, 5],
    )


def solution(mesh):
    both = P(("dp", "tensor"), None)
    rows_split = P("dp", "tensor")
    cols_split = P("tensor", "dp")
    by_row = P("dp", None)
    by_col = P(None, "dp")
    flat = P("dp")
    return jax.shard_map(
        local,
        mesh=mesh,
        in_specs=(
            (both, both, P(), P(), rows_split, rows_split, rows_split, cols_split)
            + (by_row, by_col, rows_split, rows_split, cols_split, by_row, by_col)
            + (flat,) * 8
            + (both,)
        ),
        out_specs=(
            (both, both, both, rows_split, rows_split, rows_split, cols_split)
            + (by_row, by_col, rows_split, rows_split, cols_split, by_row, by_col)
            + (flat,) * 8
        ),
        check_vma=False,
    )
```

time: 2820 us -> 1060 us (0.38)
  waiting for transfers between devices: 2160 us -> 291 us
  blocking collectives: 249 us -> 0 us
  local copies, waits for them, and re-layouts: 31.9 us -> 250 us
  starting transfers between devices: 21.2 us -> 144 us
  other arithmetic: 65.9 us -> 119 us
    reduce_scatter x15 -> x0, waiting for transfers between devices: 1520 us -> none  [the longest x1 338 us: local(): lax.psum_scatter(grad_down, 'dp', scatter_dimension=1, tiled=True)]
    all_gather x13 -> x0, waiting for transfers between devices: 622 us -> none  [the longest x1 129 us: local(): lax.all_gather(w_gate, 'dp', axis=0, tiled=True)]
    ppermute x8 -> x133, waiting for transfers between devices: 0.02 us -> 291 us  [the longest x52 165 us: up(): return lax.ppermute(values, 'dp', self.cw)]
    all_gather x8 -> x0, blocking collectives: 152 us -> none  [the longest x1 23.1 us: local(): lax.all_gather(gain_input, 'dp', axis=0, tiled=True)]
    ppermute x8 -> x133, starting transfers between devices: 20 us -> 144 us  [the longest x52 62 us: up(): return lax.ppermute(values, 'dp', self.cw)]
    unnamed x2 -> x0, blocking collectives: 89.6 us -> none
    dynamic_update_slice x0 -> x51, local copies, waits for them, and re-layouts: none -> 70.7 us  [assemble(): whole = lax.dynamic_update_slice_in_dim(whole, part, start, 0)]
    ppermute x0 -> x24, local copies, waits for them, and re-layouts: none -> 34.4 us  [the longest x12 17.4 us: up(): return lax.ppermute(values, 'dp', self.cw)]
  transfers between devices with their start and end apart: 37 -> 133, of which waited for: 24 -> 46; matrix products, arithmetic and copies ran while one was open for 8% -> 45% of each run, Pallas kernels for 0% -> 0%
where the time goes in v1:
time: 1060 us; the launch traced here: 1040 us
  waiting for transfers between devices  291 us (27%)
  local copies, waits for them, and re-layouts  250 us (24%)
  matrix products  233 us (22%)
  starting transfers between devices  144 us (14%)
  other arithmetic  119 us (11%)
    ppermute x52, waiting for transfers between devices, up(): return lax.ppermute(values, 'dp', self.cw)  165 us
    dot_general x38, matrix products, product_l(): lax.dot_general(left_in, right_in, (((0,), (0,)), ((), ())), preferred_el...  78.8 us
    dot_general x11, matrix products, product(): return jnp.dot(left_in, right_in, preferred_element_type=F32)  71.9 us
    dynamic_update_slice x51, local copies, waits for them, and re-layouts, assemble(): whole = lax.dynamic_update_slice_in_dim(whole, part, start, 0)  70.7 us
    ppermute x10, waiting for transfers between devices, across(): return lax.ppermute(values, 'tensor', [(0, 1), (1, 0)])  66.4 us
    ppermute x52, starting transfers between devices, up(): return lax.ppermute(values, 'dp', self.cw)  62 us
    dot_general x11, matrix products, product_t(): lax.dot_general(left_in, right_in, (((1,), (1,)), ((), ())), preferred_el...  61.4 us
    ppermute x52, starting transfers between devices, down(): return lax.ppermute(values, 'dp', self.ccw)  58.6 us
  transfers between devices with their start and end apart: 133, of which 46 were waited for; matrix products, arithmetic and copies ran while one was open for 45% of the time, Pallas kernels for 0%

profile of v1, /device:TPU:0, one launch (start us, length us, event | category | flops | bytes accessed | tf_op | source)
XLA Modules:
  0.0 1041.1 jit_solution(1788021673143966234)
XLA Ops:
  52.3 4.4 broadcast.555.clone
  61.1 4.4 broadcast.555.clone.1
  93.7 4.9 collective-permute-done.4
  106.0 4.4 collective-permute-done.6
  124.5 14.4 %collective-permute-done.25 = bf16[256,2048]{0,1:T(8,128)(2,1)} collective-permute-done((bf16[256,2048]{0,1:T(8,128)(2,1)}, bf16[256,2048]{0,1:T(8,128)(2,1)}, u32[]{:S(2)}, u32[]{:S(2)}) %collective-permute-start.25) | collective-permute-done | bytes 1048608 | tf_op jit(solution)/shard_map/ppermute | solution.py:96
  141.0 20.4 %collective-permute-done.34 = bf16[256,2048]{0,1:T(8,128)(2,1)} collective-permute-done((bf16[256,2048]{0,1:T(8,128)(2,1)}, bf16[256,2048]{0,1:T(8,128)(2,1)}, u32[]{:S(2)}, u32[]{:S(2)}) %collective-permute-start.34) | collective-permute-done | bytes 1048608 | tf_op jit(solution)/shard_map/ppermute | solution.py:96
  173.0 10.9 %collective-permute-done.27 = bf16[256,2048]{0,1:T(8,128)(2,1)} collective-permute-done((bf16[256,2048]{0,1:T(8,128)(2,1)}, bf16[256,2048]{0,1:T(8,128)(2,1)}, u32[]{:S(2)}, u32[]{:S(2)}) %collective-permute-start.27) | collective-permute-done | bytes 1048608 | tf_op jit(solution)/shard_map/ppermute | solution.py:96
  185.9 20.4 %collective-permute-done.36 = bf16[256,2048]{0,1:T(8,128)(2,1)} collective-permute-done((bf16[256,2048]{0,1:T(8,128)(2,1)}, bf16[256,2048]{0,1:T(8,128)(2,1)}, u32[]{:S(2)}, u32[]{:S(2)}) %collective-permute-start.36) | collective-permute-done | bytes 1048608 | tf_op jit(solution)/shard_map/ppermute | solution.py:96
  219.9 8.8 collective-permute-done.29
  232.6 18.5 %collective-permute-done.38 = bf16[256,2048]{0,1:T(8,128)(2,1)S(1)} collective-permute-done((bf16[256,2048]{0,1:T(8,128)(2,1)}, bf16[256,2048]{0,1:T(8,128)(2,1)S(1)}, u32[]{:S(2)}, u32[]{:S(2)}) %collective-permute-start.38) | collective-permute-done | bytes 1048608 | tf_op jit(solution)/shard_map/ppermute | solution.py:96
  260.6 4.8 maximum_select_fusion
  268.3 4.5 slice_reduce_fusion
  276.6 5.2 fusion.29
  295.6 6.8 maximum_select_fusion.1
  306.9 4.7 collective-permute-start.51
  350.0 9.0 collective-permute-done.21
  391.9 5.6 collective-permute-done.47
  426.3 7.5 pad_maximum_fusion
  433.8 14.5 %fusion.275 = f32[1024,2048]{1,0:T(8,128)} fusion(bf16[2048,2048]{0,1:T(8,128)(2,1)} %constant_dynamic-update-slice_fusion.27, bf16[512,2048]{1,0:T(8,128)(2,1)} %collective-permute-done.23, bf16[256,2048]{1,0:T(8,128)(2,1)} %collective-permute-done.22, bf16[256,2048]{1,0:T(8,128)(2,1)} %multiply_convert_fusion.2), kind=kOutput, calls=%fused_computation.598 | convolution fusion | flops 8602517504 | bytes 20971520 | tf_op jit(solution)/shard_map/dot_general | solution.py:57
  448.4 17.1 %multiply_convert_fusion.1 = (bf16[1024,2048]{1,0:T(8,128)(2,1)S(1)}, f32[1024,2048]{1,0:T(8,128)}) fusion(f32[1024,2048]{1,0:T(8,128)} %fusion.275, bf16[2048,2048]{0,1:T(8,128)(2,1)} %constant_dynamic-update-slice_fusion.18, bf16[512,2048]{1,0:T(8,128)(2,1)} %collective-permute-done.23, bf16[256,2048]{1,0:T(8,128)(2,1)} %collective-permute-done.22, ...), kind=kOutput, calls=%fused_computation.22 | convolution fusion | flops 8623489024 | bytes 33554432 | tf_op jit(solution)/shard_map/dot_general | solution.py:57
  465.5 13.0 %fusion.286 = f32[1024,2048]{1,0:T(8,128)S(1)} fusion(bf16[1024,2048]{1,0:T(8,128)(2,1)S(1)} %get-tuple-element.318, bf16[2048,2048]{1,0:T(8,128)(2,1)} %bitcast.420), kind=kOutput, calls=%fused_computation.607 | convolution fusion | flops 8589934592 | bytes 20971520 | tf_op jit(solution)/shard_map/dot_general | solution.py:61
  478.9 4.1 collective-permute-done.59
  485.5 23.5 %collective-permute-done.60 = bf16[256,2048]{1,0:T(8,128)(2,1)S(1)} collective-permute-done((bf16[256,2048]{1,0:T(8,128)(2,1)S(1)}, bf16[256,2048]{1,0:T(8,128)(2,1)S(1)}, u32[]{:S(2)}, u32[]{:S(2)}) %collective-permute-start.60) | collective-permute-done | bytes 1048608 | tf_op jit(solution)/shard_map/ppermute | solution.py:106
  520.8 22.7 %collective-permute-done.61 = bf16[256,2048]{1,0:T(8,128)(2,1)S(1)} collective-permute-done((bf16[256,2048]{1,0:T(8,128)(2,1)S(1)}, bf16[256,2048]{1,0:T(8,128)(2,1)S(1)}, u32[]{:S(2)}, u32[]{:S(2)}) %collective-permute-start.61) | collective-permute-done | bytes 1048608 | tf_op jit(solution)/shard_map/ppermute | solution.py:106
  545.3 3.9 pad_maximum_fusion.1
  554.8 24.0 %fusion.11 = (bf16[1024,2048]{1,0:T(8,128)(2,1)}, bf16[1024,2048]{1,0:T(8,128)(2,1)}) fusion(f32[1024,2048]{1,0:T(8,128)} %fusion.275, f32[1024,2048]{1,0:T(8,128)} %get-tuple-element.319, bf16[2048,2048]{1,0:T(8,128)(2,1)} %bitcast.421, bf16[512,2048]{1,0:T(8,128)(2,1)} %collective-permute-done.62, bf16[256,2048]{1,0:T(8,128)(2,1)} %copy-done.66, ...), kind=kOutput, calls=%fused_computation.19 | convolution fusion | flops 8652849152 | bytes 37748736 | tf_op jit(solution)/shard_map/dot_general | solution.py:57
  578.8 14.7 %fusion.287 = f32[1024,2048]{1,0:T(8,128)} fusion(bf16[1024,2048]{1,0:T(8,128)(2,1)} %get-tuple-element.41, bf16[2048,2048]{0,1:T(8,128)(2,1)} %constant_dynamic-update-slice_fusion.18), kind=kOutput, calls=%fused_computation.608 | convolution fusion | flops 8589934592 | bytes 20971520 | tf_op jit(solution)/shard_map/dot_general | solution.py:61
  597.8 5.0 collective-permute-done.98
  612.1 7.6 collective-permute-done.99
  623.3 7.6 collective-permute-done.107
  634.5 7.6 collective-permute-done.100
  645.8 7.6 collective-permute-done.108
  657.9 14.6 %convolution_add_fusion = f32[1024,2048]{1,0:T(8,128)} fusion(f32[1024,2048]{1,0:T(8,128)} %fusion.287, bf16[1024,2048]{1,0:T(8,128)(2,1)S(1)} %copy-done.39, bf16[2048,2048]{0,1:T(8,128)(2,1)} %constant_dynamic-update-slice_fusion.27), kind=kOutput, calls=%fused_computation.52 | convolution fusion | flops 8592031744 | bytes 29360128 | tf_op jit(solution)/shard_map/dot_general | solution.py:61
  722.8 5.3 multiply_reduce_fusion.3
  737.4 3.5 fusion.43
  741.9 3.8 fusion.40
  749.6 3.6 fusion.49
  754.3 3.5 fusion.46
  764.9 6.2 fusion
  772.6 4.6 fusion.16
  777.2 4.9 convolution_bitcast_fusion.1
  797.8 4.1 copy.446
  802.5 5.0 fusion.27
  815.3 3.5 fusion.42
  820.0 3.6 fusion.39
  825.1 3.6 fusion.48
  844.9 4.7 fusion.91
  856.0 3.8 fusion.37
  861.3 10.3 collective-permute-done.130
  871.6 4.6 collective-permute-done.126
  881.9 3.5 fusion.72
  886.7 9.3 reshape.704
  896.0 7.3 constant_dynamic-slice_fusion.6
  903.3 8.2 copy.453
  911.5 3.7 fusion.84
  915.3 3.7 bitcast_add_fusion.1
  924.5 6.0 copy.428
  933.7 4.0 maximum_select_fusion.2
  944.3 4.9 bitcast_add_fusion
  950.7 11.1 %collective-permute-done.88 = bf16[8,64,768]{2,1,0:T(8,128)(2,1)S(1)} collective-permute-done((bf16[8,64,768]{2,1,0:T(8,128)(2,1)S(1)}, bf16[8,64,768]{2,1,0:T(8,128)(2,1)S(1)}, u32[]{:S(2)}, u32[]{:S(2)}) %collective-permute-start.88) | collective-permute-done | bytes 786464 | tf_op jit(solution)/shard_map/ppermute | solution.py:106
  970.5 4.7 collective-permute-done.90
  978.9 6.8 collective-permute-done.91
  997.8 6.5 collective-permute-done.74
  1011.6 6.8 collective-permute-done.75
  (882 shorter events, 525.2 us)
Async XLA Ops:
  8.2 27.5 %collective-permute-start.12 = (bf16[128,1664]{0,1:T(8,128)(2,1)}, bf16[128,1664]{0,1:T(8,128)(2,1)}, u32[]{:S(2)}, u32[]{:S(2)}) collective-permute-start(bf16[128,1664]{0,1:T(8,128)(2,1)} %bitcast_dynamic-update-slice_fusion.1), channel_id=1, source_target_pairs={{0,8},{2,10},{8,16},{10,18},{16,24},{18,26},{24,28},{26,30},{28,20... | collective-permute-start | bytes 1277960 | tf_op jit(solution)/shard_map/ppermute | solution.py:96
  11.2 26.0 %collective-permute-start.13 = (bf16[128,1664]{0,1:T(8,128)(2,1)}, bf16[128,1664]{0,1:T(8,128)(2,1)}, u32[]{:S(2)}, u32[]{:S(2)}) collective-permute-start(bf16[128,1664]{0,1:T(8,128)(2,1)} %bitcast_dynamic-update-slice_fusion.1), channel_id=1, source_target_pairs={{8,0},{10,2},{16,8},{18,10},{24,16},{26,18},{28,24},{30,26},{20,28... | collective-permute-start | bytes 1277960 | tf_op jit(solution)/shard_map/ppermute | solution.py:99
  13.9 26.6 %collective-permute-start = (bf16[128,1664]{1,0:T(8,128)(2,1)}, bf16[128,1664]{1,0:T(8,128)(2,1)}, u32[]{:S(2)}, u32[]{:S(2)}) collective-permute-start(bf16[128,1664]{1,0:T(8,128)(2,1)} %get-tuple-element.287), channel_id=1, source_target_pairs={{0,8},{2,10},{8,16},{10,18},{16,24},{18,26},{24,28},{26,30},{28,20... | collective-permute-start | bytes 1277960 | tf_op jit(solution)/shard_map/ppermute | solution.py:96
  15.9 26.6 %collective-permute-start.1 = (bf16[128,1664]{1,0:T(8,128)(2,1)}, bf16[128,1664]{1,0:T(8,128)(2,1)}, u32[]{:S(2)}, u32[]{:S(2)}) collective-permute-start(bf16[128,1664]{1,0:T(8,128)(2,1)} %get-tuple-element.287), channel_id=1, source_target_pairs={{8,0},{10,2},{16,8},{18,10},{24,16},{26,18},{28,24},{30,26},{20,28... | collective-permute-start | bytes 1277960 | tf_op jit(solution)/shard_map/ppermute | solution.py:99
  17.6 69.5 %collective-permute-start.9 = (bf16[256,2048]{1,0:T(8,128)(2,1)S(1)}, bf16[256,2048]{1,0:T(8,128)(2,1)}, u32[]{:S(2)}, u32[]{:S(2)}) collective-permute-start(bf16[256,2048]{1,0:T(8,128)(2,1)S(1)} %copy-done.11), channel_id=1, source_target_pairs={{0,1},{1,0},{2,3},{3,2},{4,5},{5,4},{6,7},{7,6},{8,9},{9,8},{10,11... | collective-permute-start | bytes 3145736 | tf_op jit(solution)/shard_map/ppermute | solution.py:106
  42.5 32.7 %collective-permute-start.14 = (bf16[128,1664]{0,1:T(8,128)(2,1)}, bf16[128,1664]{0,1:T(8,128)(2,1)}, u32[]{:S(2)}, u32[]{:S(2)}) collective-permute-start(bf16[128,1664]{0,1:T(8,128)(2,1)} %collective-permute-done.12), channel_id=1, source_target_pairs={{0,8},{2,10},{8,16},{10,18},{16,24},{18,26},{24,28},{26,30},{28,20... | collective-permute-start | bytes 1277960 | tf_op jit(solution)/shard_map/ppermute | solution.py:96
  44.8 32.2 %collective-permute-start.15 = (bf16[128,1664]{0,1:T(8,128)(2,1)}, bf16[128,1664]{0,1:T(8,128)(2,1)}, u32[]{:S(2)}, u32[]{:S(2)}) collective-permute-start(bf16[128,1664]{0,1:T(8,128)(2,1)} %collective-permute-done.13), channel_id=1, source_target_pairs={{8,0},{10,2},{16,8},{18,10},{24,16},{26,18},{28,24},{30,26},{20,28... | collective-permute-start | bytes 1277960 | tf_op jit(solution)/shard_map/ppermute | solution.py:99
  51.7 28.1 %collective-permute-start.2 = (bf16[128,1664]{1,0:T(8,128)(2,1)}, bf16[128,1664]{1,0:T(8,128)(2,1)}, u32[]{:S(2)}, u32[]{:S(2)}) collective-permute-start(bf16[128,1664]{1,0:T(8,128)(2,1)} %collective-permute-done), channel_id=1, source_target_pairs={{0,8},{2,10},{8,16},{10,18},{16,24},{18,26},{24,28},{26,30},{28,20... | collective-permute-start | bytes 1277960 | tf_op jit(solution)/shard_map/ppermute | solution.py:96
  112.1 26.8 %collective-permute-start.25 = (bf16[256,2048]{0,1:T(8,128)(2,1)}, bf16[256,2048]{0,1:T(8,128)(2,1)}, u32[]{:S(2)}, u32[]{:S(2)}) collective-permute-start(bf16[256,2048]{0,1:T(8,128)(2,1)} %get-tuple-element.33), channel_id=1, source_target_pairs={{0,8},{2,10},{8,16},{10,18},{16,24},{18,26},{24,28},{26,30},{28,20... | collective-permute-start | bytes 3145736 | tf_op jit(solution)/shard_map/ppermute | solution.py:96
  114.1 26.4 %collective-permute-start.26 = (bf16[256,2048]{0,1:T(8,128)(2,1)}, bf16[256,2048]{0,1:T(8,128)(2,1)}, u32[]{:S(2)}, u32[]{:S(2)}) collective-permute-start(bf16[256,2048]{0,1:T(8,128)(2,1)} %get-tuple-element.33), channel_id=1, source_target_pairs={{8,0},{10,2},{16,8},{18,10},{24,16},{26,18},{28,24},{30,26},{20,28... | collective-permute-start | bytes 3145736 | tf_op jit(solution)/shard_map/ppermute | solution.py:99
  114.5 46.8 %collective-permute-start.34 = (bf16[256,2048]{0,1:T(8,128)(2,1)}, bf16[256,2048]{0,1:T(8,128)(2,1)}, u32[]{:S(2)}, u32[]{:S(2)}) collective-permute-start(bf16[256,2048]{0,1:T(8,128)(2,1)} %get-tuple-element.35), channel_id=1, source_target_pairs={{0,8},{2,10},{8,16},{10,18},{16,24},{18,26},{24,28},{26,30},{28,20... | collective-permute-start | bytes 3145736 | tf_op jit(solution)/shard_map/ppermute | solution.py:96
  116.1 46.9 %collective-permute-start.35 = (bf16[256,2048]{0,1:T(8,128)(2,1)}, bf16[256,2048]{0,1:T(8,128)(2,1)}, u32[]{:S(2)}, u32[]{:S(2)}) collective-permute-start(bf16[256,2048]{0,1:T(8,128)(2,1)} %get-tuple-element.35), channel_id=1, source_target_pairs={{8,0},{10,2},{16,8},{18,10},{24,16},{26,18},{28,24},{30,26},{20,28... | collective-permute-start | bytes 3145736 | tf_op jit(solution)/shard_map/ppermute | solution.py:99
  123.3 135.9 %collective-permute-start.8 = (bf16[1024,1664]{1,0:T(8,128)(2,1)}, bf16[1024,1664]{1,0:T(8,128)(2,1)}, u32[]{:S(2)}, u32[]{:S(2)}) collective-permute-start(bf16[1024,1664]{1,0:T(8,128)(2,1)} %constant_dynamic-update-slice_fusion.45), channel_id=1, source_target_pairs={{0,2},{2,0},{4,6},{6,4},{8,10},{10,8},{12,14},{14,12},{16,18},{18,... | collective-permute-start | bytes 10223624 | tf_op jit(solution)/shard_map/ppermute | solution.py:102
  138.9 44.9 %collective-permute-start.27 = (bf16[256,2048]{0,1:T(8,128)(2,1)}, bf16[256,2048]{0,1:T(8,128)(2,1)}, u32[]{:S(2)}, u32[]{:S(2)}) collective-permute-start(bf16[256,2048]{0,1:T(8,128)(2,1)} %collective-permute-done.25), channel_id=1, source_target_pairs={{0,8},{2,10},{8,16},{10,18},{16,24},{18,26},{24,28},{26,30},{28,20... | collective-permute-start | bytes 3145736 | tf_op jit(solution)/shard_map/ppermute | solution.py:96
  140.5 44.9 %collective-permute-start.28 = (bf16[256,2048]{0,1:T(8,128)(2,1)}, bf16[256,2048]{0,1:T(8,128)(2,1)}, u32[]{:S(2)}, u32[]{:S(2)}) collective-permute-start(bf16[256,2048]{0,1:T(8,128)(2,1)} %collective-permute-done.26), channel_id=1, source_target_pairs={{8,0},{10,2},{16,8},{18,10},{24,16},{26,18},{28,24},{30,26},{20,28... | collective-permute-start | bytes 3145736 | tf_op jit(solution)/shard_map/ppermute | solution.py:99
  161.4 44.9 %collective-permute-start.36 = (bf16[256,2048]{0,1:T(8,128)(2,1)}, bf16[256,2048]{0,1:T(8,128)(2,1)}, u32[]{:S(2)}, u32[]{:S(2)}) collective-permute-start(bf16[256,2048]{0,1:T(8,128)(2,1)} %collective-permute-done.34), channel_id=1, source_target_pairs={{0,8},{2,10},{8,16},{10,18},{16,24},{18,26},{24,28},{26,30},{28,20... | collective-permute-start | bytes 3145736 | tf_op jit(solution)/shard_map/ppermute | solution.py:96
  162.9 44.9 %collective-permute-start.37 = (bf16[256,2048]{0,1:T(8,128)(2,1)}, bf16[256,2048]{0,1:T(8,128)(2,1)}, u32[]{:S(2)}, u32[]{:S(2)}) collective-permute-start(bf16[256,2048]{0,1:T(8,128)(2,1)} %collective-permute-done.35), channel_id=1, source_target_pairs={{8,0},{10,2},{16,8},{18,10},{24,16},{26,18},{28,24},{30,26},{20,28... | collective-permute-start | bytes 3145736 | tf_op jit(solution)/shard_map/ppermute | solution.py:99
  183.9 44.8 %collective-permute-start.29 = (bf16[256,2048]{0,1:T(8,128)(2,1)}, bf16[256,2048]{0,1:T(8,128)(2,1)S(1)}, u32[]{:S(2)}, u32[]{:S(2)}) collective-permute-start(bf16[256,2048]{0,1:T(8,128)(2,1)} %collective-permute-done.27), channel_id=1, source_target_pairs={{0,8},{2,10},{8,16},{10,18},{16,24},{18,26},{24,28},{26,30},{28,20... | collective-permute-start | bytes 3145736 | tf_op jit(solution)/shard_map/ppermute | solution.py:96
  185.4 44.8 %collective-permute-start.30 = (bf16[256,2048]{0,1:T(8,128)(2,1)}, bf16[256,2048]{0,1:T(8,128)(2,1)S(1)}, u32[]{:S(2)}, u32[]{:S(2)}) collective-permute-start(bf16[256,2048]{0,1:T(8,128)(2,1)} %collective-permute-done.28), channel_id=1, source_target_pairs={{8,0},{10,2},{16,8},{18,10},{24,16},{26,18},{28,24},{30,26},{20,28... | collective-permute-start | bytes 3145736 | tf_op jit(solution)/shard_map/ppermute | solution.py:99
  206.3 44.8 %collective-permute-start.38 = (bf16[256,2048]{0,1:T(8,128)(2,1)}, bf16[256,2048]{0,1:T(8,128)(2,1)S(1)}, u32[]{:S(2)}, u32[]{:S(2)}) collective-permute-start(bf16[256,2048]{0,1:T(8,128)(2,1)} %collective-permute-done.36), channel_id=1, source_target_pairs={{0,8},{2,10},{8,16},{10,18},{16,24},{18,26},{24,28},{26,30},{28,20... | collective-permute-start | bytes 3145736 | tf_op jit(solution)/shard_map/ppermute | solution.py:96
  207.9 45.6 %collective-permute-start.39 = (bf16[256,2048]{0,1:T(8,128)(2,1)}, bf16[256,2048]{0,1:T(8,128)(2,1)S(1)}, u32[]{:S(2)}, u32[]{:S(2)}) collective-permute-start(bf16[256,2048]{0,1:T(8,128)(2,1)} %collective-permute-done.37), channel_id=1, source_target_pairs={{8,0},{10,2},{16,8},{18,10},{24,16},{26,18},{28,24},{30,26},{20,28... | collective-permute-start | bytes 3145736 | tf_op jit(solution)/shard_map/ppermute | solution.py:99
  228.7 65.5 %collective-permute-start.20 = (bf16[1024,1664]{1,0:T(8,128)(2,1)}, bf16[1024,1664]{1,0:T(8,128)(2,1)}, u32[]{:S(2)}, u32[]{:S(2)}) collective-permute-start(bf16[1024,1664]{1,0:T(8,128)(2,1)} %constant_dynamic-update-slice_fusion.36), channel_id=1, source_target_pairs={{0,2},{2,0},{4,6},{6,4},{8,10},{10,8},{12,14},{14,12},{16,18},{18,... | collective-permute-start | bytes 10223624 | tf_op jit(solution)/shard_map/ppermute | solution.py:102
  230.2 81.3 %collective-permute-start.31 = (bf16[128,2048]{0,1:T(8,128)(2,1)}, bf16[128,2048]{0,1:T(8,128)(2,1)}, u32[]{:S(2)}, u32[]{:S(2)}) collective-permute-start(bf16[128,2048]{0,1:T(8,128)(2,1)} %slice.442), channel_id=1, source_target_pairs={{0,8},{2,10},{8,16},{10,18},{16,24},{18,26},{24,28},{26,30},{28,20... | collective-permute-start | bytes 1572872 | tf_op jit(solution)/shard_map/ppermute | solution.py:96
  251.2 60.6 %collective-permute-start.32 = (bf16[128,2048]{0,1:T(8,128)(2,1)}, bf16[128,2048]{0,1:T(8,128)(2,1)}, u32[]{:S(2)}, u32[]{:S(2)}) collective-permute-start(bf16[128,2048]{0,1:T(8,128)(2,1)} %slice.443), channel_id=1, source_target_pairs={{8,0},{10,2},{16,8},{18,10},{24,16},{26,18},{28,24},{30,26},{20,28... | collective-permute-start | bytes 1572872 | tf_op jit(solution)/shard_map/ppermute | solution.py:99
  253.5 52.1 %collective-permute-start.40 = (bf16[128,2048]{0,1:T(8,128)(2,1)}, bf16[128,2048]{0,1:T(8,128)(2,1)}, u32[]{:S(2)}, u32[]{:S(2)}) collective-permute-start(bf16[128,2048]{0,1:T(8,128)(2,1)} %slice.444), channel_id=1, source_target_pairs={{0,8},{2,10},{8,16},{10,18},{16,24},{18,26},{24,28},{26,30},{28,20... | collective-permute-start | bytes 1572872 | tf_op jit(solution)/shard_map/ppermute | solution.py:96
  259.2 47.7 %collective-permute-start.41 = (bf16[128,2048]{0,1:T(8,128)(2,1)}, bf16[128,2048]{0,1:T(8,128)(2,1)}, u32[]{:S(2)}, u32[]{:S(2)}) collective-permute-start(bf16[128,2048]{0,1:T(8,128)(2,1)} %slice.445), channel_id=1, source_target_pairs={{8,0},{10,2},{16,8},{18,10},{24,16},{26,18},{28,24},{30,26},{20,28... | collective-permute-start | bytes 1572872 | tf_op jit(solution)/shard_map/ppermute | solution.py:99
  306.9 30.5 %collective-permute-start.51 = (bf16[128,2048]{0,1:T(8,128)(2,1)S(1)}, bf16[128,2048]{0,1:T(8,128)(2,1)}, u32[]{:S(2)}, u32[]{:S(2)}) collective-permute-start(bf16[128,2048]{0,1:T(8,128)(2,1)S(1)} %copy-done.78), channel_id=1, source_target_pairs={{0,8},{2,10},{8,16},{10,18},{16,24},{18,26},{24,28},{26,30},{28,20... | collective-permute-start | bytes 1572872 | tf_op jit(solution)/shard_map/ppermute | solution.py:96
  311.5 28.4 %collective-permute-start.52 = (bf16[128,2048]{0,1:T(8,128)(2,1)S(1)}, bf16[128,2048]{0,1:T(8,128)(2,1)}, u32[]{:S(2)}, u32[]{:S(2)}) collective-permute-start(bf16[128,2048]{0,1:T(8,128)(2,1)S(1)} %copy-done.78), channel_id=1, source_target_pairs={{8,0},{10,2},{16,8},{18,10},{24,16},{26,18},{28,24},{30,26},{20,28... | collective-permute-start | bytes 1572872 | tf_op jit(solution)/shard_map/ppermute | solution.py:99
  311.7 30.4 %collective-permute-start.43 = (bf16[128,2048]{0,1:T(8,128)(2,1)}, bf16[128,2048]{0,1:T(8,128)(2,1)}, u32[]{:S(2)}, u32[]{:S(2)}) collective-permute-start(bf16[128,2048]{0,1:T(8,128)(2,1)} %get-tuple-element.37), channel_id=1, source_target_pairs={{0,8},{2,10},{8,16},{10,18},{16,24},{18,26},{24,28},{26,30},{28,20... | collective-permute-start | bytes 1572872 | tf_op jit(solution)/shard_map/ppermute | solution.py:96
  317.4 27.3 %collective-permute-start.44 = (bf16[128,2048]{0,1:T(8,128)(2,1)}, bf16[128,2048]{0,1:T(8,128)(2,1)}, u32[]{:S(2)}, u32[]{:S(2)}) collective-permute-start(bf16[128,2048]{0,1:T(8,128)(2,1)} %get-tuple-element.37), channel_id=1, source_target_pairs={{8,0},{10,2},{16,8},{18,10},{24,16},{26,18},{28,24},{30,26},{20,28... | collective-permute-start | bytes 1572872 | tf_op jit(solution)/shard_map/ppermute | solution.py:99
  333.1 25.9 %collective-permute-start.21 = (bf16[256,2048]{1,0:T(8,128)(2,1)}, bf16[256,2048]{1,0:T(8,128)(2,1)S(1)}, u32[]{:S(2)}, u32[]{:S(2)}) collective-permute-start(bf16[256,2048]{1,0:T(8,128)(2,1)} %slice.634), channel_id=1, source_target_pairs={{0,1},{1,0},{2,3},{3,2},{4,5},{5,4},{6,7},{7,6},{8,9},{9,8},{10,11... | collective-permute-start | bytes 3145736 | tf_op jit(solution)/shard_map/ppermute | solution.py:106
  338.7 30.0 %collective-permute-start.53 = (bf16[128,2048]{0,1:T(8,128)(2,1)}, bf16[128,2048]{0,1:T(8,128)(2,1)}, u32[]{:S(2)}, u32[]{:S(2)}) collective-permute-start(bf16[128,2048]{0,1:T(8,128)(2,1)} %collective-permute-done.51), channel_id=1, source_target_pairs={{0,8},{2,10},{8,16},{10,18},{16,24},{18,26},{24,28},{26,30},{28,20... | collective-permute-start | bytes 1572872 | tf_op jit(solution)/shard_map/ppermute | solution.py:96
  341.3 31.1 %collective-permute-start.54 = (bf16[128,2048]{0,1:T(8,128)(2,1)}, bf16[128,2048]{0,1:T(8,128)(2,1)}, u32[]{:S(2)}, u32[]{:S(2)}) collective-permute-start(bf16[128,2048]{0,1:T(8,128)(2,1)} %collective-permute-done.52), channel_id=1, source_target_pairs={{8,0},{10,2},{16,8},{18,10},{24,16},{26,18},{28,24},{30,26},{20,28... | collective-permute-start | bytes 1572872 | tf_op jit(solution)/shard_map/ppermute | solution.py:99
  343.3 31.9 %collective-permute-start.45 = (bf16[128,2048]{0,1:T(8,128)(2,1)}, bf16[128,2048]{0,1:T(8,128)(2,1)}, u32[]{:S(2)}, u32[]{:S(2)}) collective-permute-start(bf16[128,2048]{0,1:T(8,128)(2,1)} %collective-permute-done.43), channel_id=1, source_target_pairs={{0,8},{2,10},{8,16},{10,18},{16,24},{18,26},{24,28},{26,30},{28,20... | collective-permute-start | bytes 1572872 | tf_op jit(solution)/shard_map/ppermute | solution.py:96
  346.7 29.7 %collective-permute-start.46 = (bf16[128,2048]{0,1:T(8,128)(2,1)}, bf16[128,2048]{0,1:T(8,128)(2,1)}, u32[]{:S(2)}, u32[]{:S(2)}) collective-permute-start(bf16[128,2048]{0,1:T(8,128)(2,1)} %collective-permute-done.44), channel_id=1, source_target_pairs={{8,0},{10,2},{16,8},{18,10},{24,16},{26,18},{28,24},{30,26},{20,28... | collective-permute-start | bytes 1572872 | tf_op jit(solution)/shard_map/ppermute | solution.py:99
  367.3 38.4 %collective-permute-start.22 = (bf16[256,2048]{1,0:T(8,128)(2,1)}, bf16[256,2048]{1,0:T(8,128)(2,1)}, u32[]{:S(2)}, u32[]{:S(2)}) collective-permute-start(bf16[256,2048]{1,0:T(8,128)(2,1)} %multiply_convert_fusion.2), channel_id=1, source_target_pairs={{0,1},{1,0},{2,3},{3,2},{4,5},{5,4},{6,7},{7,6},{8,9},{9,8},{10,11... | collective-permute-start | bytes 3145736 | tf_op jit(solution)/shard_map/ppermute | solution.py:106
  388.9 28.1 %collective-permute-start.57 = (bf16[64,2048]{0,1:T(8,128)(2,1)}, bf16[64,2048]{0,1:T(8,128)(2,1)}, u32[]{:S(2)}, u32[]{:S(2)}) collective-permute-start(bf16[64,2048]{0,1:T(8,128)(2,1)} %bitcast.387), channel_id=1, source_target_pairs={{0,8},{2,10},{8,16},{10,18},{16,24},{18,26},{24,28},{26,30},{28,20... | collective-permute-start | bytes 786440 | tf_op jit(solution)/shard_map/ppermute | solution.py:96
  391.2 27.0 %collective-permute-start.58 = (bf16[64,2048]{0,1:T(8,128)(2,1)}, bf16[64,2048]{0,1:T(8,128)(2,1)}, u32[]{:S(2)}, u32[]{:S(2)}) collective-permute-start(bf16[64,2048]{0,1:T(8,128)(2,1)} %slice.451), channel_id=1, source_target_pairs={{8,0},{10,2},{16,8},{18,10},{24,16},{26,18},{28,24},{30,26},{20,28... | collective-permute-start | bytes 786440 | tf_op jit(solution)/shard_map/ppermute | solution.py:99
  642.9 32.4 %collective-permute-start.101 = (bf16[128,2048]{1,0:T(8,128)(2,1)S(1)}, bf16[128,2048]{1,0:T(8,128)(2,1)S(1)}, u32[]{:S(2)}, u32[]{:S(2)}) collective-permute-start(bf16[128,2048]{1,0:T(8,128)(2,1)S(1)} %fusion.57), channel_id=1, source_target_pairs={{0,8},{2,10},{8,16},{10,18},{16,24},{18,26},{24,28},{26,30},{28,20... | collective-permute-start | bytes 1572872 | tf_op jit(solution)/shard_map/ppermute | solution.py:96
  644.0 31.2 %collective-permute-start.105 = (bf16[128,2048]{1,0:T(8,128)(2,1)S(1)}, bf16[128,2048]{1,0:T(8,128)(2,1)S(1)}, u32[]{:S(2)}, u32[]{:S(2)}) collective-permute-start(bf16[128,2048]{1,0:T(8,128)(2,1)S(1)} %fusion.60), channel_id=1, source_target_pairs={{8,0},{10,2},{16,8},{18,10},{24,16},{26,18},{28,24},{30,26},{20,28... | collective-permute-start | bytes 1572872 | tf_op jit(solution)/shard_map/ppermute | solution.py:99
  686.7 26.9 %collective-permute-start.132 = (f32[128,2048]{1,0:T(8,128)S(1)}, f32[128,2048]{1,0:T(8,128)S(1)}, u32[]{:S(2)}, u32[]{:S(2)}) collective-permute-start(f32[128,2048]{1,0:T(8,128)S(1)} %get-tuple-element.250), channel_id=1, source_target_pairs={{0,2},{2,0},{4,6},{6,4},{8,10},{10,8},{12,14},{14,12},{16,18},{18,... | collective-permute-start | bytes 3145736 | tf_op jit(solution)/shard_map/ppermute | solution.py:102
  698.5 38.9 %collective-permute-start.119 = (bf16[256,2048]{1,0:T(8,128)(2,1)}, bf16[256,2048]{1,0:T(8,128)(2,1)}, u32[]{:S(2)}, u32[]{:S(2)}) collective-permute-start(bf16[256,2048]{1,0:T(8,128)(2,1)} %fusion.44), channel_id=1, source_target_pairs={{8,0},{10,2},{16,8},{18,10},{24,16},{26,18},{28,24},{30,26},{20,28... | collective-permute-start | bytes 3145736 | tf_op jit(solution)/shard_map/ppermute | solution.py:99
  704.7 37.2 %collective-permute-start.115 = (bf16[256,2048]{1,0:T(8,128)(2,1)}, bf16[256,2048]{1,0:T(8,128)(2,1)}, u32[]{:S(2)}, u32[]{:S(2)}) collective-permute-start(bf16[256,2048]{1,0:T(8,128)(2,1)} %fusion.41), channel_id=1, source_target_pairs={{0,8},{2,10},{8,16},{10,18},{16,24},{18,26},{24,28},{26,30},{28,20... | collective-permute-start | bytes 3145736 | tf_op jit(solution)/shard_map/ppermute | solution.py:96
  709.5 40.1 %collective-permute-start.128 = (bf16[256,2048]{1,0:T(8,128)(2,1)}, bf16[256,2048]{1,0:T(8,128)(2,1)}, u32[]{:S(2)}, u32[]{:S(2)}) collective-permute-start(bf16[256,2048]{1,0:T(8,128)(2,1)} %fusion.50), channel_id=1, source_target_pairs={{8,0},{10,2},{16,8},{18,10},{24,16},{26,18},{28,24},{30,26},{20,28... | collective-permute-start | bytes 3145736 | tf_op jit(solution)/shard_map/ppermute | solution.py:99
  713.6 40.7 %collective-permute-start.124 = (bf16[256,2048]{1,0:T(8,128)(2,1)}, bf16[256,2048]{1,0:T(8,128)(2,1)}, u32[]{:S(2)}, u32[]{:S(2)}) collective-permute-start(bf16[256,2048]{1,0:T(8,128)(2,1)} %fusion.47), channel_id=1, source_target_pairs={{0,8},{2,10},{8,16},{10,18},{16,24},{18,26},{24,28},{26,30},{28,20... | collective-permute-start | bytes 3145736 | tf_op jit(solution)/shard_map/ppermute | solution.py:96
  729.4 29.7 %collective-permute-start.65 = (bf16[256,2048]{1,0:T(8,128)(2,1)S(1)}, bf16[256,2048]{1,0:T(8,128)(2,1)S(1)}, u32[]{:S(2)}, u32[]{:S(2)}) collective-permute-start(bf16[256,2048]{1,0:T(8,128)(2,1)S(1)} %get-tuple-element.255), channel_id=1, source_target_pairs={{0,1},{1,0},{2,3},{3,2},{4,5},{5,4},{6,7},{7,6},{8,9},{9,8},{10,11... | collective-permute-start | bytes 3145736 | tf_op jit(solution)/shard_map/ppermute | solution.py:106
  741.0 70.7 %collective-permute-start.120 = (bf16[256,2048]{1,0:T(8,128)(2,1)}, bf16[256,2048]{1,0:T(8,128)(2,1)}, u32[]{:S(2)}, u32[]{:S(2)}) collective-permute-start(bf16[256,2048]{1,0:T(8,128)(2,1)} %fusion.43), channel_id=1, source_target_pairs={{8,0},{10,2},{16,8},{18,10},{24,16},{26,18},{28,24},{30,26},{20,28... | collective-permute-start | bytes 3145736 | tf_op jit(solution)/shard_map/ppermute | solution.py:99
  745.7 73.0 %collective-permute-start.116 = (bf16[256,2048]{1,0:T(8,128)(2,1)}, bf16[256,2048]{1,0:T(8,128)(2,1)}, u32[]{:S(2)}, u32[]{:S(2)}) collective-permute-start(bf16[256,2048]{1,0:T(8,128)(2,1)} %fusion.40), channel_id=1, source_target_pairs={{0,8},{2,10},{8,16},{10,18},{16,24},{18,26},{24,28},{26,30},{28,20... | collective-permute-start | bytes 3145736 | tf_op jit(solution)/shard_map/ppermute | solution.py:96
  753.2 70.4 %collective-permute-start.129 = (bf16[256,2048]{1,0:T(8,128)(2,1)}, bf16[256,2048]{1,0:T(8,128)(2,1)}, u32[]{:S(2)}, u32[]{:S(2)}) collective-permute-start(bf16[256,2048]{1,0:T(8,128)(2,1)} %fusion.49), channel_id=1, source_target_pairs={{8,0},{10,2},{16,8},{18,10},{24,16},{26,18},{28,24},{30,26},{20,28... | collective-permute-start | bytes 3145736 | tf_op jit(solution)/shard_map/ppermute | solution.py:99
  757.8 70.9 %collective-permute-start.125 = (bf16[256,2048]{1,0:T(8,128)(2,1)}, bf16[256,2048]{1,0:T(8,128)(2,1)}, u32[]{:S(2)}, u32[]{:S(2)}) collective-permute-start(bf16[256,2048]{1,0:T(8,128)(2,1)} %fusion.46), channel_id=1, source_target_pairs={{0,8},{2,10},{8,16},{10,18},{16,24},{18,26},{24,28},{26,30},{28,20... | collective-permute-start | bytes 3145736 | tf_op jit(solution)/shard_map/ppermute | solution.py:96
  793.4 41.0 %collective-permute-start.66 = (bf16[512,2,256]{0,2,1:T(8,128)(2,1)S(1)}, bf16[512,2,256]{0,2,1:T(8,128)(2,1)S(1)}, u32[]{:S(2)}, u32[]{:S(2)}) collective-permute-start(bf16[512,2,256]{0,2,1:T(8,128)(2,1)S(1)} %slice.466), channel_id=1, source_target_pairs={{2,0},{4,2},{6,4},{8,6},{10,8},{12,10},{14,12},{16,14},{18,16},{20... | collective-permute-start | bytes 1572872 | tf_op jit(solution)/shard_map/ppermute | solution.py:524
  818.8 96.5 %collective-permute-start.78 = (bf16[8,128,1024]{2,1,0:T(8,128)(2,1)}, bf16[8,128,1024]{2,1,0:T(8,128)(2,1)}, u32[]{:S(2)}, u32[]{:S(2)}) collective-permute-start(bf16[8,128,1024]{2,1,0:T(8,128)(2,1)} %fusion.87), channel_id=1, source_target_pairs={{0,2},{2,0},{4,6},{6,4},{8,10},{10,8},{12,14},{14,12},{16,18},{18,... | collective-permute-start | bytes 6291464 | tf_op jit(solution)/shard_map/ppermute | solution.py:102
  823.6 28.2 %collective-permute-start.121 = (bf16[256,2048]{1,0:T(8,128)(2,1)}, bf16[256,2048]{1,0:T(8,128)(2,1)}, u32[]{:S(2)}, u32[]{:S(2)}) collective-permute-start(bf16[256,2048]{1,0:T(8,128)(2,1)} %fusion.42), channel_id=1, source_target_pairs={{8,0},{10,2},{16,8},{18,10},{24,16},{26,18},{28,24},{30,26},{20,28... | collective-permute-start | bytes 3145736 | tf_op jit(solution)/shard_map/ppermute | solution.py:99
  828.7 26.4 %collective-permute-start.117 = (bf16[256,2048]{1,0:T(8,128)(2,1)}, bf16[256,2048]{1,0:T(8,128)(2,1)}, u32[]{:S(2)}, u32[]{:S(2)}) collective-permute-start(bf16[256,2048]{1,0:T(8,128)(2,1)} %fusion.39), channel_id=1, source_target_pairs={{0,8},{2,10},{8,16},{10,18},{16,24},{18,26},{24,28},{26,30},{28,20... | collective-permute-start | bytes 3145736 | tf_op jit(solution)/shard_map/ppermute | solution.py:96
  832.7 38.8 %collective-permute-start.130 = (bf16[256,2048]{1,0:T(8,128)(2,1)}, bf16[256,2048]{1,0:T(8,128)(2,1)}, u32[]{:S(2)}, u32[]{:S(2)}) collective-permute-start(bf16[256,2048]{1,0:T(8,128)(2,1)} %fusion.48), channel_id=1, source_target_pairs={{8,0},{10,2},{16,8},{18,10},{24,16},{26,18},{28,24},{30,26},{20,28... | collective-permute-start | bytes 3145736 | tf_op jit(solution)/shard_map/ppermute | solution.py:99
  834.3 41.8 %collective-permute-start.126 = (bf16[256,2048]{1,0:T(8,128)(2,1)}, bf16[256,2048]{1,0:T(8,128)(2,1)}, u32[]{:S(2)}, u32[]{:S(2)}) collective-permute-start(bf16[256,2048]{1,0:T(8,128)(2,1)} %fusion.45), channel_id=1, source_target_pairs={{0,8},{2,10},{8,16},{10,18},{16,24},{18,26},{24,28},{26,30},{28,20... | collective-permute-start | bytes 3145736 | tf_op jit(solution)/shard_map/ppermute | solution.py:96
  851.8 29.2 %collective-permute-start.68 = (bf16[256,2048]{1,0:T(8,128)(2,1)S(1)}, bf16[256,2048]{1,0:T(8,128)(2,1)S(1)}, u32[]{:S(2)}, u32[]{:S(2)}) collective-permute-start(bf16[256,2048]{1,0:T(8,128)(2,1)S(1)} %copy-done.84), channel_id=1, source_target_pairs={{0,1},{1,0},{2,3},{3,2},{4,5},{5,4},{6,7},{7,6},{8,9},{9,8},{10,11... | collective-permute-start | bytes 3145736 | tf_op jit(solution)/shard_map/ppermute | solution.py:106
  855.1 89.2 %collective-permute-start.69 = (bf16[8,128,1536]{2,1,0:T(8,128)(2,1)}, bf16[8,128,1536]{2,1,0:T(8,128)(2,1)}, u32[]{:S(2)}, u32[]{:S(2)}) collective-permute-start(bf16[8,128,1536]{2,1,0:T(8,128)(2,1)} %fusion.31), channel_id=1, source_target_pairs={{0,2},{2,0},{4,6},{6,4},{8,10},{10,8},{12,14},{14,12},{16,18},{18,... | collective-permute-start | bytes 9437192 | tf_op jit(solution)/shard_map/ppermute | solution.py:102
  871.5 61.3 %collective-permute-start.122 = (f32[128,2048]{1,0:T(8,128)}, f32[128,2048]{1,0:T(8,128)}, u32[]{:S(2)}, u32[]{:S(2)}) collective-permute-start(f32[128,2048]{1,0:T(8,128)} %get-tuple-element.254), channel_id=1, source_target_pairs={{0,2},{2,0},{4,6},{6,4},{8,10},{10,8},{12,14},{14,12},{16,18},{18,... | collective-permute-start | bytes 3145736 | tf_op jit(solution)/shard_map/ppermute | solution.py:102
  880.9 56.8 %collective-permute-start.131 = (f32[128,2048]{1,0:T(8,128)}, f32[128,2048]{1,0:T(8,128)}, u32[]{:S(2)}, u32[]{:S(2)}) collective-permute-start(f32[128,2048]{1,0:T(8,128)} %get-tuple-element.252), channel_id=1, source_target_pairs={{0,2},{2,0},{4,6},{6,4},{8,10},{10,8},{12,14},{14,12},{16,18},{18,... | collective-permute-start | bytes 3145736 | tf_op jit(solution)/shard_map/ppermute | solution.py:102
  911.5 29.2 %collective-permute-start.87 = (bf16[8,128,768]{2,1,0:T(8,128)(2,1)}, bf16[8,128,768]{2,1,0:T(8,128)(2,1)}, u32[]{:S(2)}, u32[]{:S(2)}) collective-permute-start(bf16[8,128,768]{2,1,0:T(8,128)(2,1)} %bitcast.427), channel_id=1, source_target_pairs={{0,2},{2,0},{4,6},{6,4},{8,10},{10,8},{12,14},{14,12},{16,18},{18,... | collective-permute-start | bytes 4718600 | tf_op jit(solution)/shard_map/ppermute | solution.py:102
  930.5 46.2 %collective-permute-start.83 = (bf16[64,1024]{1,0:T(8,128)(2,1)S(1)}, bf16[64,1024]{1,0:T(8,128)(2,1)S(1)}, u32[]{:S(2)}, u32[]{:S(2)}) collective-permute-start(bf16[64,1024]{1,0:T(8,128)(2,1)S(1)} %get-tuple-element.296), channel_id=1, source_target_pairs={{8,0},{10,2},{16,8},{18,10},{24,16},{26,18},{28,24},{30,26},{20,28... | collective-permute-start | bytes 393224 | tf_op jit(solution)/shard_map/ppermute | solution.py:99
  932.8 30.8 %collective-permute-start.80 = (bf16[128,1024]{1,0:T(8,128)(2,1)S(1)}, bf16[128,1024]{1,0:T(8,128)(2,1)S(1)}, u32[]{:S(2)}, u32[]{:S(2)}) collective-permute-start(bf16[128,1024]{1,0:T(8,128)(2,1)S(1)} %fusion.140), channel_id=1, source_target_pairs={{0,8},{2,10},{8,16},{10,18},{16,24},{18,26},{24,28},{26,30},{28,20... | collective-permute-start | bytes 786440 | tf_op jit(solution)/shard_map/ppermute | solution.py:96
  977.4 42.2 %collective-permute-start.82 = (bf16[128,1024]{1,0:T(8,128)(2,1)S(1)}, bf16[128,1024]{1,0:T(8,128)(2,1)S(1)}, u32[]{:S(2)}, u32[]{:S(2)}) collective-permute-start(bf16[128,1024]{1,0:T(8,128)(2,1)S(1)} %get-tuple-element.241), channel_id=1, source_target_pairs={{0,8},{2,10},{8,16},{10,18},{16,24},{18,26},{24,28},{26,30},{28,20... | collective-permute-start | bytes 786440 | tf_op jit(solution)/shard_map/ppermute | solution.py:96
  (235 other events, 3621.6 us)

commit v2 on v1

v2 whole, which is shorter than its diff:
```python
import functools

import jax
import jax.numpy as jnp
from jax import lax
from jax.experimental import pallas as pl
from jax.experimental.pallas import tpu as pltpu
from jax.sharding import PartitionSpec as P

HD = 256
EPS = 1e-06
ROOT_HALF = 0.7071067811865476
NEGATIVE = -1e30
F32 = jnp.float32
BF16 = jnp.bfloat16


def norm_gain(values, gains):
    return values * lax.rsqrt(jnp.mean(values * values, axis=-1, keepdims=True) + EPS) * gains


def norm_plain(values):
    return values * lax.rsqrt(jnp.mean(values * values, axis=-1, keepdims=True) + EPS)


def gelu_tanh(values):
    return jax.nn.gelu(values, approximate=True)


def rope_tables(positions, head_width):
    positions = positions.astype(F32)[:, None]
    frequency = 10000.0 ** (-2.0 * jnp.arange(head_width // 2, dtype=F32) / head_width)
    angles = positions * frequency[None, :]
    return (jnp.cos(angles), jnp.sin(angles))


def rotate(values, cosines, sines):
    half_width = values.shape[-1] // 2
    front_half = values[..., :half_width]
    back_half = values[..., half_width:]
    cos_wide = cosines[:, None, :]
    sin_wide = sines[:, None, :]
    return jnp.concatenate(
        [
            front_half * cos_wide - back_half * sin_wide,
            back_half * cos_wide + front_half * sin_wide,
        ],
        axis=-1,
    )


def to_float(values):
    return values.astype(F32)


def low(values):
    return values.astype(BF16)


def product(left_in, right_in):
    return jnp.dot(left_in, right_in, preferred_element_type=F32)


def product_t(left_in, right_in):
    return lax.dot_general(left_in, right_in, (((1,), (1,)), ((), ())), preferred_element_type=F32)


def product_l(left_in, right_in):
    return lax.dot_general(left_in, right_in, (((0,), (0,)), ((), ())), preferred_element_type=F32)


def tie(*values):
    return lax.optimization_barrier(values)


class Ring:
    def __init__(self):
        self.devices = lax.axis_size("dp")
        self.chips = self.devices // 2
        order = list(range(0, self.chips, 2)) + list(range(self.chips - 1, 0, -2))
        self.cw = [
            (2 * order[p] + c, 2 * order[(p + 1) % self.chips] + c)
            for p in range(self.chips)
            for c in range(2)
        ]
        self.ccw = [(b, a) for a, b in self.cw]
        self.core_pairs = [(d, d ^ 1) for d in range(self.devices)]
        me = lax.axis_index("dp")
        self.core = lax.rem(me, 2)
        self.chip = me // 2
        self.place = jnp.where(
            lax.rem(self.chip, 2) == 0, self.chip // 2, self.chips - 1 - self.chip // 2
        )

    def chip_at(self, offset):
        place = lax.rem(self.place + offset + self.chips, self.chips)
        return jnp.where(place < self.chips // 2, 2 * place, 2 * (self.chips - 1 - place) + 1)

    def up(self, values):
        return lax.ppermute(values, "dp", self.cw)

    def down(self, values):
        return lax.ppermute(values, "dp", self.ccw)

    def swap(self, values):
        return lax.ppermute(values, "dp", self.core_pairs)


def across(values):
    return lax.ppermute(values, "tensor", [(0, 1), (1, 0)])


def remote(source, target, sends, receives, index, device):
    return pltpu.make_async_remote_copy(
        src_ref=source,
        dst_ref=target,
        send_sem=sends.at[index],
        recv_sem=receives.at[index],
        device_id=device,
        device_id_type=pl.DeviceIdType.MESH,
    )


def greet(devices):
    barrier = pltpu.get_barrier_semaphore()
    for device in devices:
        pl.semaphore_signal(
            barrier, inc=1, device_id=device, device_id_type=pl.DeviceIdType.MESH
        )
    pl.semaphore_wait(barrier, len(devices))


def block_rows(ref, start, count):
    return ref.at[pl.ds(pl.multiple_of(start, 16), count)]


class Hops:
    def __init__(self):
        me = lax.axis_index("dp")
        self.chips = lax.axis_size("dp") // 2
        self.core = lax.rem(me, 2)
        self.chip = me // 2
        self.place = jnp.where(
            lax.rem(self.chip, 2) == 0, self.chip // 2, self.chips - 1 - self.chip // 2
        )
        self.partner = {"dp": self.chip * 2 + 1 - self.core}
        self.above = {"dp": self.chip_at(1) * 2 + self.core}
        self.below = {"dp": self.chip_at(-1) * 2 + self.core}
        self.across = {"tensor": 1 - lax.axis_index("tensor")}

    def chip_at(self, offset):
        place = lax.rem(self.place + offset + self.chips, self.chips)
        return jnp.where(place < self.chips // 2, 2 * place, 2 * (self.chips - 1 - place) + 1)


def first_kernel(count, ff_cols, *refs):
    blocks, refs = refs[:count], refs[count:]
    (gate, up, down, tokens), refs = refs[:4], refs[4:]
    wholes, refs = refs[:count], refs[count:]
    (gate_up_own, down_own, other_tokens), refs = refs[:3], refs[3:]
    stages, refs = refs[: 3 + count], refs[3 + count :]
    in_sems, out_sems, ring_send, ring_recv, pair_send, pair_recv, ff_send, ff_recv = refs
    hops = Hops()
    half = hops.chips // 2
    rows = blocks[0].shape[0]
    greet([hops.above, hops.below, hops.partner, hops.across])
    started = []

    def place(ref, offset, top, size):
        return block_rows(ref, (2 * hops.chip_at(offset) + hops.core) * rows + top, size)

    def to_partner(number, which, offset, top, size, source=None):
        spot = place(wholes[which], offset, top, size)
        copy = remote(
            spot if source is None else source,
            spot,
            pair_send,
            pair_recv,
            (number, which),
            hops.partner,
        )
        copy.start()
        started.append(copy)
        pairs.append(copy)

    def onward(direction, k, which, offset, top, size, source=None):
        spot = place(wholes[which], offset, top, size)
        copy = remote(
            spot if source is None else source,
            spot,
            ring_send,
            ring_recv,
            (direction, k, which),
            hops.above if direction == 0 else hops.below,
        )
        copy.start()
        started.append(copy)
        arrivals[(direction, k, which)] = copy

    pairs, arrivals, locals_ = [], {}, []
    for which in range(count):
        for direction in range(2):
            onward(direction, 0, which, 0, 0, rows, blocks[which])
    own_rows = pl.ds(pl.multiple_of(hops.core * rows, 16), rows)
    mine = pl.ds(pl.multiple_of(hops.core * ff_cols, 128), ff_cols)
    theirs = pl.ds(pl.multiple_of((1 - hops.core) * ff_cols, 128), ff_cols)
    targets = [
        gate_up_own.at[own_rows, pl.ds(0, ff_cols)],
        gate_up_own.at[own_rows, pl.ds(ff_cols, ff_cols)],
        down_own.at[own_rows],
    ]
    ff_copies = [remote(tokens, other_tokens, ff_send, ff_recv, (3,), hops.across)]
    ff_copies[0].start()
    for number, (weight, target) in enumerate(zip((gate, up, down), targets)):
        copy = remote(
            weight.at[:, theirs], target, ff_send, ff_recv, (number,), hops.partner
        )
        copy.start()
        ff_copies.append(copy)
        locals_.append((weight.at[:, mine], target, number))
    for which in range(count):
        to_partner(0, which, 0, 0, rows, blocks[which])
        locals_.append((blocks[which], place(wholes[which], 0, 0, rows), 3 + which))
    loads = [
        pltpu.make_async_copy(source, stages[number], in_sems.at[number])
        for source, _, number in locals_
    ]
    for copy in loads:
        copy.start()
    stores = [
        pltpu.make_async_copy(stages[number], target, out_sems.at[number])
        for _, target, number in locals_
    ]
    for load, store in zip(loads, stores):
        load.wait()
        store.start()
    cut = rows // 2
    for k in range(1, half + 1):
        for which in range(count):
            for direction in range(2):
                arrivals[(direction, k - 1, which)].wait_recv()
                offset = -k if direction == 0 else k
                if k < half - 1:
                    onward(direction, k, which, offset, 0, rows)
                elif k == half - 1:
                    onward(direction, k, which, offset, direction * cut, cut)
                if k < half:
                    to_partner(2 * k - 1 + direction, which, offset, 0, rows)
                else:
                    to_partner(2 * k - 1 + direction, which, half, direction * cut, cut)
    for copy in ff_copies + pairs:
        copy.wait_recv()
    for copy in ff_copies + started:
        copy.wait_send()
    for copy in stores:
        copy.wait()


ANY = pl.BlockSpec(memory_space=pl.ANY)


def comm_call(kernel, number, operands, shapes, stages, semaphores, name):
    moved = sum(v.size * 2 for v in shapes)
    return pl.pallas_call(
        kernel,
        out_shape=shapes,
        in_specs=[ANY] * len(operands),
        out_specs=[ANY] * len(shapes),
        scratch_shapes=stages + [pltpu.SemaphoreType.DMA(shape) for shape in semaphores],
        compiler_params=pltpu.CompilerParams(
            collective_id=number, has_side_effects=True, vmem_limit_bytes=16 * 2**20
        ),
        cost_estimate=pl.CostEstimate(flops=0, bytes_accessed=8 * moved, transcendentals=0),
        name=name,
    )(*operands)


def first_gather(blocks, gate, up, down, tokens):
    chips = lax.axis_size("dp") // 2
    half = chips // 2
    rows = blocks[0].shape[0]
    ff_cols = gate.shape[1] // 2
    count = len(blocks)
    shapes = [
        jax.ShapeDtypeStruct((2 * chips * rows, block.shape[1]), block.dtype) for block in blocks
    ] + [
        jax.ShapeDtypeStruct((2 * rows, 2 * ff_cols), gate.dtype),
        jax.ShapeDtypeStruct((2 * rows, ff_cols), gate.dtype),
        jax.ShapeDtypeStruct(tokens.shape, tokens.dtype),
    ]
    stages = [pltpu.VMEM((rows, ff_cols), gate.dtype)] * 3 + [
        pltpu.VMEM(block.shape, block.dtype) for block in blocks
    ]
    semaphores = [
        (3 + count,),
        (3 + count,),
        (2, half, count),
        (2, half, count),
        (2 * half + 1, count),
        (2 * half + 1, count),
        (4,),
        (4,),
    ]
    out = comm_call(
        functools.partial(first_kernel, count, ff_cols),
        0,
        (*blocks, gate, up, down, tokens),
        shapes,
        stages,
        semaphores,
        "first_gather",
    )
    return out[:count], out[count:]


GELU_SCALE = 0.7978845608028654
GELU_CUBE = 0.044715
ROW_TILE = 1024


def fill(spots, whole, parts):
    for number, part in enumerate(parts):
        size = part.shape[0]
        whole[pl.ds(pl.multiple_of(spots[number], size), size), :] = part[...]


def gate_up_kernel(count, spots, x, *refs):
    gate_parts, up_parts = refs[:count], refs[count : 2 * count]
    raw, hidden, weights = refs[2 * count :]
    gate_w, up_w = weights.at[0], weights.at[1]
    fill(spots, gate_w, gate_parts)
    fill(spots, up_w, up_parts)

    @pl.loop(0, x.shape[0] // min(ROW_TILE, x.shape[0]))
    def _(i):
        at = pl.ds(pl.multiple_of(i * ROW_TILE, ROW_TILE), ROW_TILE)
        rows = x[at, :]
        gate = product(rows, gate_w[...])
        up = product(rows, up_w[...])
        raw[0, at, :] = low(gate)
        raw[1, at, :] = low(up)
        bend = jnp.tanh(GELU_SCALE * (gate + GELU_CUBE * gate * gate * gate))
        hidden[at, :] = low(0.5 * gate * (1.0 + bend) * up)


def hidden_back_kernel(count, spots, x, raw, *refs):
    parts, (out, whole) = refs[:count], refs[count:]
    fill(spots, whole, parts)

    @pl.loop(0, x.shape[0] // min(ROW_TILE, x.shape[0]))
    def _(i):
        at = pl.ds(pl.multiple_of(i * ROW_TILE, ROW_TILE), ROW_TILE)
        d_hidden = product(x[at, :], whole[...])
        gate = to_float(raw[0, at, :])
        up = to_float(raw[1, at, :])
        square = gate * gate
        bend = jnp.tanh(GELU_SCALE * gate * (1.0 + GELU_CUBE * square))
        plus = 0.5 * (1.0 + bend)
        slope = plus + 0.5 * gate * (1.0 - bend * bend) * GELU_SCALE * (
            1.0 + 3.0 * GELU_CUBE * square
        )
        out[0, at, :] = low(d_hidden * up * slope)
        out[1, at, :] = low(d_hidden * gate * plus)


def columns_kernel(count, spots, h, *refs):
    parts, (out, whole) = refs[:count], refs[count:]
    fill(spots, whole, parts)
    step = pl.program_id(0)
    width = out.shape[1]
    cols = min(512, width)


    @pl.loop(0, width // cols)
    def _(j):
        across_ = pl.ds(pl.multiple_of(j * cols, cols), cols)
        term = product_t(h[0], whole[across_, :])

        @pl.when(step == 0)
        def _():
            out[:, across_] = term

        @pl.when(step > 0)
        def _():
            out[:, across_] = out[:, across_] + term


def block_kernel(where, spots, x, d, *refs):
    got, (out, turned) = refs[:-2], refs[-2:]

    @pl.when(pl.program_id(0) == 0)
    def _():
        turned[...] = x[...].T

    term = product(turned[...], d[0])
    if where == "none":
        out[...] = term.astype(out.dtype)
    elif where == "all":
        out[...] = low(term + to_float(got[0][...]))
    else:
        cut = got[0].shape[0]
        top, bottom = term[:cut], term[cut:]
        if where == "top":
            top = top + to_float(got[0][...])
        else:
            bottom = bottom + to_float(got[0][...])
        out[:cut, :] = low(top)
        out[cut:, :] = low(bottom)


def grid_call(kernel, spots, grid, operands, in_specs, shapes, out_specs, scratch, flops, name):
    moved = sum(v.size * v.dtype.itemsize for v in (*operands, *jax.tree.leaves(shapes)))
    return pl.pallas_call(
        kernel,
        grid_spec=pltpu.PrefetchScalarGridSpec(
            num_scalar_prefetch=1,
            grid=grid,
            in_specs=in_specs,
            out_specs=out_specs,
            scratch_shapes=scratch,
        ),
        out_shape=shapes,
        compiler_params=pltpu.CompilerParams(
            dimension_semantics=("arbitrary",) * len(grid), vmem_limit_bytes=56 * 2**20
        ),
        cost_estimate=pl.CostEstimate(flops=flops, bytes_accessed=moved, transcendentals=0),
        name=name,
    )(spots, *operands)


def once(shape):
    return pl.BlockSpec(
        shape, lambda *index: (0,) * len(shape), pipeline_mode=pl.Buffered(buffer_count=1)
    )


def gate_up(x, spots, parts, tile=512):
    count, (m, width), ff = len(parts), x.shape, parts[0].shape[1] // 2
    tiles = ff // tile
    part_specs = [pl.BlockSpec((p.shape[0], tile), lambda n, s: (0, n)) for p in parts] + [
        pl.BlockSpec((p.shape[0], tile), lambda n, s: (0, n + tiles)) for p in parts
    ]
    return grid_call(
        functools.partial(gate_up_kernel, count),
        spots,
        (tiles,),
        (x, *parts, *parts),
        [once((m, width))] + part_specs,
        [
            jax.ShapeDtypeStruct((2, m, ff), BF16),
            jax.ShapeDtypeStruct((m, ff), BF16),
            jax.ShapeDtypeStruct((2, width, ff), BF16),
        ],
        [
            pl.BlockSpec((2, m, tile), lambda n, s: (0, 0, n)),
            pl.BlockSpec((m, tile), lambda n, s: (0, n)),
            pl.BlockSpec((2, width, tile), lambda n, s: (0, 0, n)),
        ],
        [],
        4 * m * width * ff,
        "gate_up",
    )


def hidden_back(x, raw, spots, parts, tile=256):
    count, (m, width), ff = len(parts), x.shape, parts[0].shape[1]
    part_specs = [pl.BlockSpec((p.shape[0], tile), lambda n, s: (0, n)) for p in parts]
    return grid_call(
        functools.partial(hidden_back_kernel, count),
        spots,
        (ff // tile,),
        (x, raw, *parts),
        [once((m, width)), pl.BlockSpec((2, m, tile), lambda n, s: (0, 0, n))] + part_specs,
        jax.ShapeDtypeStruct((2, m, ff), BF16),
        pl.BlockSpec((2, m, tile), lambda n, s: (0, 0, n)),
        [pltpu.VMEM((width, tile), BF16)],
        2 * m * width * ff,
        "hidden_back",
    )


def columns_out(h, spots, parts, width, tile=1024):
    count, (groups, m, ff) = len(parts), h.shape
    tile = min(tile, ff)
    tiles = ff // tile
    part_specs = [pl.BlockSpec((p.shape[0], tile), lambda f, s: (0, f)) for p in parts]
    return grid_call(
        functools.partial(columns_kernel, count),
        spots,
        (groups * tiles,),
        (h, *parts),
        [pl.BlockSpec((1, m, tile), lambda f, s: (f // tiles, 0, f % tiles))] + part_specs,
        jax.ShapeDtypeStruct((m, width), F32),
        once((m, width)),
        [pltpu.VMEM((width, tile), BF16)],
        2 * groups * m * width * ff,
        "columns_out",
    )


def block_grad(x, d, chip, size, got=None, where="none", dtype=BF16, tile=2048):
    (m, _), (groups, _, ff) = x.shape, d.shape
    tile = min(tile, ff)
    tiles = ff // tile
    more = [] if got is None else [got]
    if size % 128:
        x = lax.dynamic_slice_in_dim(x, chip * size, size, 1)
        chip = jnp.zeros((), jnp.int32)
    return grid_call(
        functools.partial(block_kernel, where),
        chip.reshape(1).astype(jnp.int32),
        (groups * tiles,),
        (x, d, *more),
        [
            pl.BlockSpec((m, size), lambda f, s: (0, s[0])),
            pl.BlockSpec((1, m, tile), lambda f, s: (f // tiles, 0, f % tiles)),
        ]
        + [pl.BlockSpec((v.shape[0], tile), lambda f, s: (0, f)) for v in more],
        jax.ShapeDtypeStruct((size, groups * ff), dtype),
        pl.BlockSpec((size, tile), lambda f, s: (0, f)),
        [pltpu.VMEM((size, m), BF16)],
        2 * groups * m * size * ff,
        "block_grad",
    )


def row_kernel(pairs, spots, *refs):
    xs, ds = refs[:pairs], refs[pairs : 2 * pairs]
    more, out = refs[2 * pairs : -1], refs[-1]
    start = 0
    for x, d in zip(xs, ds):
        cols = d.shape[1]
        out[:, start : start + cols] = product_l(x[...], d[...]).astype(out.dtype)
        start += cols
    out[:, start:] = more[0][...].astype(out.dtype)
    if len(more) > 1:
        out[...] = out[...] + more[1][...].astype(out.dtype)


def row_grads(pairs, last, which, chips, rows, got, dtype):
    xs, ds = [x for x, _ in pairs], [d for _, d in pairs]
    cols = sum(d.shape[1] for d in ds) + last.shape[1]
    more = [] if got is None else [got]
    return grid_call(
        functools.partial(row_kernel, len(pairs)),
        (2 * jnp.arange(chips) + which).astype(jnp.int32),
        (chips,),
        (*xs, *ds, last, *more),
        [pl.BlockSpec((x.shape[0], rows), lambda j, s: (0, s[j])) for x in xs]
        + [once(d.shape) for d in ds]
        + [pl.BlockSpec((rows, last.shape[1]), lambda j, s: (s[j], 0))]
        + [pl.BlockSpec((rows, cols), lambda j, s: (j, 0)) for _ in more],
        jax.ShapeDtypeStruct((chips * rows, cols), dtype),
        pl.BlockSpec((rows, cols), lambda j, s: (j, 0)),
        [],
        sum(2 * d.size * chips * rows for d in ds),
        "row_grads",
    )


def last_kernel(count, *refs):
    terms, refs = refs[:count], refs[count:]
    outs, refs = refs[:count], refs[count:]
    sent, refs = refs[:count], refs[count:]
    got, refs = refs[:count], refs[count:]
    ring_send, ring_recv = refs
    hops = Hops()
    half = hops.chips // 2
    rows = outs[0].shape[0]
    cut = rows // 2
    greet([hops.above, hops.below])
    copies = {}

    def term(which, offset, top, size):
        at = pl.multiple_of(hops.chip_at(offset) * rows + top, 16)
        return terms[which][pl.ds(at, size), :]

    def send(which, direction, k, size):
        copy = remote(
            sent[which].at[direction, k, pl.ds(0, size)],
            got[which].at[direction, k, pl.ds(0, size)],
            ring_send,
            ring_recv,
            (direction, k, which),
            hops.above if direction == 0 else hops.below,
        )
        copy.start()
        copies[(which, direction, k)] = copy

    for which in range(count):
        for direction in range(2):
            sent[which][direction, 0, :cut, :] = low(term(which, half, direction * cut, cut))
            send(which, direction, 0, cut)
    for k in range(1, half):
        offset = half - k
        for which in range(count):
            for direction in range(2):
                there = offset if direction == 0 else -offset
                copies[(which, direction, k - 1)].wait_recv()
                came = got[which].at[direction, k - 1]
                if k == 1:
                    near, far = direction * cut, (1 - direction) * cut
                    sent[which][direction, k, near : near + cut, :] = low(
                        term(which, there, near, cut) + to_float(came[:cut, :])
                    )
                    sent[which][direction, k, far : far + cut, :] = low(
                        term(which, there, far, cut)
                    )
                else:
                    sent[which][direction, k] = low(
                        term(which, there, 0, rows) + to_float(came[...])
                    )
                send(which, direction, k, rows)
    for which in range(count):
        for direction in range(2):
            copies[(which, direction, half - 1)].wait_recv()
        outs[which][...] = (
            term(which, 0, 0, rows)
            + to_float(got[which][0, half - 1])
            + to_float(got[which][1, half - 1])
        )
    for copy in copies.values():
        copy.wait_send()


def last_reduce(terms):
    chips = lax.axis_size("dp") // 2
    half = chips // 2
    rows = terms[0].shape[0] // chips
    count = len(terms)
    moved = sum(v.size * 2 for v in terms)
    vmem = pl.BlockSpec(memory_space=pltpu.VMEM)
    buffers = [pltpu.VMEM((2, half, rows, v.shape[1]), BF16) for v in terms]
    return pl.pallas_call(
        functools.partial(last_kernel, count),
        out_shape=[jax.ShapeDtypeStruct((rows, v.shape[1]), F32) for v in terms],
        in_specs=[vmem] * count,
        out_specs=[vmem] * count,
        scratch_shapes=buffers
        + buffers
        + [pltpu.SemaphoreType.DMA((2, half, count)), pltpu.SemaphoreType.DMA((2, half, count))],
        compiler_params=pltpu.CompilerParams(
            collective_id=2, has_side_effects=True, vmem_limit_bytes=48 * 2**20
        ),
        cost_estimate=pl.CostEstimate(flops=0, bytes_accessed=8 * moved, transcendentals=0),
        name="last_reduce",
    )(*terms)


class Gather:
    def __init__(self, ring, block):
        self.ring = ring
        self.rows = block.shape[0]
        self.held = [block, block]
        self.parts = [(0, 0, block)]
        self.step_count = 0

    def step(self):
        ring, half = self.ring, self.ring.chips // 2
        self.step_count += 1
        k = self.step_count
        going_up, going_down = self.held
        if k < half:
            self.held = [ring.up(going_up), ring.down(going_down)]
            self.parts += [(-k, 0, self.held[0]), (k, 0, self.held[1])]
        else:
            cut = self.rows // 2
            self.held = [ring.up(going_up[:cut]), ring.down(going_down[cut:])]
            self.parts += [(half, 0, self.held[0]), (half, cut, self.held[1])]

    def pieces(self):
        spots = [self.ring.chip_at(o) * self.rows + row for o, row, _ in self.parts]
        return jnp.stack(spots).astype(jnp.int32), [part for _, _, part in self.parts]


class BlockReduce:
    def __init__(self, ring, x, d, size):
        self.ring, self.x, self.d, self.size = ring, x, d, size
        self.step_count = 0
        self.held = []

    def term(self, offset, got=None, where="none"):
        return block_grad(self.x, self.d, self.ring.chip_at(offset), self.size, got, where)

    def step(self):
        ring, half = self.ring, self.ring.chips // 2
        self.step_count += 1
        k = self.step_count
        if k == 1:
            term = self.term(half)
            cut = term.shape[0] // 2
            up, down = term[:cut], term[cut:]
        else:
            d = half + 1 - k
            up = self.term(d, self.held[0], "top" if k == 2 else "all")
            down = self.term(-d, self.held[1], "bottom" if k == 2 else "all")
        self.held = [ring.up(up), ring.down(down)]

    def result(self):
        term = block_grad(self.x, self.d, self.ring.chip_at(0), self.size, dtype=F32)
        return term + to_float(self.held[0]) + to_float(self.held[1])


def region(body):
    shapes = jax.eval_shape(body)
    yes = lax.optimization_barrier(jnp.array(True))
    return lax.cond(
        yes,
        body,
        lambda: jax.tree.map(lambda v: jnp.zeros(v.shape, v.dtype), shapes),
    )


def meet(rings, *values):
    held, values = tie([r.held for r in rings], values)
    for r, h in zip(rings, held):
        r.held = h
    return values if len(values) != 1 else values[0]


def local(
    tokens,
    layer_input,
    block_ids,
    block_table,
    w_query,
    w_key,
    w_value,
    w_output,
    w_left,
    w_right,
    w_gate,
    w_up,
    w_down,
    w_layer_gate,
    w_layer_proj,
    query_gain,
    key_gain,
    gain_input,
    gain_attn_out,
    gain_laurel,
    gain_ffw_in,
    gain_ffw_out,
    gain_layer_out,
    out_grad,
):
    ring = Ring()
    side = lax.axis_index("tensor")
    core = ring.core
    rows = w_query.shape[0]
    own = tokens.shape[0]
    width = tokens.shape[1]
    q_cols = w_query.shape[1]
    kv_cols = w_key.shape[1]
    rank = w_left.shape[1]
    small = w_layer_gate.shape[1]
    ff_cols = w_gate.shape[1] // 2
    chips = ring.chips

    def gain_block(query_part, key_part, parts):
        count = query_part.shape[0]
        columns = parts + [
            jnp.pad(query_part, (0, rows - count)),
            jnp.pad(key_part, (0, rows - count)),
        ]
        block = jnp.stack(columns, axis=1)
        return jnp.pad(block, ((0, 0), (0, 128 - block.shape[1])))

    gains = gain_block(
        query_gain,
        key_gain,
        [gain_input, gain_attn_out, gain_laurel, gain_ffw_in, gain_ffw_out, gain_layer_out],
    )
    half = chips // 2
    (qkv_full, output_t, small_full), (*ff_own, other_tokens) = first_gather(
        [
            jnp.concatenate([w_query, w_key, w_value], axis=1),
            w_output.T,
            jnp.concatenate([w_left, w_right.T, w_layer_gate, w_layer_proj.T, gains], axis=1),
        ],
        w_gate,
        w_up,
        w_down.T,
        tokens,
    )
    left_full = small_full[:, :rank]
    right_t = small_full[:, rank : 2 * rank]
    lgate_full = small_full[:, 2 * rank : 2 * rank + small]
    lproj_t = small_full[:, 2 * rank + small : 2 * rank + 2 * small]
    gains_full = small_full[:, 2 * rank + 2 * small :]

    gain_columns = to_float(gains_full[:, :8])
    (
        input_scale,
        attn_scale,
        laurel_scale,
        ffw_in_scale,
        ffw_out_scale,
        layer_scale,
    ) = (gain_columns[:, i] for i in range(6))
    head_part = query_gain.shape[0]

    def head_gain(column):
        return column.reshape(ring.devices, rows)[:, :head_part].reshape(HD)

    query_scale = head_gain(gain_columns[:, 6])
    key_scale = head_gain(gain_columns[:, 7])

    piece_len = 2 * own
    seq_total = block_ids.shape[1]
    per_seq = seq_total // piece_len
    dp_index = lax.axis_index("dp")
    row_index = dp_index // per_seq
    slot = lax.rem(dp_index, per_seq)
    first = slot * piece_len
    has_before = slot > 0
    has_after = slot < per_seq - 1
    natural = jnp.arange(piece_len, dtype=jnp.int32)
    here = first + lax.rem(natural + side * own, piece_len)
    cosines, sines = rope_tables(here, HD)
    reach_after = min(256, piece_len)
    forward_pairs = [(i, i + 1) for i in range(ring.devices - 1)]
    backward_pairs = [(i + 1, i) for i in range(ring.devices - 1)]

    def in_order(values):
        return jnp.where(
            side == 0, values, jnp.concatenate([values[own:], values[:own]], axis=0)
        )

    ids_row = lax.dynamic_index_in_dim(block_ids, row_index, 0, keepdims=False)
    table_row = lax.dynamic_index_in_dim(block_table, row_index, 0, keepdims=False)
    own_ids = lax.dynamic_slice_in_dim(ids_row, first, piece_len, 0)
    before_ids = lax.dynamic_slice_in_dim(ids_row, jnp.maximum(first - piece_len, 0), piece_len, 0)
    before_ids = jnp.where(has_before, before_ids, -2)
    after_ids = lax.dynamic_slice_in_dim(
        ids_row, jnp.minimum(first + piece_len, seq_total - reach_after), reach_after, 0
    )
    after_ids = jnp.where(has_after, after_ids, -2)
    key_ids = jnp.concatenate([before_ids, own_ids, after_ids], axis=0)
    query_ids = in_order(own_ids)
    block_count = block_table.shape[-1]
    number_rows = jnp.arange(block_count, dtype=jnp.int32)
    sees_last = jnp.sum(
        jnp.where(number_rows[None, :] == number_rows[:, None] - 1, table_row, 0), axis=1
    )
    query_sees = jnp.sum(
        jnp.where(query_ids[:, None] == number_rows[None, :], sees_last[None, :], 0), axis=1
    )
    previous_ids = jnp.where(query_sees == 1, query_ids - 1, query_ids)

    def prepare(qkv_in, query_gains, key_gains):
        query_in = qkv_in[:, :q_cols]
        key_in = qkv_in[:, q_cols : q_cols + kv_cols]
        value_in = qkv_in[:, q_cols + kv_cols :]
        query_out = rotate(
            norm_gain(query_in.reshape(piece_len, -1, HD), query_gains), cosines, sines
        )
        key_out = rotate(norm_gain(key_in.reshape(piece_len, -1, HD), key_gains), cosines, sines)
        return (query_out, key_out, norm_plain(value_in.reshape(piece_len, -1, HD)))

    heads_local = q_cols // HD
    kv_local = kv_cols // HD
    group = heads_local // kv_local

    def scores_for(query_low, keys_all):
        allowed = (query_ids[:, None] == key_ids[None, :]) | (
            previous_ids[:, None] == key_ids[None, :]
        )
        scores = jnp.einsum("qkgd,ckd->kgqc", query_low, keys_all, preferred_element_type=F32)
        return jnp.where(allowed[None, None], scores, NEGATIVE)

    def sum_sides(partial):
        return partial[:own] + to_float(across(low(partial[own:])))

    def both_sides(values):
        return jnp.concatenate([values, across(values)], axis=0)

    def four_ways(values):
        pair = both_sides(values)
        return jnp.concatenate([pair, ring.swap(pair)], axis=0)

    def sum_four(partial):
        pair = partial[: 2 * own] + to_float(ring.swap(low(partial[2 * own :])))
        return sum_sides(pair)

    def attend():
        normed_low = low(norm_gain(to_float(tokens), input_scale))
        seq_rows = jnp.concatenate(
            [normed_low, low(norm_gain(to_float(other_tokens), input_scale))], axis=0
        )
        qkv_raw = product(seq_rows, qkv_full)
        query_rot, key_rot, value_nrm = prepare(qkv_raw, query_scale, key_scale)
        query_low = low(query_rot).reshape(piece_len, kv_local, group, HD)
        kv_own = in_order(jnp.concatenate([low(key_rot), low(value_nrm)], axis=1))
        kv_before = lax.ppermute(kv_own, "dp", forward_pairs)
        kv_after = lax.ppermute(kv_own[:reach_after], "dp", backward_pairs)
        kv_all = jnp.concatenate([kv_before, kv_own, kv_after], axis=0)
        scores = scores_for(query_low, kv_all[:, :kv_local])
        highest = jnp.max(scores, axis=-1, keepdims=True)
        weights_exp = jnp.exp(scores - highest)
        totals = jnp.sum(weights_exp, axis=-1, keepdims=True)
        probs_low = low(weights_exp / totals)
        attended = jnp.einsum(
            "kgqc,ckd->qkgd", probs_low, kv_all[:, kv_local:], preferred_element_type=F32
        )
        log_totals = highest + jnp.log(totals)
        heads_low = low(attended.reshape(piece_len, heads_local * HD))
        return seq_rows, qkv_raw, query_low, kv_all, log_totals, heads_low

    gu = Gather(ring, ff_own[0])
    dn = Gather(ring, ff_own[1])
    gu.step()
    seq_rows, qkv_raw, query_low, kv_all, log_totals, heads_low = region(attend)
    heads_low = meet([gu], heads_low)
    gu.step()

    def join(heads_low):
        attn_out = sum_sides(product_t(heads_low, output_t))
        normed = norm_gain(to_float(tokens), input_scale)
        left_low = low(product(low(normed), left_full))
        right_out = product_t(left_low, right_t)
        laurel_normed = norm_gain(right_out, laurel_scale)
        attn_normed = norm_gain(attn_out, attn_scale)
        mixed = (to_float(tokens) + attn_normed + (normed + laurel_normed)) * ROOT_HALF
        return attn_out, left_low, right_out, mixed, low(norm_gain(mixed, ffw_in_scale))

    attn_out, left_low, right_out, mixed, ffw_low = region(lambda: join(heads_low))
    ffw_low = meet([gu], ffw_low)
    gu.step()
    ffw_rows = region(lambda: four_ways(ffw_low))
    ffw_rows = meet([gu], ffw_rows)
    for _ in range(half - 4):
        gu.step()
        ffw_rows = meet([gu], ffw_rows)
    gu.step()
    ffw_rows = meet([gu], ffw_rows)

    gu_spots, gu_parts = gu.pieces()
    dn.step()
    raw, hidden_low, gu_weights = region(lambda: gate_up(ffw_rows, gu_spots, gu_parts))
    raw, hidden_low = meet([dn], raw, hidden_low)
    for _ in range(half - 1):
        dn.step()
        raw, hidden_low = meet([dn], raw, hidden_low)
    dn_spots, dn_parts = dn.pieces()
    ffw_out = sum_four(columns_out(hidden_low[None], dn_spots, dn_parts, width))
    ffw_out_normed, ffw_out_back = jax.vjp(norm_gain, ffw_out, ffw_out_scale)
    block_mid = mixed + ffw_out_normed
    mid_low = low(block_mid)
    layer_pre = product(mid_low, lgate_full)

    def layer_gate_fn(pre_values, per_layer):
        return gelu_tanh(pre_values) * per_layer

    gated, gated_back = jax.vjp(layer_gate_fn, layer_pre, to_float(layer_input))
    gated_low = low(gated)
    layer_proj = product_t(gated_low, lproj_t)
    proj_normed, proj_back = jax.vjp(norm_gain, layer_proj, layer_scale)
    result = block_mid + proj_normed

    grad_out = to_float(out_grad)
    d_proj, d_layer_scale = proj_back(grad_out)
    d_proj_low = low(d_proj)
    d_gated = product(d_proj_low, lproj_t)
    d_pre, grad_layer_input = gated_back(d_gated)
    d_pre_low = low(d_pre)
    d_mid = grad_out + product_t(d_pre_low, lgate_full)
    d_ffw_out, d_ffw_out_scale = ffw_out_back(d_mid)
    d_ffw_rows = four_ways(low(d_ffw_out))
    d_ffw_rows, d_mid = tie(d_ffw_rows, d_mid)

    rd = BlockReduce(ring, d_ffw_rows, hidden_low[None], 2 * rows)
    rd.step()
    d_gate_up = region(lambda: hidden_back(d_ffw_rows, raw, dn_spots, dn_parts))
    d_gate_up = meet([rd], d_gate_up)
    rg = BlockReduce(ring, ffw_rows, d_gate_up, 2 * rows)
    rd.step()
    for _ in range(half - 4):
        d_gate_up = meet([rd], d_gate_up)
        rd.step()
    partial = region(
        lambda: product_t(d_gate_up[0], gu_weights[0]) + product_t(d_gate_up[1], gu_weights[1])
    )
    partial = meet([rd], partial)
    rd.step()
    rg.step()

    def back_3():
        d_ffw_normed = sum_four(partial)
        _, back = jax.vjp(norm_gain, mixed, ffw_in_scale)
        d_mixed_extra, d_ffw_in_scale = back(d_ffw_normed)
        d_branch = (d_mid + d_mixed_extra) * ROOT_HALF
        _, back = jax.vjp(norm_gain, attn_out, attn_scale)
        d_attn, d_attn_scale = back(d_branch)
        return d_ffw_in_scale, d_attn_scale, d_branch, low(d_attn)

    d_ffw_in_scale, d_attn_scale, d_branch, d_attn_low = meet([rd, rg], *region(back_3))
    rd.step()
    rg.step()

    def back_4():
        d_attn_rows = both_sides(d_attn_low)
        d_heads = low(product(d_attn_rows, output_t)).reshape(piece_len, kv_local, group, HD)
        keys_all, values_all = kv_all[:, :kv_local], kv_all[:, kv_local:]
        probs = jnp.exp(scores_for(query_low, keys_all) - log_totals)
        probs_low = low(probs)
        d_values_all = jnp.einsum(
            "kgqc,qkgd->ckd", probs_low, d_heads, preferred_element_type=F32
        )
        d_probs = jnp.einsum("qkgd,ckd->kgqc", d_heads, values_all, preferred_element_type=F32)
        deltas = jnp.sum(probs * d_probs, axis=-1, keepdims=True)
        d_scores = low(probs * (d_probs - deltas))
        d_keys_all = jnp.einsum("kgqc,qkgd->ckd", d_scores, query_low, preferred_element_type=F32)
        d_query_rot = jnp.einsum("kgqc,ckd->qkgd", d_scores, keys_all, preferred_element_type=F32)
        d_kv_all = jnp.concatenate([d_keys_all, d_values_all], axis=1)
        return d_attn_rows, d_kv_all, d_query_rot

    d_attn_rows, d_kv_all, d_query_rot = meet([rd, rg], *region(back_4))
    rg.step()
    for _ in range(half - 4):
        d_kv_all = meet([rg], d_kv_all)
        rg.step()

    def back_5():
        to_before = low(d_kv_all[:piece_len])
        to_after = low(d_kv_all[2 * piece_len :])
        from_after = to_float(lax.ppermute(to_before, "dp", backward_pairs))
        from_before = to_float(lax.ppermute(to_after, "dp", forward_pairs))
        d_kv = d_kv_all[piece_len : 2 * piece_len] + from_after
        d_kv = d_kv + jnp.pad(from_before, ((0, piece_len - reach_after), (0, 0), (0, 0)))
        d_kv = in_order(d_kv)
        _, back = jax.vjp(prepare, qkv_raw, query_scale, key_scale)
        d_qkv, query_scale_grad, key_scale_grad = back(
            (
                d_query_rot.reshape(piece_len, heads_local, HD),
                d_kv[:, :kv_local],
                d_kv[:, kv_local:],
            )
        )
        return low(d_qkv), query_scale_grad, key_scale_grad

    d_qkv_low, query_scale_grad, key_scale_grad = meet([rg], *region(back_5))
    rg.step()

    def own_columns(values, which):
        blocks = values.reshape(values.shape[0], chips, 2, rows)
        return lax.dynamic_index_in_dim(blocks, which, 2, keepdims=False).reshape(
            values.shape[0], chips * rows
        )

    def both_cores(pairs, last):
        if rows % 128 == 0:
            theirs = row_grads(pairs, last, 1 - core, chips, rows, None, BF16)
            return row_grads(pairs, last, core, chips, rows, ring.swap(theirs), F32)

        def terms(which):
            return jnp.concatenate(
                [product_l(own_columns(x, which), d) for x, d in pairs]
                + [own_columns(last.T, which).T],
                axis=1,
            )

        return terms(core) + to_float(ring.swap(low(terms(1 - core))))

    def head_gain_back(grads):
        padded = jnp.pad(grads.reshape(ring.devices, head_part), ((0, 0), (0, rows - head_part)))
        return padded.reshape(width)

    def back_6():
        normed, input_norm_back = jax.vjp(norm_gain, to_float(tokens), input_scale)
        _, laurel_back = jax.vjp(norm_gain, right_out, laurel_scale)
        d_right, d_laurel_scale = laurel_back(d_branch)
        d_right_low = low(d_right)
        d_left_low = low(product(d_right_low, right_t))
        d_normed = d_branch + product_t(d_left_low, left_full)
        d_normed = d_normed + sum_sides(product_t(d_qkv_low, qkv_full))
        d_inputs_extra, d_input_scale = input_norm_back(d_normed)
        grad_tokens = d_branch + d_inputs_extra
        gain_grads = jnp.stack(
            [
                d_input_scale,
                d_attn_scale,
                d_laurel_scale,
                d_ffw_in_scale,
                d_ffw_out_scale,
                d_layer_scale,
                head_gain_back(query_scale_grad),
                head_gain_back(key_scale_grad),
            ],
            axis=0,
        )
        gain_grads = jnp.pad(gain_grads, ((0, 120), (0, 0))).T
        summed = both_cores(
            [
                (d_attn_rows, heads_low),
                (seq_rows, d_qkv_low),
                (mid_low, d_pre_low),
                (d_proj_low, gated_low),
                (low(normed), d_left_low),
                (d_right_low, left_low),
            ],
            gain_grads,
        )
        large = 2 * q_cols + 2 * kv_cols
        part = (summed.shape[1] - large) // 2
        small_mine = lax.dynamic_slice_in_dim(summed, large + side * part, part, 1)
        small_theirs = lax.dynamic_slice_in_dim(summed, large + (1 - side) * part, part, 1)
        small_mine = small_mine + to_float(across(low(small_theirs)))
        return grad_tokens, summed[:, : large // 2], summed[:, large // 2 : large], small_mine

    grad_tokens, *blocks = meet([rg], *region(back_6))

    def finish_feed_forward():
        down_sum = rd.result()
        gate_up_sum = rg.result()
        return (
            back_to_rows(down_sum),
            back_to_rows(gate_up_sum[:, :ff_cols]),
            back_to_rows(gate_up_sum[:, ff_cols:]),
        )

    def back_to_rows(block):
        mine = lax.dynamic_slice_in_dim(block, core * rows, rows, 0)
        theirs = lax.dynamic_slice_in_dim(block, (1 - core) * rows, rows, 0)
        got = ring.swap(theirs)
        return jnp.where(
            core == 0,
            jnp.concatenate([mine, got], axis=1),
            jnp.concatenate([got, mine], axis=1),
        )

    out_down_t, out_gate, out_up = region(finish_feed_forward)
    one, two, small_half = last_reduce(blocks)
    total = jnp.concatenate([one, two], axis=1)
    out_output = total[:, :q_cols].T
    out_qkv = total[:, q_cols:]
    small_other = across(small_half)
    out_small = jnp.where(
        side == 0,
        jnp.concatenate([small_half, small_other], axis=1),
        jnp.concatenate([small_other, small_half], axis=1),
    )
    out_gains = out_small[:, 2 * rank + 2 * small :]
    return (
        low(result),
        grad_tokens,
        grad_layer_input,
        out_qkv[:, :q_cols],
        out_qkv[:, q_cols : q_cols + kv_cols],
        out_qkv[:, q_cols + kv_cols :],
        out_output,
        out_small[:, 2 * small : 2 * small + rank],
        out_small[:, 2 * small + rank : 2 * small + 2 * rank].T,
        out_gate,
        out_up,
        out_down_t.T,
        out_small[:, :small],
        out_small[:, small : 2 * small].T,
        out_gains[:head_part, 6],
        out_gains[:head_part, 7],
        out_gains[:, 0],
        out_gains[:, 1],
        out_gains[:, 2],
        out_gains[:, 3],
        out_gains[:, 4],
        out_gains[:, 5],
    )


def solution(mesh):
    both = P(("dp", "tensor"), None)
    rows_split = P("dp", "tensor")
    cols_split = P("tensor", "dp")
    by_row = P("dp", None)
    by_col = P(None, "dp")
    flat = P("dp")
    return jax.shard_map(
        local,
        mesh=mesh,
        in_specs=(
            (both, both, P(), P(), rows_split, rows_split, rows_split, cols_split)
            + (by_row, by_col, rows_split, rows_split, cols_split, by_row, by_col)
            + (flat,) * 8
            + (both,)
        ),
        out_specs=(
            (both, both, both, rows_split, rows_split, rows_split, cols_split)
            + (by_row, by_col, rows_split, rows_split, cols_split, by_row, by_col)
            + (flat,) * 8
        ),
        check_vma=False,
    )
```

time: 1060 us -> 1010 us (0.953)
  Pallas kernels: 0 us -> 316 us
  matrix products: 233 us -> 96.1 us
  local copies, waits for them, and re-layouts: 250 us -> 127 us
  starting transfers between devices: 144 us -> 68.2 us
  waiting for transfers between devices: 291 us -> 255 us
  other arithmetic: 119 us -> 133 us
    pallas_call x0 -> x23, Pallas kernels: none -> 316 us  [the longest x21 181 us: grid_call(): pl.pallas_call(kernel, grid_spec=pltpu.PrefetchScalarGridSpec(num_scalar_...]
    ppermute x52 -> x16, waiting for transfers between devices: 165 us -> 85.2 us  [up(): return lax.ppermute(values, 'dp', self.cw)]
    dot_general x43 -> x5, matrix products: 97.4 us -> 22 us  [the longest x1 7.85 us: back_4(): jnp.einsum('qkgd,ckd->kgqc', d_heads, values_all, preferred_element_type=...]
    dynamic_update_slice x51 -> x0, local copies, waits for them, and re-layouts: 70.7 us -> none  [assemble(): whole = lax.dynamic_update_slice_in_dim(whole, part, start, 0)]
    ppermute x10 -> x9, waiting for transfers between devices: 66.4 us -> 134 us  [across(): return lax.ppermute(values, 'tensor', [(0, 1), (1, 0)])]
    dot_general x11 -> x6, matrix products: 71.9 us -> 15.5 us  [product(): return jnp.dot(left_in, right_in, preferred_element_type=F32)]
    ppermute x52 -> x16, waiting for transfers between devices: 54.3 us -> 12.2 us  [down(): return lax.ppermute(values, 'dp', self.ccw)]
    ppermute x52 -> x16, starting transfers between devices: 62 us -> 25.2 us  [up(): return lax.ppermute(values, 'dp', self.cw)]
  transfers between devices with their start and end apart: 133 -> 53, of which waited for: 46 -> 29; matrix products, arithmetic and copies ran while one was open for 45% -> 29% of each run, Pallas kernels for 0% -> 13%
where the time goes in v2:
time: 1010 us; the launch traced here: 997 us
  Pallas kernels  316 us (31%)
  waiting for transfers between devices  255 us (25%)
  other arithmetic  133 us (13%)
  local copies, waits for them, and re-layouts  127 us (13%)
  matrix products  96.1 us (10%)
  starting transfers between devices  68.2 us (7%)
    pallas_call x21, Pallas kernels, grid_call(): pl.pallas_call(kernel, grid_spec=pltpu.PrefetchScalarGridSpec(num_scalar_...  181 us
    ppermute x9, waiting for transfers between devices, across(): return lax.ppermute(values, 'tensor', [(0, 1), (1, 0)])  134 us
    ppermute x16, waiting for transfers between devices, up(): return lax.ppermute(values, 'dp', self.cw)  85.2 us
    pallas_call x1, Pallas kernels, comm_call(): pl.pallas_call(kernel, out_shape=shapes, in_specs=[ANY] * len(operands),...  71 us
    pallas_call x1, Pallas kernels, last_reduce(): pl.pallas_call(functools.partial(last_kernel, count), out_shape=[jax.Shap...  64.1 us
    dot_general x8, matrix products, product_t(): lax.dot_general(left_in, right_in, (((1,), (1,)), ((), ())), preferred_el...  48.6 us
    ppermute x16, starting transfers between devices, up(): return lax.ppermute(values, 'dp', self.cw)  25.2 us
    ppermute x8, waiting for transfers between devices, swap(): return lax.ppermute(values, 'dp', self.core_pairs)  23.2 us
  transfers between devices with their start and end apart: 53, of which 29 were waited for; matrix products, arithmetic and copies ran while one was open for 29% of the time, Pallas kernels for 13%

profile of v2, /device:TPU:0, one launch (start us, length us, event | category | flops | bytes accessed | tf_op | source)
XLA Modules:
  0.0 996.7 jit_solution(9326654306960202776)
XLA Ops:
  14.5 71.0 %first_gather.1 = (bf16[2048,1536]{1,0:T(8,128)(2,1)}, bf16[2048,1024]{1,0:T(8,128)(2,1)}, bf16[2048,768]{1,0:T(8,128)(2,1)S(1)}, bf16[256,4096]{1,0:T(8,128)(2,...) custom-call(bf16[128,1536]{1,0:T(8,128)(2,1)S(1)} %pad_maximum_fusion.10.refs_0_, ...), custom_call_target="tpu_custom_call" | custom-call | bytes 142606336 | tf_op jit(solution)/shard_map/first_gather/pallas_call | solution.py:264
  96.0 5.1 fusion.136
  101.7 53.4 %conditional.11 = (bf16[512,2048]{1,0:T(8,128)(2,1)}, f32[512,1536]{1,0:T(8,128)}, bf16[512,1,4,256]{3,0,2,1:T(8,128)(2,1)}, bf16[1280,2,256]{2,0,1:T(8,128)(2,1...) conditional(s32[]{:T(128)} %convert_element_type.198, () %tuple.105, ...), branch_computations={%region_2.3_spmd, %region_3.11_spmd} | conditional | flops 5961549312 | bytes 130506152 | solution.py:707
  108.6 6.7 fusion.139
  150.1 5.1 fusion.12
  160.8 40.2 %conditional.12 = (f32[256,2048]{1,0:T(8,128)}, bf16[256,64]{0,1:T(8,128)(2,1)S(1)}, f32[256,2048]{1,0:T(8,128)}, f32[256,2048]{1,0:T(8,128)}, bf16[256,2048]{1,0:T(8,128)(2,1)}) conditional(s32[]{:T(128)} %convert_element_type.198, () %tuple.104, (bf16[512,1024]{0,1:T(8,128)(2,1)}, bf16[2048,1024]{1,0:T(8,128)(2,1)}, ...), branch_computations={%region_11.12_spmd, %region_12.17_spmd} | conditional | flops 2296923392 | bytes 64939256 | solution.py:707
  160.8 5.3 fusion.138
  179.2 12.5 %collective-permute-done.11 = bf16[256,2048]{1,0:T(8,128)(2,1)} collective-permute-done((bf16[256,2048]{1,0:T(8,128)(2,1)}, bf16[256,2048]{1,0:T(8,128)(2,1)}, u32[]{:S(2)}, u32[]{:S(2)}) %collective-permute-start.11) | collective-permute-done | bytes 1048608 | tf_op jit(solution)/shard_map/cond/branch_1_fun/ppermute | solution.py:110
  195.2 4.6 multiply_reduce_fusion.3
  208.2 31.9 %conditional.13 = (bf16[1024,2048]{1,0:T(8,128)(2,1)}) conditional(s32[]{:T(128)} %convert_element_type.198, () %tuple.111, bf16[256,2048]{1,0:T(8,128)(2,1)} %get-tuple-element.453), branch_computations={%region_17.18_spmd, %region_18.19_spmd} | conditional | flops 16777216 | bytes 25165912 | solution.py:707
  209.7 21.4 %collective-permute-done = bf16[256,2048]{1,0:T(8,128)(2,1)S(1)} collective-permute-done((bf16[256,2048]{1,0:T(8,128)(2,1)}, bf16[256,2048]{1,0:T(8,128)(2,1)S(1)}, u32[]{:S(2)}, u32[]{:S(2)}) %collective-permute-start) | collective-permute-done | bytes 1048608 | tf_op jit(solution)/shard_map/cond/branch_1_fun/ppermute | solution.py:110
  240.1 12.1 %collective-permute-done.22 = bf16[256,4096]{1,0:T(8,128)(2,1)} collective-permute-done((bf16[256,4096]{1,0:T(8,128)(2,1)}, bf16[256,4096]{1,0:T(8,128)(2,1)}, u32[]{:S(2)}, u32[]{:S(2)}) %collective-permute-start.22) | collective-permute-done | bytes 2097184 | tf_op jit(solution)/shard_map/ppermute | solution.py:100
  261.9 20.0 %collective-permute-done.24 = bf16[128,4096]{1,0:T(8,128)(2,1)} collective-permute-done((bf16[128,4096]{1,0:T(8,128)(2,1)}, bf16[128,4096]{1,0:T(8,128)(2,1)}, u32[]{:S(2)}, u32[]{:S(2)}) %collective-permute-start.24) | collective-permute-done | bytes 1048608 | tf_op jit(solution)/shard_map/ppermute | solution.py:100
  284.7 26.4 %conditional.14 = ((bf16[2,1024,2048]{2,1,0:T(8,128)(2,1)}, bf16[1024,2048]{1,0:T(8,128)(2,1)}, bf16[2,2048,2048]{2,1,0:T(8,128)(2,1)})) conditional(s32[]{:T(128)} %convert_element_type.198, () %tuple.109, (s32[9]{0:T(128)S(1)}, bf16[1024,2048]{1,0:T(8,128)(2,1)}, bf16[256,4096]{1,0:T(8,128)(2,1)}, bf16[256,4096]{1,0:T(8,128)(2,1)}, ...), branch_computations={%region_19.20_spmd, %region_20.21_spmd} | conditional | flops 17179869184 | bytes 67108872 | solution.py:707
  284.7 26.4 %gate_up.1 = (bf16[2,1024,2048]{2,1,0:T(8,128)(2,1)}, bf16[1024,2048]{1,0:T(8,128)(2,1)}, bf16[2,2048,2048]{2,1,0:T(8,128)(2,1)}) custom-call(s32[9]{0:T(128)S(1)} %get-tuple-element.237.spots, bf16[1024,2048]{1,0:T(8,128)(2,1)} %get-tuple-element.238.x, bf16[256,4096]{1,0:T(8,128)(2,1)} %get-tuple-element.239.refs_0_.refs_9_, ...), custom_call_target="tpu_custom_call" | custom-call | flops 17179869184 | bytes 67108864 | tf_op jit(solution)/shard_map/cond/branch_1_fun/gate_up/pallas_call | solution.py:413
  313.2 20.3 %collective-permute-done.26.refs_3_ = bf16[256,2048]{1,0:T(8,128)(2,1)S(1)} collective-permute-done((bf16[256,2048]{1,0:T(8,128)(2,1)}, bf16[256,2048]{1,0:T(8,128)(2,1)S(1)}, u32[]{:S(2)}, u32[]{:S(2)}) %collective-permute-start.26) | collective-permute-done | bytes 1048608 | tf_op jit(solution)/shard_map/ppermute | solution.py:100
  337.8 18.8 %collective-permute-done.28.refs_5_ = bf16[256,2048]{1,0:T(8,128)(2,1)S(1)} collective-permute-done((bf16[256,2048]{1,0:T(8,128)(2,1)S(1)}, bf16[256,2048]{1,0:T(8,128)(2,1)S(1)}, u32[]{:S(2)}, u32[]{:S(2)}) %collective-permute-start.28) | collective-permute-done | bytes 1048608 | tf_op jit(solution)/shard_map/ppermute | solution.py:100
  360.6 6.8 collective-permute-done.30.refs_7_
  370.3 18.0 %columns_out.1 = f32[1024,2048]{1,0:T(8,128)} custom-call(s32[9]{0:T(128)S(1)} %stack.102.spots, bf16[1,1024,2048]{2,1,0:T(8,128)(2,1)} %bitcast.299, bf16[256,2048]{1,0:T(8,128)(2,1)} %get-tuple-element.447.refs_0_, bf16[256,2048]{1,0:T(8,128)(2,1)} %collective-permute-done.18.refs_1_, bf16[256,2048]{1,0:T(8,128)(2,1)} %collective-permute-done.19.refs_2_, ...), custom_call_target="tpu_custom_call" | custom-call | flops 8589934592 | bytes 20971520 | tf_op jit(solution)/shard_map/columns_out/pallas_call | solution.py:413
  399.1 24.3 %collective-permute-done.33 = bf16[256,2048]{1,0:T(8,128)(2,1)S(1)} collective-permute-done((bf16[256,2048]{1,0:T(8,128)(2,1)S(1)}, bf16[256,2048]{1,0:T(8,128)(2,1)S(1)}, u32[]{:S(2)}, u32[]{:S(2)}) %collective-permute-start.33) | collective-permute-done | bytes 1048608 | tf_op jit(solution)/shard_map/ppermute | solution.py:110
  428.8 4.4 add_convert_fusion.2
  437.5 23.4 %collective-permute-done.34 = bf16[256,2048]{1,0:T(8,128)(2,1)S(1)} collective-permute-done((bf16[256,2048]{1,0:T(8,128)(2,1)S(1)}, bf16[256,2048]{1,0:T(8,128)(2,1)S(1)}, u32[]{:S(2)}, u32[]{:S(2)}) %collective-permute-start.34) | collective-permute-done | bytes 1048608 | tf_op jit(solution)/shard_map/ppermute | solution.py:110
  466.0 6.0 block_grad.18
  475.8 18.4 %conditional.15 = (bf16[2,1024,2048]{2,1,0:T(8,128)(2,1)}) conditional(s32[]{:T(128)} %convert_element_type.198, () %tuple.120, (s32[9]{0:T(128)S(1)}, bf16[1024,2048]{1,0:T(8,128)(2,1)S(1)}, bf16[2,1024,2048]{2,1,0:T(8,128)(2,1)}, bf16[256,2048]{1,0:T(8,128)(2,1)}, bf16[256,2048]{1,0:T(8,128)(2,1)}, /*index=5*/bf16[256,2048]{1,0:T(8,128)(2,1)}, ...), branch_computations={%region_25.26_spmd, %region_26.27_spmd} | conditional | flops 8589934592 | bytes 29360136 | solution.py:707
  475.9 18.4 %hidden_back.1 = bf16[2,1024,2048]{2,1,0:T(8,128)(2,1)} custom-call(s32[9]{0:T(128)S(1)} %get-tuple-element.248.spots, bf16[1024,2048]{1,0:T(8,128)(2,1)S(1)} %get-tuple-element.249.x, bf16[2,1024,2048]{2,1,0:T(8,128)(2,1)} %get-tuple-element.250.raw, bf16[256,2048]{1,0:T(8,128)(2,1)} %get-tuple-element.251.refs_0_, ...), custom_call_target="tpu_custom_call" | custom-call | flops 8589934592 | bytes 29360128 | tf_op jit(solution)/shard_map/cond/branch_1_fun/hidden_back/pallas_call | solution.py:413
  495.1 4.8 block_grad.20
  500.2 4.9 block_grad.19
  506.8 6.0 block_grad.23
  517.8 29.4 %conditional.16 = (f32[1024,2048]{1,0:T(8,128)}) conditional(s32[]{:T(128)} %convert_element_type.198, () %tuple.123, (bf16[2,1024,2048]{2,1,0:T(8,128)(2,1)}, bf16[2,2048,2048]{2,1,0:T(8,128)(2,1)}) %tuple.124), branch_computations={%region_27.28_spmd, %region_28.29_spmd} | conditional | flops 17181966336 | bytes 83886120 | solution.py:707
  517.8 14.8 %fusion.34 = f32[1024,2048]{1,0:T(8,128)} fusion(bf16[2,2048,2048]{2,1,0:T(8,128)(2,1)} %get-tuple-element.261, bf16[2,1024,2048]{2,1,0:T(8,128)(2,1)} %get-tuple-element.260), kind=kOutput, calls=%fused_computation.81 | convolution fusion | flops 8589934592 | bytes 20971520 | tf_op jit(solution)/shard_map/cond/branch_1_fun/dot_general | solution.py:65
  532.6 14.7 %fusion.40 = f32[1024,2048]{1,0:T(8,128)} fusion(f32[1024,2048]{1,0:T(8,128)} %fusion.34, bf16[2,2048,2048]{2,1,0:T(8,128)(2,1)} %get-tuple-element.261, bf16[2,1024,2048]{2,1,0:T(8,128)(2,1)S(1)} %copy-done.6), kind=kOutput, calls=%fused_computation.87 | convolution fusion | flops 8592031744 | bytes 29360128 | tf_op jit(solution)/shard_map/cond/branch_1_fun/dot_general | solution.py:65
  548.3 5.1 block_grad.22
  553.7 5.0 block_grad.21
  560.6 49.2 %conditional.17 = (f32[2048]{0:T(1024)S(1)}, f32[2048]{0:T(1024)S(1)}, f32[256,2048]{1,0:T(8,128)S(1)}, bf16[256,2048]{1,0:T(8,128)(2,1)}) conditional(s32[]{:T(128)} %convert_element_type.198, () %tuple.126, (f32[256,2048]{1,0:T(8,128)}, f32[1024,2048]{1,0:T(8,128)}, f32[256,2048]{1,0:T(8,128)}, f32[2048,1]{1,0:T(8,128)S(1)}, ...), branch_computations={%region_29.30_spmd, %region_30.37_spmd} | conditional | flops 19399680 | bytes 103960840 | solution.py:707
  578.8 21.3 %collective-permute-done.3 = bf16[256,2048]{1,0:T(8,128)(2,1)S(1)} collective-permute-done((bf16[256,2048]{1,0:T(8,128)(2,1)}, bf16[256,2048]{1,0:T(8,128)(2,1)S(1)}, u32[]{:S(2)}, u32[]{:S(2)}) %collective-permute-start.3) | collective-permute-done | bytes 1048608 | tf_op jit(solution)/shard_map/cond/branch_1_fun/ppermute | solution.py:110
  609.8 7.1 block_grad.27
  617.2 6.1 block_grad.26
  625.0 5.1 block_grad.25
  630.4 4.8 block_grad.24
  637.0 52.9 %conditional.18 = (bf16[512,2048]{1,0:T(8,128)(2,1)}, f32[1280,2,256]{2,0,1:T(8,128)}, f32[512,1,4,256]{3,0,2,1:T(8,128)}) conditional(s32[]{:T(128)} %convert_element_type.198, () %tuple.129, (bf16[256,2048]{1,0:T(8,128)(2,1)}, s32[512]{0:T(512)S(1)}, s32[1280]{0:T(1024)S(1)}, s32[512]{0:T(512)S(1)}, bf16[1280,2,256]{2,0,1:T(8,128)(2,1)}, ...), branch_computations={%region_37.38_spmd, %region_38.40_spmd} | conditional | flops 8892971008 | bytes 176080096 | solution.py:707
  639.9 7.2 fusion.68
  647.0 13.5 %collective-permute-done.12 = bf16[256,2048]{1,0:T(8,128)(2,1)S(1)} collective-permute-done((bf16[256,2048]{1,0:T(8,128)(2,1)}, bf16[256,2048]{1,0:T(8,128)(2,1)S(1)}, u32[]{:S(2)}, u32[]{:S(2)}) %collective-permute-start.12) | collective-permute-done | bytes 1048608 | tf_op jit(solution)/shard_map/cond/branch_1_fun/ppermute | solution.py:110
  667.9 7.8 fusion.53
  692.7 6.6 block_grad.29
  699.7 6.3 block_grad.28
  708.1 41.7 %conditional.19 = (bf16[512,1536]{1,0:T(8,128)(2,1)}, f32[256]{0:T(256)S(1)}, f32[256]{0:T(256)S(1)}) conditional(s32[]{:T(128)} %convert_element_type.198, () %tuple.132, (s32[]{:T(128)}, f32[1280,2,256]{2,0,1:T(8,128)}, f32[512,1536]{1,0:T(8,128)}, f32[512,128]{1,0:T(8,128)}, f32[512,128]{1,0:T(8,128)S(1)}, /*index=5*/f32[16,16]{1,0:T(8,128)S(1)}, ...), branch_computations={%region_40.41_spmd, %region_41.50_spmd} | conditional | flops 17777152 | bytes 68909256 | solution.py:707
  723.5 4.3 copy.317
  752.3 6.6 block_grad.31
  758.9 12.4 %collective-permute-start.51 = (bf16[256,4096]{1,0:T(8,128)(2,1)}, bf16[256,4096]{1,0:T(8,128)(2,1)}, u32[]{:S(2)}, u32[]{:S(2)}) collective-permute-start(bf16[256,4096]{1,0:T(8,128)(2,1)} %block_grad.31), channel_id=1, source_target_pairs={{8,0},{10,2},{16,8},{18,10},{24,16},{26,18},{28,24},{30,26},{20,28... | collective-permute-start | bytes 6291464 | tf_op jit(solution)/shard_map/ppermute | solution.py:103
  771.4 6.4 block_grad.30
  781.0 102.8 %conditional.20 = (f32[256,2048]{1,0:T(8,128)}, f32[1024,1280]{1,0:T(8,128)}, f32[1024,1280]{1,0:T(8,128)}, f32[1024,384]{1,0:T(8,128)}) conditional(s32[]{:T(128)} %convert_element_type.198, () %tuple.135, (f32[2048,1]{1,0:T(8,128)}, f32[256,2048]{1,0:T(8,128)S(1)}, f32[256,2048]{1,0:T(8,128)}, bf16[2048,64]{1,0:T(8,128)(2,1)}, ...), branch_computations={%region_52.53_spmd, %region_53.60_spmd} | conditional | flops 9417534464 | bytes 230251216 | solution.py:707
  781.0 6.0 fusion.140
  809.0 5.1 collective-permute-done.13
  814.1 4.5 fusion.91
  822.5 11.4 %row_grads.2 = bf16[1024,3328]{1,0:T(8,128)(2,1)} custom-call(s32[8]{0:T(128)} %fusion.99.spots, bf16[512,2048]{1,0:T(8,128)(2,1)S(1)} %copy-done.29, bf16[512,2048]{1,0:T(8,128)(2,1)} %get-tuple-element.295.refs_1_, bf16[256,2048]{1,0:T(8,128)(2,1)} %get-tuple-element.296.refs_2_, bf16[256,2048]{1,0:T(8,128)(2,1)} %get-tuple-element.297.refs_3_, ...), custom_call_target="tpu_custom_call" | custom-call | flops 3019898880 | bytes 19202048 | tf_op jit(solution)/shard_map/cond/branch_1_fun/row_grads/pallas_call | solution.py:413
  838.7 6.7 collective-permute-done.14.refs_13_
  845.4 14.2 %row_grads.3 = f32[1024,3328]{1,0:T(8,128)} custom-call(s32[8]{0:T(128)} %fusion.100.spots, bf16[512,2048]{1,0:T(8,128)(2,1)S(1)} %copy-done.30, bf16[512,2048]{1,0:T(8,128)(2,1)} %get-tuple-element.295.refs_1_, bf16[256,2048]{1,0:T(8,128)(2,1)S(1)} %copy-done.33, bf16[256,2048]{1,0:T(8,128)(2,1)S(1)} %copy-done.35, ...), custom_call_target="tpu_custom_call" | custom-call | flops 3019898880 | bytes 32833536 | tf_op jit(solution)/shard_map/cond/branch_1_fun/row_grads/pallas_call | solution.py:413
  862.0 8.7 fusion.132
  870.6 10.5 %collective-permute-done.15 = bf16[1024,384]{1,0:T(8,128)(2,1)S(1)} collective-permute-done((bf16[1024,384]{1,0:T(8,128)(2,1)S(1)}, bf16[1024,384]{1,0:T(8,128)(2,1)S(1)}, u32[]{:S(2)}, u32[]{:S(2)}) %collective-permute-start.15) | collective-permute-done | bytes 786464 | tf_op jit(solution)/shard_map/cond/branch_1_fun/ppermute | solution.py:110
  883.8 35.2 %conditional.21 = (f32[128,4096]{1,0:T(8,128)}, f32[128,4096]{1,0:T(8,128)}, f32[128,4096]{1,0:T(8,128)}) conditional(s32[]{:T(128)} %convert_element_type.198, () %tuple.138, (s32[]{:T(128)}, s32[]{:T(128)}, bf16[1024,2048]{1,0:T(8,128)(2,1)}, bf16[1,1024,2048]{2,1,0:T(8,128)(2,1)}, bf16[256,2048]{1,0:T(8,128)(2,1)}, ...), branch_computations={%region_60.61_spmd, %region_61.62_spmd} | conditional | flops 3232235520 | bytes 113246688 | solution.py:707
  883.8 6.6 block_grad.17
  890.4 4.3 convert_add_fusion.4
  901.9 4.9 block_grad.16
  921.8 64.1 %last_reduce.1 = (f32[128,1280]{1,0:T(8,128)S(1)}, f32[128,1280]{1,0:T(8,128)S(1)}, f32[128,384]{1,0:T(8,128)S(1)}) custom-call(f32[1024,1280]{1,0:T(8,128)} %get-tuple-element.524.refs_0_, f32[1024,1280]{1,0:T(8,128)} %get-tuple-element.525.refs_1_, f32[1024,384]{1,0:T(8,128)} %get-tuple-element.526.refs_2_), custom_call_target="tpu_custom_call" | custom-call | bytes 48234496 | tf_op jit(solution)/shard_map/last_reduce/pallas_call | solution.py:634
  (489 shorter events, 346.5 us)
Async XLA Ops:
  87.1 68.1 %collective-permute-start.16 = (bf16[256,4096]{1,0:T(8,128)(2,1)}, bf16[256,4096]{1,0:T(8,128)(2,1)}, u32[]{:S(2)}, u32[]{:S(2)}) collective-permute-start(bf16[256,4096]{1,0:T(8,128)(2,1)} %get-tuple-element.439), channel_id=1, source_target_pairs={{0,8},{2,10},{8,16},{10,18},{16,24},{18,26},{24,28},{26,30},{28,20... | collective-permute-start | bytes 6291464 | tf_op jit(solution)/shard_map/ppermute | solution.py:100
  88.6 66.6 %collective-permute-start.17 = (bf16[256,4096]{1,0:T(8,128)(2,1)}, bf16[256,4096]{1,0:T(8,128)(2,1)}, u32[]{:S(2)}, u32[]{:S(2)}) collective-permute-start(bf16[256,4096]{1,0:T(8,128)(2,1)} %get-tuple-element.439), channel_id=1, source_target_pairs={{8,0},{10,2},{16,8},{18,10},{24,16},{26,18},{28,24},{30,26},{20,28... | collective-permute-start | bytes 6291464 | tf_op jit(solution)/shard_map/ppermute | solution.py:103
  101.2 58.4 %copy-start.1 = (bf16[2048,768]{1,0:T(8,128)(2,1)S(1)}, bf16[2048,768]{1,0:T(8,128)(2,1)}, u32[]{:S(2)}) copy-start(bf16[2048,768]{1,0:T(8,128)(2,1)} %copy-done) | copy-start | bytes 9437188
  122.4 20.5 %collective-permute-start.9 = (bf16[512,2,256]{2,0,1:T(8,128)(2,1)}, bf16[512,2,256]{2,0,1:T(8,128)(2,1)}, u32[]{:S(2)}, u32[]{:S(2)}) collective-permute-start(bf16[512,2,256]{2,0,1:T(8,128)(2,1)} %maximum_select_fusion), channel_id=1, source_target_pairs={{0,2},{2,4},{4,6},{6,8},{8,10},{10,12},{12,14},{14,16},{16,18},{18... | collective-permute-start | bytes 1572872 | tf_op jit(solution)/shard_map/cond/branch_1_fun/ppermute | solution.py:895
  126.7 16.2 %collective-permute-start.10 = (bf16[256,2,256]{2,0,1:T(8,128)(2,1)}, bf16[256,2,256]{2,0,1:T(8,128)(2,1)}, u32[]{:S(2)}, u32[]{:S(2)}) collective-permute-start(bf16[256,2,256]{2,0,1:T(8,128)(2,1)} %slice.342), channel_id=1, source_target_pairs={{2,0},{4,2},{6,4},{8,6},{10,8},{12,10},{14,12},{16,14},{18,16},{20... | collective-permute-start | bytes 786440 | tf_op jit(solution)/shard_map/cond/branch_1_fun/ppermute | solution.py:896
  155.2 49.5 %collective-permute-start.20 = (bf16[256,4096]{1,0:T(8,128)(2,1)}, bf16[256,4096]{1,0:T(8,128)(2,1)}, u32[]{:S(2)}, u32[]{:S(2)}) collective-permute-start(bf16[256,4096]{1,0:T(8,128)(2,1)} %collective-permute-done.16), channel_id=1, source_target_pairs={{0,8},{2,10},{8,16},{10,18},{16,24},{18,26},{24,28},{26,30},{28,20... | collective-permute-start | bytes 6291464 | tf_op jit(solution)/shard_map/ppermute | solution.py:100
  159.4 46.8 %collective-permute-start.21 = (bf16[256,4096]{1,0:T(8,128)(2,1)}, bf16[256,4096]{1,0:T(8,128)(2,1)}, u32[]{:S(2)}, u32[]{:S(2)}) collective-permute-start(bf16[256,4096]{1,0:T(8,128)(2,1)} %collective-permute-done.17), channel_id=1, source_target_pairs={{8,0},{10,2},{16,8},{18,10},{24,16},{26,18},{28,24},{30,26},{20,28... | collective-permute-start | bytes 6291464 | tf_op jit(solution)/shard_map/ppermute | solution.py:103
  167.3 24.4 %collective-permute-start.11 = (bf16[256,2048]{1,0:T(8,128)(2,1)}, bf16[256,2048]{1,0:T(8,128)(2,1)}, u32[]{:S(2)}, u32[]{:S(2)}) collective-permute-start(bf16[256,2048]{1,0:T(8,128)(2,1)} %slice.501), channel_id=1, source_target_pairs={{0,1},{1,0},{2,3},{3,2},{4,5},{5,4},{6,7},{7,6},{8,9},{9,8},{10,11... | collective-permute-start | bytes 3145736 | tf_op jit(solution)/shard_map/cond/branch_1_fun/ppermute | solution.py:110
  177.4 17.8 %copy-start.65 = (bf16[256,64]{0,1:T(8,128)(2,1)}, bf16[256,64]{0,1:T(8,128)(2,1)S(1)}, u32[]{:S(2)}) copy-start(bf16[256,64]{0,1:T(8,128)(2,1)S(1)} %convolution_convert_fusion) | copy-start | bytes 98308 | tf_op jit(solution)/shard_map/cond
  179.2 16.0 %copy-start.20 = (bf16[256,2048]{1,0:T(8,128)(2,1)S(1)}, bf16[256,2048]{1,0:T(8,128)(2,1)}, u32[]{:S(2)}) copy-start(bf16[256,2048]{1,0:T(8,128)(2,1)} %copy-done.19) | copy-start | bytes 3145732 | tf_op jit(solution)/shard_map/cond
  206.2 46.0 %collective-permute-start.22 = (bf16[256,4096]{1,0:T(8,128)(2,1)}, bf16[256,4096]{1,0:T(8,128)(2,1)}, u32[]{:S(2)}, u32[]{:S(2)}) collective-permute-start(bf16[256,4096]{1,0:T(8,128)(2,1)} %collective-permute-done.20), channel_id=1, source_target_pairs={{0,8},{2,10},{8,16},{10,18},{16,24},{18,26},{24,28},{26,30},{28,20... | collective-permute-start | bytes 6291464 | tf_op jit(solution)/shard_map/ppermute | solution.py:100
  207.7 45.5 %collective-permute-start.23 = (bf16[256,4096]{1,0:T(8,128)(2,1)}, bf16[256,4096]{1,0:T(8,128)(2,1)}, u32[]{:S(2)}, u32[]{:S(2)}) collective-permute-start(bf16[256,4096]{1,0:T(8,128)(2,1)} %collective-permute-done.21), channel_id=1, source_target_pairs={{8,0},{10,2},{16,8},{18,10},{24,16},{26,18},{28,24},{30,26},{20,28... | collective-permute-start | bytes 6291464 | tf_op jit(solution)/shard_map/ppermute | solution.py:103
  208.2 22.9 %collective-permute-start = (bf16[256,2048]{1,0:T(8,128)(2,1)}, bf16[256,2048]{1,0:T(8,128)(2,1)S(1)}, u32[]{:S(2)}, u32[]{:S(2)}) collective-permute-start(bf16[256,2048]{1,0:T(8,128)(2,1)} %param.5), channel_id=1, source_target_pairs={{0,1},{1,0},{2,3},{3,2},{4,5},{5,4},{6,7},{7,6},{8,9},{9,8},{10,11... | collective-permute-start | bytes 3145736 | tf_op jit(solution)/shard_map/cond/branch_1_fun/ppermute | solution.py:110
  232.6 4.2 collective-permute-start.1
  255.5 26.4 %collective-permute-start.24 = (bf16[128,4096]{1,0:T(8,128)(2,1)}, bf16[128,4096]{1,0:T(8,128)(2,1)}, u32[]{:S(2)}, u32[]{:S(2)}) collective-permute-start(bf16[128,4096]{1,0:T(8,128)(2,1)} %slice.301), channel_id=1, source_target_pairs={{0,8},{2,10},{8,16},{10,18},{16,24},{18,26},{24,28},{26,30},{28,20... | collective-permute-start | bytes 3145736 | tf_op jit(solution)/shard_map/ppermute | solution.py:100
  258.3 26.4 %collective-permute-start.25 = (bf16[128,4096]{1,0:T(8,128)(2,1)}, bf16[128,4096]{1,0:T(8,128)(2,1)}, u32[]{:S(2)}, u32[]{:S(2)}) collective-permute-start(bf16[128,4096]{1,0:T(8,128)(2,1)} %slice.302), channel_id=1, source_target_pairs={{8,0},{10,2},{16,8},{18,10},{24,16},{26,18},{28,24},{30,26},{20,28... | collective-permute-start | bytes 3145736 | tf_op jit(solution)/shard_map/ppermute | solution.py:103
  259.8 51.3 %collective-permute-start.18 = (bf16[256,2048]{1,0:T(8,128)(2,1)}, bf16[256,2048]{1,0:T(8,128)(2,1)}, u32[]{:S(2)}, u32[]{:S(2)}) collective-permute-start(bf16[256,2048]{1,0:T(8,128)(2,1)} %get-tuple-element.447.refs_0_), channel_id=1, source_target_pairs={{0,8},{2,10},{8,16},{10,18},{16,24},{18,26},{24,28},{26,30},{28,20... | collective-permute-start | bytes 3145736 | tf_op jit(solution)/shard_map/ppermute | solution.py:100
  260.3 50.8 %collective-permute-start.19 = (bf16[256,2048]{1,0:T(8,128)(2,1)}, bf16[256,2048]{1,0:T(8,128)(2,1)}, u32[]{:S(2)}, u32[]{:S(2)}) collective-permute-start(bf16[256,2048]{1,0:T(8,128)(2,1)} %get-tuple-element.447.refs_0_), channel_id=1, source_target_pairs={{8,0},{10,2},{16,8},{18,10},{24,16},{26,18},{28,24},{30,26},{20,28... | collective-permute-start | bytes 3145736 | tf_op jit(solution)/shard_map/ppermute | solution.py:103
  311.2 22.3 %collective-permute-start.26 = (bf16[256,2048]{1,0:T(8,128)(2,1)}, bf16[256,2048]{1,0:T(8,128)(2,1)S(1)}, u32[]{:S(2)}, u32[]{:S(2)}) collective-permute-start(bf16[256,2048]{1,0:T(8,128)(2,1)} %collective-permute-done.18.refs_1_), channel_id=1, source_target_pairs={{0,8},{2,10},{8,16},{10,18},{16,24},{18,26},{24,28},{26,30},{28,20... | collective-permute-start | bytes 3145736 | tf_op jit(solution)/shard_map/ppermute | solution.py:100
  312.9 22.1 %collective-permute-start.27 = (bf16[256,2048]{1,0:T(8,128)(2,1)}, bf16[256,2048]{1,0:T(8,128)(2,1)S(1)}, u32[]{:S(2)}, u32[]{:S(2)}) collective-permute-start(bf16[256,2048]{1,0:T(8,128)(2,1)} %collective-permute-done.19.refs_2_), channel_id=1, source_target_pairs={{8,0},{10,2},{16,8},{18,10},{24,16},{26,18},{28,24},{30,26},{20,28... | collective-permute-start | bytes 3145736 | tf_op jit(solution)/shard_map/ppermute | solution.py:103
  333.5 54.8 %copy-start.96 = (bf16[256,2048]{1,0:T(8,128)(2,1)}, bf16[256,2048]{1,0:T(8,128)(2,1)S(1)}, u32[]{:S(2)}) copy-start(bf16[256,2048]{1,0:T(8,128)(2,1)S(1)} %collective-permute-done.26.refs_3_) | copy-start | bytes 3145732
  335.0 53.3 %copy-start.97 = (bf16[256,2048]{1,0:T(8,128)(2,1)}, bf16[256,2048]{1,0:T(8,128)(2,1)S(1)}, u32[]{:S(2)}) copy-start(bf16[256,2048]{1,0:T(8,128)(2,1)S(1)} %collective-permute-done.27.refs_4_) | copy-start | bytes 3145732
  335.0 21.6 %collective-permute-start.28 = (bf16[256,2048]{1,0:T(8,128)(2,1)S(1)}, bf16[256,2048]{1,0:T(8,128)(2,1)S(1)}, u32[]{:S(2)}, u32[]{:S(2)}) collective-permute-start(bf16[256,2048]{1,0:T(8,128)(2,1)S(1)} %collective-permute-done.26.refs_3_), channel_id=1, source_target_pairs={{0,8},{2,10},{8,16},{10,18},{16,24},{18,26},{24,28},{26,30},{28,20... | collective-permute-start | bytes 3145736 | tf_op jit(solution)/shard_map/ppermute | solution.py:100
  337.8 20.3 %collective-permute-start.29 = (bf16[256,2048]{1,0:T(8,128)(2,1)S(1)}, bf16[256,2048]{1,0:T(8,128)(2,1)S(1)}, u32[]{:S(2)}, u32[]{:S(2)}) collective-permute-start(bf16[256,2048]{1,0:T(8,128)(2,1)S(1)} %collective-permute-done.27.refs_4_), channel_id=1, source_target_pairs={{8,0},{10,2},{16,8},{18,10},{24,16},{26,18},{28,24},{30,26},{20,28... | collective-permute-start | bytes 3145736 | tf_op jit(solution)/shard_map/ppermute | solution.py:103
  356.6 31.7 %copy-start.69 = (bf16[256,2048]{1,0:T(8,128)(2,1)}, bf16[256,2048]{1,0:T(8,128)(2,1)S(1)}, u32[]{:S(2)}) copy-start(bf16[256,2048]{1,0:T(8,128)(2,1)S(1)} %collective-permute-done.28.refs_5_) | copy-start | bytes 3145732
  358.2 30.1 %copy-start.71 = (bf16[256,2048]{1,0:T(8,128)(2,1)}, bf16[256,2048]{1,0:T(8,128)(2,1)S(1)}, u32[]{:S(2)}) copy-start(bf16[256,2048]{1,0:T(8,128)(2,1)S(1)} %collective-permute-done.29.refs_6_) | copy-start | bytes 3145732
  358.2 9.2 collective-permute-start.30
  360.0 9.5 collective-permute-start.31
  390.8 4.2 collective-permute-start.32
  398.1 25.3 %collective-permute-start.33 = (bf16[256,2048]{1,0:T(8,128)(2,1)S(1)}, bf16[256,2048]{1,0:T(8,128)(2,1)S(1)}, u32[]{:S(2)}, u32[]{:S(2)}) collective-permute-start(bf16[256,2048]{1,0:T(8,128)(2,1)S(1)} %slice.506), channel_id=1, source_target_pairs={{0,1},{1,0},{2,3},{3,2},{4,5},{5,4},{6,7},{7,6},{8,9},{9,8},{10,11... | collective-permute-start | bytes 3145736 | tf_op jit(solution)/shard_map/ppermute | solution.py:110
  436.6 24.4 %collective-permute-start.34 = (bf16[256,2048]{1,0:T(8,128)(2,1)S(1)}, bf16[256,2048]{1,0:T(8,128)(2,1)S(1)}, u32[]{:S(2)}, u32[]{:S(2)}) collective-permute-start(bf16[256,2048]{1,0:T(8,128)(2,1)S(1)} %fusion.102), channel_id=1, source_target_pairs={{0,1},{1,0},{2,3},{3,2},{4,5},{5,4},{6,7},{7,6},{8,9},{9,8},{10,11... | collective-permute-start | bytes 3145736 | tf_op jit(solution)/shard_map/ppermute | solution.py:110
  461.2 4.2 collective-permute-start.35
  473.3 20.9 %collective-permute-start.36 = (bf16[128,2048]{1,0:T(8,128)(2,1)S(1)}, bf16[128,2048]{1,0:T(8,128)(2,1)S(1)}, u32[]{:S(2)}, u32[]{:S(2)}) collective-permute-start(bf16[128,2048]{1,0:T(8,128)(2,1)S(1)} %get-tuple-element.1156), channel_id=1, source_target_pairs={{0,8},{2,10},{8,16},{10,18},{16,24},{18,26},{24,28},{26,30},{28,20... | collective-permute-start | bytes 1572872 | tf_op jit(solution)/shard_map/ppermute | solution.py:100
  474.0 20.3 %collective-permute-start.37 = (bf16[128,2048]{1,0:T(8,128)(2,1)S(1)}, bf16[128,2048]{1,0:T(8,128)(2,1)S(1)}, u32[]{:S(2)}, u32[]{:S(2)}) collective-permute-start(bf16[128,2048]{1,0:T(8,128)(2,1)S(1)} %get-tuple-element.1155), channel_id=1, source_target_pairs={{8,0},{10,2},{16,8},{18,10},{24,16},{26,18},{28,24},{30,26},{20,28... | collective-permute-start | bytes 1572872 | tf_op jit(solution)/shard_map/ppermute | solution.py:103
  499.9 47.4 %collective-permute-start.39 = (bf16[256,2048]{1,0:T(8,128)(2,1)}, bf16[256,2048]{1,0:T(8,128)(2,1)S(1)}, u32[]{:S(2)}, u32[]{:S(2)}) collective-permute-start(bf16[256,2048]{1,0:T(8,128)(2,1)} %block_grad.20), channel_id=1, source_target_pairs={{8,0},{10,2},{16,8},{18,10},{24,16},{26,18},{28,24},{30,26},{20,28... | collective-permute-start | bytes 3145736 | tf_op jit(solution)/shard_map/ppermute | solution.py:103
  505.1 42.2 %collective-permute-start.38 = (bf16[256,2048]{1,0:T(8,128)(2,1)}, bf16[256,2048]{1,0:T(8,128)(2,1)S(1)}, u32[]{:S(2)}, u32[]{:S(2)}) collective-permute-start(bf16[256,2048]{1,0:T(8,128)(2,1)} %block_grad.19), channel_id=1, source_target_pairs={{0,8},{2,10},{8,16},{10,18},{16,24},{18,26},{24,28},{26,30},{28,20... | collective-permute-start | bytes 3145736 | tf_op jit(solution)/shard_map/ppermute | solution.py:100
  515.8 94.0 %collective-permute-start.42 = (bf16[128,4096]{1,0:T(8,128)(2,1)}, bf16[128,4096]{1,0:T(8,128)(2,1)}, u32[]{:S(2)}, u32[]{:S(2)}) collective-permute-start(bf16[128,4096]{1,0:T(8,128)(2,1)} %get-tuple-element.1154), channel_id=1, source_target_pairs={{0,8},{2,10},{8,16},{10,18},{16,24},{18,26},{24,28},{26,30},{28,20... | collective-permute-start | bytes 3145736 | tf_op jit(solution)/shard_map/ppermute | solution.py:100
  516.4 93.3 %collective-permute-start.43 = (bf16[128,4096]{1,0:T(8,128)(2,1)}, bf16[128,4096]{1,0:T(8,128)(2,1)}, u32[]{:S(2)}, u32[]{:S(2)}) collective-permute-start(bf16[128,4096]{1,0:T(8,128)(2,1)} %get-tuple-element.1153), channel_id=1, source_target_pairs={{8,0},{10,2},{16,8},{18,10},{24,16},{26,18},{28,24},{30,26},{20,28... | collective-permute-start | bytes 3145736 | tf_op jit(solution)/shard_map/ppermute | solution.py:103
  517.8 14.8 %copy-start.6 = (bf16[2,1024,2048]{2,1,0:T(8,128)(2,1)S(1)}, bf16[2,1024,2048]{2,1,0:T(8,128)(2,1)}, u32[]{:S(2)}) copy-start(bf16[2,1024,2048]{2,1,0:T(8,128)(2,1)} %get-tuple-element.260) | copy-start | bytes 25165828 | tf_op jit(solution)/shard_map/cond
  553.4 56.4 %collective-permute-start.41 = (bf16[256,2048]{1,0:T(8,128)(2,1)}, bf16[256,2048]{1,0:T(8,128)(2,1)}, u32[]{:S(2)}, u32[]{:S(2)}) collective-permute-start(bf16[256,2048]{1,0:T(8,128)(2,1)} %block_grad.22), channel_id=1, source_target_pairs={{8,0},{10,2},{16,8},{18,10},{24,16},{26,18},{28,24},{30,26},{20,28... | collective-permute-start | bytes 3145736 | tf_op jit(solution)/shard_map/ppermute | solution.py:103
  558.7 51.1 %collective-permute-start.40 = (bf16[256,2048]{1,0:T(8,128)(2,1)}, bf16[256,2048]{1,0:T(8,128)(2,1)}, u32[]{:S(2)}, u32[]{:S(2)}) collective-permute-start(bf16[256,2048]{1,0:T(8,128)(2,1)} %block_grad.21), channel_id=1, source_target_pairs={{0,8},{2,10},{8,16},{10,18},{16,24},{18,26},{24,28},{26,30},{28,20... | collective-permute-start | bytes 3145736 | tf_op jit(solution)/shard_map/ppermute | solution.py:100
  564.4 4.4 collective-permute-start.2
  574.7 25.4 %collective-permute-start.3 = (bf16[256,2048]{1,0:T(8,128)(2,1)}, bf16[256,2048]{1,0:T(8,128)(2,1)S(1)}, u32[]{:S(2)}, u32[]{:S(2)}) collective-permute-start(bf16[256,2048]{1,0:T(8,128)(2,1)} %slice.503), channel_id=1, source_target_pairs={{0,1},{1,0},{2,3},{3,2},{4,5},{5,4},{6,7},{7,6},{8,9},{9,8},{10,11... | collective-permute-start | bytes 3145736 | tf_op jit(solution)/shard_map/cond/branch_1_fun/ppermute | solution.py:110
  576.0 24.0 %copy-start.26 = (f32[512,2048]{1,0:T(8,128)S(1)}, f32[512,2048]{1,0:T(8,128)}, u32[]{:S(2)}) copy-start(f32[512,2048]{1,0:T(8,128)} %copy-done.25) | copy-start | bytes 12582916 | tf_op jit(solution)/shard_map/cond
  616.9 75.8 %collective-permute-start.47 = (bf16[256,4096]{1,0:T(8,128)(2,1)}, bf16[256,4096]{1,0:T(8,128)(2,1)}, u32[]{:S(2)}, u32[]{:S(2)}) collective-permute-start(bf16[256,4096]{1,0:T(8,128)(2,1)} %block_grad.27), channel_id=1, source_target_pairs={{8,0},{10,2},{16,8},{18,10},{24,16},{26,18},{28,24},{30,26},{20,28... | collective-permute-start | bytes 6291464 | tf_op jit(solution)/shard_map/ppermute | solution.py:103
  623.3 69.4 %collective-permute-start.46 = (bf16[256,4096]{1,0:T(8,128)(2,1)}, bf16[256,4096]{1,0:T(8,128)(2,1)}, u32[]{:S(2)}, u32[]{:S(2)}) collective-permute-start(bf16[256,4096]{1,0:T(8,128)(2,1)} %block_grad.26), channel_id=1, source_target_pairs={{0,8},{2,10},{8,16},{10,18},{16,24},{18,26},{24,28},{26,30},{28,20... | collective-permute-start | bytes 6291464 | tf_op jit(solution)/shard_map/ppermute | solution.py:100
  630.1 59.8 %collective-permute-start.45 = (bf16[256,2048]{1,0:T(8,128)(2,1)}, bf16[256,2048]{1,0:T(8,128)(2,1)}, u32[]{:S(2)}, u32[]{:S(2)}) collective-permute-start(bf16[256,2048]{1,0:T(8,128)(2,1)} %block_grad.25), channel_id=1, source_target_pairs={{8,0},{10,2},{16,8},{18,10},{24,16},{26,18},{28,24},{30,26},{20,28... | collective-permute-start | bytes 3145736 | tf_op jit(solution)/shard_map/ppermute | solution.py:103
  635.3 57.4 %collective-permute-start.44 = (bf16[256,2048]{1,0:T(8,128)(2,1)}, bf16[256,2048]{1,0:T(8,128)(2,1)}, u32[]{:S(2)}, u32[]{:S(2)}) collective-permute-start(bf16[256,2048]{1,0:T(8,128)(2,1)} %block_grad.24), channel_id=1, source_target_pairs={{0,8},{2,10},{8,16},{10,18},{16,24},{18,26},{24,28},{26,30},{28,20... | collective-permute-start | bytes 3145736 | tf_op jit(solution)/shard_map/ppermute | solution.py:100
  637.0 23.5 %collective-permute-start.12 = (bf16[256,2048]{1,0:T(8,128)(2,1)}, bf16[256,2048]{1,0:T(8,128)(2,1)S(1)}, u32[]{:S(2)}, u32[]{:S(2)}) collective-permute-start(bf16[256,2048]{1,0:T(8,128)(2,1)} %get-tuple-element.268), channel_id=1, source_target_pairs={{0,1},{1,0},{2,3},{3,2},{4,5},{5,4},{6,7},{7,6},{8,9},{9,8},{10,11... | collective-permute-start | bytes 3145736 | tf_op jit(solution)/shard_map/cond/branch_1_fun/ppermute | solution.py:110
  639.9 22.2 %copy-start.95 = (bf16[2048,1024]{1,0:T(8,128)(2,1)S(1)}, bf16[2048,1024]{1,0:T(8,128)(2,1)}, u32[]{:S(2)}) copy-start(bf16[2048,1024]{1,0:T(8,128)(2,1)} %get-tuple-element.275) | copy-start | bytes 12582916 | tf_op jit(solution)/shard_map/cond
  699.3 52.4 %collective-permute-start.49 = (bf16[256,4096]{1,0:T(8,128)(2,1)}, bf16[256,4096]{1,0:T(8,128)(2,1)}, u32[]{:S(2)}, u32[]{:S(2)}) collective-permute-start(bf16[256,4096]{1,0:T(8,128)(2,1)} %block_grad.29), channel_id=1, source_target_pairs={{8,0},{10,2},{16,8},{18,10},{24,16},{26,18},{28,24},{30,26},{20,28... | collective-permute-start | bytes 6291464 | tf_op jit(solution)/shard_map/ppermute | solution.py:103
  706.0 46.3 %collective-permute-start.48 = (bf16[256,4096]{1,0:T(8,128)(2,1)}, bf16[256,4096]{1,0:T(8,128)(2,1)}, u32[]{:S(2)}, u32[]{:S(2)}) collective-permute-start(bf16[256,4096]{1,0:T(8,128)(2,1)} %block_grad.28), channel_id=1, source_target_pairs={{0,8},{2,10},{8,16},{10,18},{16,24},{18,26},{24,28},{26,30},{28,20... | collective-permute-start | bytes 6291464 | tf_op jit(solution)/shard_map/ppermute | solution.py:100
  710.8 31.8 %collective-permute-start.4 = (bf16[512,2,256]{2,0,1:T(8,128)(2,1)}, bf16[512,2,256]{2,0,1:T(8,128)(2,1)}, u32[]{:S(2)}, u32[]{:S(2)}) collective-permute-start(bf16[512,2,256]{2,0,1:T(8,128)(2,1)} %slice.350), channel_id=1, source_target_pairs={{2,0},{4,2},{6,4},{8,6},{10,8},{12,10},{14,12},{16,14},{18,16},{20... | collective-permute-start | bytes 1572872 | tf_op jit(solution)/shard_map/cond/branch_1_fun/ppermute | solution.py:1027
  712.8 29.8 %collective-permute-start.5 = (bf16[256,2,256]{2,0,1:T(8,128)(2,1)}, bf16[256,2,256]{2,0,1:T(8,128)(2,1)}, u32[]{:S(2)}, u32[]{:S(2)}) collective-permute-start(bf16[256,2,256]{2,0,1:T(8,128)(2,1)} %slice.351), channel_id=1, source_target_pairs={{0,2},{2,4},{4,6},{6,8},{8,10},{10,12},{12,14},{14,16},{16,18},{18... | collective-permute-start | bytes 786440 | tf_op jit(solution)/shard_map/cond/branch_1_fun/ppermute | solution.py:1028
  752.3 19.0 %copy-start.10 = (bf16[1024,2048]{1,0:T(8,128)(2,1)S(1)}, bf16[1024,2048]{1,0:T(8,128)(2,1)}, u32[]{:S(2)}) copy-start(bf16[1024,2048]{1,0:T(8,128)(2,1)} %get-tuple-element.1253.x) | copy-start | bytes 12582916
  758.9 124.9 %collective-permute-start.51 = (bf16[256,4096]{1,0:T(8,128)(2,1)}, bf16[256,4096]{1,0:T(8,128)(2,1)}, u32[]{:S(2)}, u32[]{:S(2)}) collective-permute-start(bf16[256,4096]{1,0:T(8,128)(2,1)} %block_grad.31), channel_id=1, source_target_pairs={{8,0},{10,2},{16,8},{18,10},{24,16},{26,18},{28,24},{30,26},{20,28... | collective-permute-start | bytes 6291464 | tf_op jit(solution)/shard_map/ppermute | solution.py:103
  777.7 106.0 %collective-permute-start.50 = (bf16[256,4096]{1,0:T(8,128)(2,1)}, bf16[256,4096]{1,0:T(8,128)(2,1)}, u32[]{:S(2)}, u32[]{:S(2)}) collective-permute-start(bf16[256,4096]{1,0:T(8,128)(2,1)} %block_grad.30), channel_id=1, source_target_pairs={{0,8},{2,10},{8,16},{10,18},{16,24},{18,26},{24,28},{26,30},{28,20... | collective-permute-start | bytes 6291464 | tf_op jit(solution)/shard_map/ppermute | solution.py:100
  788.3 25.8 %collective-permute-start.13 = (bf16[256,2048]{1,0:T(8,128)(2,1)}, bf16[256,2048]{1,0:T(8,128)(2,1)}, u32[]{:S(2)}, u32[]{:S(2)}) collective-permute-start(bf16[256,2048]{1,0:T(8,128)(2,1)} %slice.504), channel_id=1, source_target_pairs={{0,1},{1,0},{2,3},{3,2},{4,5},{5,4},{6,7},{7,6},{8,9},{9,8},{10,11... | collective-permute-start | bytes 3145736 | tf_op jit(solution)/shard_map/cond/branch_1_fun/ppermute | solution.py:110
  833.9 11.5 %collective-permute-start.14 = (bf16[1024,3328]{1,0:T(8,128)(2,1)}, bf16[1024,3328]{1,0:T(8,128)(2,1)}, u32[]{:S(2)}, u32[]{:S(2)}) collective-permute-start(bf16[1024,3328]{1,0:T(8,128)(2,1)} %row_grads.2), channel_id=1, source_target_pairs={{0,2},{2,0},{4,6},{6,4},{8,10},{10,8},{12,14},{14,12},{16,18},{18,... | collective-permute-start | bytes 20447240 | tf_op jit(solution)/shard_map/cond/branch_1_fun/ppermute | solution.py:106
  861.1 19.9 %collective-permute-start.15 = (bf16[1024,384]{1,0:T(8,128)(2,1)S(1)}, bf16[1024,384]{1,0:T(8,128)(2,1)S(1)}, u32[]{:S(2)}, u32[]{:S(2)}) collective-permute-start(bf16[1024,384]{1,0:T(8,128)(2,1)S(1)} %dynamic-slice_convert_fusion), channel_id=1, source_target_pairs={{0,1},{1,0},{2,3},{3,2},{4,5},{5,4},{6,7},{7,6},{8,9},{9,8},{10,11... | collective-permute-start | bytes 2359304 | tf_op jit(solution)/shard_map/cond/branch_1_fun/ppermute | solution.py:110
  899.0 12.0 %collective-permute-start.8 = (f32[128,2048]{1,0:T(8,128)}, f32[128,2048]{1,0:T(8,128)}, u32[]{:S(2)}, u32[]{:S(2)}) collective-permute-start(f32[128,2048]{1,0:T(8,128)} %get-tuple-element.1134), channel_id=1, source_target_pairs={{0,2},{2,0},{4,6},{6,4},{8,10},{10,8},{12,14},{14,12},{16,18},{18,... | collective-permute-start | bytes 3145736 | tf_op jit(solution)/shard_map/cond/branch_1_fun/ppermute | solution.py:106
  900.5 13.8 %collective-permute-start.7 = (f32[128,2048]{1,0:T(8,128)}, f32[128,2048]{1,0:T(8,128)S(1)}, u32[]{:S(2)}, u32[]{:S(2)}) collective-permute-start(f32[128,2048]{1,0:T(8,128)} %get-tuple-element.1136), channel_id=1, source_target_pairs={{0,2},{2,0},{4,6},{6,4},{8,10},{10,8},{12,14},{14,12},{16,18},{18,... | collective-permute-start | bytes 3145736 | tf_op jit(solution)/shard_map/cond/branch_1_fun/ppermute | solution.py:106
  910.5 5.2 collective-permute-start.6
  985.9 6.0 collective-permute-start.52
  (92 other events, 469.9 us)

commit v3 on v2

--- a/solution.py
+++ b/solution.py
@@ -385,31 +385,23 @@
             out[:, across_] = out[:, across_] + term
 
 
-def block_kernel(where, spots, x, d, *refs):
-    got, (out, turned) = refs[:-2], refs[-2:]
+def block_kernel(count, spots, *refs):
+    xs, d = refs[:count], refs[count]
+    outs, turned = refs[count + 1 : 2 * count + 1], refs[2 * count + 1 :]
 
     @pl.when(pl.program_id(0) == 0)
     def _():
-        turned[...] = x[...].T
-
-    term = product(turned[...], d[0])
-    if where == "none":
-        out[...] = term.astype(out.dtype)
-    elif where == "all":
-        out[...] = low(term + to_float(got[0][...]))
-    else:
-        cut = got[0].shape[0]
-        top, bottom = term[:cut], term[cut:]
-        if where == "top":
-            top = top + to_float(got[0][...])
-        else:
-            bottom = bottom + to_float(got[0][...])
-        out[:cut, :] = low(top)
-        out[cut:, :] = low(bottom)
+        for x, t in zip(xs, turned):
+            t[...] = x[...].T
+
+    for t, out in zip(turned, outs):
+        out[...] = low(product(t[...], d[0]))
 
 
 def grid_call(kernel, spots, grid, operands, in_specs, shapes, out_specs, scratch, flops, name):
     moved = sum(v.size * v.dtype.itemsize for v in (*operands, *jax.tree.leaves(shapes)))
+    if flops == 0:
+        moved = 0
     return pl.pallas_call(
         kernel,
         grid_spec=pltpu.PrefetchScalarGridSpec(
@@ -498,153 +490,532 @@
     )
 
 
-def block_grad(x, d, chip, size, got=None, where="none", dtype=BF16, tile=2048):
+def block_grads(x, d, chips, size, tile=1024):
     (m, _), (groups, _, ff) = x.shape, d.shape
+    count = len(chips)
     tile = min(tile, ff)
     tiles = ff // tile
-    more = [] if got is None else [got]
+    spots = jnp.stack(chips).astype(jnp.int32)
     if size % 128:
-        x = lax.dynamic_slice_in_dim(x, chip * size, size, 1)
-        chip = jnp.zeros((), jnp.int32)
+        xs = [lax.dynamic_slice_in_dim(x, chip * size, size, 1) for chip in chips]
+        x_specs = [once((m, size))] * count
+    else:
+        xs = [x] * count
+        x_specs = [
+            pl.BlockSpec((m, size), functools.partial(lambda i, f, s: (0, s[i]), i))
+            for i in range(count)
+        ]
     return grid_call(
-        functools.partial(block_kernel, where),
-        chip.reshape(1).astype(jnp.int32),
+        functools.partial(block_kernel, count),
+        spots,
         (groups * tiles,),
-        (x, d, *more),
-        [
-            pl.BlockSpec((m, size), lambda f, s: (0, s[0])),
-            pl.BlockSpec((1, m, tile), lambda f, s: (f // tiles, 0, f % tiles)),
-        ]
-        + [pl.BlockSpec((v.shape[0], tile), lambda f, s: (0, f)) for v in more],
-        jax.ShapeDtypeStruct((size, groups * ff), dtype),
-        pl.BlockSpec((size, tile), lambda f, s: (0, f)),
-        [pltpu.VMEM((size, m), BF16)],
-        2 * groups * m * size * ff,
-        "block_grad",
+        (*xs, d),
+        x_specs + [pl.BlockSpec((1, m, tile), lambda f, s: (f // tiles, 0, f % tiles))],
+        [jax.ShapeDtypeStruct((size, groups * ff), BF16)] * count,
+        [pl.BlockSpec((size, tile), lambda f, s: (0, f))] * count,
+        [pltpu.VMEM((size, m), BF16)] * count,
+        0,
+        "block_grads",
     )
 
 
 def row_kernel(pairs, spots, *refs):
     xs, ds = refs[:pairs], refs[pairs : 2 * pairs]
-    more, out = refs[2 * pairs : -1], refs[-1]
+    last, mine, theirs, both = refs[2 * pairs :]
+    rows = mine.shape[0]
+    core = spots[0]
     start = 0
     for x, d in zip(xs, ds):
         cols = d.shape[1]
-        out[:, start : start + cols] = product_l(x[...], d[...]).astype(out.dtype)
+        both[:, start : start + cols] = product_l(x[...], d[...])
         start += cols
-    out[:, start:] = more[0][...].astype(out.dtype)
-    if len(more) > 1:
-        out[...] = out[...] + more[1][...].astype(out.dtype)
-
-
-def row_grads(pairs, last, which, chips, rows, got, dtype):
+    both[:, start:] = last[...]
+    mine[...] = both[pl.ds(pl.multiple_of(core * rows, 128), rows), :]
+    theirs[...] = low(both[pl.ds(pl.multiple_of((1 - core) * rows, 128), rows), :])
+
+
+def row_grads(pairs, last, core, chips, rows):
     xs, ds = [x for x, _ in pairs], [d for _, d in pairs]
     cols = sum(d.shape[1] for d in ds) + last.shape[1]
-    more = [] if got is None else [got]
+    if rows % 128:
+
+        def own_columns(values, which):
+            blocks = values.reshape(values.shape[0], chips, 2, rows)
+            return lax.dynamic_index_in_dim(blocks, which, 2, keepdims=False).reshape(
+                values.shape[0], chips * rows
+            )
+
+        def terms(which):
+            return jnp.concatenate(
+                [product_l(own_columns(x, which), d) for x, d in pairs]
+                + [own_columns(last.T, which).T],
+                axis=1,
+            )
+
+        return terms(core), low(terms(1 - core))
+    block = pl.BlockSpec((rows, cols), lambda j, s: (j, 0))
     return grid_call(
         functools.partial(row_kernel, len(pairs)),
-        (2 * jnp.arange(chips) + which).astype(jnp.int32),
+        core.reshape(1).astype(jnp.int32),
         (chips,),
-        (*xs, *ds, last, *more),
-        [pl.BlockSpec((x.shape[0], rows), lambda j, s: (0, s[j])) for x in xs]
+        (*xs, *ds, last),
+        [pl.BlockSpec((x.shape[0], 2 * rows), lambda j, s: (0, j)) for x in xs]
         + [once(d.shape) for d in ds]
-        + [pl.BlockSpec((rows, last.shape[1]), lambda j, s: (s[j], 0))]
-        + [pl.BlockSpec((rows, cols), lambda j, s: (j, 0)) for _ in more],
-        jax.ShapeDtypeStruct((chips * rows, cols), dtype),
-        pl.BlockSpec((rows, cols), lambda j, s: (j, 0)),
-        [],
-        sum(2 * d.size * chips * rows for d in ds),
+        + [pl.BlockSpec((2 * rows, last.shape[1]), lambda j, s: (j, 0))],
+        [
+            jax.ShapeDtypeStruct((chips * rows, cols), F32),
+            jax.ShapeDtypeStruct((chips * rows, cols), BF16),
+        ],
+        [block, block],
+        [pltpu.VMEM((2 * rows, cols), F32)],
+        sum(4 * d.size * chips * rows for d in ds),
         "row_grads",
     )
 
 
-def last_kernel(count, *refs):
-    terms, refs = refs[:count], refs[count:]
-    outs, refs = refs[:count], refs[count:]
-    sent, refs = refs[:count], refs[count:]
-    got, refs = refs[:count], refs[count:]
-    ring_send, ring_recv = refs
+def last_kernel(large, *refs):
+    mine, theirs, refs = refs[0], refs[1], refs[2:]
+    ff_terms, refs = refs[:6], refs[6:]
+    (main, little, *ff_outs), refs = refs[:5], refs[5:]
+    own, core_got, side_sent, side_got, first, got, refs = *refs[:6], refs[6:]
+    ff_held, (ff_sent,), refs = refs[:6], refs[6:7], refs[7:]
+    loads, core_send, core_recv, side_send, side_recv, ring_send, ring_recv, ff_send, ff_recv = refs
     hops = Hops()
+    side = lax.axis_index("tensor")
     half = hops.chips // 2
-    rows = outs[0].shape[0]
+    rows = main.shape[0]
+    part = little.shape[1]
+    ff_cols = ff_sent.shape[2]
     cut = rows // 2
-    greet([hops.above, hops.below])
+    greet([hops.above, hops.below, hops.partner, hops.across])
+    order = [half]
+    for k in range(1, half):
+        order += [half - k, k - half]
+    order.append(0)
+
+    def rows_at(offset, top=0, size=rows):
+        return pl.ds(pl.multiple_of(hops.chip_at(offset) * rows + top, 16), size)
+
+    started, arriving = [], []
+    for i, offset in enumerate(order):
+        at = rows_at(offset)
+        copy = remote(
+            theirs.at[at], core_got.at[at], core_send, core_recv, (i,), hops.partner
+        )
+        copy.start()
+        load = pltpu.make_async_copy(mine.at[at], own.at[at], loads.at[i])
+        load.start()
+        started.append(copy)
+        arriving.append((copy, load))
+    ff_loads = [
+        pltpu.make_async_copy(source, target, loads.at[len(order) + i])
+        for i, (source, target) in enumerate(zip(ff_terms, ff_held))
+    ]
+    for load in ff_loads:
+        load.start()
+
+    sides = {}
+    my_part = pl.ds(pl.multiple_of(large + side * part, 128), part)
+    their_part = pl.ds(pl.multiple_of(large + (1 - side) * part, 128), part)
+
+    def ready(i):
+        at = rows_at(order[i])
+        copy, load = arriving[i]
+        load.wait()
+        copy.wait_recv()
+        own[at, :] = own[at, :] + to_float(core_got[at, :])
+        side_sent[at, :] = low(own[at, their_part])
+        copy = remote(
+            side_sent.at[at], side_got.at[at], side_send, side_recv, (i,), hops.across
+        )
+        copy.start()
+        started.append(copy)
+        sides[order[i]] = copy
+
+    pieces = [(0, large // 2), (large // 2, large // 2), (large, part)]
     copies = {}
 
     def term(which, offset, top, size):
-        at = pl.multiple_of(hops.chip_at(offset) * rows + top, 16)
-        return terms[which][pl.ds(at, size), :]
-
-    def send(which, direction, k, size):
+        at = rows_at(offset, top, size)
+        start, cols = pieces[which]
+        if which < 2:
+            return own[at, start : start + cols]
+        return own[at, my_part] + to_float(side_got[at, :])
+
+    def send(which, direction, k, source, top, size):
+        start, cols = pieces[which]
         copy = remote(
-            sent[which].at[direction, k, pl.ds(0, size)],
-            got[which].at[direction, k, pl.ds(0, size)],
+            source,
+            got.at[direction, k, pl.ds(top, size), pl.ds(start, cols)],
             ring_send,
             ring_recv,
             (direction, k, which),
             hops.above if direction == 0 else hops.below,
         )
         copy.start()
+        started.append(copy)
         copies[(which, direction, k)] = copy
 
-    for which in range(count):
+    def step(which, k):
+        start, cols = pieces[which]
         for direction in range(2):
-            sent[which][direction, 0, :cut, :] = low(term(which, half, direction * cut, cut))
-            send(which, direction, 0, cut)
+            near, far = direction * cut, (1 - direction) * cut
+            if k == 0:
+                first[direction, :, start : start + cols] = low(term(which, half, near, cut))
+                source = first.at[direction, :, pl.ds(start, cols)]
+                send(which, direction, 0, source, near, cut)
+                continue
+            offset = (half - k) * (1 if direction == 0 else -1)
+            copies[(which, direction, k - 1)].wait_recv()
+            if k == 1:
+                held = got[direction, 0, near : near + cut, start : start + cols]
+                got[direction, 0, near : near + cut, start : start + cols] = low(
+                    term(which, offset, near, cut) + to_float(held)
+                )
+                got[direction, 0, far : far + cut, start : start + cols] = low(
+                    term(which, offset, far, cut)
+                )
+            else:
+                held = got[direction, k - 1, :, start : start + cols]
+                got[direction, k - 1, :, start : start + cols] = low(
+                    term(which, offset, 0, rows) + to_float(held)
+                )
+            source = got.at[direction, k - 1, :, pl.ds(start, cols)]
+            send(which, direction, k, source, 0, rows)
+
+    def end_feed_forward():
+        for load in ff_loads:
+            load.wait()
+        wide, wide_up, wide_down, narrow, narrow_up, narrow_down = ff_held
+        my_rows = pl.ds(pl.multiple_of(hops.core * rows, 16), rows)
+        their_rows = pl.ds(pl.multiple_of((1 - hops.core) * rows, 16), rows)
+        my_cols = pl.ds(pl.multiple_of(hops.core * ff_cols, 128), ff_cols)
+        groups = [
+            (wide, wide_up, wide_down, 0),
+            (wide, wide_up, wide_down, ff_cols),
+            (narrow, narrow_up, narrow_down, 0),
+        ]
+        for i, (base, up, down, start) in enumerate(groups):
+            cols = slice(start, start + ff_cols)
+
+            def total(at):
+                return to_float(base[at, cols]) + to_float(up[at, cols]) + to_float(down[at, cols])
+
+            ff_sent[i] = total(their_rows)
+            copy = remote(
+                ff_sent.at[i], ff_outs[i].at[:, my_cols], ff_send, ff_recv, (i,), hops.partner
+            )
+            copy.start()
+            ff_copies.append(copy)
+            ff_outs[i][:, my_cols] = total(my_rows)
+
+    ff_copies = []
+    ready(0)
+    step(0, 0)
+    step(1, 0)
+    ready(1)
+    ready(2)
+    sides[half].wait_recv()
+    step(2, 0)
     for k in range(1, half):
-        offset = half - k
-        for which in range(count):
-            for direction in range(2):
-                there = offset if direction == 0 else -offset
-                copies[(which, direction, k - 1)].wait_recv()
-                came = got[which].at[direction, k - 1]
-                if k == 1:
-                    near, far = direction * cut, (1 - direction) * cut
-                    sent[which][direction, k, near : near + cut, :] = low(
-                        term(which, there, near, cut) + to_float(came[:cut, :])
-                    )
-                    sent[which][direction, k, far : far + cut, :] = low(
-                        term(which, there, far, cut)
-                    )
-                else:
-                    sent[which][direction, k] = low(
-                        term(which, there, 0, rows) + to_float(came[...])
-                    )
-                send(which, direction, k, rows)
-    for which in range(count):
+        step(0, k)
+        step(1, k)
+        if k == 1:
+            end_feed_forward()
+        for i in range(2 * k + 1, min(2 * k + 3, len(order))):
+            ready(i)
+        sides[half - k].wait_recv()
+        sides[k - half].wait_recv()
+        step(2, k)
+    sides[0].wait_recv()
+    for which, (start, cols) in enumerate(pieces):
         for direction in range(2):
             copies[(which, direction, half - 1)].wait_recv()
-        outs[which][...] = (
+        total = (
             term(which, 0, 0, rows)
-            + to_float(got[which][0, half - 1])
-            + to_float(got[which][1, half - 1])
-        )
-    for copy in copies.values():
+            + to_float(got[0, half - 1, :, start : start + cols])
+            + to_float(got[1, half - 1, :, start : start + cols])
+        )
+        if which < 2:
+            main[:, start : start + cols] = total
+        else:
+            little[...] = total
+    for copy in ff_copies:
+        copy.wait_recv()
+    for copy in ff_copies + started:
         copy.wait_send()
 
 
-def last_reduce(terms):
+def last_reduce(mine, theirs, large, ff_terms):
     chips = lax.axis_size("dp") // 2
     half = chips // 2
-    rows = terms[0].shape[0] // chips
-    count = len(terms)
-    moved = sum(v.size * 2 for v in terms)
+    tall, cols = mine.shape
+    rows = tall // chips
+    part = (cols - large) // 2
+    ff = ff_terms[3].shape[1]
     vmem = pl.BlockSpec(memory_space=pltpu.VMEM)
-    buffers = [pltpu.VMEM((2, half, rows, v.shape[1]), BF16) for v in terms]
+    dma = pltpu.SemaphoreType.DMA
     return pl.pallas_call(
-        functools.partial(last_kernel, count),
-        out_shape=[jax.ShapeDtypeStruct((rows, v.shape[1]), F32) for v in terms],
-        in_specs=[vmem] * count,
-        out_specs=[vmem] * count,
-        scratch_shapes=buffers
-        + buffers
-        + [pltpu.SemaphoreType.DMA((2, half, count)), pltpu.SemaphoreType.DMA((2, half, count))],
+        functools.partial(last_kernel, large),
+        out_shape=[
+            jax.ShapeDtypeStruct((rows, large), F32),
+            jax.ShapeDtypeStruct((rows, part), F32),
+        ]
+        + [jax.ShapeDtypeStruct((rows, 2 * ff), F32)] * 3,
+        in_specs=[ANY] * 8,
+        out_specs=[vmem] * 5,
+        scratch_shapes=[
+            pltpu.VMEM((tall, cols), F32),
+            pltpu.VMEM((tall, cols), BF16),
+            pltpu.VMEM((tall, part), BF16),
+            pltpu.VMEM((tall, part), BF16),
+            pltpu.VMEM((2, rows // 2, large + part), BF16),
+            pltpu.VMEM((2, half, rows, large + part), BF16),
+        ]
+        + [pltpu.VMEM(v.shape, v.dtype) for v in ff_terms]
+        + [
+            pltpu.VMEM((3, rows, ff), F32),
+            dma((2 * half + 6,)),
+            dma((2 * half,)),
+            dma((2 * half,)),
+            dma((2 * half,)),
+            dma((2 * half,)),
+            dma((2, half, 3)),
+            dma((2, half, 3)),
+            dma((3,)),
+            dma((3,)),
+        ],
         compiler_params=pltpu.CompilerParams(
-            collective_id=2, has_side_effects=True, vmem_limit_bytes=48 * 2**20
+            collective_id=2, has_side_effects=True, vmem_limit_bytes=56 * 2**20
         ),
-        cost_estimate=pl.CostEstimate(flops=0, bytes_accessed=8 * moved, transcendentals=0),
+        cost_estimate=pl.CostEstimate(
+            flops=0, bytes_accessed=20 * mine.size * 4, transcendentals=0
+        ),
         name="last_reduce",
-    )(*terms)
+    )(mine, theirs, *ff_terms)
+
+
+def forward_kernel(hops_done, tile, x_own, *refs):
+    count = 2 * hops_done + 1
+    gu_parts, (dn_own,), refs = refs[:count], refs[count : count + 1], refs[count + 1 :]
+    (x_out, gu_full, gu_land, dn_full, raw, hidden, result), refs = refs[:7], refs[7:]
+    x, dn, hidden_v, pairs, core_sent, core_got, side_sent, side_got, refs = *refs[:8], refs[8:]
+    x_send, x_recv, gu_send, gu_recv, dn_send, dn_recv, core_sems, side_sems, loads, stores = refs
+    hops = Hops()
+    half, chips = hops.chips // 2, hops.chips
+    own = x_own.shape[0]
+    size, ff = dn_own.shape
+    cut = size // 2
+    greet([hops.above, hops.below, hops.partner, hops.across])
+    started, saved = [], []
+
+    def begin(copy, where=started):
+        copy.start()
+        where.append(copy)
+        return copy
+
+    def spot(ref, offset, top=0, tall=size):
+        return block_rows(ref, hops.chip_at(offset) * size + top, tall)
+
+    def span(k):
+        return (0, size) if k < half else (None, cut)
+
+    def gu_hop(k):
+        copies = []
+        for direction, ahead in ((0, hops.above), (1, hops.below)):
+            offset = (1 - k) * (1 if direction == 0 else -1)
+            top, tall = (0, size) if k < half else (direction * cut, cut)
+            target = spot(gu_land, offset, top, tall)
+            if k == hops_done + 1:
+                held = gu_parts[2 * k - 3 + direction] if k > 1 else gu_parts[0]
+                source = block_rows(held, top, tall)
+            else:
+                source = target
+            index = (direction, k - hops_done - 1)
+            copies.append(begin(remote(source, target, gu_send, gu_recv, index, ahead)))
+        return copies
+
+    def dn_hop(k):
+        copies = []
+        for direction, ahead in ((0, hops.above), (1, hops.below)):
+            offset = (1 - k) * (1 if direction == 0 else -1)
+            top, tall = (0, size) if k < half else (direction * cut, cut)
+            block = spot(dn, offset, top, tall)
+            copies.append(begin(remote(block, block, dn_send, dn_recv, (direction, k - 1), ahead)))
+        return copies
+
+    def arrive(copies):
+        for copy in copies:
+            copy.wait_recv()
+
+    moving = gu_hop(hops_done + 1)
+    mine, far = pl.ds(0, own), pl.ds(own, own)
+    near, opposite = pl.ds(2 * own, own), pl.ds(3 * own, own)
+    load_x = begin(pltpu.make_async_copy(x_own, x.at[mine], loads.at[0]), saved)
+    load_dn = begin(pltpu.make_async_copy(dn_own, spot(dn, 0), loads.at[1]), saved)
+    from_far = begin(remote(x_own, x.at[far], x_send, x_recv, (0,), hops.across))
+    from_near = begin(remote(x_own, x.at[near], x_send, x_recv, (1,), hops.partner))
+    from_far.wait_recv()
+    passed = begin(remote(x.at[far], x.at[opposite], x_send, x_recv, (2,), hops.partner))
+    from_near.wait_recv()
+    passed.wait_recv()
+    load_x.wait()
+    begin(pltpu.make_async_copy(x, x_out, stores.at[0]), saved)
+    load_dn.wait()
+    arrive(moving)
+    for k in range(hops_done + 2, half + 1):
+        moving = gu_hop(k)
+        arrive(moving)
+    moving = dn_hop(1)
+
+    offsets = list(range(hops_done + 1, half)) + list(range(-half + 1, -hops_done)) + [half]
+    order = [0]
+    for k in range(1, hops_done + 1):
+        order += [-k, k]
+    tiles = ff // tile
+
+    def body(*tiles_of):
+        ins, (raw_tile, hidden_tile, weights) = tiles_of[:-3], tiles_of[-3:]
+        step = pl.program_id(0)
+        every = order + offsets
+        for group in range(2):
+            for number, offset in enumerate(every):
+                at = pl.ds(pl.multiple_of(hops.chip_at(offset) * size, size), size)
+                weights[group, at, :] = ins[group * len(every) + number][...]
+        gate = product(x[...], weights[0])
+        up = product(x[...], weights[1])
+        raw_tile[0] = low(gate)
+        raw_tile[1] = low(up)
+        bend = jnp.tanh(GELU_SCALE * (gate + GELU_CUBE * gate * gate * gate))
+        value = low(0.5 * gate * (1.0 + bend) * up)
+        hidden_tile[...] = value
+        hidden_v[:, pl.ds(pl.multiple_of(step * tile, tile), tile)] = value
+
+    def part_spec(row, group):
+        return pl.BlockSpec((size, tile), lambda n: (row, n + group * tiles))
+
+    in_specs, operands = [], []
+    for group in range(2):
+        for ref in gu_parts:
+            in_specs.append(part_spec(0, group))
+            operands.append(ref)
+        for offset in offsets:
+            in_specs.append(part_spec(hops.chip_at(offset), group))
+            operands.append(gu_land)
+    m, width = x.shape
+    pltpu.emit_pipeline(
+        body,
+        grid=(tiles,),
+        in_specs=in_specs,
+        out_specs=[
+            pl.BlockSpec((2, m, tile), lambda n: (0, 0, n)),
+            pl.BlockSpec((m, tile), lambda n: (0, n)),
+            pl.BlockSpec((2, width, tile), lambda n: (0, 0, n)),
+        ],
+    )(*operands, raw, hidden, gu_full)
+
+    order, core_copies, side_copies = [], [], []
+
+    def block_out(offset):
+        i = len(order)
+        order.append(offset)
+        at = pl.ds(pl.multiple_of(hops.chip_at(offset) * size, size), size)
+        out = product_t(hidden_v[...], dn[at, :])
+        pairs[i] = out[: 2 * own]
+        core_sent[i] = low(out[2 * own :])
+        copy = remote(
+            core_sent.at[i], core_got.at[i], core_sems.at[0], core_sems.at[1], (i,), hops.partner
+        )
+        core_copies.append(begin(copy))
+
+    def core_sum():
+        i = len(side_copies)
+        core_copies[i].wait_recv()
+        both = pairs[i] + to_float(core_got[i])
+        side_sent[i] = low(both[own:])
+        copy = remote(
+            side_sent.at[i], side_got.at[i], side_sems.at[0], side_sems.at[1], (i,), hops.across
+        )
+        side_copies.append(begin(copy))
+        at = pl.ds(pl.multiple_of(hops.chip_at(order[i]) * size, size), size)
+        result[:, at] = both[:own]
+
+    for k in range(1, half + 1):
+        arrive(moving)
+        if k < half:
+            moving = dn_hop(k + 1)
+        if k == 1:
+            block_out(0)
+        if k < half:
+            block_out(-k)
+            core_sum()
+            block_out(k)
+            core_sum()
+        else:
+            block_out(half)
+            core_sum()
+    begin(pltpu.make_async_copy(dn, dn_full, stores.at[1]), saved)
+    core_sum()
+    for i, copy in enumerate(side_copies):
+        copy.wait_recv()
+        at = pl.ds(pl.multiple_of(hops.chip_at(order[i]) * size, size), size)
+        result[:, at] = result[:, at] + to_float(side_got[i])
+    for copy in started:
+        copy.wait_send()
+    for copy in saved[2:]:
+        copy.wait()
+
+
+def forward(x_own, gu_parts, dn_own, hops_done, tile=512):
+    chips = lax.axis_size("dp") // 2
+    half = chips // 2
+    own, width = x_own.shape
+    size, ff = dn_own.shape
+    tile = min(tile, ff)
+    m = 4 * own
+    dma = pltpu.SemaphoreType.DMA
+    vmem = pl.BlockSpec(memory_space=pltpu.VMEM)
+    return pl.pallas_call(
+        functools.partial(forward_kernel, hops_done, tile),
+        out_shape=[
+            jax.ShapeDtypeStruct((m, width), BF16),
+            jax.ShapeDtypeStruct((2, width, ff), BF16),
+            jax.ShapeDtypeStruct((width, 2 * ff), BF16),
+            jax.ShapeDtypeStruct((width, ff), BF16),
+            jax.ShapeDtypeStruct((2, m, ff), BF16),
+            jax.ShapeDtypeStruct((m, ff), BF16),
+            jax.ShapeDtypeStruct((own, width), F32),
+        ],
+        in_specs=[ANY] * (len(gu_parts) + 2),
+        out_specs=[ANY] * 6 + [vmem],
+        scratch_shapes=[
+            pltpu.VMEM((m, width), BF16),
+            pltpu.VMEM((width, ff), BF16),
+            pltpu.VMEM((m, ff), BF16),
+            pltpu.VMEM((chips, 2 * own, size), F32),
+            pltpu.VMEM((chips, 2 * own, size), BF16),
+            pltpu.VMEM((chips, 2 * own, size), BF16),
+            pltpu.VMEM((chips, own, size), BF16),
+            pltpu.VMEM((chips, own, size), BF16),
+            dma((3,)),
+            dma((3,)),
+            dma((2, half - hops_done)),
+            dma((2, half - hops_done)),
+            dma((2, half)),
+            dma((2, half)),
+            dma((2, chips)),
+            dma((2, chips)),
+            dma((2,)),
+            dma((2,)),
+        ],
+        compiler_params=pltpu.CompilerParams(
+            collective_id=3, has_side_effects=True, vmem_limit_bytes=60 * 2**20
+        ),
+        cost_estimate=pl.CostEstimate(
+            flops=6 * m * width * ff, bytes_accessed=0, transcendentals=0
+        ),
+        name="forward",
+    )(x_own, *gu_parts, dn_own)
 
 
 class Gather:
@@ -679,26 +1050,33 @@
         self.step_count = 0
         self.held = []
 
-    def term(self, offset, got=None, where="none"):
-        return block_grad(self.x, self.d, self.ring.chip_at(offset), self.size, got, where)
-
-    def step(self):
+    def terms(self, ahead=0):
+        half = self.ring.chips // 2
+        k = self.step_count + 1 + ahead
+        if k == 1:
+            offsets = (half,)
+        elif k > half:
+            offsets = (0,)
+        else:
+            offsets = (half + 1 - k, k - 1 - half)
+        return block_grads(self.x, self.d, [self.ring.chip_at(o) for o in offsets], self.size)
+
+    def step(self, terms):
         ring, half = self.ring, self.ring.chips // 2
         self.step_count += 1
         k = self.step_count
+        cut = self.size // 2
         if k == 1:
-            term = self.term(half)
-            cut = term.shape[0] // 2
-            up, down = term[:cut], term[cut:]
+            up, down = terms[0][:cut], terms[0][cut:]
         else:
-            d = half + 1 - k
-            up = self.term(d, self.held[0], "top" if k == 2 else "all")
-            down = self.term(-d, self.held[1], "bottom" if k == 2 else "all")
+            up, down = terms
+            if k == 2:
+                up = up.at[:cut].set(low(to_float(up[:cut]) + to_float(self.held[0])))
+                down = down.at[cut:].set(low(to_float(down[cut:]) + to_float(self.held[1])))
+            else:
+                up = low(to_float(up) + to_float(self.held[0]))
+                down = low(to_float(down) + to_float(self.held[1]))
         self.held = [ring.up(up), ring.down(down)]
-
-    def result(self):
-        term = block_grad(self.x, self.d, self.ring.chip_at(0), self.size, dtype=F32)
-        return term + to_float(self.held[0]) + to_float(self.held[1])
 
 
 def region(body):
@@ -869,19 +1247,27 @@
         scores = jnp.einsum("qkgd,ckd->kgqc", query_low, keys_all, preferred_element_type=F32)
         return jnp.where(allowed[None, None], scores, NEGATIVE)
 
-    def sum_sides(partial):
-        return partial[:own] + to_float(across(low(partial[own:])))
-
-    def both_sides(values):
-        return jnp.concatenate([values, across(values)], axis=0)
+    def sum_sides(partial, beside=None):
+        got = across(low(partial[own:]))
+        if beside is None:
+            return partial[:own] + to_float(got)
+        got, beside = tie(got, beside())
+        return partial[:own] + to_float(got), beside
+
+    def both_sides(values, beside=None):
+        got = across(values)
+        if beside is None:
+            return jnp.concatenate([values, got], axis=0)
+        got, beside = tie(got, beside())
+        return jnp.concatenate([values, got], axis=0), beside
 
     def four_ways(values):
         pair = both_sides(values)
         return jnp.concatenate([pair, ring.swap(pair)], axis=0)
 
-    def sum_four(partial):
+    def sum_four(partial, beside=None):
         pair = partial[: 2 * own] + to_float(ring.swap(low(partial[2 * own :])))
-        return sum_sides(pair)
+        return sum_sides(pair, beside)
 
     def attend():
         normed_low = low(norm_gain(to_float(tokens), input_scale))
@@ -926,24 +1312,31 @@
 
     attn_out, left_low, right_out, mixed, ffw_low = region(lambda: join(heads_low))
     ffw_low = meet([gu], ffw_low)
-    gu.step()
-    ffw_rows = region(lambda: four_ways(ffw_low))
-    ffw_rows = meet([gu], ffw_rows)
-    for _ in range(half - 4):
+    if (2 * rows) % 256 == 0:
+        parts = [part for _, _, part in gu.parts]
+        ffw_rows, gu_weights, _, dn_whole, raw, hidden_low, ffw_out = forward(
+            ffw_low, parts, ff_own[1], 2
+        )
+        dn_spots, dn_parts = jnp.zeros((1,), jnp.int32), [dn_whole]
+    else:
+        gu.step()
+        ffw_rows = region(lambda: four_ways(ffw_low))
+        ffw_rows = meet([gu], ffw_rows)
+        for _ in range(half - 4):
+            gu.step()
+            ffw_rows = meet([gu], ffw_rows)
         gu.step()
         ffw_rows = meet([gu], ffw_rows)
-    gu.step()
-    ffw_rows = meet([gu], ffw_rows)
-
-    gu_spots, gu_parts = gu.pieces()
-    dn.step()
-    raw, hidden_low, gu_weights = region(lambda: gate_up(ffw_rows, gu_spots, gu_parts))
-    raw, hidden_low = meet([dn], raw, hidden_low)
-    for _ in range(half - 1):
+
+        gu_spots, gu_parts = gu.pieces()
         dn.step()
+        raw, hidden_low, gu_weights = region(lambda: gate_up(ffw_rows, gu_spots, gu_parts))
         raw, hidden_low = meet([dn], raw, hidden_low)
-    dn_spots, dn_parts = dn.pieces()
-    ffw_out = sum_four(columns_out(hidden_low[None], dn_spots, dn_parts, width))
+        for _ in range(half - 1):
+            dn.step()
+            raw, hidden_low = meet([dn], raw, hidden_low)
+        dn_spots, dn_parts = dn.pieces()
+        ffw_out = sum_four(columns_out(hidden_low[None], dn_spots, dn_parts, width))
     ffw_out_normed, ffw_out_back = jax.vjp(norm_gain, ffw_out, ffw_out_scale)
     block_mid = mixed + ffw_out_normed
     mid_low = low(block_mid)
@@ -970,36 +1363,39 @@
     d_ffw_rows, d_mid = tie(d_ffw_rows, d_mid)
 
     rd = BlockReduce(ring, d_ffw_rows, hidden_low[None], 2 * rows)
-    rd.step()
-    d_gate_up = region(lambda: hidden_back(d_ffw_rows, raw, dn_spots, dn_parts))
-    d_gate_up = meet([rd], d_gate_up)
+    rd.step(rd.terms())
+    d_gate_up, down_terms = region(
+        lambda: (hidden_back(d_ffw_rows, raw, dn_spots, dn_parts), rd.terms())
+    )
+    d_gate_up, down_terms = meet([rd], d_gate_up, down_terms)
+    rd.step(down_terms)
     rg = BlockReduce(ring, ffw_rows, d_gate_up, 2 * rows)
-    rd.step()
     for _ in range(half - 4):
-        d_gate_up = meet([rd], d_gate_up)
-        rd.step()
-    partial = region(
-        lambda: product_t(d_gate_up[0], gu_weights[0]) + product_t(d_gate_up[1], gu_weights[1])
-    )
-    partial = meet([rd], partial)
-    rd.step()
-    rg.step()
+        rd.step(meet([rd], region(rd.terms)))
+
+    def back_2():
+        partial = product_t(d_gate_up[0], gu_weights[0]) + product_t(d_gate_up[1], gu_weights[1])
+        return partial, rd.terms(), rg.terms()
+
+    partial, down_terms, terms = meet([rd], *region(back_2))
+    rd.step(down_terms)
+    rg.step(terms)
 
     def back_3():
-        d_ffw_normed = sum_four(partial)
+        d_ffw_normed, terms = sum_four(partial, lambda: (rd.terms(), rg.terms()))
         _, back = jax.vjp(norm_gain, mixed, ffw_in_scale)
         d_mixed_extra, d_ffw_in_scale = back(d_ffw_normed)
         d_branch = (d_mid + d_mixed_extra) * ROOT_HALF
         _, back = jax.vjp(norm_gain, attn_out, attn_scale)
         d_attn, d_attn_scale = back(d_branch)
-        return d_ffw_in_scale, d_attn_scale, d_branch, low(d_attn)
-
-    d_ffw_in_scale, d_attn_scale, d_branch, d_attn_low = meet([rd, rg], *region(back_3))
-    rd.step()
-    rg.step()
+        return terms, d_ffw_in_scale, d_attn_scale, d_branch, low(d_attn)
+
+    terms, d_ffw_in_scale, d_attn_scale, d_branch, d_attn_low = meet([rd, rg], *region(back_3))
+    rd.step(terms[0])
+    rg.step(terms[1])
 
     def back_4():
-        d_attn_rows = both_sides(d_attn_low)
+        d_attn_rows, terms = both_sides(d_attn_low, rg.terms)
         d_heads = low(product(d_attn_rows, output_t)).reshape(piece_len, kv_local, group, HD)
         keys_all, values_all = kv_all[:, :kv_local], kv_all[:, kv_local:]
         probs = jnp.exp(scores_for(query_low, keys_all) - log_totals)
@@ -1013,19 +1409,19 @@
         d_keys_all = jnp.einsum("kgqc,qkgd->ckd", d_scores, query_low, preferred_element_type=F32)
         d_query_rot = jnp.einsum("kgqc,ckd->qkgd", d_scores, keys_all, preferred_element_type=F32)
         d_kv_all = jnp.concatenate([d_keys_all, d_values_all], axis=1)
-        return d_attn_rows, d_kv_all, d_query_rot
-
-    d_attn_rows, d_kv_all, d_query_rot = meet([rd, rg], *region(back_4))
-    rg.step()
+        return terms, d_attn_rows, d_kv_all, d_query_rot
+
+    terms, d_attn_rows, d_kv_all, d_query_rot = meet([rd, rg], *region(back_4))
+    rg.step(terms)
     for _ in range(half - 4):
-        d_kv_all = meet([rg], d_kv_all)
-        rg.step()
+        rg.step(meet([rg], region(rg.terms)))
 
     def back_5():
         to_before = low(d_kv_all[:piece_len])
         to_after = low(d_kv_all[2 * piece_len :])
         from_after = to_float(lax.ppermute(to_before, "dp", backward_pairs))
         from_before = to_float(lax.ppermute(to_after, "dp", forward_pairs))
+        from_after, from_before, terms = tie(from_after, from_before, rg.terms())
         d_kv = d_kv_all[piece_len : 2 * piece_len] + from_after
         d_kv = d_kv + jnp.pad(from_before, ((0, piece_len - reach_after), (0, 0), (0, 0)))
         d_kv = in_order(d_kv)
@@ -1037,30 +1433,10 @@
                 d_kv[:, kv_local:],
             )
         )
-        return low(d_qkv), query_scale_grad, key_scale_grad
-
-    d_qkv_low, query_scale_grad, key_scale_grad = meet([rg], *region(back_5))
-    rg.step()
-
-    def own_columns(values, which):
-        blocks = values.reshape(values.shape[0], chips, 2, rows)
-        return lax.dynamic_index_in_dim(blocks, which, 2, keepdims=False).reshape(
-            values.shape[0], chips * rows
-        )
-
-    def both_cores(pairs, last):
-        if rows % 128 == 0:
-            theirs = row_grads(pairs, last, 1 - core, chips, rows, None, BF16)
-            return row_grads(pairs, last, core, chips, rows, ring.swap(theirs), F32)
-
-        def terms(which):
-            return jnp.concatenate(
-                [product_l(own_columns(x, which), d) for x, d in pairs]
-                + [own_columns(last.T, which).T],
-                axis=1,
-            )
-
-        return terms(core) + to_float(ring.swap(low(terms(1 - core))))
+        return terms, low(d_qkv), query_scale_grad, key_scale_grad
+
+    terms, d_qkv_low, query_scale_grad, key_scale_grad = meet([rg], *region(back_5))
+    rg.step(terms)
 
     def head_gain_back(grads):
         padded = jnp.pad(grads.reshape(ring.devices, head_part), ((0, 0), (0, rows - head_part)))
@@ -1073,7 +1449,10 @@
         d_right_low = low(d_right)
         d_left_low = low(product(d_right_low, right_t))
         d_normed = d_branch + product_t(d_left_low, left_full)
-        d_normed = d_normed + sum_sides(product_t(d_qkv_low, qkv_full))
+        d_more, ends = sum_sides(
+            product_t(d_qkv_low, qkv_full), lambda: (rd.terms(), rg.terms())
+        )
+        d_normed = d_normed + d_more
         d_inputs_extra, d_input_scale = input_norm_back(d_normed)
         grad_tokens = d_branch + d_inputs_extra
         gain_grads = jnp.stack(
@@ -1090,48 +1469,23 @@
             axis=0,
         )
         gain_grads = jnp.pad(gain_grads, ((0, 120), (0, 0))).T
-        summed = both_cores(
-            [
-                (d_attn_rows, heads_low),
-                (seq_rows, d_qkv_low),
-                (mid_low, d_pre_low),
-                (d_proj_low, gated_low),
-                (low(normed), d_left_low),
-                (d_right_low, left_low),
-            ],
-            gain_grads,
-        )
-        large = 2 * q_cols + 2 * kv_cols
-        part = (summed.shape[1] - large) // 2
-        small_mine = lax.dynamic_slice_in_dim(summed, large + side * part, part, 1)
-        small_theirs = lax.dynamic_slice_in_dim(summed, large + (1 - side) * part, part, 1)
-        small_mine = small_mine + to_float(across(low(small_theirs)))
-        return grad_tokens, summed[:, : large // 2], summed[:, large // 2 : large], small_mine
-
-    grad_tokens, *blocks = meet([rg], *region(back_6))
-
-    def finish_feed_forward():
-        down_sum = rd.result()
-        gate_up_sum = rg.result()
-        return (
-            back_to_rows(down_sum),
-            back_to_rows(gate_up_sum[:, :ff_cols]),
-            back_to_rows(gate_up_sum[:, ff_cols:]),
-        )
-
-    def back_to_rows(block):
-        mine = lax.dynamic_slice_in_dim(block, core * rows, rows, 0)
-        theirs = lax.dynamic_slice_in_dim(block, (1 - core) * rows, rows, 0)
-        got = ring.swap(theirs)
-        return jnp.where(
-            core == 0,
-            jnp.concatenate([mine, got], axis=1),
-            jnp.concatenate([got, mine], axis=1),
-        )
-
-    out_down_t, out_gate, out_up = region(finish_feed_forward)
-    one, two, small_half = last_reduce(blocks)
-    total = jnp.concatenate([one, two], axis=1)
+        pairs = [
+            (d_attn_rows, heads_low),
+            (seq_rows, d_qkv_low),
+            (mid_low, d_pre_low),
+            (d_proj_low, gated_low),
+            (low(normed), d_left_low),
+            (d_right_low, left_low),
+        ]
+        return grad_tokens, ends, row_grads(pairs, gain_grads, core, chips, rows)
+
+    grad_tokens, (down_end, gate_up_end), (mine, theirs) = meet([rg], *region(back_6))
+    total, small_half, out_gate, out_up, out_down_t = last_reduce(
+        mine,
+        theirs,
+        2 * q_cols + 2 * kv_cols,
+        [gate_up_end[0], *rg.held, down_end[0], *rd.held],
+    )
     out_output = total[:, :q_cols].T
     out_qkv = total[:, q_cols:]
     small_other = across(small_half)

time: 1010 us -> 880 us (0.87)
  waiting for transfers between devices: 255 us -> 59.1 us
  Pallas kernels: 316 us -> 408 us
  starting transfers between devices: 68.2 us -> 39.3 us
  other arithmetic: 133 us -> 157 us
  local copies, waits for them, and re-layouts: 127 us -> 108 us
    pallas_call x1 -> x2, Pallas kernels: 64.1 us -> 231 us  [the longest x1 165 us: forward(): pl.pallas_call(functools.partial(forward_kernel, hops_done, tile), out_sh...]
    ppermute x9 -> x6, waiting for transfers between devices: 134 us -> 45.2 us  [across(): return lax.ppermute(values, 'tensor', [(0, 1), (1, 0)])]
    ppermute x16 -> x10, waiting for transfers between devices: 85.2 us -> 3.57 us  [up(): return lax.ppermute(values, 'dp', self.cw)]
    pallas_call x21 -> x12, Pallas kernels: 181 us -> 105 us  [grid_call(): pl.pallas_call(kernel, grid_spec=pltpu.PrefetchScalarGridSpec(num_scalar_...]
    convert_element_type x8 -> x16, other arithmetic: 18.3 us -> 47.2 us  [low(): return values.astype(BF16)]
    slice x12 -> x5, local copies, waits for them, and re-layouts: 23.1 us -> 6.57 us  [the longest x3 3.77 us: sum_sides(): got = across(low(partial[own:]))]
    ppermute x8 -> x2, waiting for transfers between devices: 23.2 us -> 8.65 us  [swap(): return lax.ppermute(values, 'dp', self.core_pairs)]
    ppermute x16 -> x10, starting transfers between devices: 25.2 us -> 12.2 us  [up(): return lax.ppermute(values, 'dp', self.cw)]
  transfers between devices with their start and end apart: 53 -> 32, of which waited for: 29 -> 9; matrix products, arithmetic and copies ran while one was open for 29% -> 34% of each run, Pallas kernels for 13% -> 11%
where the time goes in v3:
time: 880 us; the launch traced here: 869 us
  Pallas kernels  408 us (46%)
  other arithmetic  157 us (18%)
  local copies, waits for them, and re-layouts  108 us (12%)
  matrix products  96.8 us (11%)
  waiting for transfers between devices  59.1 us (7%)
  starting transfers between devices  39.3 us (4%)
    pallas_call x1, Pallas kernels, forward(): pl.pallas_call(functools.partial(forward_kernel, hops_done, tile), out_sh...  165 us
    pallas_call x12, Pallas kernels, grid_call(): pl.pallas_call(kernel, grid_spec=pltpu.PrefetchScalarGridSpec(num_scalar_...  105 us
    pallas_call x1, Pallas kernels, comm_call(): pl.pallas_call(kernel, out_shape=shapes, in_specs=[ANY] * len(operands),...  71 us
    pallas_call x1, Pallas kernels, last_reduce(): pl.pallas_call(functools.partial(last_kernel, large), out_shape=[jax.Shap...  66.9 us
    convert_element_type x16, other arithmetic, low(): return values.astype(BF16)  47.2 us
    ppermute x6, waiting for transfers between devices, across(): return lax.ppermute(values, 'tensor', [(0, 1), (1, 0)])  45.2 us
    dot_general x8, matrix products, product_t(): lax.dot_general(left_in, right_in, (((1,), (1,)), ((), ())), preferred_el...  43.4 us
    unnamed x94, local copies, waits for them, and re-layouts  24.4 us
  transfers between devices with their start and end apart: 32, of which 9 were waited for; matrix products, arithmetic and copies ran while one was open for 34% of the time, Pallas kernels for 11%

profile of v3, /device:TPU:0, one launch (start us, length us, event | category | flops | bytes accessed | tf_op | source)
XLA Modules:
  0.0 869.3 jit_solution(6388037683330454153)
XLA Ops:
  15.4 71.0 %first_gather.1 = (bf16[2048,1536]{1,0:T(8,128)(2,1)}, bf16[2048,1024]{1,0:T(8,128)(2,1)}, bf16[2048,768]{1,0:T(8,128)(2,1)S(1)}, bf16[256,4096]{1,0:T(8,128)(2,...) custom-call(bf16[128,1536]{1,0:T(8,128)(2,1)S(1)} %pad_maximum_fusion.7.refs_0_, ...), custom_call_target="tpu_custom_call" | custom-call | bytes 142606336 | tf_op jit(solution)/shard_map/first_gather/pallas_call | solution.py:264
  97.9 5.2 fusion.137
  103.7 53.7 %conditional.8 = (bf16[512,2048]{1,0:T(8,128)(2,1)}, f32[512,1536]{1,0:T(8,128)}, bf16[512,1,4,256]{3,0,2,1:T(8,128)(2,1)}, bf16[1280,2,256]{2,0,1:T(8,128)(2,1)...) conditional(s32[]{:T(128)} %convert_element_type.279, () %tuple.102, (bf16[256,2048]{1,0:T(8,128)(2,1)}, ...), branch_computations={%region_2.3_spmd, %region_3.11_spmd} | conditional | flops 5961549312 | bytes 123166088 | solution.py:1085
  111.5 6.7 fusion.140
  130.6 3.2 slice.369
  133.9 3.2 reshape.787
  152.3 5.1 fusion.12
  157.3 4.2 collective-permute-start.11
  163.1 40.2 %conditional.9 = (f32[256,2048]{1,0:T(8,128)}, bf16[256,64]{0,1:T(8,128)(2,1)S(1)}, f32[256,2048]{1,0:T(8,128)}, f32[256,2048]{1,0:T(8,128)}, bf16[256,2048]{1,0:T(8,128)(2,1)}) conditional(s32[]{:T(128)} %convert_element_type.279, () %tuple.101, (bf16[512,1024]{0,1:T(8,128)(2,1)}, bf16[2048,1024]{1,0:T(8,128)(2,1)}, ...), branch_computations={%region_11.12_spmd, %region_12.17_spmd} | conditional | flops 2296923392 | bytes 64939256 | solution.py:1085
  163.1 5.3 fusion.138
  181.5 12.5 %collective-permute-done.6 = bf16[256,2048]{1,0:T(8,128)(2,1)} collective-permute-done((bf16[256,2048]{1,0:T(8,128)(2,1)}, bf16[256,2048]{1,0:T(8,128)(2,1)}, u32[]{:S(2)}, u32[]{:S(2)}) %collective-permute-start.6) | collective-permute-done | bytes 1048608 | tf_op jit(solution)/shard_map/cond/branch_1_fun/ppermute | solution.py:110
  194.0 3.5 multiply_reduce_fusion.5
  197.6 4.6 multiply_reduce_fusion.3
  203.3 3.5 collective-permute-done.11.refs_3_
  208.6 164.6 %forward.1 = (bf16[1024,2048]{1,0:T(8,128)(2,1)}, bf16[2,2048,2048]{2,1,0:T(8,128)(2,1)}, bf16[2048,4096]{1,0:T(8,128)(2,1)}, bf16[2048,2048]{1,0:T(8,128)(2,1)}...) custom-call(bf16[256,2048]{1,0:T(8,128)(2,1)} %get-tuple-element.502.x_own, ...), custom_call_target="tpu_custom_call" | custom-call | flops 25769803776 | tf_op jit(solution)/shard_map/forward/pallas_call | solution.py:978
  380.2 4.8 add_convert_fusion.12
  389.3 23.7 %collective-permute-done.13 = bf16[256,2048]{1,0:T(8,128)(2,1)S(1)} collective-permute-done((bf16[256,2048]{1,0:T(8,128)(2,1)S(1)}, bf16[256,2048]{1,0:T(8,128)(2,1)S(1)}, u32[]{:S(2)}, u32[]{:S(2)}) %collective-permute-start.13) | collective-permute-done | bytes 1048608 | tf_op jit(solution)/shard_map/ppermute | solution.py:110
  414.5 4.5 collective-permute-done.14
  420.8 5.6 block_grads.19
  429.8 26.1 %conditional.10 = (bf16[2,1024,2048]{2,1,0:T(8,128)(2,1)}, bf16[256,2048]{1,0:T(8,128)(2,1)}, bf16[256,2048]{1,0:T(8,128)(2,1)}) conditional(s32[]{:T(128)} %convert_element_type.279, () %tuple.108, (bf16[1024,2048]{1,0:T(8,128)(2,1)S(1)}, bf16[2,1024,2048]{2,1,0:T(8,128)(2,1)}, bf16[2048,2048]{1,0:T(8,128)(2,1)}, s32[]{:T(128)}, ...), branch_computations={%region_21.22_spmd, %region_22.23_spmd} | conditional | flops 8589934592 | bytes 46137692 | solution.py:1085
  429.8 19.3 %hidden_back.1 = bf16[2,1024,2048]{2,1,0:T(8,128)(2,1)} custom-call(s32[1]{0:T(128)} %constant.367.clone.spots, bf16[1024,2048]{1,0:T(8,128)(2,1)S(1)} %get-tuple-element.257.x.refs_0_.refs_1_, bf16[2,1024,2048]{2,1,0:T(8,128)(2,1)} %get-tuple-element.258.raw, bf16[2048,2048]{1,0:T(8,128)(2,1)} %get-tuple-element.259.refs_0_), custom_call_target="tpu_custom_call" | custom-call | flops 8589934592 | bytes 29360128 | tf_op jit(solution)/shard_map/cond/branch_1_fun/hidden_back/pallas_call | solution.py:405
  449.7 6.3 block_grads.10
  461.9 39.9 %conditional.11 = (f32[1024,2048]{1,0:T(8,128)}, bf16[256,2048]{1,0:T(8,128)(2,1)S(1)}, bf16[256,2048]{1,0:T(8,128)(2,1)}, bf16[256,4096]{1,0:T(8,128)(2,1)S(1)}) conditional(s32[]{:T(128)} %convert_element_type.279, () %tuple.111, (bf16[2,1024,2048]{2,1,0:T(8,128)(2,1)}, bf16[2,2048,2048]{2,1,0:T(8,128)(2,1)}, s32[]{:T(128)}, ...), branch_computations={%region_23.24_spmd, %region_24.25_spmd} | conditional | flops 17181966336 | bytes 50332116 | solution.py:1085
  461.9 12.6 %fusion.34 = f32[1024,2048]{1,0:T(8,128)S(1)} fusion(bf16[2,2048,2048]{2,1,0:T(8,128)(2,1)} %get-tuple-element.265, bf16[2,1024,2048]{2,1,0:T(8,128)(2,1)} %get-tuple-element.264.refs_1_), kind=kOutput, calls=%fused_computation.80 | convolution fusion | flops 8589934592 | bytes 20971520 | tf_op jit(solution)/shard_map/cond/branch_1_fun/dot_general | solution.py:65
  474.4 14.5 %fusion.40 = f32[1024,2048]{1,0:T(8,128)} fusion(f32[1024,2048]{1,0:T(8,128)S(1)} %fusion.34, bf16[2,2048,2048]{2,1,0:T(8,128)(2,1)} %get-tuple-element.265, bf16[2,1024,2048]{2,1,0:T(8,128)(2,1)} %get-tuple-element.264.refs_1_), kind=kOutput, calls=%fused_computation.86 | convolution fusion | flops 8592031744 | bytes 29360128 | tf_op jit(solution)/shard_map/cond/branch_1_fun/dot_general | solution.py:65
  489.5 6.3 block_grads.11
  495.8 5.9 block_grads.12
  512.9 45.9 %conditional.12 = (bf16[256,2048]{1,0:T(8,128)(2,1)}, bf16[256,2048]{1,0:T(8,128)(2,1)}, bf16[256,4096]{1,0:T(8,128)(2,1)}, bf16[256,4096]{1,0:T(8,128)(2,1)}, f...) conditional(s32[]{:T(128)} %convert_element_type.279, ...), branch_computations={%region_25.26_spmd, %region_26.33_spmd} | conditional | flops 19399736 | bytes 103928680 | solution.py:1085
  515.5 4.1 collective-permute-done
  526.0 6.5 block_grads.13
  533.1 9.5 %block_grads.14 = (bf16[256,4096]{1,0:T(8,128)(2,1)}, bf16[256,4096]{1,0:T(8,128)(2,1)}) custom-call(s32[2]{0:T(128)} %pad_add_fusion.3.spots, bf16[1024,2048]{1,0:T(8,128)(2,1)} %get-tuple-element.278.refs_0_.refs_1_, bf16[1024,2048]{1,0:T(8,128)(2,1)} %get-tuple-element.278.refs_0_.refs_1_, bf16[2,1024,2048]{2,1,0:T(8,128)(2,1)} %get-tuple-element.279.refs_2_), custom_call_target="tpu_custom_call" | custom-call | tf_op jit(solution)/shard_map/cond/branch_1_fun/block_grads/pallas_call | solution.py:405
  545.3 3.8 collective-permute-done.1
  551.9 3.9 multiply_reduce_fusion.6
  555.8 3.0 fusion.48
  566.4 2.9 add_convert_fusion.9
  574.4 61.2 %conditional.13 = (bf16[256,4096]{1,0:T(8,128)(2,1)}, bf16[256,4096]{1,0:T(8,128)(2,1)}, bf16[512,2048]{1,0:T(8,128)(2,1)}, f32[1280,2,256]{2,0,1:T(8,128)}, f32[512,1,4,256]{3,0,2,1:T(8,128)}) conditional(s32[]{:T(128)} %convert_element_type.279, () %tuple.117, (bf16[256,2048]{1,0:T(8,128)(2,1)}, s32[]{:T(128)}, bf16[1024,2048]{1,0:T(8,128)(2,1)}, ...), branch_computations={%region_33.34_spmd, %region_34.36_spmd} | conditional | flops 8892971008 | bytes 188663328 | solution.py:1085
  578.2 9.6 %block_grads.15 = (bf16[256,4096]{1,0:T(8,128)(2,1)}, bf16[256,4096]{1,0:T(8,128)(2,1)}) custom-call(s32[2]{0:T(128)} %pad_add_fusion.4.spots, bf16[1024,2048]{1,0:T(8,128)(2,1)} %get-tuple-element.294.refs_0_.refs_1_, bf16[1024,2048]{1,0:T(8,128)(2,1)} %get-tuple-element.294.refs_0_.refs_1_, bf16[2,1024,2048]{2,1,0:T(8,128)(2,1)} %get-tuple-element.295.refs_2_), custom_call_target="tpu_custom_call" | custom-call | tf_op jit(solution)/shard_map/cond/branch_1_fun/block_grads/pallas_call | solution.py:405
  588.3 7.2 fusion.68
  600.4 5.0 convolution_convert_fusion.1
  607.7 6.7 fusion.64
  614.4 6.0 fusion.53
  620.4 5.0 fusion.60
  625.4 4.5 convolution_bitcast_fusion
  629.9 4.0 convolution_bitcast_fusion.1
  635.6 4.4 add_convert_fusion.5
  640.9 4.3 add_convert_fusion.4
  646.4 58.6 %conditional.14 = (bf16[256,4096]{1,0:T(8,128)(2,1)}, bf16[256,4096]{1,0:T(8,128)(2,1)}, bf16[512,1536]{1,0:T(8,128)(2,1)}, f32[256]{0:T(256)S(1)}, f32[256]{0:T(256)S(1)}) conditional(s32[]{:T(128)} %convert_element_type.279, () %tuple.120, (f32[1280,2,256]{2,0,1:T(8,128)}, s32[]{:T(128)}, bf16[1024,2048]{1,0:T(8,128)(2,1)}, ...), branch_computations={%region_36.37_spmd, %region_37.46_spmd} | conditional | flops 17646108 | bytes 88832576 | solution.py:1085
  651.1 3.7 collective-permute-start.3
  654.8 3.2 slice.280
  657.9 3.2 reshape.802
  664.3 4.3 copy.317
  675.8 4.8 add_add_fusion.2
  682.6 3.4 copy.313
  686.1 9.4 %block_grads.16 = (bf16[256,4096]{1,0:T(8,128)(2,1)}, bf16[256,4096]{1,0:T(8,128)(2,1)}) custom-call(s32[2]{0:T(128)} %pad_add_fusion.8.spots, bf16[1024,2048]{1,0:T(8,128)(2,1)} %get-tuple-element.310.refs_0_.refs_1_, bf16[1024,2048]{1,0:T(8,128)(2,1)} %get-tuple-element.310.refs_0_.refs_1_, bf16[2,1024,2048]{2,1,0:T(8,128)(2,1)} %get-tuple-element.311.refs_2_), custom_call_target="tpu_custom_call" | custom-call | tf_op jit(solution)/shard_map/cond/branch_1_fun/block_grads/pallas_call | solution.py:405
  704.9 4.4 add_convert_fusion.3
  709.5 4.4 add_convert_fusion.2
  718.4 65.5 %conditional.15 = (f32[256,2048]{1,0:T(8,128)}, bf16[256,2048]{1,0:T(8,128)(2,1)}, bf16[256,4096]{1,0:T(8,128)(2,1)}, f32[1024,3328]{1,0:T(8,128)}, bf16[1024,3328]{1,0:T(8,128)(2,1)}) conditional(s32[]{:T(128)} %convert_element_type.279, () %tuple.123, (f32[2048,1]{1,0:T(8,128)}, f32[256,2048]{1,0:T(8,128)S(1)}, f32[256,2048]{1,0:T(8,128)}, ...), branch_computations={%region_48.49_spmd, %region_49.56_spmd} | conditional | flops 9416748032 | bytes 192424544 | solution.py:1085
  718.4 6.2 fusion.139
  732.6 3.2 fusion.92
  740.5 4.3 block_grads.17
  744.9 6.8 block_grads.18
  758.8 3.5 fusion.91
  768.0 15.9 %row_grads.1 = (f32[1024,3328]{1,0:T(8,128)}, bf16[1024,3328]{1,0:T(8,128)(2,1)}) custom-call(s32[1]{0:T(128)} %bitcast.79.spots, bf16[512,2048]{1,0:T(8,128)(2,1)} %get-tuple-element.343.refs_0_, bf16[512,2048]{1,0:T(8,128)(2,1)} %get-tuple-element.344.refs_1_, bf16[256,2048]{1,0:T(8,128)(2,1)S(1)} %copy-done.51, bf16[256,2048]{1,0:T(8,128)(2,1)S(1)} %copy-done.53, ...), custom_call_target="tpu_custom_call" | custom-call | flops 6039797760 | bytes 32833536 | tf_op jit(solution)/shard_map/cond/branch_1_fun/row_grads/pallas_call | solution.py:405
  783.9 66.9 %last_reduce.1 = (f32[128,2560]{1,0:T(8,128)}, f32[128,384]{1,0:T(8,128)}, f32[128,4096]{1,0:T(8,128)}, f32[128,4096]{1,0:T(8,128)}, f32[128,4096]{1,0:T(8,128)}) custom-call(f32[1024,3328]{1,0:T(8,128)} %get-tuple-element.588.refs_0_, bf16[1024,3328]{1,0:T(8,128)(2,1)} %get-tuple-element.589.refs_1_, bf16[256,4096]{1,0:T(8,128)(2,1)} %get-tuple-element.590.refs_2_, ...), custom_call_target="tpu_custom_call" | custom-call | bytes 272629760 | tf_op jit(solution)/shard_map/last_reduce/pallas_call | solution.py:758
  (397 shorter events, 233.6 us)
Async XLA Ops:
  0.7 12.8 %copy-start.2 = (bf16[128,4096]{1,0:T(8,128)(2,1)S(1)}, bf16[128,4096]{1,0:T(8,128)(2,1)}, u32[]{:S(2)}) copy-start(bf16[128,4096]{1,0:T(8,128)(2,1)} %refs_3_.1) | copy-start | bytes 3145732
  0.7 12.8 %copy-start.3 = (bf16[128,4096]{1,0:T(8,128)(2,1)S(1)}, bf16[128,4096]{1,0:T(8,128)(2,1)}, u32[]{:S(2)}) copy-start(bf16[128,4096]{1,0:T(8,128)(2,1)} %refs_4_.1) | copy-start | bytes 3145732
  89.0 68.3 %collective-permute-start.9 = (bf16[256,4096]{1,0:T(8,128)(2,1)}, bf16[256,4096]{1,0:T(8,128)(2,1)}, u32[]{:S(2)}, u32[]{:S(2)}) collective-permute-start(bf16[256,4096]{1,0:T(8,128)(2,1)} %get-tuple-element.491.refs_0_), channel_id=1, source_target_pairs={{0,8},{2,10},{8,16},{10,18},{16,24},{18,26},{24,28},{26,30},{28,20... | collective-permute-start | bytes 6291464 | tf_op jit(solution)/shard_map/ppermute | solution.py:100
  90.5 66.8 %collective-permute-start.10 = (bf16[256,4096]{1,0:T(8,128)(2,1)}, bf16[256,4096]{1,0:T(8,128)(2,1)}, u32[]{:S(2)}, u32[]{:S(2)}) collective-permute-start(bf16[256,4096]{1,0:T(8,128)(2,1)} %get-tuple-element.491.refs_0_), channel_id=1, source_target_pairs={{8,0},{10,2},{16,8},{18,10},{24,16},{26,18},{28,24},{30,26},{20,28... | collective-permute-start | bytes 6291464 | tf_op jit(solution)/shard_map/ppermute | solution.py:103
  96.7 6.4 copy-start.31
  103.1 58.8 %copy-start.1 = (bf16[2048,768]{1,0:T(8,128)(2,1)S(1)}, bf16[2048,768]{1,0:T(8,128)(2,1)}, u32[]{:S(2)}) copy-start(bf16[2048,768]{1,0:T(8,128)(2,1)} %copy-done) | copy-start | bytes 9437188
  124.7 20.3 %collective-permute-start.4 = (bf16[512,2,256]{2,0,1:T(8,128)(2,1)}, bf16[512,2,256]{2,0,1:T(8,128)(2,1)}, u32[]{:S(2)}, u32[]{:S(2)}) collective-permute-start(bf16[512,2,256]{2,0,1:T(8,128)(2,1)} %maximum_select_fusion), channel_id=1, source_target_pairs={{0,2},{2,4},{4,6},{6,8},{8,10},{10,12},{12,14},{14,16},{16,18},{18... | collective-permute-start | bytes 1572872 | tf_op jit(solution)/shard_map/cond/branch_1_fun/ppermute | solution.py:1281
  129.0 4.8 copy-start.65
  129.0 16.0 %collective-permute-start.5 = (bf16[256,2,256]{2,0,1:T(8,128)(2,1)}, bf16[256,2,256]{2,0,1:T(8,128)(2,1)}, u32[]{:S(2)}, u32[]{:S(2)}) collective-permute-start(bf16[256,2,256]{2,0,1:T(8,128)(2,1)} %slice.378), channel_id=1, source_target_pairs={{2,0},{4,2},{6,4},{8,6},{10,8},{12,10},{14,12},{16,14},{18,16},{20... | collective-permute-start | bytes 786440 | tf_op jit(solution)/shard_map/cond/branch_1_fun/ppermute | solution.py:1282
  157.3 5.8 copy-start.62
  157.3 5.8 copy-start.10
  157.3 49.5 %collective-permute-start.11 = (bf16[256,4096]{1,0:T(8,128)(2,1)}, bf16[256,4096]{1,0:T(8,128)(2,1)}, u32[]{:S(2)}, u32[]{:S(2)}) collective-permute-start(bf16[256,4096]{1,0:T(8,128)(2,1)} %collective-permute-done.9.refs_1_), channel_id=1, source_target_pairs={{0,8},{2,10},{8,16},{10,18},{16,24},{18,26},{24,28},{26,30},{28,20... | collective-permute-start | bytes 6291464 | tf_op jit(solution)/shard_map/ppermute | solution.py:100
  161.5 47.1 %collective-permute-start.12 = (bf16[256,4096]{1,0:T(8,128)(2,1)}, bf16[256,4096]{1,0:T(8,128)(2,1)}, u32[]{:S(2)}, u32[]{:S(2)}) collective-permute-start(bf16[256,4096]{1,0:T(8,128)(2,1)} %collective-permute-done.10.refs_2_), channel_id=1, source_target_pairs={{8,0},{10,2},{16,8},{18,10},{24,16},{26,18},{28,24},{30,26},{20,28... | collective-permute-start | bytes 6291464 | tf_op jit(solution)/shard_map/ppermute | solution.py:103
  163.1 8.1 copy-start.12
  169.7 24.3 %collective-permute-start.6 = (bf16[256,2048]{1,0:T(8,128)(2,1)}, bf16[256,2048]{1,0:T(8,128)(2,1)}, u32[]{:S(2)}, u32[]{:S(2)}) collective-permute-start(bf16[256,2048]{1,0:T(8,128)(2,1)} %slice.519), channel_id=1, source_target_pairs={{0,1},{1,0},{2,3},{3,2},{4,5},{5,4},{6,7},{7,6},{8,9},{9,8},{10,11... | collective-permute-start | bytes 3145736 | tf_op jit(solution)/shard_map/cond/branch_1_fun/ppermute | solution.py:110
  179.7 17.8 %copy-start.54 = (bf16[256,64]{0,1:T(8,128)(2,1)}, bf16[256,64]{0,1:T(8,128)(2,1)S(1)}, u32[]{:S(2)}) copy-start(bf16[256,64]{0,1:T(8,128)(2,1)S(1)} %convolution_convert_fusion) | copy-start | bytes 98308 | tf_op jit(solution)/shard_map/cond
  181.5 16.0 %copy-start.13 = (bf16[256,2048]{1,0:T(8,128)(2,1)S(1)}, bf16[256,2048]{1,0:T(8,128)(2,1)}, u32[]{:S(2)}) copy-start(bf16[256,2048]{1,0:T(8,128)(2,1)} %copy-done.12) | copy-start | bytes 3145732 | tf_op jit(solution)/shard_map/cond
  203.3 169.8 %copy-start.56 = (bf16[256,64]{0,1:T(8,128)(2,1)}, bf16[256,64]{0,1:T(8,128)(2,1)S(1)}, u32[]{:S(2)}) copy-start(bf16[256,64]{0,1:T(8,128)(2,1)S(1)} %get-tuple-element.581) | copy-start | bytes 98308
  388.5 24.6 %collective-permute-start.13 = (bf16[256,2048]{1,0:T(8,128)(2,1)S(1)}, bf16[256,2048]{1,0:T(8,128)(2,1)S(1)}, u32[]{:S(2)}, u32[]{:S(2)}) collective-permute-start(bf16[256,2048]{1,0:T(8,128)(2,1)S(1)} %fusion.100), channel_id=1, source_target_pairs={{0,1},{1,0},{2,3},{3,2},{4,5},{5,4},{6,7},{7,6},{8,9},{9,8},{10,11... | collective-permute-start | bytes 3145736 | tf_op jit(solution)/shard_map/ppermute | solution.py:110
  414.5 4.5 collective-permute-start.14
  420.8 9.0 %copy-start.7 = (bf16[1024,2048]{1,0:T(8,128)(2,1)}, bf16[1024,2048]{1,0:T(8,128)(2,1)S(1)}, u32[]{:S(2)}) copy-start(bf16[1024,2048]{1,0:T(8,128)(2,1)S(1)} %pad_maximum_fusion.5.refs_0_) | copy-start | bytes 12582916
  427.7 28.2 %collective-permute-start.15 = (bf16[128,2048]{1,0:T(8,128)(2,1)S(1)}, bf16[128,2048]{1,0:T(8,128)(2,1)S(1)}, u32[]{:S(2)}, u32[]{:S(2)}) collective-permute-start(bf16[128,2048]{1,0:T(8,128)(2,1)S(1)} %get-tuple-element.1286), channel_id=1, source_target_pairs={{0,8},{2,10},{8,16},{10,18},{16,24},{18,26},{24,28},{26,30},{28,20... | collective-permute-start | bytes 1572872 | tf_op jit(solution)/shard_map/ppermute | solution.py:100
  428.6 27.3 %collective-permute-start.16 = (bf16[128,2048]{1,0:T(8,128)(2,1)S(1)}, bf16[128,2048]{1,0:T(8,128)(2,1)S(1)}, u32[]{:S(2)}, u32[]{:S(2)}) collective-permute-start(bf16[128,2048]{1,0:T(8,128)(2,1)S(1)} %get-tuple-element.1285), channel_id=1, source_target_pairs={{8,0},{10,2},{16,8},{18,10},{24,16},{26,18},{28,24},{30,26},{20,28... | collective-permute-start | bytes 1572872 | tf_op jit(solution)/shard_map/ppermute | solution.py:103
  429.8 19.3 %copy-start.8 = (bf16[1024,2048]{1,0:T(8,128)(2,1)}, bf16[1024,2048]{1,0:T(8,128)(2,1)S(1)}, u32[]{:S(2)}) copy-start(bf16[1024,2048]{1,0:T(8,128)(2,1)S(1)} %get-tuple-element.257.x.refs_0_.refs_1_) | copy-start | bytes 12582916 | tf_op jit(solution)/shard_map/cond
  457.9 43.9 %collective-permute-start.17 = (bf16[256,2048]{1,0:T(8,128)(2,1)}, bf16[256,2048]{1,0:T(8,128)(2,1)}, u32[]{:S(2)}, u32[]{:S(2)}) collective-permute-start(bf16[256,2048]{1,0:T(8,128)(2,1)} %fusion.111), channel_id=1, source_target_pairs={{0,8},{2,10},{8,16},{10,18},{16,24},{18,26},{24,28},{26,30},{28,20... | collective-permute-start | bytes 3145736 | tf_op jit(solution)/shard_map/ppermute | solution.py:100
  460.7 41.0 %collective-permute-start.18 = (bf16[256,2048]{1,0:T(8,128)(2,1)}, bf16[256,2048]{1,0:T(8,128)(2,1)}, u32[]{:S(2)}, u32[]{:S(2)}) collective-permute-start(bf16[256,2048]{1,0:T(8,128)(2,1)} %fusion.112), channel_id=1, source_target_pairs={{8,0},{10,2},{16,8},{18,10},{24,16},{26,18},{28,24},{30,26},{20,28... | collective-permute-start | bytes 3145736 | tf_op jit(solution)/shard_map/ppermute | solution.py:103
  504.4 54.4 %collective-permute-start.19 = (bf16[256,2048]{1,0:T(8,128)(2,1)}, bf16[256,2048]{1,0:T(8,128)(2,1)}, u32[]{:S(2)}, u32[]{:S(2)}) collective-permute-start(bf16[256,2048]{1,0:T(8,128)(2,1)} %add_convert_fusion.11), channel_id=1, source_target_pairs={{0,8},{2,10},{8,16},{10,18},{16,24},{18,26},{24,28},{26,30},{28,20... | collective-permute-start | bytes 3145736 | tf_op jit(solution)/shard_map/ppermute | solution.py:100
  508.2 4.7 copy-start.25
  508.2 4.7 copy-start.26
  508.2 50.6 %collective-permute-start.20 = (bf16[256,2048]{1,0:T(8,128)(2,1)}, bf16[256,2048]{1,0:T(8,128)(2,1)}, u32[]{:S(2)}, u32[]{:S(2)}) collective-permute-start(bf16[256,2048]{1,0:T(8,128)(2,1)} %add_convert_fusion.10), channel_id=1, source_target_pairs={{8,0},{10,2},{16,8},{18,10},{24,16},{26,18},{28,24},{30,26},{20,28... | collective-permute-start | bytes 3145736 | tf_op jit(solution)/shard_map/ppermute | solution.py:103
  510.9 47.9 %collective-permute-start.21 = (bf16[128,4096]{1,0:T(8,128)(2,1)}, bf16[128,4096]{1,0:T(8,128)(2,1)}, u32[]{:S(2)}, u32[]{:S(2)}) collective-permute-start(bf16[128,4096]{1,0:T(8,128)(2,1)} %get-tuple-element.1280), channel_id=1, source_target_pairs={{0,8},{2,10},{8,16},{10,18},{16,24},{18,26},{24,28},{26,30},{28,20... | collective-permute-start | bytes 3145736 | tf_op jit(solution)/shard_map/ppermute | solution.py:100
  511.8 47.0 %collective-permute-start.22 = (bf16[128,4096]{1,0:T(8,128)(2,1)}, bf16[128,4096]{1,0:T(8,128)(2,1)}, u32[]{:S(2)}, u32[]{:S(2)}) collective-permute-start(bf16[128,4096]{1,0:T(8,128)(2,1)} %get-tuple-element.1279), channel_id=1, source_target_pairs={{8,0},{10,2},{16,8},{18,10},{24,16},{26,18},{28,24},{30,26},{20,28... | collective-permute-start | bytes 3145736 | tf_op jit(solution)/shard_map/ppermute | solution.py:103
  515.4 4.2 collective-permute-start
  523.7 25.4 %collective-permute-start.1 = (bf16[256,2048]{1,0:T(8,128)(2,1)}, bf16[256,2048]{1,0:T(8,128)(2,1)S(1)}, u32[]{:S(2)}, u32[]{:S(2)}) collective-permute-start(bf16[256,2048]{1,0:T(8,128)(2,1)} %slice.521), channel_id=1, source_target_pairs={{0,1},{1,0},{2,3},{3,2},{4,5},{5,4},{6,7},{7,6},{8,9},{9,8},{10,11... | collective-permute-start | bytes 3145736 | tf_op jit(solution)/shard_map/cond/branch_1_fun/ppermute | solution.py:110
  542.6 6.6 copy-start.20
  561.6 74.0 %collective-permute-start.25 = (bf16[256,4096]{1,0:T(8,128)(2,1)}, bf16[256,4096]{1,0:T(8,128)(2,1)}, u32[]{:S(2)}, u32[]{:S(2)}) collective-permute-start(bf16[256,4096]{1,0:T(8,128)(2,1)} %fusion.101), channel_id=1, source_target_pairs={{0,8},{2,10},{8,16},{10,18},{16,24},{18,26},{24,28},{26,30},{28,20... | collective-permute-start | bytes 6291464 | tf_op jit(solution)/shard_map/ppermute | solution.py:100
  565.2 70.4 %collective-permute-start.26 = (bf16[256,4096]{1,0:T(8,128)(2,1)}, bf16[256,4096]{1,0:T(8,128)(2,1)}, u32[]{:S(2)}, u32[]{:S(2)}) collective-permute-start(bf16[256,4096]{1,0:T(8,128)(2,1)} %fusion.102), channel_id=1, source_target_pairs={{8,0},{10,2},{16,8},{18,10},{24,16},{26,18},{28,24},{30,26},{20,28... | collective-permute-start | bytes 6291464 | tf_op jit(solution)/shard_map/ppermute | solution.py:103
  569.3 5.0 copy-start.63
  569.3 5.0 copy-start.68
  569.3 5.0 copy-start.71
  569.3 5.0 copy-start.74
  569.3 66.3 %collective-permute-start.23 = (bf16[256,2048]{1,0:T(8,128)(2,1)}, bf16[256,2048]{1,0:T(8,128)(2,1)}, u32[]{:S(2)}, u32[]{:S(2)}) collective-permute-start(bf16[256,2048]{1,0:T(8,128)(2,1)} %add_convert_fusion.9), channel_id=1, source_target_pairs={{0,8},{2,10},{8,16},{10,18},{16,24},{18,26},{24,28},{26,30},{28,20... | collective-permute-start | bytes 3145736 | tf_op jit(solution)/shard_map/ppermute | solution.py:100
  573.2 62.4 %collective-permute-start.24 = (bf16[256,2048]{1,0:T(8,128)(2,1)}, bf16[256,2048]{1,0:T(8,128)(2,1)}, u32[]{:S(2)}, u32[]{:S(2)}) collective-permute-start(bf16[256,2048]{1,0:T(8,128)(2,1)} %add_convert_fusion.8), channel_id=1, source_target_pairs={{8,0},{10,2},{16,8},{18,10},{24,16},{26,18},{28,24},{30,26},{20,28... | collective-permute-start | bytes 3145736 | tf_op jit(solution)/shard_map/ppermute | solution.py:103
  574.4 23.7 %collective-permute-start.7 = (bf16[256,2048]{1,0:T(8,128)(2,1)}, bf16[256,2048]{1,0:T(8,128)(2,1)}, u32[]{:S(2)}, u32[]{:S(2)}) collective-permute-start(bf16[256,2048]{1,0:T(8,128)(2,1)} %get-tuple-element.292), channel_id=1, source_target_pairs={{0,1},{1,0},{2,3},{3,2},{4,5},{5,4},{6,7},{7,6},{8,9},{9,8},{10,11... | collective-permute-start | bytes 3145736 | tf_op jit(solution)/shard_map/cond/branch_1_fun/ppermute | solution.py:110
  588.3 12.1 %copy-start.77 = (bf16[2048,1024]{1,0:T(8,128)(2,1)S(1)}, bf16[2048,1024]{1,0:T(8,128)(2,1)}, u32[]{:S(2)}) copy-start(bf16[2048,1024]{1,0:T(8,128)(2,1)} %get-tuple-element.307) | copy-start | bytes 12582916 | tf_op jit(solution)/shard_map/cond
  607.7 6.7 copy-start.39
  607.7 12.7 %slice-start = ((s8[10485760]{0:T(1024)(128)(4,1)}), s8[4194304]{0:T(1024)(128)(4,1)S(1)}, s32[]{:S(2)}) async-start(s8[10485760]{0:T(1024)(128)(4,1)} %bitcast.298), calls=%async_computation | async-start | bytes 8388608 | tf_op jit(solution)/shard_map/cond
  607.7 12.7 %slice-start.1 = ((s8[10485760]{0:T(1024)(128)(4,1)}), s8[4194304]{0:T(1024)(128)(4,1)S(1)}, s32[]{:S(2)}) async-start(s8[10485760]{0:T(1024)(128)(4,1)} %bitcast.298), calls=%async_computation.1 | async-start | bytes 8388608 | tf_op jit(solution)/shard_map/cond
  614.4 6.0 slice-start.2
  625.4 4.5 copy-start.36
  640.0 6.4 copy-start.32
  640.0 6.4 copy-start.64
  640.0 6.4 copy-start.67
  640.0 65.0 %collective-permute-start.27 = (bf16[256,4096]{1,0:T(8,128)(2,1)}, bf16[256,4096]{1,0:T(8,128)(2,1)}, u32[]{:S(2)}, u32[]{:S(2)}) collective-permute-start(bf16[256,4096]{1,0:T(8,128)(2,1)} %add_convert_fusion.5), channel_id=1, source_target_pairs={{0,8},{2,10},{8,16},{10,18},{16,24},{18,26},{24,28},{26,30},{28,20... | collective-permute-start | bytes 6291464 | tf_op jit(solution)/shard_map/ppermute | solution.py:100
  645.2 59.7 %collective-permute-start.28 = (bf16[256,4096]{1,0:T(8,128)(2,1)}, bf16[256,4096]{1,0:T(8,128)(2,1)}, u32[]{:S(2)}, u32[]{:S(2)}) collective-permute-start(bf16[256,4096]{1,0:T(8,128)(2,1)} %add_convert_fusion.4), channel_id=1, source_target_pairs={{8,0},{10,2},{16,8},{18,10},{24,16},{26,18},{28,24},{30,26},{20,28... | collective-permute-start | bytes 6291464 | tf_op jit(solution)/shard_map/ppermute | solution.py:103
  649.1 47.4 %collective-permute-start.2 = (bf16[512,2,256]{2,0,1:T(8,128)(2,1)}, bf16[512,2,256]{2,0,1:T(8,128)(2,1)}, u32[]{:S(2)}, u32[]{:S(2)}) collective-permute-start(bf16[512,2,256]{2,0,1:T(8,128)(2,1)} %slice.386), channel_id=1, source_target_pairs={{2,0},{4,2},{6,4},{8,6},{10,8},{12,10},{14,12},{16,14},{18,16},{20... | collective-permute-start | bytes 1572872 | tf_op jit(solution)/shard_map/cond/branch_1_fun/ppermute | solution.py:1422
  651.1 44.4 %collective-permute-start.3 = (bf16[256,2,256]{2,0,1:T(8,128)(2,1)}, bf16[256,2,256]{2,0,1:T(8,128)(2,1)}, u32[]{:S(2)}, u32[]{:S(2)}) collective-permute-start(bf16[256,2,256]{2,0,1:T(8,128)(2,1)} %slice.387), channel_id=1, source_target_pairs={{0,2},{2,4},{4,6},{6,8},{8,10},{10,12},{12,14},{14,16},{16,18},{18... | collective-permute-start | bytes 786440 | tf_op jit(solution)/shard_map/cond/branch_1_fun/ppermute | solution.py:1423
  709.3 7.5 copy-start.24
  709.3 74.6 %collective-permute-start.29 = (bf16[256,4096]{1,0:T(8,128)(2,1)}, bf16[256,4096]{1,0:T(8,128)(2,1)}, u32[]{:S(2)}, u32[]{:S(2)}) collective-permute-start(bf16[256,4096]{1,0:T(8,128)(2,1)} %add_convert_fusion.3), channel_id=1, source_target_pairs={{0,8},{2,10},{8,16},{10,18},{16,24},{18,26},{24,28},{26,30},{28,20... | collective-permute-start | bytes 6291464 | tf_op jit(solution)/shard_map/ppermute | solution.py:100
  714.0 70.0 %collective-permute-start.30 = (bf16[256,4096]{1,0:T(8,128)(2,1)}, bf16[256,4096]{1,0:T(8,128)(2,1)}, u32[]{:S(2)}, u32[]{:S(2)}) collective-permute-start(bf16[256,4096]{1,0:T(8,128)(2,1)} %add_convert_fusion.2), channel_id=1, source_target_pairs={{8,0},{10,2},{16,8},{18,10},{24,16},{26,18},{28,24},{30,26},{20,28... | collective-permute-start | bytes 6291464 | tf_op jit(solution)/shard_map/ppermute | solution.py:103
  725.9 32.4 %collective-permute-start.8 = (bf16[256,2048]{1,0:T(8,128)(2,1)}, bf16[256,2048]{1,0:T(8,128)(2,1)}, u32[]{:S(2)}, u32[]{:S(2)}) collective-permute-start(bf16[256,2048]{1,0:T(8,128)(2,1)} %slice.522), channel_id=1, source_target_pairs={{0,1},{1,0},{2,3},{3,2},{4,5},{5,4},{6,7},{7,6},{8,9},{9,8},{10,11... | collective-permute-start | bytes 3145736 | tf_op jit(solution)/shard_map/cond/branch_1_fun/ppermute | solution.py:110
  744.9 6.8 copy-start.38
  854.1 6.9 collective-permute-start.31
  856.6 8.9 %copy-start.47 = (f32[128,4096]{1,0:T(8,128)S(1)}, f32[128,4096]{1,0:T(8,128)}, u32[]{:S(2)}) copy-start(f32[128,4096]{1,0:T(8,128)} %get-tuple-element.1430) | copy-start | bytes 6291460
  (52 other events, 126.4 us)

commit v4 on v3

--- a/solution.py
+++ b/solution.py
@@ -385,17 +385,27 @@
             out[:, across_] = out[:, across_] + term
 
 
-def block_kernel(count, spots, *refs):
-    xs, d = refs[:count], refs[count]
-    outs, turned = refs[count + 1 : 2 * count + 1], refs[2 * count + 1 :]
+def block_kernel(count, came, spots, *refs):
+    xs, d, refs = refs[:count], refs[count], refs[count + 1 :]
+    gots, refs = refs[:came], refs[came:]
+    outs, turned = refs[:count], refs[count:]
 
     @pl.when(pl.program_id(0) == 0)
     def _():
         for x, t in zip(xs, turned):
             t[...] = x[...].T
 
-    for t, out in zip(turned, outs):
-        out[...] = low(product(t[...], d[0]))
+    for i, (t, out) in enumerate(zip(turned, outs)):
+        term = product(t[...], d[0])
+        if came == 0:
+            out[...] = low(term)
+        elif gots[i].shape == out.shape:
+            out[...] = low(term + to_float(gots[i][...]))
+        else:
+            cut = gots[i].shape[0]
+            near, far = slice(i * cut, (i + 1) * cut), slice((1 - i) * cut, (2 - i) * cut)
+            out[near, :] = low(term[near] + to_float(gots[i][...]))
+            out[far, :] = low(term[far])
 
 
 def grid_call(kernel, spots, grid, operands, in_specs, shapes, out_specs, scratch, flops, name):
@@ -490,7 +500,7 @@
     )
 
 
-def block_grads(x, d, chips, size, tile=1024):
+def block_grads(x, d, chips, size, gots=(), tile=1024):
     (m, _), (groups, _, ff) = x.shape, d.shape
     count = len(chips)
     tile = min(tile, ff)
@@ -506,11 +516,13 @@
             for i in range(count)
         ]
     return grid_call(
-        functools.partial(block_kernel, count),
+        functools.partial(block_kernel, count, len(gots)),
         spots,
         (groups * tiles,),
-        (*xs, d),
-        x_specs + [pl.BlockSpec((1, m, tile), lambda f, s: (f // tiles, 0, f % tiles))],
+        (*xs, d, *gots),
+        x_specs
+        + [pl.BlockSpec((1, m, tile), lambda f, s: (f // tiles, 0, f % tiles))]
+        + [pl.BlockSpec((v.shape[0], tile), lambda f, s: (0, f)) for v in gots],
         [jax.ShapeDtypeStruct((size, groups * ff), BF16)] * count,
         [pl.BlockSpec((size, tile), lambda f, s: (0, f))] * count,
         [pltpu.VMEM((size, m), BF16)] * count,
@@ -1018,6 +1030,335 @@
     )(x_own, *gu_parts, dn_own)
 
 
+def backward_kernel(d_own, hidden, raw, dn_full, gu_full, rows_in, *refs):
+    (x_out, d_gu_out, held_up, held_down, wide_up, wide_down, result), refs = refs[:7], refs[7:]
+    x, dn, hid, d_gu, raw_v, gu_v, first, got, refs = *refs[:8], refs[8:]
+    pairs, core_sent, core_got, side_sent, side_got, refs = *refs[:5], refs[5:]
+    rows_v, wide_first, refs = *refs[:2], refs[2:]
+    x_send, x_recv, ring_send, ring_recv, core_sems, side_sems, wide_sems, loads, stores = refs
+    hops = Hops()
+    half, chips = hops.chips // 2, hops.chips
+    own = d_own.shape[0]
+    size, ff = held_up.shape
+    cut = size // 2
+    m = x.shape[0]
+    cols = min(512, ff)
+    greet([hops.above, hops.below, hops.partner, hops.across])
+    started, saved = [], []
+
+    def begin(copy, where=started):
+        copy.start()
+        where.append(copy)
+        return copy
+
+    def load(source, target, number):
+        copy = pltpu.make_async_copy(source, target, loads.at[number])
+        copy.start()
+        return copy
+
+    def part(r):
+        return pl.ds(r * own, own)
+
+    from_far = begin(remote(d_own, x.at[part(1)], x_send, x_recv, (0,), hops.across))
+    from_near = begin(remote(d_own, x.at[part(2)], x_send, x_recv, (1,), hops.partner))
+    load_x = load(d_own, x.at[part(0)], 0)
+    load_dn = load(dn_full, dn, 1)
+    rows_order = (0, 2, 1, 3)
+    raw_loads = {}
+
+    def load_raw(i):
+        r = rows_order[i]
+        raw_loads[r] = load(raw.at[:, part(r)], raw_v.at[i % 2], 3 + i)
+
+    def load_gu(j):
+        return load(gu_full.at[:, pl.ds(j * size, size)], gu_v.at[j % 2], 7 + j)
+
+    load_raw(0)
+    load_raw(1)
+    load_hid = load(hidden, hid, 2)
+    far_block = pl.ds(pl.multiple_of(hops.chip_at(half) * size, size), size)
+    load_rows = load(rows_in.at[:, far_block], rows_v, 7 + chips)
+
+    def hidden_part(i):
+        r = rows_order[i]
+        at = part(r)
+        raw_loads[r].wait()
+
+        @pl.loop(0, ff // cols)
+        def _(c):
+            across_ = pl.ds(pl.multiple_of(c * cols, cols), cols)
+            d_hidden = product(x[at, :], dn[:, across_])
+            gate = to_float(raw_v[i % 2, 0, :, across_])
+            up = to_float(raw_v[i % 2, 1, :, across_])
+            square = gate * gate
+            bend = jnp.tanh(GELU_SCALE * gate * (1.0 + GELU_CUBE * square))
+            plus = 0.5 * (1.0 + bend)
+            slope = plus + 0.5 * gate * (1.0 - bend * bend) * GELU_SCALE * (
+                1.0 + 3.0 * GELU_CUBE * square
+            )
+            d_gu[0, at, across_] = low(d_hidden * up * slope)
+            d_gu[1, at, across_] = low(d_hidden * gate * plus)
+
+        if i + 2 < 4:
+            load_raw(i + 2)
+
+    copies = {}
+
+    def ring_step(k):
+        for direction, ahead in ((0, hops.above), (1, hops.below)):
+            near, far = direction * cut, (1 - direction) * cut
+            offset = (half - k) * (1 if direction == 0 else -1)
+            at = pl.ds(pl.multiple_of(hops.chip_at(offset) * size, size), size)
+            term = product_l(x[:, at], hid[...])
+            if k == 0:
+                first[direction] = low(term[near : near + cut])
+                source = first.at[direction]
+                target = got.at[direction, 0, pl.ds(near, cut)]
+            else:
+                copies[(direction, k - 1)].wait_recv()
+                came = got.at[direction, k - 1]
+                if k == 1:
+                    came[near : near + cut, :] = low(
+                        term[near : near + cut] + to_float(came[near : near + cut, :])
+                    )
+                    came[far : far + cut, :] = low(term[far : far + cut])
+                else:
+                    came[...] = low(term + to_float(came[...]))
+                source = came
+                if k < half - 2:
+                    target = got.at[direction, k]
+                else:
+                    target = held_up if direction == 0 else held_down
+            copies[(direction, k)] = begin(
+                remote(source, target, ring_send, ring_recv, (direction, k), ahead)
+            )
+
+    core_copies, side_copies = [], []
+
+    def block_out(j, loading):
+        loading.wait()
+        out = product_t(d_gu[0], gu_v[j % 2, 0]) + product_t(d_gu[1], gu_v[j % 2, 1])
+        pairs[j] = out[: 2 * own]
+        core_sent[j] = low(out[2 * own :])
+        copy = remote(
+            core_sent.at[j], core_got.at[j], core_sems.at[0], core_sems.at[1], (j,), hops.partner
+        )
+        core_copies.append(begin(copy))
+
+    def core_sum(j):
+        core_copies[j].wait_recv()
+        both = pairs[j] + to_float(core_got[j])
+        side_sent[j] = low(both[own:])
+        copy = remote(
+            side_sent.at[j], side_got.at[j], side_sems.at[0], side_sems.at[1], (j,), hops.across
+        )
+        side_copies.append(begin(copy))
+        result[:, j * size : (j + 1) * size] = both[:own]
+
+    load_x.wait()
+    load_dn.wait()
+    hidden_part(0)
+    from_near.wait_recv()
+    hidden_part(1)
+    from_far.wait_recv()
+    passed = begin(remote(x.at[part(1)], x.at[part(3)], x_send, x_recv, (2,), hops.partner))
+    hidden_part(2)
+    passed.wait_recv()
+    load_hid.wait()
+    ring_step(0)
+    gu_loads = {0: load_gu(0), 1: load_gu(1)}
+    hidden_part(3)
+    load_rows.wait()
+    for group in range(2):
+        wide = product_l(rows_v[...], d_gu[group])
+        for direction in range(2):
+            wide_first[direction, :, group * ff : (group + 1) * ff] = low(
+                wide[direction * cut : (direction + 1) * cut]
+            )
+    wide_copies = [
+        begin(
+            remote(
+                wide_first.at[direction],
+                target,
+                wide_sems.at[0],
+                wide_sems.at[1],
+                (direction,),
+                ahead,
+            )
+        )
+        for direction, target, ahead in (
+            (0, wide_up, hops.above),
+            (1, wide_down, hops.below),
+        )
+    ]
+    begin(pltpu.make_async_copy(x, x_out, stores.at[0]), saved)
+    begin(pltpu.make_async_copy(d_gu, d_gu_out, stores.at[1]), saved)
+    steps = [half - 1 - (half - 1 - k) for k in range(1, half - 1)]
+    for j in range(chips):
+        block_out(j, gu_loads[j])
+        if j + 2 < chips:
+            gu_loads[j + 2] = load_gu(j + 2)
+        if j > 0:
+            core_sum(j - 1)
+        if j % 3 == 2 and steps:
+            ring_step(steps.pop(0))
+    core_sum(chips - 1)
+    for k in steps:
+        ring_step(k)
+    for j, copy in enumerate(side_copies):
+        copy.wait_recv()
+        at = slice(j * size, (j + 1) * size)
+        result[:, at] = result[:, at] + to_float(side_got[j])
+    for direction in range(2):
+        copies[(direction, half - 2)].wait_recv()
+        wide_copies[direction].wait_recv()
+    for copy in started:
+        copy.wait_send()
+    for copy in saved:
+        copy.wait()
+
+
+def backward(d_own, hidden, raw, dn_full, gu_full, rows_in):
+    chips = lax.axis_size("dp") // 2
+    half = chips // 2
+    own, width = d_own.shape
+    m, ff = hidden.shape
+    size = width // chips
+    dma = pltpu.SemaphoreType.DMA
+    vmem = pl.BlockSpec(memory_space=pltpu.VMEM)
+    return pl.pallas_call(
+        backward_kernel,
+        out_shape=[
+            jax.ShapeDtypeStruct((m, width), BF16),
+            jax.ShapeDtypeStruct((2, m, ff), BF16),
+            jax.ShapeDtypeStruct((size, ff), BF16),
+            jax.ShapeDtypeStruct((size, ff), BF16),
+            jax.ShapeDtypeStruct((size // 2, 2 * ff), BF16),
+            jax.ShapeDtypeStruct((size // 2, 2 * ff), BF16),
+            jax.ShapeDtypeStruct((own, width), F32),
+        ],
+        in_specs=[ANY] * 6,
+        out_specs=[ANY] * 6 + [vmem],
+        scratch_shapes=[
+            pltpu.VMEM((m, width), BF16),
+            pltpu.VMEM((width, ff), BF16),
+            pltpu.VMEM((m, ff), BF16),
+            pltpu.VMEM((2, m, ff), BF16),
+            pltpu.VMEM((2, 2, own, ff), BF16),
+            pltpu.VMEM((2, 2, size, ff), BF16),
+            pltpu.VMEM((2, size // 2, ff), BF16),
+            pltpu.VMEM((2, half - 2, size, ff), BF16),
+            pltpu.VMEM((chips, 2 * own, size), F32),
+            pltpu.VMEM((chips, 2 * own, size), BF16),
+            pltpu.VMEM((chips, 2 * own, size), BF16),
+            pltpu.VMEM((chips, own, size), BF16),
+            pltpu.VMEM((chips, own, size), BF16),
+            pltpu.VMEM((m, size), BF16),
+            pltpu.VMEM((2, size // 2, 2 * ff), BF16),
+            dma((3,)),
+            dma((3,)),
+            dma((2, half - 1)),
+            dma((2, half - 1)),
+            dma((2, chips)),
+            dma((2, chips)),
+            dma((2, 2)),
+            dma((8 + chips,)),
+            dma((2,)),
+        ],
+        compiler_params=pltpu.CompilerParams(
+            collective_id=4, has_side_effects=True, vmem_limit_bytes=60 * 2**20
+        ),
+        cost_estimate=pl.CostEstimate(
+            flops=6 * m * width * ff, bytes_accessed=0, transcendentals=0
+        ),
+        name="backward",
+    )(d_own, hidden, raw, dn_full, gu_full, rows_in)
+
+
+def prepare_back_kernel(q_cols, kv_cols, spots, raw, d_q, d_kv, after, before, cos, sin, gains, *refs):
+    out, gain_grads = refs
+    tall = raw.shape[0]
+    turn = HD // 2
+    cosines, sines = cos[...], sin[...]
+
+    @pl.when(pl.program_id(0) == 0)
+    def _():
+        gain_grads[...] = jnp.zeros_like(gain_grads)
+
+    early = spots[1 + pl.program_id(0)] < spots[0]
+    more = to_float(after[...]) + jnp.where(early, to_float(before[...]), 0.0)
+
+    def back(values, d, gain):
+        scale = lax.rsqrt(jnp.mean(values * values, axis=-1, keepdims=True) + EPS)
+        d_gain = d if gain is None else d * gain
+        inner = jnp.mean(values * d_gain, axis=-1, keepdims=True)
+        return scale * d_gain - values * (scale * scale * scale * inner), values * scale * d
+
+    def unturn(d):
+        front, rear = d[:, :turn], d[:, turn:]
+        return jnp.concatenate(
+            [front * cosines + rear * sines, rear * cosines - front * sines], axis=1
+        )
+
+    for start in range(0, q_cols + 2 * kv_cols, HD):
+        at = slice(start, start + HD)
+        values = raw[:, at]
+        if start < q_cols:
+            d, which = unturn(d_q[:, at]), 0
+        else:
+            here = slice(start - q_cols, start - q_cols + HD)
+            d = d_kv[:, here] + more[:, here]
+            which = 1
+            if start < q_cols + kv_cols:
+                d = unturn(d)
+        if start < q_cols + kv_cols:
+            d_values, for_gain = back(values, d, gains[which : which + 1, :])
+            gain_grads[which : which + 1, :] = gain_grads[which : which + 1, :] + jnp.sum(
+                for_gain, axis=0, keepdims=True
+            )
+        else:
+            d_values, _ = back(values, d, None)
+        out[:, at] = low(d_values)
+
+
+def prepare_back(raw, d_q, d_kv, after, before, cos, sin, gains, side, own, tile=128):
+    tall, cols = raw.shape
+    kv_cols = d_kv.shape[1] // 2
+    q_cols = cols - 2 * kv_cols
+    tiles = tall // tile
+    near = before.shape[0] // tile
+    natural = lax.rem(jnp.arange(tiles) + side * (own // tile), tiles)
+    spots = jnp.concatenate([jnp.full((1,), near), natural]).astype(jnp.int32)
+
+    def straight(width):
+        return pl.BlockSpec((tile, width), lambda t, s: (t, 0))
+
+    def ordered(width):
+        return pl.BlockSpec((tile, width), lambda t, s: (s[1 + t], 0))
+
+    return grid_call(
+        functools.partial(prepare_back_kernel, q_cols, kv_cols),
+        spots,
+        (tiles,),
+        (raw, d_q, d_kv, after, before, cos, sin, gains),
+        [
+            straight(cols),
+            straight(q_cols),
+            ordered(2 * kv_cols),
+            ordered(2 * kv_cols),
+            pl.BlockSpec((tile, 2 * kv_cols), lambda t, s: (jnp.minimum(s[1 + t], near - 1), 0)),
+            straight(HD // 2),
+            straight(HD // 2),
+            once(gains.shape),
+        ],
+        [jax.ShapeDtypeStruct((tall, cols), BF16), jax.ShapeDtypeStruct((8, HD), F32)],
+        [straight(cols), once((8, HD))],
+        [],
+        10 * raw.size,
+        "prepare_back",
+    )
+
+
 class Gather:
     def __init__(self, ring, block):
         self.ring = ring
@@ -1050,33 +1391,37 @@
         self.step_count = 0
         self.held = []
 
-    def terms(self, ahead=0):
+    def offsets(self):
         half = self.ring.chips // 2
-        k = self.step_count + 1 + ahead
-        if k == 1:
-            offsets = (half,)
-        elif k > half:
-            offsets = (0,)
-        else:
-            offsets = (half + 1 - k, k - 1 - half)
-        return block_grads(self.x, self.d, [self.ring.chip_at(o) for o in offsets], self.size)
-
-    def step(self, terms):
+        k = self.step_count + 1
+        return (half,) if k == 1 else (half + 1 - k, k - 1 - half)
+
+    def blocks(self, offsets, gots=()):
+        chips = [self.ring.chip_at(o) for o in offsets]
+        return block_grads(self.x, self.d, chips, self.size, gots)
+
+    def terms(self):
+        return self.blocks(self.offsets())
+
+    def last_term(self):
+        return self.blocks((0,))[0]
+
+    def step(self, terms=None, *beside):
         ring, half = self.ring, self.ring.chips // 2
         self.step_count += 1
         k = self.step_count
         cut = self.size // 2
         if k == 1:
-            up, down = terms[0][:cut], terms[0][cut:]
+            (term,) = self.blocks((half,))
+            up, down = term[:cut], term[cut:]
+        elif terms is None:
+            up, down = self.blocks((half + 1 - k, k - 1 - half), self.held)
         else:
-            up, down = terms
-            if k == 2:
-                up = up.at[:cut].set(low(to_float(up[:cut]) + to_float(self.held[0])))
-                down = down.at[cut:].set(low(to_float(down[cut:]) + to_float(self.held[1])))
-            else:
-                up = low(to_float(up) + to_float(self.held[0]))
-                down = low(to_float(down) + to_float(self.held[1]))
+            up = low(to_float(terms[0]) + to_float(self.held[0]))
+            down = low(to_float(terms[1]) + to_float(self.held[1]))
+        up, down, beside = tie(up, down, beside)
         self.held = [ring.up(up), ring.down(down)]
+        return beside
 
 
 def region(body):
@@ -1312,7 +1657,8 @@
 
     attn_out, left_low, right_out, mixed, ffw_low = region(lambda: join(heads_low))
     ffw_low = meet([gu], ffw_low)
-    if (2 * rows) % 256 == 0:
+    fused = (2 * rows) % 256 == 0
+    if fused:
         parts = [part for _, _, part in gu.parts]
         ffw_rows, gu_weights, _, dn_whole, raw, hidden_low, ffw_out = forward(
             ffw_low, parts, ff_own[1], 2
@@ -1359,43 +1705,38 @@
     d_pre_low = low(d_pre)
     d_mid = grad_out + product_t(d_pre_low, lgate_full)
     d_ffw_out, d_ffw_out_scale = ffw_out_back(d_mid)
-    d_ffw_rows = four_ways(low(d_ffw_out))
-    d_ffw_rows, d_mid = tie(d_ffw_rows, d_mid)
-
-    rd = BlockReduce(ring, d_ffw_rows, hidden_low[None], 2 * rows)
-    rd.step(rd.terms())
-    d_gate_up, down_terms = region(
-        lambda: (hidden_back(d_ffw_rows, raw, dn_spots, dn_parts), rd.terms())
-    )
-    d_gate_up, down_terms = meet([rd], d_gate_up, down_terms)
-    rd.step(down_terms)
-    rg = BlockReduce(ring, ffw_rows, d_gate_up, 2 * rows)
-    for _ in range(half - 4):
-        rd.step(meet([rd], region(rd.terms)))
-
-    def back_2():
-        partial = product_t(d_gate_up[0], gu_weights[0]) + product_t(d_gate_up[1], gu_weights[1])
-        return partial, rd.terms(), rg.terms()
-
-    partial, down_terms, terms = meet([rd], *region(back_2))
-    rd.step(down_terms)
-    rg.step(terms)
-
-    def back_3():
-        d_ffw_normed, terms = sum_four(partial, lambda: (rd.terms(), rg.terms()))
+    if fused:
+        d_ffw_rows, d_gate_up, *held, d_ffw_normed = backward(
+            low(d_ffw_out), hidden_low, raw, dn_whole, gu_weights, ffw_rows
+        )
+        rd = BlockReduce(ring, d_ffw_rows, hidden_low[None], 2 * rows)
+        rd.held, rd.step_count = held[:2], half - 1
+        rg = BlockReduce(ring, ffw_rows, d_gate_up, 2 * rows)
+        rg.held, rg.step_count = held[2:], 1
+    else:
+        d_ffw_rows = four_ways(low(d_ffw_out))
+        rd = BlockReduce(ring, d_ffw_rows, hidden_low[None], 2 * rows)
+        for _ in range(half - 1):
+            rd.step()
+            meet([rd])
+        d_gate_up = hidden_back(d_ffw_rows, raw, dn_spots, dn_parts)
+        d_ffw_normed = sum_four(
+            product_t(d_gate_up[0], gu_weights[0]) + product_t(d_gate_up[1], gu_weights[1])
+        )
+        rg = BlockReduce(ring, ffw_rows, d_gate_up, 2 * rows)
+        for _ in range(half - 3):
+            rg.step()
+            meet([rg])
+    rd.step()
+    rg.step()
+
+    def back_34():
         _, back = jax.vjp(norm_gain, mixed, ffw_in_scale)
         d_mixed_extra, d_ffw_in_scale = back(d_ffw_normed)
         d_branch = (d_mid + d_mixed_extra) * ROOT_HALF
         _, back = jax.vjp(norm_gain, attn_out, attn_scale)
         d_attn, d_attn_scale = back(d_branch)
-        return terms, d_ffw_in_scale, d_attn_scale, d_branch, low(d_attn)
-
-    terms, d_ffw_in_scale, d_attn_scale, d_branch, d_attn_low = meet([rd, rg], *region(back_3))
-    rd.step(terms[0])
-    rg.step(terms[1])
-
-    def back_4():
-        d_attn_rows, terms = both_sides(d_attn_low, rg.terms)
+        d_attn_rows, terms = both_sides(low(d_attn), rg.terms)
         d_heads = low(product(d_attn_rows, output_t)).reshape(piece_len, kv_local, group, HD)
         keys_all, values_all = kv_all[:, :kv_local], kv_all[:, kv_local:]
         probs = jnp.exp(scores_for(query_low, keys_all) - log_totals)
@@ -1408,35 +1749,44 @@
         d_scores = low(probs * (d_probs - deltas))
         d_keys_all = jnp.einsum("kgqc,qkgd->ckd", d_scores, query_low, preferred_element_type=F32)
         d_query_rot = jnp.einsum("kgqc,ckd->qkgd", d_scores, keys_all, preferred_element_type=F32)
-        d_kv_all = jnp.concatenate([d_keys_all, d_values_all], axis=1)
-        return terms, d_attn_rows, d_kv_all, d_query_rot
-
-    terms, d_attn_rows, d_kv_all, d_query_rot = meet([rd, rg], *region(back_4))
-    rg.step(terms)
-    for _ in range(half - 4):
-        rg.step(meet([rg], region(rg.terms)))
-
-    def back_5():
+        kv_shape = (kv_all.shape[0], kv_cols)
+        d_kv_all = jnp.concatenate(
+            [d_keys_all.reshape(kv_shape), d_values_all.reshape(kv_shape)], axis=1
+        )
         to_before = low(d_kv_all[:piece_len])
         to_after = low(d_kv_all[2 * piece_len :])
-        from_after = to_float(lax.ppermute(to_before, "dp", backward_pairs))
-        from_before = to_float(lax.ppermute(to_after, "dp", forward_pairs))
-        from_after, from_before, terms = tie(from_after, from_before, rg.terms())
-        d_kv = d_kv_all[piece_len : 2 * piece_len] + from_after
-        d_kv = d_kv + jnp.pad(from_before, ((0, piece_len - reach_after), (0, 0), (0, 0)))
-        d_kv = in_order(d_kv)
-        _, back = jax.vjp(prepare, qkv_raw, query_scale, key_scale)
-        d_qkv, query_scale_grad, key_scale_grad = back(
-            (
-                d_query_rot.reshape(piece_len, heads_local, HD),
-                d_kv[:, :kv_local],
-                d_kv[:, kv_local:],
-            )
-        )
-        return terms, low(d_qkv), query_scale_grad, key_scale_grad
-
-    terms, d_qkv_low, query_scale_grad, key_scale_grad = meet([rg], *region(back_5))
-    rg.step(terms)
+        d_kv_own = d_kv_all[piece_len : 2 * piece_len]
+        moving = (to_before, to_after)
+        kept = (d_ffw_in_scale, d_attn_scale, d_branch, d_attn_rows, d_kv_own)
+        return terms, moving, kept, d_query_rot.reshape(piece_len, q_cols)
+
+    terms, moving, kept, d_query_rot = meet([rd, rg], *region(back_34))
+    d_ffw_in_scale, d_attn_scale, d_branch, d_attn_rows, d_kv_own = kept
+    from_after = lax.ppermute(moving[0], "dp", backward_pairs)
+    from_before = lax.ppermute(moving[1], "dp", forward_pairs)
+    from_after, from_before = rg.step(terms, from_after, from_before)
+
+    def back_5():
+        both_gains = jnp.stack([query_scale, key_scale])
+        d_qkv_low, gain_sums = prepare_back(
+            qkv_raw,
+            d_query_rot,
+            d_kv_own,
+            from_after,
+            from_before,
+            cosines,
+            sines,
+            jnp.pad(both_gains, ((0, 6), (0, 0))),
+            side,
+            own,
+        )
+        d_more, ends = sum_sides(
+            product_t(d_qkv_low, qkv_full), lambda: (rd.last_term(), rg.last_term())
+        )
+        return d_more, ends, d_qkv_low, gain_sums[0], gain_sums[1]
+
+    d_more, ends, d_qkv_low, query_scale_grad, key_scale_grad = meet([rg], *region(back_5))
+    rg.step()
 
     def head_gain_back(grads):
         padded = jnp.pad(grads.reshape(ring.devices, head_part), ((0, 0), (0, rows - head_part)))
@@ -1449,9 +1799,6 @@
         d_right_low = low(d_right)
         d_left_low = low(product(d_right_low, right_t))
         d_normed = d_branch + product_t(d_left_low, left_full)
-        d_more, ends = sum_sides(
-            product_t(d_qkv_low, qkv_full), lambda: (rd.terms(), rg.terms())
-        )
         d_normed = d_normed + d_more
         d_inputs_extra, d_input_scale = input_norm_back(d_normed)
         grad_tokens = d_branch + d_inputs_extra
@@ -1477,14 +1824,15 @@
             (low(normed), d_left_low),
             (d_right_low, left_low),
         ]
-        return grad_tokens, ends, row_grads(pairs, gain_grads, core, chips, rows)
-
-    grad_tokens, (down_end, gate_up_end), (mine, theirs) = meet([rg], *region(back_6))
+        return grad_tokens, row_grads(pairs, gain_grads, core, chips, rows)
+
+    grad_tokens, (mine, theirs) = meet([rg], *region(back_6))
+    down_end, gate_up_end = ends
     total, small_half, out_gate, out_up, out_down_t = last_reduce(
         mine,
         theirs,
         2 * q_cols + 2 * kv_cols,
-        [gate_up_end[0], *rg.held, down_end[0], *rd.held],
+        [gate_up_end, *rg.held, down_end, *rd.held],
     )
     out_output = total[:, :q_cols].T
     out_qkv = total[:, q_cols:]

time: 880 us -> 825 us (0.938)
  Pallas kernels: 408 us -> 489 us
  other arithmetic: 157 us -> 102 us
  matrix products: 96.8 us -> 71.6 us
  local copies, waits for them, and re-layouts: 108 us -> 85.4 us
  waiting for transfers between devices: 59.1 us -> 40.2 us
  starting transfers between devices: 39.3 us -> 26.2 us
    pallas_call x0 -> x1, Pallas kernels: none -> 118 us  [backward(): pl.pallas_call(backward_kernel, out_shape=[jax.ShapeDtypeStruct((m, width...]
    pallas_call x12 -> x8, Pallas kernels: 105 us -> 69.8 us  [grid_call(): pl.pallas_call(kernel, grid_spec=pltpu.PrefetchScalarGridSpec(num_scalar_...]
    dot_general x8 -> x6, matrix products: 43.4 us -> 18.2 us  [product_t(): lax.dot_general(left_in, right_in, (((1,), (1,)), ((), ())), preferred_el...]
    convert_element_type x16 -> x9, other arithmetic: 47.2 us -> 26.9 us  [low(): return values.astype(BF16)]
    ppermute x6 -> x4, waiting for transfers between devices: 45.2 us -> 31.8 us  [across(): return lax.ppermute(values, 'tensor', [(0, 1), (1, 0)])]
    scatter x4 -> x0, other arithmetic: 9.46 us -> none  [the longest x2 4.73 us: step(): up = up.at[:cut].set(low(to_float(up[:cut]) + to_float(self.held[0])))]
    reduce_sum x7 -> x4, other arithmetic: 18.8 us -> 13.1 us  [norm_gain(): values * lax.rsqrt(jnp.mean(values * values, axis=-1, keepdims=True) + EPS)]
    reduce_sum x10 -> x9, other arithmetic: 23.5 us -> 20.5 us  [norm_gain(): jnp.mean(values * values, axis=-1, keepdims=True) + EPS]
  transfers between devices with their start and end apart: 32 -> 20, of which waited for: 9 -> 8; matrix products, arithmetic and copies ran while one was open for 34% -> 26% of each run, Pallas kernels for 11% -> 6%
where the time goes in v4:
time: 825 us; the launch traced here: 816 us
  Pallas kernels  489 us (59%)
  other arithmetic  102 us (12%)
  local copies, waits for them, and re-layouts  85.4 us (10%)
  matrix products  71.6 us (9%)
  waiting for transfers between devices  40.2 us (5%)
  starting transfers between devices  26.2 us (3%)
    pallas_call x1, Pallas kernels, forward(): pl.pallas_call(functools.partial(forward_kernel, hops_done, tile), out_sh...  165 us
    pallas_call x1, Pallas kernels, backward(): pl.pallas_call(backward_kernel, out_shape=[jax.ShapeDtypeStruct((m, width...  118 us
    pallas_call x1, Pallas kernels, comm_call(): pl.pallas_call(kernel, out_shape=shapes, in_specs=[ANY] * len(operands),...  71 us
    pallas_call x8, Pallas kernels, grid_call(): pl.pallas_call(kernel, grid_spec=pltpu.PrefetchScalarGridSpec(num_scalar_...  69.8 us
    pallas_call x1, Pallas kernels, last_reduce(): pl.pallas_call(functools.partial(last_kernel, large), out_shape=[jax.Shap...  65.6 us
    ppermute x4, waiting for transfers between devices, across(): return lax.ppermute(values, 'tensor', [(0, 1), (1, 0)])  31.8 us
    convert_element_type x9, other arithmetic, low(): return values.astype(BF16)  26.9 us
    unnamed x88, local copies, waits for them, and re-layouts  23.5 us
  transfers between devices with their start and end apart: 20, of which 8 were waited for; matrix products, arithmetic and copies ran while one was open for 26% of the time, Pallas kernels for 6%

profile of v4, /device:TPU:0, one launch (start us, length us, event | category | flops | bytes accessed | tf_op | source)
XLA Modules:
  0.0 815.9 jit_solution(11682633192919965740)
XLA Ops:
  15.4 71.0 %first_gather.1 = (bf16[2048,1536]{1,0:T(8,128)(2,1)}, bf16[2048,1024]{1,0:T(8,128)(2,1)}, bf16[2048,768]{1,0:T(8,128)(2,1)S(1)}, bf16[256,4096]{1,0:T(8,128)(2,...) custom-call(bf16[128,1536]{1,0:T(8,128)(2,1)S(1)} %pad_maximum_fusion.6.refs_0_, ...), custom_call_target="tpu_custom_call" | custom-call | bytes 142606336 | tf_op jit(solution)/shard_map/first_gather/pallas_call | solution.py:264
  97.9 5.2 fusion.111
  103.7 54.0 %conditional.5 = (bf16[512,2048]{1,0:T(8,128)(2,1)}, f32[512,1536]{1,0:T(8,128)}, bf16[512,1,4,256]{3,0,2,1:T(8,128)(2,1)}, bf16[1280,2,256]{2,0,1:T(8,128)(2,1)...) conditional(s32[]{:T(128)} %convert_element_type.169, () %tuple.57, (bf16[256,2048]{1,0:T(8,128)(2,1)}, ...), branch_computations={%region_2.3_spmd, %region_3.11_spmd} | conditional | flops 5961549312 | bytes 123166088 | solution.py:1430
  107.7 2.2 fusion.7
  111.5 6.7 fusion.113
  122.7 2.1 maximum_select_fusion
  124.8 2.6 collective-permute-start
  131.0 3.2 slice.228
  134.2 3.2 reshape.590
  137.4 2.9 multiply_reduce_fusion
  145.4 2.5 pad_maximum_fusion.1
  147.9 2.9 fusion
  152.6 5.1 fusion.12
  157.7 4.2 collective-permute-start.7
  163.9 40.2 %conditional.6 = (f32[256,2048]{1,0:T(8,128)}, bf16[256,64]{0,1:T(8,128)(2,1)S(1)}, f32[256,2048]{1,0:T(8,128)}, f32[256,2048]{1,0:T(8,128)}, bf16[256,2048]{1,0:T(8,128)(2,1)}) conditional(s32[]{:T(128)} %convert_element_type.169, () %tuple.56, (bf16[512,1024]{0,1:T(8,128)(2,1)}, bf16[2048,1024]{1,0:T(8,128)(2,1)}, ...), branch_computations={%region_11.12_spmd, %region_12.17_spmd} | conditional | flops 2296923392 | bytes 64939256 | solution.py:1430
  163.9 5.3 fusion.112
  182.4 12.4 %collective-permute-done.2 = bf16[256,2048]{1,0:T(8,128)(2,1)} collective-permute-done((bf16[256,2048]{1,0:T(8,128)(2,1)}, bf16[256,2048]{1,0:T(8,128)(2,1)}, u32[]{:S(2)}, u32[]{:S(2)}) %collective-permute-start.2) | collective-permute-done | bytes 1048608 | tf_op jit(solution)/shard_map/cond/branch_1_fun/ppermute | solution.py:110
  194.8 3.5 multiply_reduce_fusion.5
  198.3 4.6 multiply_reduce_fusion.3
  204.1 3.1 collective-permute-done.7.refs_3_
  208.7 164.6 %forward.1 = (bf16[1024,2048]{1,0:T(8,128)(2,1)}, bf16[2,2048,2048]{2,1,0:T(8,128)(2,1)}, bf16[2048,4096]{1,0:T(8,128)(2,1)}, bf16[2048,2048]{1,0:T(8,128)(2,1)}...) custom-call(bf16[256,2048]{1,0:T(8,128)(2,1)} %get-tuple-element.371.x_own, ...), custom_call_target="tpu_custom_call" | custom-call | flops 25769803776 | tf_op jit(solution)/shard_map/forward/pallas_call | solution.py:990
  380.4 4.8 add_convert_fusion.3
  388.8 117.8 %backward.1 = (bf16[1024,2048]{1,0:T(8,128)(2,1)}, bf16[2,1024,2048]{2,1,0:T(8,128)(2,1)}, bf16[256,2048]{1,0:T(8,128)(2,1)}, bf16[256,2048]{1,0:T(8,128)(2,1)},...) custom-call(bf16[256,2048]{1,0:T(8,128)(2,1)} %fusion.81.d_own, ...), custom_call_target="tpu_custom_call" | custom-call | flops 25769803776 | tf_op jit(solution)/shard_map/backward/pallas_call | solution.py:1229
  506.6 10.0 %block_grads.10 = (bf16[256,4096]{1,0:T(8,128)(2,1)}, bf16[256,4096]{1,0:T(8,128)(2,1)}) custom-call(s32[2]{0:T(128)} %pad_add_fusion.4.spots, bf16[1024,2048]{1,0:T(8,128)(2,1)} %get-tuple-element.374.rows_in.refs_0_.refs_1_, bf16[1024,2048]{1,0:T(8,128)(2,1)} %get-tuple-element.374.rows_in.refs_0_.refs_1_, ...), custom_call_target="tpu_custom_call" | custom-call | tf_op jit(solution)/shard_map/block_grads/pallas_call | solution.py:415
  519.2 6.9 block_grads.9
  528.1 75.4 %conditional.7 = (bf16[256,4096]{1,0:T(8,128)(2,1)}, bf16[256,4096]{1,0:T(8,128)(2,1)}, bf16[512,512]{0,1:T(8,128)(2,1)}, bf16[256,512]{0,1:T(8,128)(2,1)S(1)}, ...) conditional(s32[]{:T(128)} %convert_element_type.169, () %tuple.62, ...), branch_computations={%region_21.22_spmd, %region_22.30_spmd} | conditional | flops 8914598912 | bytes 227350160 | solution.py:1430
  530.5 3.0 multiply_reduce_fusion.7
  533.9 4.6 multiply_reduce_fusion.6
  538.6 3.0 fusion.52
  542.2 9.6 %block_grads.6 = (bf16[256,4096]{1,0:T(8,128)(2,1)}, bf16[256,4096]{1,0:T(8,128)(2,1)}) custom-call(s32[2]{0:T(128)} %pad_add_fusion.spots, bf16[1024,2048]{1,0:T(8,128)(2,1)} %get-tuple-element.182.refs_0_.refs_1_, bf16[1024,2048]{1,0:T(8,128)(2,1)} %get-tuple-element.182.refs_0_.refs_1_, bf16[2,1024,2048]{2,1,0:T(8,128)(2,1)} %get-tuple-element.183.refs_2_), custom_call_target="tpu_custom_call" | custom-call | tf_op jit(solution)/shard_map/cond/branch_1_fun/block_grads/pallas_call | solution.py:415
  552.3 7.0 fusion.55
  559.3 4.4 collective-permute-done.3
  563.7 3.3 pad_maximum_fusion.5
  567.0 5.0 convolution_convert_fusion.1
  571.9 2.3 copy.288
  574.2 7.0 fusion.47
  581.2 6.0 fusion.36
  587.2 4.8 fusion.43
  592.0 4.3 convolution_bitcast_fusion
  599.5 4.0 fusion.59
  607.7 3.0 collective-permute-start.14
  610.8 4.3 add_convert_fusion.2
  615.1 4.4 add_convert_fusion.1
  621.6 49.9 %conditional.8 = (f32[256,2048]{1,0:T(8,128)}, bf16[256,2048]{1,0:T(8,128)(2,1)}, bf16[256,4096]{1,0:T(8,128)(2,1)}, bf16[512,1536]{1,0:T(8,128)(2,1)}, f32[256]{0:T(256)S(1)}, /*index=5*/f32[256]{0:T(256)S(1)}) conditional(s32[]{:T(128)} %convert_element_type.169, () %tuple.66, (s32[]{:T(128)}, f32[16,16]{1,0:T(8,128)S(1)}, ...), branch_computations={%region_30.31_spmd, %region_31.32_spmd} | conditional | flops 3230146560 | bytes 72649064 | solution.py:1430
  621.6 2.9 copy.263.d_q
  624.5 2.5 copy.264.d_kv
  628.4 5.9 prepare_back.1
  634.3 6.0 fusion.114
  640.3 2.1 copy-done.29
  643.7 4.3 block_grads.7
  648.0 6.8 block_grads.8
  655.6 12.6 %collective-permute-done.4 = bf16[256,2048]{1,0:T(8,128)(2,1)S(1)} collective-permute-done((bf16[256,2048]{1,0:T(8,128)(2,1)}, bf16[256,2048]{1,0:T(8,128)(2,1)S(1)}, u32[]{:S(2)}, u32[]{:S(2)}) %collective-permute-start.4) | collective-permute-done | bytes 1048608 | tf_op jit(solution)/shard_map/cond/branch_1_fun/ppermute | solution.py:110
  668.2 3.3 slice_add_fusion.1
  671.5 10.5 %block_grads.11 = (bf16[256,4096]{1,0:T(8,128)(2,1)}, bf16[256,4096]{1,0:T(8,128)(2,1)}) custom-call(s32[2]{0:T(128)} %pad_add_fusion.3.spots, bf16[1024,2048]{1,0:T(8,128)(2,1)} %get-tuple-element.374.rows_in.refs_0_.refs_1_, bf16[1024,2048]{1,0:T(8,128)(2,1)} %get-tuple-element.374.rows_in.refs_0_.refs_1_, ...), custom_call_target="tpu_custom_call" | custom-call | tf_op jit(solution)/shard_map/block_grads/pallas_call | solution.py:415
  685.9 41.7 %conditional.9 = (f32[256,2048]{1,0:T(8,128)}, f32[1024,3328]{1,0:T(8,128)}, bf16[1024,3328]{1,0:T(8,128)(2,1)}) conditional(s32[]{:T(128)} %convert_element_type.169, () %tuple.69, (f32[2048,1]{1,0:T(8,128)}, f32[256,2048]{1,0:T(8,128)S(1)}, f32[256,2048]{1,0:T(8,128)}, bf16[2048,64]{1,0:T(8,128)(2,1)}, bf16[2048,64]{1,0:T(8,128)(2,1)}, ...), branch_computations={%region_34.35_spmd, %region_35.42_spmd.clone} | conditional | flops 6194473984 | bytes 91760792 | solution.py:1430
  689.3 2.1 multiply_reduce_fusion.14
  691.4 3.3 fusion.74
  698.1 3.7 fusion.73
  703.7 2.4 copy.267.refs_6_
  706.9 3.4 multiply_reduce_fusion.12
  712.0 15.7 %row_grads.1 = (f32[1024,3328]{1,0:T(8,128)}, bf16[1024,3328]{1,0:T(8,128)(2,1)}) custom-call(s32[1]{0:T(128)} %bitcast.84.spots, bf16[512,2048]{1,0:T(8,128)(2,1)} %get-tuple-element.472.refs_0_, bf16[512,2048]{1,0:T(8,128)(2,1)} %get-tuple-element.473.refs_1_, bf16[256,2048]{1,0:T(8,128)(2,1)S(1)} %copy-done.37, bf16[256,2048]{1,0:T(8,128)(2,1)S(1)} %copy-done.39, ...), custom_call_target="tpu_custom_call" | custom-call | flops 6039797760 | bytes 32833536 | tf_op jit(solution)/shard_map/cond/branch_1_fun/row_grads/pallas_call | solution.py:415
  731.4 65.6 %last_reduce.1 = (f32[128,2560]{1,0:T(8,128)}, f32[128,384]{1,0:T(8,128)}, f32[128,4096]{1,0:T(8,128)}, f32[128,4096]{1,0:T(8,128)}, f32[128,4096]{1,0:T(8,128)}) custom-call(f32[1024,3328]{1,0:T(8,128)} %get-tuple-element.442.refs_0_, bf16[1024,3328]{1,0:T(8,128)(2,1)} %get-tuple-element.443.refs_1_, bf16[256,4096]{1,0:T(8,128)(2,1)} %get-tuple-element.444.refs_2_, ...), custom_call_target="tpu_custom_call" | custom-call | bytes 272629760 | tf_op jit(solution)/shard_map/last_reduce/pallas_call | solution.py:770
  797.1 2.2 slice_bitcast_fusion.4
  804.9 2.4 collective-permute-done.19
  (292 shorter events, 129.4 us)
Async XLA Ops:
  0.7 12.8 %copy-start.2 = (bf16[128,4096]{1,0:T(8,128)(2,1)S(1)}, bf16[128,4096]{1,0:T(8,128)(2,1)}, u32[]{:S(2)}) copy-start(bf16[128,4096]{1,0:T(8,128)(2,1)} %refs_3_.1) | copy-start | bytes 3145732
  0.7 12.8 %copy-start.3 = (bf16[128,4096]{1,0:T(8,128)(2,1)S(1)}, bf16[128,4096]{1,0:T(8,128)(2,1)}, u32[]{:S(2)}) copy-start(bf16[128,4096]{1,0:T(8,128)(2,1)} %refs_4_.1) | copy-start | bytes 3145732
  89.0 68.7 %collective-permute-start.5 = (bf16[256,4096]{1,0:T(8,128)(2,1)}, bf16[256,4096]{1,0:T(8,128)(2,1)}, u32[]{:S(2)}, u32[]{:S(2)}) collective-permute-start(bf16[256,4096]{1,0:T(8,128)(2,1)} %get-tuple-element.360.refs_0_), channel_id=1, source_target_pairs={{0,8},{2,10},{8,16},{10,18},{16,24},{18,26},{24,28},{26,30},{28,20... | collective-permute-start | bytes 6291464 | tf_op jit(solution)/shard_map/ppermute | solution.py:100
  90.6 67.1 %collective-permute-start.6 = (bf16[256,4096]{1,0:T(8,128)(2,1)}, bf16[256,4096]{1,0:T(8,128)(2,1)}, u32[]{:S(2)}, u32[]{:S(2)}) collective-permute-start(bf16[256,4096]{1,0:T(8,128)(2,1)} %get-tuple-element.360.refs_0_), channel_id=1, source_target_pairs={{8,0},{10,2},{16,8},{18,10},{24,16},{26,18},{28,24},{30,26},{20,28... | collective-permute-start | bytes 6291464 | tf_op jit(solution)/shard_map/ppermute | solution.py:103
  94.3 2.4 copy-start.54
  96.7 6.4 copy-start.23
  103.1 59.6 %copy-start.1 = (bf16[2048,768]{1,0:T(8,128)(2,1)S(1)}, bf16[2048,768]{1,0:T(8,128)(2,1)}, u32[]{:S(2)}) copy-start(bf16[2048,768]{1,0:T(8,128)(2,1)} %copy-done) | copy-start | bytes 9437188
  107.7 3.8 copy-start.60
  118.2 2.9 copy-start.26
  124.8 20.6 %collective-permute-start = (bf16[512,2,256]{2,0,1:T(8,128)(2,1)}, bf16[512,2,256]{2,0,1:T(8,128)(2,1)}, u32[]{:S(2)}, u32[]{:S(2)}) collective-permute-start(bf16[512,2,256]{2,0,1:T(8,128)(2,1)} %maximum_select_fusion), channel_id=1, source_target_pairs={{0,2},{2,4},{4,6},{6,8},{8,10},{10,12},{12,14},{14,16},{16,18},{18... | collective-permute-start | bytes 1572872 | tf_op jit(solution)/shard_map/cond/branch_1_fun/ppermute | solution.py:1626
  129.1 5.0 copy-start.49
  129.1 16.3 %collective-permute-start.1 = (bf16[256,2,256]{2,0,1:T(8,128)(2,1)}, bf16[256,2,256]{2,0,1:T(8,128)(2,1)}, u32[]{:S(2)}, u32[]{:S(2)}) collective-permute-start(bf16[256,2,256]{2,0,1:T(8,128)(2,1)} %slice.237), channel_id=1, source_target_pairs={{2,0},{4,2},{6,4},{8,6},{10,8},{12,10},{14,12},{16,14},{18,16},{20... | collective-permute-start | bytes 786440 | tf_op jit(solution)/shard_map/cond/branch_1_fun/ppermute | solution.py:1627
  137.4 4.0 copy-start.53
  137.4 4.0 copy-start.56
  137.4 4.0 copy-start.59
  157.7 49.5 %collective-permute-start.7 = (bf16[256,4096]{1,0:T(8,128)(2,1)}, bf16[256,4096]{1,0:T(8,128)(2,1)}, u32[]{:S(2)}, u32[]{:S(2)}) collective-permute-start(bf16[256,4096]{1,0:T(8,128)(2,1)} %collective-permute-done.5.refs_1_), channel_id=1, source_target_pairs={{0,8},{2,10},{8,16},{10,18},{16,24},{18,26},{24,28},{26,30},{28,20... | collective-permute-start | bytes 6291464 | tf_op jit(solution)/shard_map/ppermute | solution.py:100
  161.9 46.8 %collective-permute-start.8 = (bf16[256,4096]{1,0:T(8,128)(2,1)}, bf16[256,4096]{1,0:T(8,128)(2,1)}, u32[]{:S(2)}, u32[]{:S(2)}) collective-permute-start(bf16[256,4096]{1,0:T(8,128)(2,1)} %collective-permute-done.6.refs_2_), channel_id=1, source_target_pairs={{8,0},{10,2},{16,8},{18,10},{24,16},{26,18},{28,24},{30,26},{20,28... | collective-permute-start | bytes 6291464 | tf_op jit(solution)/shard_map/ppermute | solution.py:103
  163.9 8.1 copy-start.10
  169.2 3.2 copy-start.30
  170.5 24.3 %collective-permute-start.2 = (bf16[256,2048]{1,0:T(8,128)(2,1)}, bf16[256,2048]{1,0:T(8,128)(2,1)}, u32[]{:S(2)}, u32[]{:S(2)}) collective-permute-start(bf16[256,2048]{1,0:T(8,128)(2,1)} %slice.334), channel_id=1, source_target_pairs={{0,1},{1,0},{2,3},{3,2},{4,5},{5,4},{6,7},{7,6},{8,9},{9,8},{10,11... | collective-permute-start | bytes 3145736 | tf_op jit(solution)/shard_map/cond/branch_1_fun/ppermute | solution.py:110
  180.6 17.7 %copy-start.40 = (bf16[256,64]{0,1:T(8,128)(2,1)}, bf16[256,64]{0,1:T(8,128)(2,1)S(1)}, u32[]{:S(2)}) copy-start(bf16[256,64]{0,1:T(8,128)(2,1)S(1)} %convolution_convert_fusion) | copy-start | bytes 98308 | tf_op jit(solution)/shard_map/cond
  182.4 15.9 %copy-start.11 = (bf16[256,2048]{1,0:T(8,128)(2,1)S(1)}, bf16[256,2048]{1,0:T(8,128)(2,1)}, u32[]{:S(2)}) copy-start(bf16[256,2048]{1,0:T(8,128)(2,1)} %copy-done.10) | copy-start | bytes 3145732 | tf_op jit(solution)/shard_map/cond
  204.1 169.2 %copy-start.42 = (bf16[256,64]{0,1:T(8,128)(2,1)}, bf16[256,64]{0,1:T(8,128)(2,1)S(1)}, u32[]{:S(2)}) copy-start(bf16[256,64]{0,1:T(8,128)(2,1)S(1)} %get-tuple-element.516) | copy-start | bytes 98308
  377.6 2.8 copy-start.36
  377.6 2.8 copy-start.15
  516.5 87.0 %collective-permute-start.11 = (bf16[256,4096]{1,0:T(8,128)(2,1)}, bf16[256,4096]{1,0:T(8,128)(2,1)}, u32[]{:S(2)}, u32[]{:S(2)}) collective-permute-start(bf16[256,4096]{1,0:T(8,128)(2,1)} %get-tuple-element.387), channel_id=1, source_target_pairs={{0,8},{2,10},{8,16},{10,18},{16,24},{18,26},{24,28},{26,30},{28,20... | collective-permute-start | bytes 6291464 | tf_op jit(solution)/shard_map/ppermute | solution.py:100
  516.5 87.0 %collective-permute-start.12 = (bf16[256,4096]{1,0:T(8,128)(2,1)}, bf16[256,4096]{1,0:T(8,128)(2,1)}, u32[]{:S(2)}, u32[]{:S(2)}) collective-permute-start(bf16[256,4096]{1,0:T(8,128)(2,1)} %get-tuple-element.388), channel_id=1, source_target_pairs={{8,0},{10,2},{16,8},{18,10},{24,16},{26,18},{28,24},{30,26},{20,28... | collective-permute-start | bytes 6291464 | tf_op jit(solution)/shard_map/ppermute | solution.py:103
  519.1 9.0 %copy-start.18 = (f32[2048,1]{1,0:T(8,128)S(1)}, f32[2048,1]{1,0:T(8,128)}, u32[]{:S(2)}) copy-start(f32[2048,1]{1,0:T(8,128)} %get-tuple-element.1099) | copy-start | bytes 24580
  519.2 9.0 %copy-start.52 = (s32[1280]{0:T(1024)S(1)}, s32[1280]{0:T(1024)}, u32[]{:S(2)}) copy-start(s32[1280]{0:T(1024)} %pad_add_fusion.2) | copy-start | bytes 15364
  519.2 9.0 %copy-start.55 = (s32[512]{0:T(512)S(1)}, s32[512]{0:T(512)}, u32[]{:S(2)}) copy-start(s32[512]{0:T(512)} %copy-done.54) | copy-start | bytes 6148
  519.2 9.0 %copy-start.58 = (s32[512]{0:T(512)S(1)}, s32[512]{0:T(512)}, u32[]{:S(2)}) copy-start(s32[512]{0:T(512)} %add_select_fusion) | copy-start | bytes 6148
  526.1 77.4 %collective-permute-start.9 = (bf16[256,2048]{1,0:T(8,128)(2,1)}, bf16[256,2048]{1,0:T(8,128)(2,1)}, u32[]{:S(2)}, u32[]{:S(2)}) collective-permute-start(bf16[256,2048]{1,0:T(8,128)(2,1)} %get-tuple-element.383), channel_id=1, source_target_pairs={{0,8},{2,10},{8,16},{10,18},{16,24},{18,26},{24,28},{26,30},{28,20... | collective-permute-start | bytes 3145736 | tf_op jit(solution)/shard_map/ppermute | solution.py:100
  526.1 77.4 %collective-permute-start.10 = (bf16[256,2048]{1,0:T(8,128)(2,1)}, bf16[256,2048]{1,0:T(8,128)(2,1)}, u32[]{:S(2)}, u32[]{:S(2)}) collective-permute-start(bf16[256,2048]{1,0:T(8,128)(2,1)} %get-tuple-element.384), channel_id=1, source_target_pairs={{8,0},{10,2},{16,8},{18,10},{24,16},{26,18},{28,24},{30,26},{20,28... | collective-permute-start | bytes 3145736 | tf_op jit(solution)/shard_map/ppermute | solution.py:103
  530.5 3.0 copy-start.19
  541.6 22.1 %collective-permute-start.3 = (bf16[256,2048]{1,0:T(8,128)(2,1)}, bf16[256,2048]{1,0:T(8,128)(2,1)}, u32[]{:S(2)}, u32[]{:S(2)}) collective-permute-start(bf16[256,2048]{1,0:T(8,128)(2,1)} %fusion.52), channel_id=1, source_target_pairs={{0,1},{1,0},{2,3},{3,2},{4,5},{5,4},{6,7},{7,6},{8,9},{9,8},{10,11... | collective-permute-start | bytes 3145736 | tf_op jit(solution)/shard_map/cond/branch_1_fun/ppermute | solution.py:110
  563.7 3.3 copy-start.61
  574.2 7.0 copy-start.28
  574.2 13.0 %slice-start = ((s8[10485760]{0:T(1024)(128)(4,1)}), s8[4194304]{0:T(1024)(128)(4,1)S(1)}, s32[]{:S(2)}) async-start(s8[10485760]{0:T(1024)(128)(4,1)} %bitcast.240), calls=%async_computation | async-start | bytes 8388608 | tf_op jit(solution)/shard_map/cond
  574.2 13.0 %slice-start.1 = ((s8[10485760]{0:T(1024)(128)(4,1)}), s8[4194304]{0:T(1024)(128)(4,1)S(1)}, s32[]{:S(2)}) async-start(s8[10485760]{0:T(1024)(128)(4,1)} %bitcast.240), calls=%async_computation.1 | async-start | bytes 8388608 | tf_op jit(solution)/shard_map/cond
  581.2 6.0 slice-start.2
  596.4 3.1 copy-start.21
  605.6 14.0 %collective-permute-start.13 = (bf16[512,512]{1,0:T(8,128)(2,1)}, bf16[512,512]{1,0:T(8,128)(2,1)S(1)}, u32[]{:S(2)}, u32[]{:S(2)}) collective-permute-start(bf16[512,512]{1,0:T(8,128)(2,1)} %copy.261), channel_id=1, source_target_pairs={{2,0},{4,2},{6,4},{8,6},{10,8},{12,10},{14,12},{16,14},{18,16},{20... | collective-permute-start | bytes 1572872 | tf_op jit(solution)/shard_map/ppermute | solution.py:1765
  607.7 11.8 %collective-permute-start.14 = (bf16[256,512]{1,0:T(8,128)(2,1)}, bf16[256,512]{1,0:T(8,128)(2,1)S(1)}, u32[]{:S(2)}, u32[]{:S(2)}) collective-permute-start(bf16[256,512]{1,0:T(8,128)(2,1)} %copy.262), channel_id=1, source_target_pairs={{0,2},{2,4},{4,6},{6,8},{8,10},{10,12},{12,14},{14,16},{16,18},{18... | collective-permute-start | bytes 786440 | tf_op jit(solution)/shard_map/ppermute | solution.py:1766
  615.1 6.5 copy-start.24
  615.1 6.5 copy-start.25
  615.1 6.5 copy-start.48
  615.1 6.5 copy-start.51
  619.5 52.0 %collective-permute-start.15 = (bf16[256,4096]{1,0:T(8,128)(2,1)}, bf16[256,4096]{1,0:T(8,128)(2,1)}, u32[]{:S(2)}, u32[]{:S(2)}) collective-permute-start(bf16[256,4096]{1,0:T(8,128)(2,1)} %add_convert_fusion.2), channel_id=1, source_target_pairs={{0,8},{2,10},{8,16},{10,18},{16,24},{18,26},{24,28},{26,30},{28,20... | collective-permute-start | bytes 6291464 | tf_op jit(solution)/shard_map/ppermute | solution.py:100
  619.8 51.7 %collective-permute-start.16 = (bf16[256,4096]{1,0:T(8,128)(2,1)}, bf16[256,4096]{1,0:T(8,128)(2,1)}, u32[]{:S(2)}, u32[]{:S(2)}) collective-permute-start(bf16[256,4096]{1,0:T(8,128)(2,1)} %add_convert_fusion.1), channel_id=1, source_target_pairs={{8,0},{10,2},{16,8},{18,10},{24,16},{26,18},{28,24},{30,26},{20,28... | collective-permute-start | bytes 6291464 | tf_op jit(solution)/shard_map/ppermute | solution.py:103
  643.5 24.7 %collective-permute-start.4 = (bf16[256,2048]{1,0:T(8,128)(2,1)}, bf16[256,2048]{1,0:T(8,128)(2,1)S(1)}, u32[]{:S(2)}, u32[]{:S(2)}) collective-permute-start(bf16[256,2048]{1,0:T(8,128)(2,1)} %slice.335), channel_id=1, source_target_pairs={{0,1},{1,0},{2,3},{3,2},{4,5},{5,4},{6,7},{7,6},{8,9},{9,8},{10,11... | collective-permute-start | bytes 3145736 | tf_op jit(solution)/shard_map/cond/branch_1_fun/ppermute | solution.py:110
  643.7 4.3 copy-start.7
  671.5 12.9 %copy-start.17 = (bf16[256,2048]{1,0:T(8,128)(2,1)S(1)}, bf16[256,2048]{1,0:T(8,128)(2,1)}, u32[]{:S(2)}) copy-start(bf16[256,2048]{1,0:T(8,128)(2,1)} %param.57) | copy-start | bytes 3145732
  682.0 3.9 copy-start.9
  682.0 3.9 copy-start.43
  682.0 3.9 copy-start.47
  682.0 47.3 %collective-permute-start.17 = (bf16[256,4096]{1,0:T(8,128)(2,1)}, bf16[256,4096]{1,0:T(8,128)(2,1)}, u32[]{:S(2)}, u32[]{:S(2)}) collective-permute-start(bf16[256,4096]{1,0:T(8,128)(2,1)} %get-tuple-element.425), channel_id=1, source_target_pairs={{0,8},{2,10},{8,16},{10,18},{16,24},{18,26},{24,28},{26,30},{28,20... | collective-permute-start | bytes 6291464 | tf_op jit(solution)/shard_map/ppermute | solution.py:100
  683.7 47.7 %collective-permute-start.18 = (bf16[256,4096]{1,0:T(8,128)(2,1)}, bf16[256,4096]{1,0:T(8,128)(2,1)}, u32[]{:S(2)}, u32[]{:S(2)}) collective-permute-start(bf16[256,4096]{1,0:T(8,128)(2,1)} %get-tuple-element.426), channel_id=1, source_target_pairs={{8,0},{10,2},{16,8},{18,10},{24,16},{26,18},{28,24},{30,26},{20,28... | collective-permute-start | bytes 6291464 | tf_op jit(solution)/shard_map/ppermute | solution.py:103
  698.0 3.8 copy-start.44
  703.7 3.2 copy-start.13
  797.0 3.3 copy-start.45
  797.1 4.2 copy-start.34
  800.3 7.0 collective-permute-start.19
  803.1 8.7 %copy-start.33 = (f32[128,4096]{1,0:T(8,128)S(1)}, f32[128,4096]{1,0:T(8,128)}, u32[]{:S(2)}) copy-start(f32[128,4096]{1,0:T(8,128)} %get-tuple-element.1220) | copy-start | bytes 6291460
  811.8 2.3 copy-start.32
  (23 other events, 36.3 us)

commit v5 on v4

--- a/solution.py
+++ b/solution.py
@@ -153,24 +153,68 @@
         return jnp.where(place < self.chips // 2, 2 * place, 2 * (self.chips - 1 - place) + 1)
 
 
-def first_kernel(count, ff_cols, *refs):
-    blocks, refs = refs[:count], refs[count:]
+def staged_apart(source_shape, turned, start):
+    cols = source_shape[0] if turned else source_shape[1]
+    return turned or start % 128 != 0 or cols % 128 != 0, cols
+
+
+def first_kernel(layout, down_turned, ff_cols, *refs):
+    count = len(layout)
+    sources, refs = refs[: sum(len(l) for l in layout)], refs[sum(len(l) for l in layout) :]
     (gate, up, down, tokens), refs = refs[:4], refs[4:]
     wholes, refs = refs[:count], refs[count:]
-    (gate_up_own, down_own, other_tokens), refs = refs[:3], refs[3:]
-    stages, refs = refs[: 3 + count], refs[3 + count :]
+    (gate_own, up_down_own, other_tokens), refs = refs[:3], refs[3:]
+    stages, refs = refs[:count], refs[count:]
+    (gate_v, up_v, tokens_v, down_v, down_t), refs = refs[:5], refs[5:]
+    apart, refs = list(refs[:-8]), refs[-8:]
     in_sems, out_sems, ring_send, ring_recv, pair_send, pair_recv, ff_send, ff_recv = refs
     hops = Hops()
     half = hops.chips // 2
-    rows = blocks[0].shape[0]
+    mine = pl.ds(pl.multiple_of(hops.core * ff_cols, 128), ff_cols)
+    theirs = pl.ds(pl.multiple_of((1 - hops.core) * ff_cols, 128), ff_cols)
+
+    number = 0
+
+    def load(source, target):
+        nonlocal number
+        copy = pltpu.make_async_copy(source, target, in_sems.at[number])
+        copy.start()
+        number += 1
+        return copy
+
+    taken = list(sources)
+    fills = []
+    for which, flags in enumerate(layout):
+        start, steps = 0, []
+        for turned in flags:
+            source = taken.pop(0)
+            own_buffer, cols = staged_apart(source.shape, turned, start)
+            if own_buffer:
+                buffer = apart.pop(0)
+                steps.append((load(source, buffer), buffer, turned, start, cols))
+            else:
+                target = stages[which].at[:, pl.ds(start, cols)]
+                steps.append((load(source, target), None, turned, start, cols))
+            start += cols
+        fills.append(steps)
+    load_down = load(down, down_v)
+    bounces = [(load(gate.at[:, mine], gate_v), gate_v), (load(up.at[:, mine], up_v), up_v)]
+    load_tokens = load(tokens, tokens_v)
     greet([hops.above, hops.below, hops.partner, hops.across])
-    started = []
-
-    def place(ref, offset, top, size):
-        return block_rows(ref, (2 * hops.chip_at(offset) + hops.core) * rows + top, size)
+    started, stores = [], []
+
+    def place(which, offset, top, size):
+        tall = stages[which].shape[0]
+        at = (2 * hops.chip_at(offset) + hops.core) * tall + top
+        return wholes[which].at[pl.ds(pl.multiple_of(at, 8 if tall <= 16 else 16), size)]
+
+    def store(source, target):
+        copy = pltpu.make_async_copy(source, target, out_sems.at[len(stores)])
+        copy.start()
+        stores.append(copy)
 
     def to_partner(number, which, offset, top, size, source=None):
-        spot = place(wholes[which], offset, top, size)
+        spot = place(which, offset, top, size)
         copy = remote(
             spot if source is None else source,
             spot,
@@ -184,7 +228,7 @@
         pairs.append(copy)
 
     def onward(direction, k, which, offset, top, size, source=None):
-        spot = place(wholes[which], offset, top, size)
+        spot = place(which, offset, top, size)
         copy = remote(
             spot if source is None else source,
             spot,
@@ -197,55 +241,61 @@
         started.append(copy)
         arrivals[(direction, k, which)] = copy
 
-    pairs, arrivals, locals_ = [], {}, []
-    for which in range(count):
+    pairs, arrivals = [], {}
+    for which, steps in enumerate(fills):
+        stage = stages[which]
+        for copy, buffer, turned, start, cols in steps:
+            copy.wait()
+            if buffer is not None:
+                stage[:, start : start + cols] = buffer[...].T if turned else buffer[...]
+        tall = stage.shape[0]
         for direction in range(2):
-            onward(direction, 0, which, 0, 0, rows, blocks[which])
+            onward(direction, 0, which, 0, 0, tall, stage)
+    own = tokens.shape[0]
+    theirs_at = other_tokens.at[pl.ds(own, own)]
+    ff_copies = [remote(tokens, theirs_at, ff_send, ff_recv, (3,), hops.across)]
+    ff_copies[0].start()
+    rows = gate.shape[0]
     own_rows = pl.ds(pl.multiple_of(hops.core * rows, 16), rows)
-    mine = pl.ds(pl.multiple_of(hops.core * ff_cols, 128), ff_cols)
-    theirs = pl.ds(pl.multiple_of((1 - hops.core) * ff_cols, 128), ff_cols)
     targets = [
-        gate_up_own.at[own_rows, pl.ds(0, ff_cols)],
-        gate_up_own.at[own_rows, pl.ds(ff_cols, ff_cols)],
-        down_own.at[own_rows],
+        gate_own.at[own_rows],
+        up_down_own.at[own_rows, pl.ds(0, ff_cols)],
+        up_down_own.at[own_rows, pl.ds(ff_cols, ff_cols)],
     ]
-    ff_copies = [remote(tokens, other_tokens, ff_send, ff_recv, (3,), hops.across)]
-    ff_copies[0].start()
-    for number, (weight, target) in enumerate(zip((gate, up, down), targets)):
+    load_down.wait()
+    if down_turned:
+        down_t[...] = down_v[...].T
+        down = down_t
+    else:
+        down = down_v
+    for number_, (weight, target) in enumerate(zip((gate, up, down), targets)):
         copy = remote(
-            weight.at[:, theirs], target, ff_send, ff_recv, (number,), hops.partner
+            weight.at[:, theirs], target, ff_send, ff_recv, (number_,), hops.partner
         )
         copy.start()
         ff_copies.append(copy)
-        locals_.append((weight.at[:, mine], target, number))
-    for which in range(count):
-        to_partner(0, which, 0, 0, rows, blocks[which])
-        locals_.append((blocks[which], place(wholes[which], 0, 0, rows), 3 + which))
-    loads = [
-        pltpu.make_async_copy(source, stages[number], in_sems.at[number])
-        for source, _, number in locals_
-    ]
-    for copy in loads:
-        copy.start()
-    stores = [
-        pltpu.make_async_copy(stages[number], target, out_sems.at[number])
-        for _, target, number in locals_
-    ]
-    for load, store in zip(loads, stores):
-        load.wait()
-        store.start()
-    cut = rows // 2
+    for which, stage in enumerate(stages):
+        to_partner(0, which, 0, 0, stage.shape[0], stage)
+        store(stage, place(which, 0, 0, stage.shape[0]))
+    for (copy, buffer), target in zip(bounces, targets):
+        copy.wait()
+        store(buffer, target)
+    store(down.at[:, mine], targets[2])
+    load_tokens.wait()
+    store(tokens_v, other_tokens.at[pl.ds(0, own)])
     for k in range(1, half + 1):
         for which in range(count):
+            tall = stages[which].shape[0]
+            cut = tall // 2
             for direction in range(2):
                 arrivals[(direction, k - 1, which)].wait_recv()
                 offset = -k if direction == 0 else k
                 if k < half - 1:
-                    onward(direction, k, which, offset, 0, rows)
+                    onward(direction, k, which, offset, 0, tall)
                 elif k == half - 1:
                     onward(direction, k, which, offset, direction * cut, cut)
                 if k < half:
-                    to_partner(2 * k - 1 + direction, which, offset, 0, rows)
+                    to_partner(2 * k - 1 + direction, which, offset, 0, tall)
                 else:
                     to_partner(2 * k - 1 + direction, which, half, direction * cut, cut)
     for copy in ff_copies + pairs:
@@ -268,7 +318,7 @@
         out_specs=[ANY] * len(shapes),
         scratch_shapes=stages + [pltpu.SemaphoreType.DMA(shape) for shape in semaphores],
         compiler_params=pltpu.CompilerParams(
-            collective_id=number, has_side_effects=True, vmem_limit_bytes=16 * 2**20
+            collective_id=number, has_side_effects=True, vmem_limit_bytes=60 * 2**20
         ),
         cost_estimate=pl.CostEstimate(flops=0, bytes_accessed=8 * moved, transcendentals=0),
         name=name,
@@ -278,22 +328,40 @@
 def first_gather(blocks, gate, up, down, tokens):
     chips = lax.axis_size("dp") // 2
     half = chips // 2
-    rows = blocks[0].shape[0]
+    down, down_turned = down
+    rows = gate.shape[0]
     ff_cols = gate.shape[1] // 2
     count = len(blocks)
+    stages, apart = [], []
+    for block in blocks:
+        start = 0
+        for source, turned in block:
+            own_buffer, cols = staged_apart(source.shape, turned, start)
+            if own_buffer:
+                apart.append(pltpu.VMEM(source.shape, source.dtype))
+            start += cols
+        first, turned = block[0]
+        tall = first.shape[1] if turned else first.shape[0]
+        stages.append(pltpu.VMEM((tall, start), first.dtype))
     shapes = [
-        jax.ShapeDtypeStruct((2 * chips * rows, block.shape[1]), block.dtype) for block in blocks
+        jax.ShapeDtypeStruct((2 * chips * stage.shape[0], stage.shape[1]), stage.dtype)
+        for stage in stages
     ] + [
+        jax.ShapeDtypeStruct((2 * rows, ff_cols), gate.dtype),
         jax.ShapeDtypeStruct((2 * rows, 2 * ff_cols), gate.dtype),
-        jax.ShapeDtypeStruct((2 * rows, ff_cols), gate.dtype),
-        jax.ShapeDtypeStruct(tokens.shape, tokens.dtype),
+        jax.ShapeDtypeStruct((2 * tokens.shape[0], tokens.shape[1]), tokens.dtype),
     ]
-    stages = [pltpu.VMEM((rows, ff_cols), gate.dtype)] * 3 + [
-        pltpu.VMEM(block.shape, block.dtype) for block in blocks
+    more = [
+        pltpu.VMEM((rows, ff_cols), gate.dtype),
+        pltpu.VMEM((rows, ff_cols), gate.dtype),
+        pltpu.VMEM(tokens.shape, tokens.dtype),
+        pltpu.VMEM(down.shape, down.dtype),
+        pltpu.VMEM((rows, 2 * ff_cols), down.dtype),
     ]
+    sources = [source for block in blocks for source, _ in block]
     semaphores = [
-        (3 + count,),
-        (3 + count,),
+        (len(sources) + 4,),
+        (4 + count,),
         (2, half, count),
         (2, half, count),
         (2 * half + 1, count),
@@ -301,12 +369,13 @@
         (4,),
         (4,),
     ]
+    layout = tuple(tuple(turned for _, turned in block) for block in blocks)
     out = comm_call(
-        functools.partial(first_kernel, count, ff_cols),
+        functools.partial(first_kernel, layout, down_turned, ff_cols),
         0,
-        (*blocks, gate, up, down, tokens),
+        (*sources, gate, up, down, tokens),
         shapes,
-        stages,
+        stages + more + apart,
         semaphores,
         "first_gather",
     )
@@ -436,17 +505,15 @@
     )
 
 
-def gate_up(x, spots, parts, tile=512):
-    count, (m, width), ff = len(parts), x.shape, parts[0].shape[1] // 2
+def gate_up(x, spots, parts, up_parts, tile=512):
+    count, (m, width), ff = len(parts), x.shape, parts[0].shape[1]
     tiles = ff // tile
-    part_specs = [pl.BlockSpec((p.shape[0], tile), lambda n, s: (0, n)) for p in parts] + [
-        pl.BlockSpec((p.shape[0], tile), lambda n, s: (0, n + tiles)) for p in parts
-    ]
+    part_specs = [pl.BlockSpec((p.shape[0], tile), lambda n, s: (0, n)) for p in parts] * 2
     return grid_call(
         functools.partial(gate_up_kernel, count),
         spots,
         (tiles,),
-        (x, *parts, *parts),
+        (x, *parts, *up_parts),
         [once((m, width))] + part_specs,
         [
             jax.ShapeDtypeStruct((2, m, ff), BF16),
@@ -596,7 +663,7 @@
     side = lax.axis_index("tensor")
     half = hops.chips // 2
     rows = main.shape[0]
-    part = little.shape[1]
+    part = little.shape[1] // 2
     ff_cols = ff_sent.shape[2]
     cut = rows // 2
     greet([hops.above, hops.below, hops.partner, hops.across])
@@ -730,17 +797,23 @@
     sides[half].wait_recv()
     step(2, 0)
     for k in range(1, half):
+        if k > 1:
+            sides[half - k].wait_recv()
+            sides[k - half].wait_recv()
+            step(2, k)
         step(0, k)
         step(1, k)
         if k == 1:
             end_feed_forward()
         for i in range(2 * k + 1, min(2 * k + 3, len(order))):
             ready(i)
-        sides[half - k].wait_recv()
-        sides[k - half].wait_recv()
-        step(2, k)
+        if k == 1:
+            sides[half - k].wait_recv()
+            sides[k - half].wait_recv()
+            step(2, k)
     sides[0].wait_recv()
-    for which, (start, cols) in enumerate(pieces):
+    for which in (2, 0, 1):
+        start, cols = pieces[which]
         for direction in range(2):
             copies[(which, direction, half - 1)].wait_recv()
         total = (
@@ -751,8 +824,19 @@
         if which < 2:
             main[:, start : start + cols] = total
         else:
-            little[...] = total
-    for copy in ff_copies:
+            here = pl.ds(pl.multiple_of(side * part, 128), part)
+            little[:, here] = total
+            little_copy = remote(
+                little.at[:, here],
+                little.at[:, here],
+                side_send,
+                side_recv,
+                (len(order),),
+                hops.across,
+            )
+            little_copy.start()
+            started.append(little_copy)
+    for copy in ff_copies + [little_copy]:
         copy.wait_recv()
     for copy in ff_copies + started:
         copy.wait_send()
@@ -771,7 +855,7 @@
         functools.partial(last_kernel, large),
         out_shape=[
             jax.ShapeDtypeStruct((rows, large), F32),
-            jax.ShapeDtypeStruct((rows, part), F32),
+            jax.ShapeDtypeStruct((rows, 2 * part), F32),
         ]
         + [jax.ShapeDtypeStruct((rows, 2 * ff), F32)] * 3,
         in_specs=[ANY] * 8,
@@ -790,8 +874,8 @@
             dma((2 * half + 6,)),
             dma((2 * half,)),
             dma((2 * half,)),
-            dma((2 * half,)),
-            dma((2 * half,)),
+            dma((2 * half + 1,)),
+            dma((2 * half + 1,)),
             dma((2, half, 3)),
             dma((2, half, 3)),
             dma((3,)),
@@ -808,15 +892,18 @@
 
 
 def forward_kernel(hops_done, tile, x_own, *refs):
-    count = 2 * hops_done + 1
-    gu_parts, (dn_own,), refs = refs[:count], refs[count : count + 1], refs[count + 1 :]
+    counts = [2 * done + 1 for done in hops_done]
+    gate_parts, up_down_parts, refs = refs[: counts[0]], refs[counts[0] : sum(counts)], refs[sum(counts) :]
+    gu_parts = (gate_parts, up_down_parts)
+    size, ff = gate_parts[0].shape
+    dn_parts = [ref.at[:, pl.ds(ff, ff)] for ref in up_down_parts]
+    hops_done = (*hops_done, hops_done[1])
     (x_out, gu_full, gu_land, dn_full, raw, hidden, result), refs = refs[:7], refs[7:]
     x, dn, hidden_v, pairs, core_sent, core_got, side_sent, side_got, refs = *refs[:8], refs[8:]
     x_send, x_recv, gu_send, gu_recv, dn_send, dn_recv, core_sems, side_sems, loads, stores = refs
     hops = Hops()
     half, chips = hops.chips // 2, hops.chips
     own = x_own.shape[0]
-    size, ff = dn_own.shape
     cut = size // 2
     greet([hops.above, hops.below, hops.partner, hops.across])
     started, saved = [], []
@@ -828,23 +915,23 @@
 
     def spot(ref, offset, top=0, tall=size):
         return block_rows(ref, hops.chip_at(offset) * size + top, tall)
-
-    def span(k):
-        return (0, size) if k < half else (None, cut)
 
     def gu_hop(k):
         copies = []
         for direction, ahead in ((0, hops.above), (1, hops.below)):
             offset = (1 - k) * (1 if direction == 0 else -1)
             top, tall = (0, size) if k < half else (direction * cut, cut)
-            target = spot(gu_land, offset, top, tall)
-            if k == hops_done + 1:
-                held = gu_parts[2 * k - 3 + direction] if k > 1 else gu_parts[0]
-                source = block_rows(held, top, tall)
-            else:
-                source = target
-            index = (direction, k - hops_done - 1)
-            copies.append(begin(remote(source, target, gu_send, gu_recv, index, ahead)))
+            for group in range(2):
+                if k <= hops_done[group]:
+                    continue
+                target = spot(gu_land.at[group], offset, top, tall)
+                if k == hops_done[group] + 1:
+                    held = gu_parts[group][2 * k - 3 + direction]
+                    source = held.at[pl.ds(pl.multiple_of(top, 16), tall), pl.ds(0, ff)]
+                else:
+                    source = target
+                index = (direction, k - 1, group)
+                copies.append(begin(remote(source, target, gu_send, gu_recv, index, ahead)))
         return copies
 
     def dn_hop(k):
@@ -860,40 +947,55 @@
         for copy in copies:
             copy.wait_recv()
 
-    moving = gu_hop(hops_done + 1)
+    first_hop = min(hops_done[:2]) + 1
+    moving = gu_hop(first_hop)
     mine, far = pl.ds(0, own), pl.ds(own, own)
     near, opposite = pl.ds(2 * own, own), pl.ds(3 * own, own)
     load_x = begin(pltpu.make_async_copy(x_own, x.at[mine], loads.at[0]), saved)
-    load_dn = begin(pltpu.make_async_copy(dn_own, spot(dn, 0), loads.at[1]), saved)
+    places = [0]
+    for k in range(1, hops_done[2] + 1):
+        places += [-k, k]
+    dn_loads = [
+        begin(pltpu.make_async_copy(ref, spot(dn, offset), loads.at[1 + i]), saved)
+        for i, (ref, offset) in enumerate(zip(dn_parts, places))
+    ]
+    loaded = len(saved)
     from_far = begin(remote(x_own, x.at[far], x_send, x_recv, (0,), hops.across))
     from_near = begin(remote(x_own, x.at[near], x_send, x_recv, (1,), hops.partner))
+    from_near.wait_recv()
+    load_x.wait()
+    arrive(moving)
+    if first_hop < half:
+        moving = gu_hop(first_hop + 1)
     from_far.wait_recv()
     passed = begin(remote(x.at[far], x.at[opposite], x_send, x_recv, (2,), hops.partner))
-    from_near.wait_recv()
     passed.wait_recv()
-    load_x.wait()
     begin(pltpu.make_async_copy(x, x_out, stores.at[0]), saved)
-    load_dn.wait()
-    arrive(moving)
-    for k in range(hops_done + 2, half + 1):
+    for copy in dn_loads:
+        copy.wait()
+    for k in range(first_hop + 2, half + 1):
+        arrive(moving)
         moving = gu_hop(k)
+    if first_hop < half:
         arrive(moving)
-    moving = dn_hop(1)
-
-    offsets = list(range(hops_done + 1, half)) + list(range(-half + 1, -hops_done)) + [half]
-    order = [0]
-    for k in range(1, hops_done + 1):
-        order += [-k, k]
+    moving = dn_hop(hops_done[2] + 1)
+
+    here, landed = [], []
+    for done in hops_done[:2]:
+        near_by = [0]
+        for k in range(1, done + 1):
+            near_by += [-k, k]
+        here.append(near_by)
+        landed.append([o for o in range(-half + 1, half + 1) if o not in near_by])
     tiles = ff // tile
 
     def body(*tiles_of):
         ins, (raw_tile, hidden_tile, weights) = tiles_of[:-3], tiles_of[-3:]
         step = pl.program_id(0)
-        every = order + offsets
         for group in range(2):
-            for number, offset in enumerate(every):
+            for number, offset in enumerate(here[group] + landed[group]):
                 at = pl.ds(pl.multiple_of(hops.chip_at(offset) * size, size), size)
-                weights[group, at, :] = ins[group * len(every) + number][...]
+                weights[group, at, :] = ins[group * chips + number][...]
         gate = product(x[...], weights[0])
         up = product(x[...], weights[1])
         raw_tile[0] = low(gate)
@@ -903,17 +1005,17 @@
         hidden_tile[...] = value
         hidden_v[:, pl.ds(pl.multiple_of(step * tile, tile), tile)] = value
 
-    def part_spec(row, group):
-        return pl.BlockSpec((size, tile), lambda n: (row, n + group * tiles))
+    def part_spec(row):
+        return pl.BlockSpec((size, tile), lambda n: (row, n))
 
     in_specs, operands = [], []
     for group in range(2):
-        for ref in gu_parts:
-            in_specs.append(part_spec(0, group))
+        for ref in gu_parts[group]:
+            in_specs.append(part_spec(0))
             operands.append(ref)
-        for offset in offsets:
-            in_specs.append(part_spec(hops.chip_at(offset), group))
-            operands.append(gu_land)
+        for offset in landed[group]:
+            in_specs.append(part_spec(hops.chip_at(offset)))
+            operands.append(gu_land.at[group])
     m, width = x.shape
     pltpu.emit_pipeline(
         body,
@@ -952,20 +1054,23 @@
         at = pl.ds(pl.multiple_of(hops.chip_at(order[i]) * size, size), size)
         result[:, at] = both[:own]
 
-    for k in range(1, half + 1):
+    def out_and_sum(offset):
+        block_out(offset)
+        if len(order) > 1:
+            core_sum()
+
+    for k in range(hops_done[2] + 1, half + 1):
         arrive(moving)
         if k < half:
             moving = dn_hop(k + 1)
-        if k == 1:
-            block_out(0)
+        if k == hops_done[2] + 1:
+            for offset in places:
+                out_and_sum(offset)
         if k < half:
-            block_out(-k)
-            core_sum()
-            block_out(k)
-            core_sum()
+            out_and_sum(-k)
+            out_and_sum(k)
         else:
-            block_out(half)
-            core_sum()
+            out_and_sum(half)
     begin(pltpu.make_async_copy(dn, dn_full, stores.at[1]), saved)
     core_sum()
     for i, copy in enumerate(side_copies):
@@ -974,15 +1079,16 @@
         result[:, at] = result[:, at] + to_float(side_got[i])
     for copy in started:
         copy.wait_send()
-    for copy in saved[2:]:
+    for copy in saved[loaded:]:
         copy.wait()
 
 
-def forward(x_own, gu_parts, dn_own, hops_done, tile=512):
+def forward(x_own, gate_parts, up_down_parts, tile=512):
     chips = lax.axis_size("dp") // 2
     half = chips // 2
     own, width = x_own.shape
-    size, ff = dn_own.shape
+    size, ff = gate_parts[0].shape
+    hops_done = [len(parts) // 2 for parts in (gate_parts, up_down_parts)]
     tile = min(tile, ff)
     m = 4 * own
     dma = pltpu.SemaphoreType.DMA
@@ -992,13 +1098,13 @@
         out_shape=[
             jax.ShapeDtypeStruct((m, width), BF16),
             jax.ShapeDtypeStruct((2, width, ff), BF16),
-            jax.ShapeDtypeStruct((width, 2 * ff), BF16),
+            jax.ShapeDtypeStruct((2, width, ff), BF16),
             jax.ShapeDtypeStruct((width, ff), BF16),
             jax.ShapeDtypeStruct((2, m, ff), BF16),
             jax.ShapeDtypeStruct((m, ff), BF16),
             jax.ShapeDtypeStruct((own, width), F32),
         ],
-        in_specs=[ANY] * (len(gu_parts) + 2),
+        in_specs=[ANY] * (1 + len(gate_parts) + len(up_down_parts)),
         out_specs=[ANY] * 6 + [vmem],
         scratch_shapes=[
             pltpu.VMEM((m, width), BF16),
@@ -1011,13 +1117,13 @@
             pltpu.VMEM((chips, own, size), BF16),
             dma((3,)),
             dma((3,)),
-            dma((2, half - hops_done)),
-            dma((2, half - hops_done)),
+            dma((2, half, 2)),
+            dma((2, half, 2)),
             dma((2, half)),
             dma((2, half)),
             dma((2, chips)),
             dma((2, chips)),
-            dma((2,)),
+            dma((1 + len(up_down_parts),)),
             dma((2,)),
         ],
         compiler_params=pltpu.CompilerParams(
@@ -1027,7 +1133,7 @@
             flops=6 * m * width * ff, bytes_accessed=0, transcendentals=0
         ),
         name="forward",
-    )(x_own, *gu_parts, dn_own)
+    )(x_own, *gate_parts, *up_down_parts)
 
 
 def backward_kernel(d_own, hidden, raw, dn_full, gu_full, rows_in, *refs):
@@ -1168,6 +1274,9 @@
     ring_step(0)
     gu_loads = {0: load_gu(0), 1: load_gu(1)}
     hidden_part(3)
+    steps = list(range(1, half - 1))
+    if steps:
+        ring_step(steps.pop(0))
     load_rows.wait()
     for group in range(2):
         wide = product_l(rows_v[...], d_gu[group])
@@ -1193,14 +1302,13 @@
     ]
     begin(pltpu.make_async_copy(x, x_out, stores.at[0]), saved)
     begin(pltpu.make_async_copy(d_gu, d_gu_out, stores.at[1]), saved)
-    steps = [half - 1 - (half - 1 - k) for k in range(1, half - 1)]
     for j in range(chips):
         block_out(j, gu_loads[j])
         if j + 2 < chips:
             gu_loads[j + 2] = load_gu(j + 2)
         if j > 0:
             core_sum(j - 1)
-        if j % 3 == 2 and steps:
+        if j == 3 and steps:
             ring_step(steps.pop(0))
     core_sum(chips - 1)
     for k in steps:
@@ -1275,6 +1383,70 @@
     )(d_own, hidden, raw, dn_full, gu_full, rows_in)
 
 
+def prepare_kernel(q_cols, kv_cols, spots, x, gain, w, cos, sin, gains, rows, raw, query, kv):
+    turn = HD // 2
+    values = to_float(x[...])
+    scale = lax.rsqrt(jnp.mean(values * values, axis=-1, keepdims=True) + EPS)
+    rows[...] = low(values * scale * gain[...])
+    raw[...] = product(rows[...], w[...])
+    cosines, sines = cos[...], sin[...]
+    for start in range(0, q_cols + 2 * kv_cols, HD):
+        at = slice(start, start + HD)
+        head = raw[:, at]
+        head = head * lax.rsqrt(jnp.mean(head * head, axis=-1, keepdims=True) + EPS)
+        if start < q_cols + kv_cols:
+            which = 0 if start < q_cols else 1
+            head = head * gains[which : which + 1, :]
+            front, rear = head[:, :turn], head[:, turn:]
+            head = jnp.concatenate(
+                [front * cosines - rear * sines, rear * cosines + front * sines], axis=1
+            )
+        if start < q_cols:
+            query[start // HD] = low(head)
+        else:
+            kv[:, start - q_cols : start - q_cols + HD] = low(head)
+
+
+def prepare(x, gain, w, cos, sin, gains, side, q_cols):
+    (tall, width), cols = x.shape, w.shape[1]
+    tile = tall // 2
+    kv_cols = (cols - q_cols) // 2
+    natural = lax.rem(jnp.arange(2) + side, 2).astype(jnp.int32)
+
+    def straight(columns):
+        return pl.BlockSpec((tile, columns), lambda t, s: (t, 0))
+
+    return grid_call(
+        functools.partial(prepare_kernel, q_cols, kv_cols),
+        natural,
+        (2,),
+        (x, gain, w, cos, sin, gains),
+        [
+            straight(width),
+            once(gain.shape),
+            once(w.shape),
+            straight(HD // 2),
+            straight(HD // 2),
+            once(gains.shape),
+        ],
+        [
+            jax.ShapeDtypeStruct((tall, width), BF16),
+            jax.ShapeDtypeStruct((tall, cols), F32),
+            jax.ShapeDtypeStruct((q_cols // HD, tall, HD), BF16),
+            jax.ShapeDtypeStruct((tall, 2 * kv_cols), BF16),
+        ],
+        [
+            straight(width),
+            straight(cols),
+            pl.BlockSpec((q_cols // HD, tile, HD), lambda t, s: (0, t, 0)),
+            pl.BlockSpec((tile, 2 * kv_cols), lambda t, s: (s[t], 0)),
+        ],
+        [],
+        2 * tall * width * cols,
+        "prepare",
+    )
+
+
 def prepare_back_kernel(q_cols, kv_cols, spots, raw, d_q, d_kv, after, before, cos, sin, gains, *refs):
     out, gain_grads = refs
     tall = raw.shape[0]
@@ -1304,7 +1476,7 @@
         at = slice(start, start + HD)
         values = raw[:, at]
         if start < q_cols:
-            d, which = unturn(d_q[:, at]), 0
+            d, which = unturn(d_q[start // HD]), 0
         else:
             here = slice(start - q_cols, start - q_cols + HD)
             d = d_kv[:, here] + more[:, here]
@@ -1343,7 +1515,7 @@
         (raw, d_q, d_kv, after, before, cos, sin, gains),
         [
             straight(cols),
-            straight(q_cols),
+            pl.BlockSpec((q_cols // HD, tile, HD), lambda t, s: (0, t, 0)),
             ordered(2 * kv_cols),
             ordered(2 * kv_cols),
             pl.BlockSpec((tile, 2 * kv_cols), lambda t, s: (jnp.minimum(s[1 + t], near - 1), 0)),
@@ -1480,39 +1652,42 @@
     ff_cols = w_gate.shape[1] // 2
     chips = ring.chips
 
-    def gain_block(query_part, key_part, parts):
-        count = query_part.shape[0]
-        columns = parts + [
-            jnp.pad(query_part, (0, rows - count)),
-            jnp.pad(key_part, (0, rows - count)),
-        ]
-        block = jnp.stack(columns, axis=1)
-        return jnp.pad(block, ((0, 0), (0, 128 - block.shape[1])))
-
-    gains = gain_block(
+    gain_list = [
+        gain_input,
+        gain_attn_out,
+        gain_laurel,
+        gain_ffw_in,
+        gain_ffw_out,
+        gain_layer_out,
         query_gain,
         key_gain,
-        [gain_input, gain_attn_out, gain_laurel, gain_ffw_in, gain_ffw_out, gain_layer_out],
-    )
+    ]
+    gains = jnp.stack([jnp.pad(to_float(v), (0, 128 - v.shape[0])) for v in gain_list])
+    gains = jnp.pad(gains, ((0, 8), (0, 0)))
     half = chips // 2
-    (qkv_full, output_t, small_full), (*ff_own, other_tokens) = first_gather(
-        [
-            jnp.concatenate([w_query, w_key, w_value], axis=1),
-            w_output.T,
-            jnp.concatenate([w_left, w_right.T, w_layer_gate, w_layer_proj.T, gains], axis=1),
-        ],
-        w_gate,
-        w_up,
-        w_down.T,
-        tokens,
+    if rows % 128 == 0:
+        blocks = [
+            [(w_query, False), (w_key, False), (w_value, False)],
+            [(w_output, True)],
+            [(w_left, False), (w_right, True), (w_layer_gate, False), (w_layer_proj, True)],
+        ]
+        down_source = (w_down, True)
+    else:
+        blocks = [
+            [(jnp.concatenate([w_query, w_key, w_value], axis=1), False)],
+            [(w_output.T, False)],
+            [(jnp.concatenate([w_left, w_right.T, w_layer_gate, w_layer_proj.T], axis=1), False)],
+        ]
+        down_source = (w_down.T, False)
+    (qkv_full, output_t, small_full, gains_full), (*ff_own, both_tokens) = first_gather(
+        blocks + [[(gains, False)]], w_gate, w_up, down_source, tokens
     )
     left_full = small_full[:, :rank]
     right_t = small_full[:, rank : 2 * rank]
     lgate_full = small_full[:, 2 * rank : 2 * rank + small]
     lproj_t = small_full[:, 2 * rank + small : 2 * rank + 2 * small]
-    gains_full = small_full[:, 2 * rank + 2 * small :]
-
-    gain_columns = to_float(gains_full[:, :8])
+    gains_full = gains_full.reshape(ring.devices, 16, 128)
+    head_part = query_gain.shape[0]
     (
         input_scale,
         attn_scale,
@@ -1520,14 +1695,8 @@
         ffw_in_scale,
         ffw_out_scale,
         layer_scale,
-    ) = (gain_columns[:, i] for i in range(6))
-    head_part = query_gain.shape[0]
-
-    def head_gain(column):
-        return column.reshape(ring.devices, rows)[:, :head_part].reshape(HD)
-
-    query_scale = head_gain(gain_columns[:, 6])
-    key_scale = head_gain(gain_columns[:, 7])
+    ) = (gains_full[:, i, :rows].reshape(width) for i in range(6))
+    query_scale, key_scale = (gains_full[:, i, :head_part].reshape(HD) for i in (6, 7))
 
     piece_len = 2 * own
     seq_total = block_ids.shape[1]
@@ -1571,26 +1740,17 @@
     )
     previous_ids = jnp.where(query_sees == 1, query_ids - 1, query_ids)
 
-    def prepare(qkv_in, query_gains, key_gains):
-        query_in = qkv_in[:, :q_cols]
-        key_in = qkv_in[:, q_cols : q_cols + kv_cols]
-        value_in = qkv_in[:, q_cols + kv_cols :]
-        query_out = rotate(
-            norm_gain(query_in.reshape(piece_len, -1, HD), query_gains), cosines, sines
-        )
-        key_out = rotate(norm_gain(key_in.reshape(piece_len, -1, HD), key_gains), cosines, sines)
-        return (query_out, key_out, norm_plain(value_in.reshape(piece_len, -1, HD)))
+    both_gains = jnp.pad(jnp.stack([query_scale, key_scale]), ((0, 6), (0, 0)))
 
     heads_local = q_cols // HD
-    kv_local = kv_cols // HD
-    group = heads_local // kv_local
-
-    def scores_for(query_low, keys_all):
+    all_rows = heads_local * piece_len
+
+    def scores_for(query_low, keys):
         allowed = (query_ids[:, None] == key_ids[None, :]) | (
             previous_ids[:, None] == key_ids[None, :]
         )
-        scores = jnp.einsum("qkgd,ckd->kgqc", query_low, keys_all, preferred_element_type=F32)
-        return jnp.where(allowed[None, None], scores, NEGATIVE)
+        scores = product_t(query_low, keys).reshape(heads_local, piece_len, -1)
+        return jnp.where(allowed[None], scores, NEGATIVE)
 
     def sum_sides(partial, beside=None):
         got = across(low(partial[own:]))
@@ -1614,37 +1774,34 @@
         pair = partial[: 2 * own] + to_float(ring.swap(low(partial[2 * own :])))
         return sum_sides(pair, beside)
 
-    def attend():
-        normed_low = low(norm_gain(to_float(tokens), input_scale))
-        seq_rows = jnp.concatenate(
-            [normed_low, low(norm_gain(to_float(other_tokens), input_scale))], axis=0
-        )
-        qkv_raw = product(seq_rows, qkv_full)
-        query_rot, key_rot, value_nrm = prepare(qkv_raw, query_scale, key_scale)
-        query_low = low(query_rot).reshape(piece_len, kv_local, group, HD)
-        kv_own = in_order(jnp.concatenate([low(key_rot), low(value_nrm)], axis=1))
-        kv_before = lax.ppermute(kv_own, "dp", forward_pairs)
-        kv_after = lax.ppermute(kv_own[:reach_after], "dp", backward_pairs)
-        kv_all = jnp.concatenate([kv_before, kv_own, kv_after], axis=0)
-        scores = scores_for(query_low, kv_all[:, :kv_local])
+    def attend(query_low, kv_all):
+        scores = scores_for(query_low, kv_all[:, :HD])
         highest = jnp.max(scores, axis=-1, keepdims=True)
         weights_exp = jnp.exp(scores - highest)
         totals = jnp.sum(weights_exp, axis=-1, keepdims=True)
-        probs_low = low(weights_exp / totals)
-        attended = jnp.einsum(
-            "kgqc,ckd->qkgd", probs_low, kv_all[:, kv_local:], preferred_element_type=F32
-        )
-        log_totals = highest + jnp.log(totals)
-        heads_low = low(attended.reshape(piece_len, heads_local * HD))
-        return seq_rows, qkv_raw, query_low, kv_all, log_totals, heads_low
-
-    gu = Gather(ring, ff_own[0])
-    dn = Gather(ring, ff_own[1])
-    gu.step()
-    seq_rows, qkv_raw, query_low, kv_all, log_totals, heads_low = region(attend)
-    heads_low = meet([gu], heads_low)
-    gu.step()
-
+        probs_low = low(weights_exp / totals).reshape(all_rows, -1)
+        attended = low(product(probs_low, kv_all[:, HD:]))
+        attended = attended.reshape(heads_local, piece_len, HD).transpose(1, 0, 2)
+        return highest + jnp.log(totals), attended.reshape(piece_len, q_cols)
+
+    fused = (2 * rows) % 256 == 0
+    gate_ring, more_ring = (Gather(ring, v) for v in ff_own)
+    gate_ring.step()
+    seq_rows, qkv_raw, query_low, kv_own = region(
+        lambda: prepare(
+            both_tokens, input_scale[None], qkv_full, cosines, sines, both_gains, side, q_cols
+        )
+    )
+    query_low = query_low.reshape(all_rows, HD)
+    kv_own = meet([gate_ring], kv_own)
+    kv_before = lax.ppermute(kv_own, "dp", forward_pairs)
+    kv_after = lax.ppermute(kv_own[:reach_after], "dp", backward_pairs)
+    kv_before, kv_after, more_ring.held, gate_ring.held = tie(
+        kv_before, kv_after, more_ring.held, gate_ring.held
+    )
+    more_ring.step()
+    gate_ring.step()
+    kv_all = jnp.concatenate([kv_before, kv_own, kv_after], axis=0)
     def join(heads_low):
         attn_out = sum_sides(product_t(heads_low, output_t))
         normed = norm_gain(to_float(tokens), input_scale)
@@ -1655,33 +1812,30 @@
         mixed = (to_float(tokens) + attn_normed + (normed + laurel_normed)) * ROOT_HALF
         return attn_out, left_low, right_out, mixed, low(norm_gain(mixed, ffw_in_scale))
 
-    attn_out, left_low, right_out, mixed, ffw_low = region(lambda: join(heads_low))
-    ffw_low = meet([gu], ffw_low)
-    fused = (2 * rows) % 256 == 0
+    def attend_and_join():
+        log_totals, heads_low = attend(query_low, kv_all)
+        return log_totals, heads_low, *join(heads_low)
+
+    log_totals, heads_low, attn_out, left_low, right_out, mixed, ffw_low = region(attend_and_join)
+    ffw_low = meet([gate_ring, more_ring], ffw_low)
+
     if fused:
-        parts = [part for _, _, part in gu.parts]
         ffw_rows, gu_weights, _, dn_whole, raw, hidden_low, ffw_out = forward(
-            ffw_low, parts, ff_own[1], 2
+            ffw_low,
+            [part for _, _, part in gate_ring.parts],
+            [part for _, _, part in more_ring.parts],
         )
         dn_spots, dn_parts = jnp.zeros((1,), jnp.int32), [dn_whole]
     else:
-        gu.step()
-        ffw_rows = region(lambda: four_ways(ffw_low))
-        ffw_rows = meet([gu], ffw_rows)
-        for _ in range(half - 4):
-            gu.step()
-            ffw_rows = meet([gu], ffw_rows)
-        gu.step()
-        ffw_rows = meet([gu], ffw_rows)
-
-        gu_spots, gu_parts = gu.pieces()
-        dn.step()
-        raw, hidden_low, gu_weights = region(lambda: gate_up(ffw_rows, gu_spots, gu_parts))
-        raw, hidden_low = meet([dn], raw, hidden_low)
-        for _ in range(half - 1):
-            dn.step()
-            raw, hidden_low = meet([dn], raw, hidden_low)
-        dn_spots, dn_parts = dn.pieces()
+        ffw_rows = four_ways(ffw_low)
+        for weights_ring in (gate_ring, more_ring):
+            while weights_ring.step_count < half:
+                weights_ring.step()
+        gu_spots, gate_parts = gate_ring.pieces()
+        dn_spots, more_parts = more_ring.pieces()
+        up_parts = [part[:, :ff_cols] for part in more_parts]
+        dn_parts = [part[:, ff_cols:] for part in more_parts]
+        raw, hidden_low, gu_weights = gate_up(ffw_rows, gu_spots, gate_parts, up_parts)
         ffw_out = sum_four(columns_out(hidden_low[None], dn_spots, dn_parts, width))
     ffw_out_normed, ffw_out_back = jax.vjp(norm_gain, ffw_out, ffw_out_scale)
     block_mid = mixed + ffw_out_normed
@@ -1737,28 +1891,23 @@
         _, back = jax.vjp(norm_gain, attn_out, attn_scale)
         d_attn, d_attn_scale = back(d_branch)
         d_attn_rows, terms = both_sides(low(d_attn), rg.terms)
-        d_heads = low(product(d_attn_rows, output_t)).reshape(piece_len, kv_local, group, HD)
-        keys_all, values_all = kv_all[:, :kv_local], kv_all[:, kv_local:]
-        probs = jnp.exp(scores_for(query_low, keys_all) - log_totals)
-        probs_low = low(probs)
-        d_values_all = jnp.einsum(
-            "kgqc,qkgd->ckd", probs_low, d_heads, preferred_element_type=F32
-        )
-        d_probs = jnp.einsum("qkgd,ckd->kgqc", d_heads, values_all, preferred_element_type=F32)
+        d_heads = low(product(d_attn_rows, output_t)).reshape(piece_len, heads_local, HD)
+        d_heads = d_heads.transpose(1, 0, 2).reshape(all_rows, HD)
+        keys, values = kv_all[:, :HD], kv_all[:, HD:]
+        probs = jnp.exp(scores_for(query_low, keys) - log_totals)
+        d_values = product_l(low(probs).reshape(all_rows, -1), d_heads)
+        d_probs = product_t(d_heads, values).reshape(probs.shape)
         deltas = jnp.sum(probs * d_probs, axis=-1, keepdims=True)
-        d_scores = low(probs * (d_probs - deltas))
-        d_keys_all = jnp.einsum("kgqc,qkgd->ckd", d_scores, query_low, preferred_element_type=F32)
-        d_query_rot = jnp.einsum("kgqc,ckd->qkgd", d_scores, keys_all, preferred_element_type=F32)
-        kv_shape = (kv_all.shape[0], kv_cols)
-        d_kv_all = jnp.concatenate(
-            [d_keys_all.reshape(kv_shape), d_values_all.reshape(kv_shape)], axis=1
-        )
+        d_scores = low(probs * (d_probs - deltas)).reshape(all_rows, -1)
+        d_keys = product_l(d_scores, query_low)
+        d_query_rot = product(d_scores, keys).reshape(heads_local, piece_len, HD)
+        d_kv_all = jnp.concatenate([d_keys, d_values], axis=1)
         to_before = low(d_kv_all[:piece_len])
         to_after = low(d_kv_all[2 * piece_len :])
         d_kv_own = d_kv_all[piece_len : 2 * piece_len]
         moving = (to_before, to_after)
         kept = (d_ffw_in_scale, d_attn_scale, d_branch, d_attn_rows, d_kv_own)
-        return terms, moving, kept, d_query_rot.reshape(piece_len, q_cols)
+        return terms, moving, kept, d_query_rot
 
     terms, moving, kept, d_query_rot = meet([rd, rg], *region(back_34))
     d_ffw_in_scale, d_attn_scale, d_branch, d_attn_rows, d_kv_own = kept
@@ -1767,7 +1916,6 @@
     from_after, from_before = rg.step(terms, from_after, from_before)
 
     def back_5():
-        both_gains = jnp.stack([query_scale, key_scale])
         d_qkv_low, gain_sums = prepare_back(
             qkv_raw,
             d_query_rot,
@@ -1776,7 +1924,7 @@
             from_before,
             cosines,
             sines,
-            jnp.pad(both_gains, ((0, 6), (0, 0))),
+            both_gains,
             side,
             own,
         )
@@ -1828,7 +1976,7 @@
 
     grad_tokens, (mine, theirs) = meet([rg], *region(back_6))
     down_end, gate_up_end = ends
-    total, small_half, out_gate, out_up, out_down_t = last_reduce(
+    total, out_small, out_gate, out_up, out_down_t = last_reduce(
         mine,
         theirs,
         2 * q_cols + 2 * kv_cols,
@@ -1836,12 +1984,6 @@
     )
     out_output = total[:, :q_cols].T
     out_qkv = total[:, q_cols:]
-    small_other = across(small_half)
-    out_small = jnp.where(
-        side == 0,
-        jnp.concatenate([small_half, small_other], axis=1),
-        jnp.concatenate([small_other, small_half], axis=1),
-    )
     out_gains = out_small[:, 2 * rank + 2 * small :]
     return (
         low(result),

time: 825 us -> 783 us (0.949)
  local copies, waits for them, and re-layouts: 85.4 us -> 50.3 us
  other arithmetic: 102 us -> 68 us
  waiting for transfers between devices: 40.2 us -> 71.4 us
  matrix products: 71.6 us -> 55.8 us
  Pallas kernels: 489 us -> 499 us
    dot_general x7 -> x2, matrix products: 36.2 us -> 9.5 us  [product_l(): lax.dot_general(left_in, right_in, (((0,), (0,)), ((), ())), preferred_el...]
    another operation x18 -> x6, local copies, waits for them, and re-layouts: 24.1 us -> 3.64 us
    ppermute x6 -> x7, waiting for transfers between devices: 4.83 us -> 23.5 us  [up(): return lax.ppermute(values, 'dp', self.cw)]
    dot_general x6 -> x9, matrix products: 18.2 us -> 33.7 us  [product_t(): lax.dot_general(left_in, right_in, (((1,), (1,)), ((), ())), preferred_el...]
    reduce_sum x9 -> x6, other arithmetic: 20.5 us -> 10.4 us  [norm_gain(): jnp.mean(values * values, axis=-1, keepdims=True) + EPS]
    ppermute x6 -> x7, starting transfers between devices: 7.74 us -> 16.7 us  [up(): return lax.ppermute(values, 'dp', self.cw)]
    slice x4 -> x3, local copies, waits for them, and re-layouts: 10.8 us -> 2.31 us  [the longest x1 1.33 us: local(): gains_full[:, i, :rows].reshape(width)]
    ppermute x4 -> x3, waiting for transfers between devices: 31.8 us -> 40 us  [across(): return lax.ppermute(values, 'tensor', [(0, 1), (1, 0)])]
  transfers between devices with their start and end apart: 20 -> 21, of which waited for: 8 -> 11; matrix products, arithmetic and copies ran while one was open for 26% -> 17% of each run, Pallas kernels for 6% -> 7%
where the time goes in v5:
time: 783 us; the launch traced here: 777 us
  Pallas kernels  499 us (64%)
  waiting for transfers between devices  71.4 us (9%)
  other arithmetic  68 us (9%)
  matrix products  55.8 us (7%)
  local copies, waits for them, and re-layouts  50.3 us (6%)
  starting transfers between devices  30.4 us (4%)
    pallas_call x1, Pallas kernels, forward(): pl.pallas_call(functools.partial(forward_kernel, hops_done, tile), out_sh...  169 us
    pallas_call x1, Pallas kernels, backward(): pl.pallas_call(backward_kernel, out_shape=[jax.ShapeDtypeStruct((m, width...  114 us
    pallas_call x9, Pallas kernels, grid_call(): pl.pallas_call(kernel, grid_spec=pltpu.PrefetchScalarGridSpec(num_scalar_...  77.4 us
    pallas_call x1, Pallas kernels, comm_call(): pl.pallas_call(kernel, out_shape=shapes, in_specs=[ANY] * len(operands),...  69.9 us
    pallas_call x1, Pallas kernels, last_reduce(): pl.pallas_call(functools.partial(last_kernel, large), out_shape=[jax.Shap...  68.5 us
    ppermute x3, waiting for transfers between devices, across(): return lax.ppermute(values, 'tensor', [(0, 1), (1, 0)])  40 us
    dot_general x9, matrix products, product_t(): lax.dot_general(left_in, right_in, (((1,), (1,)), ((), ())), preferred_el...  33.7 us
    ppermute x7, waiting for transfers between devices, up(): return lax.ppermute(values, 'dp', self.cw)  23.5 us
  transfers between devices with their start and end apart: 21, of which 11 were waited for; matrix products, arithmetic and copies ran while one was open for 17% of the time, Pallas kernels for 7%

profile of v5, /device:TPU:0, one launch (start us, length us, event | category | flops | bytes accessed | tf_op | source)
XLA Modules:
  0.0 776.6 jit_solution(14920894727134407163)
XLA Ops:
  4.1 69.9 %first_gather.1 = (bf16[2048,1536]{1,0:T(8,128)(2,1)}, bf16[2048,1024]{1,0:T(8,128)(2,1)}, bf16[2048,640]{1,0:T(8,128)(2,1)}, f32[256,128]{1,0:T(8,128)}, bf16[2...) custom-call(bf16[128,1024]{1,0:T(8,128)(2,1)} %refs_0_.1, bf16[128,256]{1,0:T(8,128)(2,1)} %refs_1_.1, ...), custom_call_target="tpu_custom_call" | custom-call | bytes 147324928 | tf_op jit(solution)/shard_map/first_gather/pallas_call | solution.py:314
  80.5 9.6 %conditional.5 = (bf16[512,2048]{1,0:T(8,128)(2,1)}, f32[512,1536]{1,0:T(8,128)}, bf16[512,512]{1,0:T(8,128)(2,1)S(1)}, bf16[2048,256]{1,0:T(8,128)(2,1)}) conditional(s32[]{:T(128)} %convert_element_type.130, () %tuple.60, (s32[]{:T(128)}, f32[16,1,128]{2,1,0:T(1,128)S(1)}, bf16[512,2048]{1,0:T(8,128)(2,1)S(1)}, bf16[2048,1536]{1,0:T(8,128)(2,1)}, ...), branch_computations={%region_0.1_spmd, %region_1.2_spmd} | conditional | flops 3221225472 | bytes 15745068 | solution.py:1602
  81.0 9.1 %prepare.1 = (bf16[512,2048]{1,0:T(8,128)(2,1)}, f32[512,1536]{1,0:T(8,128)}, bf16[4,512,256]{2,1,0:T(8,128)(2,1)}, bf16[512,512]{1,0:T(8,128)(2,1)S(1)}) custom-call(s32[2]{0:T(128)} %compare_select_fusion.spots, bf16[512,2048]{1,0:T(8,128)(2,1)S(1)} %get-tuple-element.156.x, f32[1,2048]{1,0:T(1,128)S(1)} %bitcast.132, ...), custom_call_target="tpu_custom_call" | custom-call | flops 3221225472 | bytes 15745024 | tf_op jit(solution)/shard_map/cond/branch_1_fun/prepare/pallas_call | solution.py:484
  90.1 9.9 %collective-permute-done.3.refs_1_ = bf16[256,2048]{1,0:T(8,128)(2,1)} collective-permute-done((bf16[256,2048]{1,0:T(8,128)(2,1)}, bf16[256,2048]{1,0:T(8,128)(2,1)}, u32[]{:S(2)}, u32[]{:S(2)}) %collective-permute-start.3) | collective-permute-done | bytes 1048608 | tf_op jit(solution)/shard_map/ppermute | solution.py:100
  104.0 2.7 collective-permute-done.6
  106.7 7.6 collective-permute-start.9
  116.8 2.1 collective-permute-start.7
  119.2 2.4 fusion.79
  122.8 51.3 %conditional.6 = (f32[4,512,1]{1,0,2:T(4,128)S(1)}, bf16[512,1024]{1,0:T(8,128)(2,1)}, f32[256,2048]{1,0:T(8,128)}, bf16[256,64]{0,1:T(8,128)(2,1)}, f32[256,204...) conditional(s32[]{:T(128)} %convert_element_type.130, () %tuple.59, (s32[512]{0:T(512)S(1)}, ...), branch_computations={%region_4.5_spmd, %region_5.12_spmd} | conditional | flops 5002117120 | bytes 139807008 | solution.py:1602
  123.3 2.6 broadcast_in_dim.54
  127.5 2.8 fusion.78
  131.8 2.1 fusion.3
  135.1 3.6 fusion.83
  138.7 2.0 copy-done.20
  145.2 21.5 %collective-permute-done = bf16[256,2048]{1,0:T(8,128)(2,1)} collective-permute-done((bf16[256,2048]{1,0:T(8,128)(2,1)S(1)}, bf16[256,2048]{1,0:T(8,128)(2,1)}, u32[]{:S(2)}, u32[]{:S(2)}) %collective-permute-start) | collective-permute-done | bytes 1048608 | tf_op jit(solution)/shard_map/cond/branch_1_fun/ppermute | solution.py:110
  166.7 2.8 multiply_reduce_fusion.2
  169.6 3.3 multiply_reduce_fusion
  174.1 7.3 collective-permute-done.7.refs_3_
  181.4 2.8 collective-permute-done.8.refs_4_
  184.2 169.5 %forward.1 = (bf16[1024,2048]{1,0:T(8,128)(2,1)}, bf16[2,2048,2048]{2,1,0:T(8,128)(2,1)}, bf16[2,2048,2048]{2,1,0:T(8,128)(2,1)}, bf16[2048,2048]{1,0:T(8,128)(2...) custom-call(bf16[256,2048]{1,0:T(8,128)(2,1)} %get-tuple-element.390.x_own, ...), custom_call_target="tpu_custom_call" | custom-call | flops 25769803776 | tf_op jit(solution)/shard_map/forward/pallas_call | solution.py:1096
  353.7 2.0 multiply_reduce_fusion.18
  356.4 2.2 copy-done.27
  359.9 3.2 add_convert_fusion.2
  366.7 113.5 %backward.1 = (bf16[1024,2048]{1,0:T(8,128)(2,1)}, bf16[2,1024,2048]{2,1,0:T(8,128)(2,1)}, bf16[256,2048]{1,0:T(8,128)(2,1)}, bf16[256,2048]{1,0:T(8,128)(2,1)},...) custom-call(bf16[256,2048]{1,0:T(8,128)(2,1)} %fusion.51.d_own, ...), custom_call_target="tpu_custom_call" | custom-call | flops 25769803776 | tf_op jit(solution)/shard_map/backward/pallas_call | solution.py:1337
  480.2 9.9 %block_grads.10 = (bf16[256,4096]{1,0:T(8,128)(2,1)}, bf16[256,4096]{1,0:T(8,128)(2,1)}) custom-call(s32[2]{0:T(128)} %pad_add_fusion.4.spots, bf16[1024,2048]{1,0:T(8,128)(2,1)} %get-tuple-element.392.rows_in.refs_0_.refs_1_, bf16[1024,2048]{1,0:T(8,128)(2,1)} %get-tuple-element.392.rows_in.refs_0_.refs_1_, ...), custom_call_target="tpu_custom_call" | custom-call | tf_op jit(solution)/shard_map/block_grads/pallas_call | solution.py:484
  492.7 7.4 block_grads.9
  502.2 66.0 %conditional.7 = (bf16[256,4096]{1,0:T(8,128)(2,1)}, bf16[256,4096]{1,0:T(8,128)(2,1)}, bf16[512,512]{0,1:T(8,128)(2,1)}, bf16[256,512]{0,1:T(8,128)(2,1)S(1)}, ...) conditional(s32[]{:T(128)} %convert_element_type.130, () %tuple.66, ...), branch_computations={%region_16.17_spmd, %region_17.25_spmd} | conditional | flops 8914598912 | bytes 204252848 | solution.py:1602
  502.4 2.9 multiply_reduce_fusion.5
  505.3 4.6 multiply_reduce_fusion.4
  509.9 2.0 fusion.25
  513.3 9.6 %block_grads.6 = (bf16[256,4096]{1,0:T(8,128)(2,1)}, bf16[256,4096]{1,0:T(8,128)(2,1)}) custom-call(s32[2]{0:T(128)} %pad_add_fusion.spots, bf16[1024,2048]{1,0:T(8,128)(2,1)} %get-tuple-element.186.refs_0_.refs_1_, bf16[1024,2048]{1,0:T(8,128)(2,1)} %get-tuple-element.186.refs_0_.refs_1_, bf16[2,1024,2048]{2,1,0:T(8,128)(2,1)} %get-tuple-element.187.refs_2_), custom_call_target="tpu_custom_call" | custom-call | tf_op jit(solution)/shard_map/cond/branch_1_fun/block_grads/pallas_call | solution.py:484
  523.5 6.8 fusion.33
  530.3 3.4 collective-permute-done.1
  533.6 2.9 pad_maximum_fusion.1
  536.5 4.9 convolution_convert_fusion.1
  543.0 6.6 fusion.20
  549.6 7.1 multiply_reduce_fusion.3
  556.8 3.2 multiply_convert_fusion.1
  560.0 2.9 fusion.84
  565.2 3.0 fusion.27
  570.9 3.0 collective-permute-start.16
  574.0 4.3 add_convert_fusion.1
  578.3 4.4 add_convert_fusion
  584.7 46.6 %conditional.8 = (f32[256,2048]{1,0:T(8,128)}, bf16[256,2048]{1,0:T(8,128)(2,1)S(1)}, bf16[256,4096]{1,0:T(8,128)(2,1)S(1)}, bf16[512,1536]{1,0:T(8,128)(2,1)}, f32[256]{0:T(256)S(1)}, /*index=5*/f32[256]{0:T(256)S(1)}) conditional(s32[]{:T(128)} %convert_element_type.130, () %tuple.70, (s32[]{:T(128)}, f32[512,1536]{1,0:T(8,128)}, ...), branch_computations={%region_25.26_spmd, %region_26.27_spmd} | conditional | flops 3230138368 | bytes 69489024 | solution.py:1602
  586.6 5.9 prepare_back.1
  592.6 6.0 fusion.82
  598.6 2.1 copy-done.19
  602.4 3.6 block_grads.7
  606.0 5.8 block_grads.8
  612.6 15.2 %collective-permute-done.2 = bf16[256,2048]{1,0:T(8,128)(2,1)} collective-permute-done((bf16[256,2048]{1,0:T(8,128)(2,1)}, bf16[256,2048]{1,0:T(8,128)(2,1)}, u32[]{:S(2)}, u32[]{:S(2)}) %collective-permute-start.2) | collective-permute-done | bytes 1048608 | tf_op jit(solution)/shard_map/cond/branch_1_fun/ppermute | solution.py:110
  627.8 3.5 slice_add_fusion.1
  633.0 10.5 %block_grads.11 = (bf16[256,4096]{1,0:T(8,128)(2,1)}, bf16[256,4096]{1,0:T(8,128)(2,1)}) custom-call(s32[2]{0:T(128)} %pad_add_fusion.3.spots, bf16[1024,2048]{1,0:T(8,128)(2,1)} %get-tuple-element.392.rows_in.refs_0_.refs_1_, bf16[1024,2048]{1,0:T(8,128)(2,1)} %get-tuple-element.392.rows_in.refs_0_.refs_1_, ...), custom_call_target="tpu_custom_call" | custom-call | tf_op jit(solution)/shard_map/block_grads/pallas_call | solution.py:484
  647.4 37.6 %conditional.9 = (f32[256,2048]{1,0:T(8,128)}, f32[1024,3328]{1,0:T(8,128)}, bf16[1024,3328]{1,0:T(8,128)(2,1)}) conditional(s32[]{:T(128)} %convert_element_type.130, () %tuple.73, (f32[16,1,128]{2,1,0:T(1,128)S(1)}, f32[256,2048]{1,0:T(8,128)}, f32[256,2048]{1,0:T(8,128)}, bf16[2048,64]{1,0:T(8,128)(2,1)S(1)}, ...), branch_computations={%region_29.30_spmd, %region_30.37_spmd.clone} | conditional | flops 6194473984 | bytes 90155184 | solution.py:1602
  647.4 1.8 multiply_reduce_fusion.14
  649.2 2.7 multiply_reduce_fusion.12
  652.0 2.8 fusion.44
  655.3 4.1 fusion.43
  659.5 3.5 fusion.45
  663.7 3.4 multiply_reduce_fusion.10
  669.5 15.5 %row_grads.1 = (f32[1024,3328]{1,0:T(8,128)}, bf16[1024,3328]{1,0:T(8,128)(2,1)}) custom-call(s32[1]{0:T(128)} %bitcast.53.spots, bf16[512,2048]{1,0:T(8,128)(2,1)} %get-tuple-element.489.refs_0_, bf16[512,2048]{1,0:T(8,128)(2,1)S(1)} %copy-done.22, bf16[256,2048]{1,0:T(8,128)(2,1)S(1)} %copy-done.30, bf16[256,2048]{1,0:T(8,128)(2,1)} %get-tuple-element.492.refs_3_, ...), custom_call_target="tpu_custom_call" | custom-call | flops 6039797760 | bytes 32833536 | tf_op jit(solution)/shard_map/cond/branch_1_fun/row_grads/pallas_call | solution.py:484
  685.1 6.3 collective-permute-done.19.refs_3_
  691.9 68.5 %last_reduce.1 = (f32[128,2560]{1,0:T(8,128)}, f32[128,768]{1,0:T(8,128)}, f32[128,4096]{1,0:T(8,128)}, f32[128,4096]{1,0:T(8,128)}, f32[128,4096]{1,0:T(8,128)}) custom-call(f32[1024,3328]{1,0:T(8,128)} %get-tuple-element.459.refs_0_, bf16[1024,3328]{1,0:T(8,128)(2,1)} %get-tuple-element.460.refs_1_, bf16[256,4096]{1,0:T(8,128)(2,1)} %copy-done.10, ...), custom_call_target="tpu_custom_call" | custom-call | bytes 272629760 | tf_op jit(solution)/shard_map/last_reduce/pallas_call | solution.py:854
  760.5 2.1 slice_bitcast_fusion
  769.0 3.0 copy.115
  (253 shorter events, 74.5 us)
Async XLA Ops:
  74.1 25.9 %collective-permute-start.3 = (bf16[256,2048]{1,0:T(8,128)(2,1)}, bf16[256,2048]{1,0:T(8,128)(2,1)}, u32[]{:S(2)}, u32[]{:S(2)}) collective-permute-start(bf16[256,2048]{1,0:T(8,128)(2,1)} %get-tuple-element.370.refs_0_), channel_id=1, source_target_pairs={{0,8},{2,10},{8,16},{10,18},{16,24},{18,26},{24,28},{26,30},{28,20... | collective-permute-start | bytes 3145736 | tf_op jit(solution)/shard_map/ppermute | solution.py:100
  75.7 25.6 %collective-permute-start.4 = (bf16[256,2048]{1,0:T(8,128)(2,1)}, bf16[256,2048]{1,0:T(8,128)(2,1)}, u32[]{:S(2)}, u32[]{:S(2)}) collective-permute-start(bf16[256,2048]{1,0:T(8,128)(2,1)} %get-tuple-element.370.refs_0_), channel_id=1, source_target_pairs={{8,0},{10,2},{16,8},{18,10},{24,16},{26,18},{28,24},{30,26},{20,28... | collective-permute-start | bytes 3145736 | tf_op jit(solution)/shard_map/ppermute | solution.py:103
  78.7 43.1 %copy-start.39 = (f32[16,1,128]{2,1,0:T(1,128)}, f32[16,1,128]{2,1,0:T(1,128)S(1)}, u32[]{:S(2)}) copy-start(f32[16,1,128]{2,1,0:T(1,128)S(1)} %get-tuple-element.898) | copy-start | bytes 24580
  78.7 43.1 %copy-start.41 = (f32[16,1,128]{2,1,0:T(1,128)}, f32[16,1,128]{2,1,0:T(1,128)S(1)}, u32[]{:S(2)}) copy-start(f32[16,1,128]{2,1,0:T(1,128)S(1)} %get-tuple-element.901) | copy-start | bytes 24580
  78.7 43.1 %copy-start.43 = (f32[16,1,128]{2,1,0:T(1,128)}, f32[16,1,128]{2,1,0:T(1,128)S(1)}, u32[]{:S(2)}) copy-start(f32[16,1,128]{2,1,0:T(1,128)S(1)} %get-tuple-element.899) | copy-start | bytes 24580
  79.7 36.8 %copy-start.53 = (s32[1,64,64]{2,1,0:T(8,128)S(1)}, s32[1,64,64]{2,1,0:T(8,128)}, u32[]{:S(2)}) copy-start(s32[1,64,64]{2,1,0:T(8,128)} %param.37) | copy-start | bytes 49156
  101.2 5.5 collective-permute-start.5
  102.6 4.1 collective-permute-start.6
  106.7 77.5 %collective-permute-start.9 = (bf16[256,4096]{1,0:T(8,128)(2,1)}, bf16[256,4096]{1,0:T(8,128)(2,1)}, u32[]{:S(2)}, u32[]{:S(2)}) collective-permute-start(bf16[256,4096]{1,0:T(8,128)(2,1)} %get-tuple-element.388.refs_5_), channel_id=1, source_target_pairs={{0,8},{2,10},{8,16},{10,18},{16,24},{18,26},{24,28},{26,30},{28,20... | collective-permute-start | bytes 6291464 | tf_op jit(solution)/shard_map/ppermute | solution.py:100
  114.3 70.0 %collective-permute-start.10 = (bf16[256,4096]{1,0:T(8,128)(2,1)}, bf16[256,4096]{1,0:T(8,128)(2,1)}, u32[]{:S(2)}, u32[]{:S(2)}) collective-permute-start(bf16[256,4096]{1,0:T(8,128)(2,1)} %get-tuple-element.388.refs_5_), channel_id=1, source_target_pairs={{8,0},{10,2},{16,8},{18,10},{24,16},{26,18},{28,24},{30,26},{20,28... | collective-permute-start | bytes 6291464 | tf_op jit(solution)/shard_map/ppermute | solution.py:103
  116.5 5.3 copy-start.45
  116.7 5.1 copy-start.47
  116.8 64.6 %collective-permute-start.7 = (bf16[256,2048]{1,0:T(8,128)(2,1)}, bf16[256,2048]{1,0:T(8,128)(2,1)}, u32[]{:S(2)}, u32[]{:S(2)}) collective-permute-start(bf16[256,2048]{1,0:T(8,128)(2,1)} %collective-permute-done.3.refs_1_), channel_id=1, source_target_pairs={{0,8},{2,10},{8,16},{10,18},{16,24},{18,26},{24,28},{26,30},{28,20... | collective-permute-start | bytes 3145736 | tf_op jit(solution)/shard_map/ppermute | solution.py:100
  118.9 65.4 %collective-permute-start.8 = (bf16[256,2048]{1,0:T(8,128)(2,1)}, bf16[256,2048]{1,0:T(8,128)(2,1)}, u32[]{:S(2)}, u32[]{:S(2)}) collective-permute-start(bf16[256,2048]{1,0:T(8,128)(2,1)} %collective-permute-done.4.refs_2_), channel_id=1, source_target_pairs={{8,0},{10,2},{16,8},{18,10},{24,16},{26,18},{28,24},{30,26},{20,28... | collective-permute-start | bytes 3145736 | tf_op jit(solution)/shard_map/ppermute | solution.py:103
  119.2 2.6 copy-start.54
  131.8 3.3 copy-start.56
  140.7 2.7 copy-start.13
  140.9 25.8 %collective-permute-start = (bf16[256,2048]{1,0:T(8,128)(2,1)S(1)}, bf16[256,2048]{1,0:T(8,128)(2,1)}, u32[]{:S(2)}, u32[]{:S(2)}) collective-permute-start(bf16[256,2048]{1,0:T(8,128)(2,1)S(1)} %slice.249), channel_id=1, source_target_pairs={{0,1},{1,0},{2,3},{3,2},{4,5},{5,4},{6,7},{7,6},{8,9},{9,8},{10,11... | collective-permute-start | bytes 3145736 | tf_op jit(solution)/shard_map/cond/branch_1_fun/ppermute | solution.py:110
  142.9 23.8 %copy-start.21 = (f32[512,2048]{1,0:T(8,128)S(1)}, f32[512,2048]{1,0:T(8,128)}, u32[]{:S(2)}) copy-start(f32[512,2048]{1,0:T(8,128)} %copy-done.20) | copy-start | bytes 12582916 | tf_op jit(solution)/shard_map/cond
  143.4 26.1 %copy-start.36 = (bf16[256,64]{0,1:T(8,128)(2,1)}, bf16[256,64]{0,1:T(8,128)(2,1)S(1)}, u32[]{:S(2)}) copy-start(bf16[256,64]{0,1:T(8,128)(2,1)S(1)} %convolution_convert_fusion) | copy-start | bytes 98308 | tf_op jit(solution)/shard_map/cond
  355.9 2.7 copy-start.58
  356.3 2.8 copy-start.29
  356.4 3.5 copy-start.7
  356.4 2.7 copy-start.8
  490.1 78.1 %collective-permute-start.13 = (bf16[256,4096]{1,0:T(8,128)(2,1)}, bf16[256,4096]{1,0:T(8,128)(2,1)}, u32[]{:S(2)}, u32[]{:S(2)}) collective-permute-start(bf16[256,4096]{1,0:T(8,128)(2,1)} %get-tuple-element.405), channel_id=1, source_target_pairs={{0,8},{2,10},{8,16},{10,18},{16,24},{18,26},{24,28},{26,30},{28,20... | collective-permute-start | bytes 6291464 | tf_op jit(solution)/shard_map/ppermute | solution.py:100
  491.7 76.4 %collective-permute-start.14 = (bf16[256,4096]{1,0:T(8,128)(2,1)}, bf16[256,4096]{1,0:T(8,128)(2,1)}, u32[]{:S(2)}, u32[]{:S(2)}) collective-permute-start(bf16[256,4096]{1,0:T(8,128)(2,1)} %get-tuple-element.406), channel_id=1, source_target_pairs={{8,0},{10,2},{16,8},{18,10},{24,16},{26,18},{28,24},{30,26},{20,28... | collective-permute-start | bytes 6291464 | tf_op jit(solution)/shard_map/ppermute | solution.py:103
  492.7 9.4 %copy-start.4 = (f32[256,2048]{1,0:T(8,128)S(1)}, f32[256,2048]{1,0:T(8,128)}, u32[]{:S(2)}) copy-start(f32[256,2048]{1,0:T(8,128)} %copy-done.3) | copy-start | bytes 6291460
  492.7 9.4 %copy-start.11 = (f32[256,2048]{1,0:T(8,128)S(1)}, f32[256,2048]{1,0:T(8,128)}, u32[]{:S(2)}) copy-start(f32[256,2048]{1,0:T(8,128)} %get-tuple-element.407) | copy-start | bytes 6291460
  492.7 9.4 %copy-start.44 = (f32[16,1,128]{2,1,0:T(1,128)S(1)}, f32[16,1,128]{2,1,0:T(1,128)}, u32[]{:S(2)}) copy-start(f32[16,1,128]{2,1,0:T(1,128)} %copy-done.43) | copy-start | bytes 24580
  500.1 68.1 %collective-permute-start.11 = (bf16[256,2048]{1,0:T(8,128)(2,1)}, bf16[256,2048]{1,0:T(8,128)(2,1)}, u32[]{:S(2)}, u32[]{:S(2)}) collective-permute-start(bf16[256,2048]{1,0:T(8,128)(2,1)} %get-tuple-element.401), channel_id=1, source_target_pairs={{0,8},{2,10},{8,16},{10,18},{16,24},{18,26},{24,28},{26,30},{28,20... | collective-permute-start | bytes 3145736 | tf_op jit(solution)/shard_map/ppermute | solution.py:100
  501.8 66.4 %collective-permute-start.12 = (bf16[256,2048]{1,0:T(8,128)(2,1)}, bf16[256,2048]{1,0:T(8,128)(2,1)}, u32[]{:S(2)}, u32[]{:S(2)}) collective-permute-start(bf16[256,2048]{1,0:T(8,128)(2,1)} %get-tuple-element.402), channel_id=1, source_target_pairs={{8,0},{10,2},{16,8},{18,10},{24,16},{26,18},{28,24},{30,26},{20,28... | collective-permute-start | bytes 3145736 | tf_op jit(solution)/shard_map/ppermute | solution.py:103
  511.9 21.7 %collective-permute-start.1 = (bf16[256,2048]{1,0:T(8,128)(2,1)S(1)}, bf16[256,2048]{1,0:T(8,128)(2,1)}, u32[]{:S(2)}, u32[]{:S(2)}) collective-permute-start(bf16[256,2048]{1,0:T(8,128)(2,1)S(1)} %fusion.25), channel_id=1, source_target_pairs={{0,1},{1,0},{2,3},{3,2},{4,5},{5,4},{6,7},{7,6},{8,9},{9,8},{10,11... | collective-permute-start | bytes 3145736 | tf_op jit(solution)/shard_map/cond/branch_1_fun/ppermute | solution.py:110
  513.3 9.6 %copy-start.46 = (s32[1280]{0:T(1024)S(1)}, s32[1280]{0:T(1024)}, u32[]{:S(2)}) copy-start(s32[1280]{0:T(1024)} %get-tuple-element.193) | copy-start | bytes 15364 | tf_op jit(solution)/shard_map/cond
  513.3 9.6 %copy-start.48 = (s32[512]{0:T(512)S(1)}, s32[512]{0:T(512)}, u32[]{:S(2)}) copy-start(s32[512]{0:T(512)} %get-tuple-element.192) | copy-start | bytes 6148 | tf_op jit(solution)/shard_map/cond
  513.3 9.6 %copy-start.55 = (s32[512]{0:T(512)S(1)}, s32[512]{0:T(512)}, u32[]{:S(2)}) copy-start(s32[512]{0:T(512)} %get-tuple-element.194) | copy-start | bytes 6148 | tf_op jit(solution)/shard_map/cond
  513.3 10.1 %copy-start.17 = (bf16[1280,512]{1,0:T(8,128)(2,1)S(1)}, bf16[1280,512]{1,0:T(8,128)(2,1)}, u32[]{:S(2)}) copy-start(bf16[1280,512]{1,0:T(8,128)(2,1)} %get-tuple-element.196) | copy-start | bytes 3932164 | tf_op jit(solution)/shard_map/cond
  533.6 2.9 copy-start.57
  543.0 13.8 %slice-start = ((s8[10485760]{0:T(1024)(128)(4,1)}), s8[4194304]{0:T(1024)(128)(4,1)S(1)}, s32[]{:S(2)}) async-start(s8[10485760]{0:T(1024)(128)(4,1)} %bitcast.114), calls=%async_computation | async-start | bytes 8388608 | tf_op jit(solution)/shard_map/cond
  543.0 13.8 %slice-start.1 = ((s8[10485760]{0:T(1024)(128)(4,1)}), s8[4194304]{0:T(1024)(128)(4,1)S(1)}, s32[]{:S(2)}) async-start(s8[10485760]{0:T(1024)(128)(4,1)} %bitcast.114), calls=%async_computation.1 | async-start | bytes 8388608 | tf_op jit(solution)/shard_map/cond
  549.6 7.1 slice-start.2
  569.5 13.2 %collective-permute-start.15 = (bf16[512,512]{1,0:T(8,128)(2,1)S(1)}, bf16[512,512]{1,0:T(8,128)(2,1)}, u32[]{:S(2)}, u32[]{:S(2)}) collective-permute-start(bf16[512,512]{1,0:T(8,128)(2,1)S(1)} %copy.108), channel_id=1, source_target_pairs={{2,0},{4,2},{6,4},{8,6},{10,8},{12,10},{14,12},{16,14},{18,16},{20... | collective-permute-start | bytes 1572872 | tf_op jit(solution)/shard_map/ppermute | solution.py:1914
  570.9 11.8 %collective-permute-start.16 = (bf16[256,512]{1,0:T(8,128)(2,1)S(1)}, bf16[256,512]{1,0:T(8,128)(2,1)S(1)}, u32[]{:S(2)}, u32[]{:S(2)}) collective-permute-start(bf16[256,512]{1,0:T(8,128)(2,1)S(1)} %copy.109), channel_id=1, source_target_pairs={{0,2},{2,4},{4,6},{6,8},{8,10},{10,12},{12,14},{14,16},{16,18},{18... | collective-permute-start | bytes 786440 | tf_op jit(solution)/shard_map/ppermute | solution.py:1915
  578.3 6.4 copy-start.33
  578.3 6.4 copy-start.50
  582.7 48.6 %collective-permute-start.17 = (bf16[256,4096]{1,0:T(8,128)(2,1)}, bf16[256,4096]{1,0:T(8,128)(2,1)}, u32[]{:S(2)}, u32[]{:S(2)}) collective-permute-start(bf16[256,4096]{1,0:T(8,128)(2,1)} %add_convert_fusion.1), channel_id=1, source_target_pairs={{0,8},{2,10},{8,16},{10,18},{16,24},{18,26},{24,28},{26,30},{28,20... | collective-permute-start | bytes 6291464 | tf_op jit(solution)/shard_map/ppermute | solution.py:100
  584.3 47.6 %collective-permute-start.18 = (bf16[256,4096]{1,0:T(8,128)(2,1)}, bf16[256,4096]{1,0:T(8,128)(2,1)}, u32[]{:S(2)}, u32[]{:S(2)}) collective-permute-start(bf16[256,4096]{1,0:T(8,128)(2,1)} %add_convert_fusion), channel_id=1, source_target_pairs={{8,0},{10,2},{16,8},{18,10},{24,16},{26,18},{28,24},{30,26},{20,28... | collective-permute-start | bytes 6291464 | tf_op jit(solution)/shard_map/ppermute | solution.py:103
  601.8 26.0 %collective-permute-start.2 = (bf16[256,2048]{1,0:T(8,128)(2,1)}, bf16[256,2048]{1,0:T(8,128)(2,1)}, u32[]{:S(2)}, u32[]{:S(2)}) collective-permute-start(bf16[256,2048]{1,0:T(8,128)(2,1)} %slice.250), channel_id=1, source_target_pairs={{0,1},{1,0},{2,3},{3,2},{4,5},{5,4},{6,7},{7,6},{8,9},{9,8},{10,11... | collective-permute-start | bytes 3145736 | tf_op jit(solution)/shard_map/cond/branch_1_fun/ppermute | solution.py:110
  602.4 3.6 copy-start
  633.0 12.8 %copy-start.9 = (bf16[256,2048]{1,0:T(8,128)(2,1)S(1)}, bf16[256,2048]{1,0:T(8,128)(2,1)}, u32[]{:S(2)}) copy-start(bf16[256,2048]{1,0:T(8,128)(2,1)} %param.57) | copy-start | bytes 3145732
  633.0 14.4 %copy-start.12 = (bf16[2048,64]{1,0:T(8,128)(2,1)S(1)}, bf16[2048,64]{1,0:T(8,128)(2,1)}, u32[]{:S(2)}) copy-start(bf16[2048,64]{1,0:T(8,128)(2,1)} %get-tuple-element.883) | copy-start | bytes 786436
  633.0 14.4 %copy-start.25 = (bf16[2048,64]{1,0:T(8,128)(2,1)S(1)}, bf16[2048,64]{1,0:T(8,128)(2,1)}, u32[]{:S(2)}) copy-start(bf16[2048,64]{1,0:T(8,128)(2,1)} %get-tuple-element.884) | copy-start | bytes 786436
  633.0 14.4 %copy-start.37 = (bf16[256,64]{0,1:T(8,128)(2,1)S(1)}, bf16[256,64]{0,1:T(8,128)(2,1)}, u32[]{:S(2)}) copy-start(bf16[256,64]{0,1:T(8,128)(2,1)} %get-tuple-element.533) | copy-start | bytes 98308
  633.0 14.4 %copy-start.42 = (f32[16,1,128]{2,1,0:T(1,128)S(1)}, f32[16,1,128]{2,1,0:T(1,128)}, u32[]{:S(2)}) copy-start(f32[16,1,128]{2,1,0:T(1,128)} %copy-done.41) | copy-start | bytes 24580
  633.0 14.4 %copy-start.51 = (f32[2048]{0:T(1024)S(1)}, f32[2048]{0:T(1024)}, u32[]{:S(2)}) copy-start(f32[2048]{0:T(1024)} %get-tuple-element.520) | copy-start | bytes 24580
  633.0 14.4 %copy-start.52 = (f32[2048]{0:T(1024)S(1)}, f32[2048]{0:T(1024)}, u32[]{:S(2)}) copy-start(f32[2048]{0:T(1024)} %get-tuple-element.519) | copy-start | bytes 24580
  643.5 3.9 copy-start.2
  643.5 3.9 copy-start.5
  643.5 3.9 copy-start.40
  643.5 47.8 %collective-permute-start.19 = (bf16[256,4096]{1,0:T(8,128)(2,1)}, bf16[256,4096]{1,0:T(8,128)(2,1)}, u32[]{:S(2)}, u32[]{:S(2)}) collective-permute-start(bf16[256,4096]{1,0:T(8,128)(2,1)} %get-tuple-element.441), channel_id=1, source_target_pairs={{0,8},{2,10},{8,16},{10,18},{16,24},{18,26},{24,28},{26,30},{28,20... | collective-permute-start | bytes 6291464 | tf_op jit(solution)/shard_map/ppermute | solution.py:100
  644.1 47.8 %collective-permute-start.20 = (bf16[256,4096]{1,0:T(8,128)(2,1)}, bf16[256,4096]{1,0:T(8,128)(2,1)}, u32[]{:S(2)}, u32[]{:S(2)}) collective-permute-start(bf16[256,4096]{1,0:T(8,128)(2,1)} %get-tuple-element.442), channel_id=1, source_target_pairs={{8,0},{10,2},{16,8},{18,10},{24,16},{26,18},{28,24},{30,26},{20,28... | collective-permute-start | bytes 6291464 | tf_op jit(solution)/shard_map/ppermute | solution.py:103
  654.8 4.6 copy-start.14
  655.3 4.2 copy-start.38
  760.5 3.8 copy-start.28
  768.9 3.8 copy-start.24
  (21 other events, 36.1 us)

commit v6 on v5

--- a/solution.py
+++ b/solution.py
@@ -567,7 +567,7 @@
     )
 
 
-def block_grads(x, d, chips, size, gots=(), tile=1024):
+def block_grads(x, d, chips, size, gots=(), tile=2048):
     (m, _), (groups, _, ff) = x.shape, d.shape
     count = len(chips)
     tile = min(tile, ff)
@@ -595,6 +595,31 @@
         [pltpu.VMEM((size, m), BF16)] * count,
         0,
         "block_grads",
+    )
+
+
+def add_kernel(count, spots, *refs):
+    terms, gots, outs = refs[:count], refs[count : 2 * count], refs[2 * count :]
+    for term, got, out in zip(terms, gots, outs):
+        out[...] = low(to_float(term[...]) + to_float(got[...]))
+
+
+def add_blocks(terms, gots, tile=1024):
+    tall, wide = terms[0].shape
+    tile = min(tile, wide)
+    count = len(terms)
+    block = pl.BlockSpec((tall, tile), lambda f, s: (0, f))
+    return grid_call(
+        functools.partial(add_kernel, count),
+        jnp.zeros((1,), jnp.int32),
+        (wide // tile,),
+        (*terms, *gots),
+        [block] * (2 * count),
+        [jax.ShapeDtypeStruct((tall, wide), BF16)] * count,
+        [block] * count,
+        [],
+        terms[0].size,
+        "add_blocks",
     )
 
 
@@ -1231,10 +1256,7 @@
                 else:
                     came[...] = low(term + to_float(came[...]))
                 source = came
-                if k < half - 2:
-                    target = got.at[direction, k]
-                else:
-                    target = held_up if direction == 0 else held_down
+                target = got.at[direction, k]
             copies[(direction, k)] = begin(
                 remote(source, target, ring_send, ring_recv, (direction, k), ahead)
             )
@@ -1317,8 +1339,14 @@
         copy.wait_recv()
         at = slice(j * size, (j + 1) * size)
         result[:, at] = result[:, at] + to_float(side_got[j])
-    for direction in range(2):
+    for direction, target in ((0, held_up), (1, held_down)):
+        offset = 1 if direction == 0 else -1
+        at = pl.ds(pl.multiple_of(hops.chip_at(offset) * size, size), size)
+        term = product_l(x[:, at], hid[...])
         copies[(direction, half - 2)].wait_recv()
+        came = got.at[direction, half - 2]
+        came[...] = low(term + to_float(came[...]))
+        begin(pltpu.make_async_copy(came, target, stores.at[2 + direction]), saved)
         wide_copies[direction].wait_recv()
     for copy in started:
         copy.wait_send()
@@ -1355,7 +1383,7 @@
             pltpu.VMEM((2, 2, own, ff), BF16),
             pltpu.VMEM((2, 2, size, ff), BF16),
             pltpu.VMEM((2, size // 2, ff), BF16),
-            pltpu.VMEM((2, half - 2, size, ff), BF16),
+            pltpu.VMEM((2, half - 1, size, ff), BF16),
             pltpu.VMEM((chips, 2 * own, size), F32),
             pltpu.VMEM((chips, 2 * own, size), BF16),
             pltpu.VMEM((chips, 2 * own, size), BF16),
@@ -1371,7 +1399,7 @@
             dma((2, chips)),
             dma((2, 2)),
             dma((8 + chips,)),
-            dma((2,)),
+            dma((4,)),
         ],
         compiler_params=pltpu.CompilerParams(
             collective_id=4, has_side_effects=True, vmem_limit_bytes=60 * 2**20
@@ -1589,8 +1617,7 @@
         elif terms is None:
             up, down = self.blocks((half + 1 - k, k - 1 - half), self.held)
         else:
-            up = low(to_float(terms[0]) + to_float(self.held[0]))
-            down = low(to_float(terms[1]) + to_float(self.held[1]))
+            up, down = add_blocks(terms, self.held)
         up, down, beside = tie(up, down, beside)
         self.held = [ring.up(up), ring.down(down)]
         return beside
@@ -1793,7 +1820,18 @@
         )
     )
     query_low = query_low.reshape(all_rows, HD)
-    kv_own = meet([gate_ring], kv_own)
+    kv_own, query_ids, previous_ids, key_ids, *small_parts = meet(
+        [gate_ring],
+        kv_own,
+        query_ids,
+        previous_ids,
+        key_ids,
+        left_full,
+        right_t,
+        lgate_full,
+        lproj_t,
+    )
+    left_full, right_t, lgate_full, lproj_t = small_parts
     kv_before = lax.ppermute(kv_own, "dp", forward_pairs)
     kv_after = lax.ppermute(kv_own[:reach_after], "dp", backward_pairs)
     kv_before, kv_after, more_ring.held, gate_ring.held = tie(
@@ -1864,7 +1902,7 @@
             low(d_ffw_out), hidden_low, raw, dn_whole, gu_weights, ffw_rows
         )
         rd = BlockReduce(ring, d_ffw_rows, hidden_low[None], 2 * rows)
-        rd.held, rd.step_count = held[:2], half - 1
+        rd.held, rd.step_count = [ring.up(held[0]), ring.down(held[1])], half
         rg = BlockReduce(ring, ffw_rows, d_gate_up, 2 * rows)
         rg.held, rg.step_count = held[2:], 1
     else:
@@ -1881,7 +1919,7 @@
         for _ in range(half - 3):
             rg.step()
             meet([rg])
-    rd.step()
+        rd.step()
     rg.step()
 
     def back_34():
@@ -1929,12 +1967,13 @@
             own,
         )
         d_more, ends = sum_sides(
-            product_t(d_qkv_low, qkv_full), lambda: (rd.last_term(), rg.last_term())
+            product_t(d_qkv_low, qkv_full), lambda: (rd.last_term(), rg.last_term(), rg.terms())
         )
         return d_more, ends, d_qkv_low, gain_sums[0], gain_sums[1]
 
     d_more, ends, d_qkv_low, query_scale_grad, key_scale_grad = meet([rg], *region(back_5))
-    rg.step()
+    *ends, terms = ends
+    rg.step(terms)
 
     def head_gain_back(grads):
         padded = jnp.pad(grads.reshape(ring.devices, head_part), ((0, 0), (0, rows - head_part)))

time: 783 us -> 772 us (0.986)
  other arithmetic: 68 us -> 54.8 us
    ppermute x3, waiting for transfers between devices: 40 us -> 28.9 us  [across(): return lax.ppermute(values, 'tensor', [(0, 1), (1, 0)])]
    convert_element_type x9 -> x7, other arithmetic: 23.3 us -> 14.6 us  [low(): return values.astype(BF16)]
    pallas_call x9 -> x10, Pallas kernels: 77.4 us -> 82.5 us  [grid_call(): pl.pallas_call(kernel, grid_spec=pltpu.PrefetchScalarGridSpec(num_scalar_...]
    unnamed x92 -> x104, local copies, waits for them, and re-layouts: 16.8 us -> 16.8 us
  transfers between devices with their start and end apart: 21 -> 21, of which waited for: 11 -> 13; matrix products, arithmetic and copies ran while one was open for 17% -> 15% of each run, Pallas kernels for 7% -> 9%
where the time goes in v6:
time: 772 us; the launch traced here: 765 us
  Pallas kernels  506 us (66%)
  waiting for transfers between devices  66.7 us (9%)
  other arithmetic  54.8 us (7%)
  local copies, waits for them, and re-layouts  52.5 us (7%)
  matrix products  50.4 us (7%)
  starting transfers between devices  32.5 us (4%)
    pallas_call x1, Pallas kernels, forward(): pl.pallas_call(functools.partial(forward_kernel, hops_done, tile), out_sh...  169 us
    pallas_call x1, Pallas kernels, backward(): pl.pallas_call(backward_kernel, out_shape=[jax.ShapeDtypeStruct((m, width...  116 us
    pallas_call x10, Pallas kernels, grid_call(): pl.pallas_call(kernel, grid_spec=pltpu.PrefetchScalarGridSpec(num_scalar_...  82.5 us
    pallas_call x1, Pallas kernels, comm_call(): pl.pallas_call(kernel, out_shape=shapes, in_specs=[ANY] * len(operands),...  69.9 us
    pallas_call x1, Pallas kernels, last_reduce(): pl.pallas_call(functools.partial(last_kernel, large), out_shape=[jax.Shap...  68.4 us
    dot_general x9, matrix products, product_t(): lax.dot_general(left_in, right_in, (((1,), (1,)), ((), ())), preferred_el...  33.5 us
    ppermute x7, waiting for transfers between devices, up(): return lax.ppermute(values, 'dp', self.cw)  30.9 us
    ppermute x3, waiting for transfers between devices, across(): return lax.ppermute(values, 'tensor', [(0, 1), (1, 0)])  28.9 us
  transfers between devices with their start and end apart: 21, of which 13 were waited for; matrix products, arithmetic and copies ran while one was open for 15% of the time, Pallas kernels for 9%

profile of v6, /device:TPU:0, one launch (start us, length us, event | category | flops | bytes accessed | tf_op | source)
XLA Modules:
  0.0 764.6 jit_solution(16734618651658820502)
XLA Ops:
  4.1 69.9 %first_gather.1 = (bf16[2048,1536]{1,0:T(8,128)(2,1)}, bf16[2048,1024]{1,0:T(8,128)(2,1)}, bf16[2048,640]{1,0:T(8,128)(2,1)}, f32[256,128]{1,0:T(8,128)}, bf16[2...) custom-call(bf16[128,1024]{1,0:T(8,128)(2,1)} %refs_0_.1, bf16[128,256]{1,0:T(8,128)(2,1)} %refs_1_.1, ...), custom_call_target="tpu_custom_call" | custom-call | bytes 147324928 | tf_op jit(solution)/shard_map/first_gather/pallas_call | solution.py:314
  82.3 10.0 %conditional.5 = (bf16[512,2048]{1,0:T(8,128)(2,1)}, f32[512,1536]{1,0:T(8,128)}, bf16[512,512]{1,0:T(8,128)(2,1)S(1)}, bf16[2048,256]{1,0:T(8,128)(2,1)}) conditional(s32[]{:T(128)} %convert_element_type.112, () %tuple.60, (s32[]{:T(128)}, f32[16,1,128]{2,1,0:T(1,128)S(1)}, bf16[512,2048]{1,0:T(8,128)(2,1)}, bf16[2048,1536]{1,0:T(8,128)(2,1)}, ...), branch_computations={%region_0.1_spmd, %region_1.2_spmd} | conditional | flops 3221225472 | bytes 15745068 | solution.py:1629
  82.8 9.5 %prepare.1 = (bf16[512,2048]{1,0:T(8,128)(2,1)}, f32[512,1536]{1,0:T(8,128)}, bf16[4,512,256]{2,1,0:T(8,128)(2,1)}, bf16[512,512]{1,0:T(8,128)(2,1)S(1)}) custom-call(s32[2]{0:T(128)} %compare_select_fusion.spots, bf16[512,2048]{1,0:T(8,128)(2,1)} %get-tuple-element.157.x, f32[1,2048]{1,0:T(1,128)S(1)} %bitcast.136, ...), custom_call_target="tpu_custom_call" | custom-call | flops 3221225472 | bytes 15745024 | tf_op jit(solution)/shard_map/cond/branch_1_fun/prepare/pallas_call | solution.py:484
  95.0 5.0 collective-permute-done.3.refs_1_
  103.9 2.8 collective-permute-done.6
  106.7 5.5 collective-permute-start.10
  112.2 2.1 collective-permute-start.9
  114.3 2.0 collective-permute-start.7
  119.4 50.0 %conditional.6 = (f32[4,512,1]{1,0,2:T(4,128)S(1)}, bf16[512,1024]{1,0:T(8,128)(2,1)}, f32[256,2048]{1,0:T(8,128)}, bf16[256,64]{0,1:T(8,128)(2,1)}, f32[256,204...) conditional(s32[]{:T(128)} %convert_element_type.112, () %tuple.59, (s32[512]{0:T(512)S(1)}, ...), branch_computations={%region_4.5_spmd, %region_5.12_spmd} | conditional | flops 5002117120 | bytes 144001344 | solution.py:1629
  119.9 2.6 broadcast_in_dim.55
  127.2 2.1 fusion.3
  130.4 3.6 fusion.77
  134.0 2.0 copy-done.30
  136.2 1.7 collective-permute-start
  138.7 1.8 multiply_reduce_fusion.1
  140.5 21.4 %collective-permute-done = bf16[256,2048]{1,0:T(8,128)(2,1)} collective-permute-done((bf16[256,2048]{1,0:T(8,128)(2,1)S(1)}, bf16[256,2048]{1,0:T(8,128)(2,1)}, u32[]{:S(2)}, u32[]{:S(2)}) %collective-permute-start) | collective-permute-done | bytes 1048608 | tf_op jit(solution)/shard_map/cond/branch_1_fun/ppermute | solution.py:110
  162.0 2.8 multiply_reduce_fusion.2
  164.8 3.3 multiply_reduce_fusion
  169.4 15.6 %collective-permute-done.7.refs_3_ = bf16[256,2048]{1,0:T(8,128)(2,1)} collective-permute-done((bf16[256,2048]{1,0:T(8,128)(2,1)}, bf16[256,2048]{1,0:T(8,128)(2,1)}, u32[]{:S(2)}, u32[]{:S(2)}) %collective-permute-start.7) | collective-permute-done | bytes 1048608 | tf_op jit(solution)/shard_map/ppermute | solution.py:100
  185.0 168.9 %forward.1 = (bf16[1024,2048]{1,0:T(8,128)(2,1)}, bf16[2,2048,2048]{2,1,0:T(8,128)(2,1)}, bf16[2,2048,2048]{2,1,0:T(8,128)(2,1)}, bf16[2048,2048]{1,0:T(8,128)(2...) custom-call(bf16[256,2048]{1,0:T(8,128)(2,1)} %get-tuple-element.411.x_own, ...), custom_call_target="tpu_custom_call" | custom-call | flops 25769803776 | tf_op jit(solution)/shard_map/forward/pallas_call | solution.py:1121
  353.9 2.0 multiply_reduce_fusion.18
  360.1 3.2 add_convert_fusion
  366.9 116.0 %backward.1 = (bf16[1024,2048]{1,0:T(8,128)(2,1)}, bf16[2,1024,2048]{2,1,0:T(8,128)(2,1)}, bf16[256,2048]{1,0:T(8,128)(2,1)}, bf16[256,2048]{1,0:T(8,128)(2,1)},...) custom-call(bf16[256,2048]{1,0:T(8,128)(2,1)} %fusion.51.d_own, ...), custom_call_target="tpu_custom_call" | custom-call | flops 25769803776 | tf_op jit(solution)/shard_map/backward/pallas_call | solution.py:1365
  483.0 10.3 %block_grads.9 = (bf16[256,4096]{1,0:T(8,128)(2,1)}, bf16[256,4096]{1,0:T(8,128)(2,1)}) custom-call(s32[2]{0:T(128)} %pad_add_fusion.4.spots, bf16[1024,2048]{1,0:T(8,128)(2,1)} %get-tuple-element.419.rows_in.refs_0_.refs_1_, bf16[1024,2048]{1,0:T(8,128)(2,1)} %get-tuple-element.419.rows_in.refs_0_.refs_1_, ...), custom_call_target="tpu_custom_call" | custom-call | tf_op jit(solution)/shard_map/block_grads/pallas_call | solution.py:484
  497.3 63.0 %conditional.7 = (bf16[256,4096]{1,0:T(8,128)(2,1)}, bf16[256,4096]{1,0:T(8,128)(2,1)}, bf16[512,512]{0,1:T(8,128)(2,1)S(1)}, bf16[256,512]{0,1:T(8,128)(2,1)S(1...) conditional(s32[]{:T(128)} %convert_element_type.112, () %tuple.66, ...), branch_computations={%region_16.17_spmd, %region_17.25_spmd} | conditional | flops 8914598912 | bytes 216835824 | solution.py:1629
  497.5 2.9 multiply_reduce_fusion.5
  500.4 4.6 multiply_reduce_fusion.4
  505.0 2.0 fusion.25
  509.0 9.4 %block_grads.5 = (bf16[256,4096]{1,0:T(8,128)(2,1)}, bf16[256,4096]{1,0:T(8,128)(2,1)}) custom-call(s32[2]{0:T(128)} %pad_add_fusion.spots, bf16[1024,2048]{1,0:T(8,128)(2,1)} %get-tuple-element.187.refs_0_.refs_1_, bf16[1024,2048]{1,0:T(8,128)(2,1)} %get-tuple-element.187.refs_0_.refs_1_, bf16[2,1024,2048]{2,1,0:T(8,128)(2,1)} %get-tuple-element.188.refs_2_), custom_call_target="tpu_custom_call" | custom-call | tf_op jit(solution)/shard_map/cond/branch_1_fun/block_grads/pallas_call | solution.py:484
  519.0 5.6 fusion.33
  524.5 4.3 collective-permute-done.1
  531.8 5.0 convolution_convert_fusion.1
  536.8 2.4 copy.119
  539.2 8.1 %multiply_reduce_fusion.3 = (f32[4,512]{1,0:T(4,128)S(1)}, f32[4,512,1280]{2,1,0:T(8,128)S(1)}) fusion(f32[4,512,1280]{2,1,0:T(8,128)} %bitcast.116, f32[4,512]{1,0:T(4,128)S(1)} %bitcast.144, pred[512,1280]{1,0:T(8,128)(4,1)S(1)} %compare_or_fusion.1, bf16[4,512,256]{1,2,0:T(8,128)(2,1)} %bitcast.124, bf16[1280,512]{1,0:T(8,128)(2,1)} %get-tuple-element.197), kind=kOutput, calls=%fused_computation.36 | convolution fusion | flops 1352660992 | bytes 23347200 | tf_op jit(solution)/shard_map/cond/branch_1_fun/dot_general | solution.py:65
  547.4 2.5 fusion.20
  549.9 3.2 multiply_convert_fusion.1
  553.2 1.6 fusion.78
  557.3 3.0 fusion.27
  565.5 4.0 collective-permute-start.16
  569.5 5.9 add_blocks.2
  577.8 44.5 %conditional.8 = (f32[256,2048]{1,0:T(8,128)}, bf16[256,2048]{1,0:T(8,128)(2,1)}, bf16[256,4096]{1,0:T(8,128)(2,1)}, bf16[256,4096]{1,0:T(8,128)(2,1)}, bf16[256...) conditional(s32[]{:T(128)} %convert_element_type.112, () %tuple.70, ...), branch_computations={%region_25.26_spmd, %region_26.27_spmd} | conditional | flops 3230138368 | bytes 68440800 | solution.py:1629
  577.8 2.5 copy.110.d_kv
  580.9 5.4 prepare_back.1
  586.4 6.0 fusion.76
  592.4 2.0 copy-done.29
  596.3 9.3 %block_grads.8 = (bf16[256,4096]{1,0:T(8,128)(2,1)}, bf16[256,4096]{1,0:T(8,128)(2,1)}) custom-call(s32[2]{0:T(128)} %pad_add_fusion.2.spots, bf16[1024,2048]{1,0:T(8,128)(2,1)} %get-tuple-element.215.refs_0_.refs_1_, bf16[1024,2048]{1,0:T(8,128)(2,1)} %get-tuple-element.215.refs_0_.refs_1_, bf16[2,1024,2048]{2,1,0:T(8,128)(2,1)} %get-tuple-element.216.refs_1_.refs_2_), custom_call_target="tpu_custom_call" | custom-call | tf_op jit(solution)/shard_map/cond/branch_1_fun/block_grads/pallas_call | solution.py:484
  605.5 6.3 block_grads.7
  611.8 3.3 block_grads.6
  615.9 3.1 collective-permute-done.2
  619.0 3.3 slice_add_fusion.1
  623.3 1.7 collective-permute-done.18.refs_3_
  625.1 6.8 add_blocks.3
  634.4 37.4 %conditional.9 = (f32[256,2048]{1,0:T(8,128)}, f32[1024,3328]{1,0:T(8,128)}, bf16[1024,3328]{1,0:T(8,128)(2,1)}) conditional(s32[]{:T(128)} %convert_element_type.112, () %tuple.73, (f32[16,1,128]{2,1,0:T(1,128)S(1)}, f32[256,2048]{1,0:T(8,128)}, f32[256,2048]{1,0:T(8,128)}, bf16[2048,64]{1,0:T(8,128)(2,1)S(1)}, bf16[2048,64]{1,0:T(8,128)(2,1)}, ...), branch_computations={%region_29.30_spmd, %region_30.37_spmd.clone} | conditional | flops 6194473984 | bytes 90691848 | solution.py:1629
  634.4 1.8 multiply_reduce_fusion.14
  636.2 2.7 multiply_reduce_fusion.12
  639.0 2.9 fusion.44
  642.4 5.4 fusion.43
  651.9 16.3 %row_grads.1 = (f32[1024,3328]{1,0:T(8,128)}, bf16[1024,3328]{1,0:T(8,128)(2,1)}) custom-call(s32[1]{0:T(128)} %bitcast.53.spots, bf16[512,2048]{1,0:T(8,128)(2,1)} %get-tuple-element.516.refs_0_, bf16[512,2048]{1,0:T(8,128)(2,1)} %get-tuple-element.517.refs_1_, bf16[256,2048]{1,0:T(8,128)(2,1)S(1)} %copy-done.38, ...), custom_call_target="tpu_custom_call" | custom-call | flops 6039797760 | bytes 32833536 | tf_op jit(solution)/shard_map/cond/branch_1_fun/row_grads/pallas_call | solution.py:484
  668.3 3.5 fusion.45
  671.8 8.2 %collective-permute-done.19.refs_3_ = bf16[256,4096]{1,0:T(8,128)(2,1)} collective-permute-done((bf16[256,4096]{1,0:T(8,128)(2,1)}, bf16[256,4096]{1,0:T(8,128)(2,1)}, u32[]{:S(2)}, u32[]{:S(2)}) %collective-permute-start.19) | collective-permute-done | bytes 2097184 | tf_op jit(solution)/shard_map/ppermute | solution.py:100
  680.0 68.4 %last_reduce.1 = (f32[128,2560]{1,0:T(8,128)}, f32[128,768]{1,0:T(8,128)}, f32[128,4096]{1,0:T(8,128)}, f32[128,4096]{1,0:T(8,128)}, f32[128,4096]{1,0:T(8,128)}) custom-call(f32[1024,3328]{1,0:T(8,128)} %get-tuple-element.486.refs_0_, bf16[1024,3328]{1,0:T(8,128)(2,1)} %get-tuple-element.487.refs_1_, bf16[256,4096]{1,0:T(8,128)(2,1)} %get-tuple-element.488.refs_2_, ...), custom_call_target="tpu_custom_call" | custom-call | bytes 272629760 | tf_op jit(solution)/shard_map/last_reduce/pallas_call | solution.py:879
  748.5 2.1 slice_bitcast_fusion
  750.6 1.7 fusion.74
  754.6 3.0 copy.115
  (277 shorter events, 78.1 us)
Async XLA Ops:
  4.1 74.2 %copy-start.62 = (s32[1,64,64]{2,1,0:T(8,128)S(1)}, s32[1,64,64]{2,1,0:T(8,128)}, u32[]{:S(2)}) copy-start(s32[1,64,64]{2,1,0:T(8,128)} %param.37) | copy-start | bytes 49156
  74.1 25.9 %collective-permute-start.3 = (bf16[256,2048]{1,0:T(8,128)(2,1)}, bf16[256,2048]{1,0:T(8,128)(2,1)}, u32[]{:S(2)}, u32[]{:S(2)}) collective-permute-start(bf16[256,2048]{1,0:T(8,128)(2,1)} %get-tuple-element.386.refs_0_), channel_id=1, source_target_pairs={{0,8},{2,10},{8,16},{10,18},{16,24},{18,26},{24,28},{26,30},{28,20... | collective-permute-start | bytes 3145736 | tf_op jit(solution)/shard_map/ppermute | solution.py:100
  75.7 25.6 %collective-permute-start.4 = (bf16[256,2048]{1,0:T(8,128)(2,1)}, bf16[256,2048]{1,0:T(8,128)(2,1)}, u32[]{:S(2)}, u32[]{:S(2)}) collective-permute-start(bf16[256,2048]{1,0:T(8,128)(2,1)} %get-tuple-element.386.refs_0_), channel_id=1, source_target_pairs={{8,0},{10,2},{16,8},{18,10},{24,16},{26,18},{28,24},{30,26},{20,28... | collective-permute-start | bytes 3145736 | tf_op jit(solution)/shard_map/ppermute | solution.py:103
  78.3 40.0 %copy-start.46 = (f32[16,1,128]{2,1,0:T(1,128)}, f32[16,1,128]{2,1,0:T(1,128)S(1)}, u32[]{:S(2)}) copy-start(f32[16,1,128]{2,1,0:T(1,128)S(1)} %get-tuple-element.927) | copy-start | bytes 24580
  78.3 40.0 %copy-start.48 = (f32[16,1,128]{2,1,0:T(1,128)}, f32[16,1,128]{2,1,0:T(1,128)S(1)}, u32[]{:S(2)}) copy-start(f32[16,1,128]{2,1,0:T(1,128)S(1)} %get-tuple-element.930) | copy-start | bytes 24580
  78.3 40.0 %copy-start.54 = (f32[16,1,128]{2,1,0:T(1,128)}, f32[16,1,128]{2,1,0:T(1,128)S(1)}, u32[]{:S(2)}) copy-start(f32[16,1,128]{2,1,0:T(1,128)S(1)} %get-tuple-element.928) | copy-start | bytes 24580
  80.2 38.2 %copy-start.58 = (s32[512]{0:T(512)}, s32[512]{0:T(512)S(1)}, u32[]{:S(2)}) copy-start(s32[512]{0:T(512)S(1)} %add_select_fusion.1) | copy-start | bytes 6148
  80.3 38.1 %copy-start.63 = (s32[512]{0:T(512)}, s32[512]{0:T(512)S(1)}, u32[]{:S(2)}) copy-start(s32[512]{0:T(512)S(1)} %add_select_fusion) | copy-start | bytes 6148
  80.5 37.9 %copy-start.56 = (s32[1280]{0:T(1024)}, s32[1280]{0:T(1024)S(1)}, u32[]{:S(2)}) copy-start(s32[1280]{0:T(1024)S(1)} %pad_add_fusion.3) | copy-start | bytes 15364
  81.5 10.8 %copy-start.24 = (bf16[2048,640]{1,0:T(8,128)(2,1)S(1)}, bf16[2048,640]{1,0:T(8,128)(2,1)}, u32[]{:S(2)}) copy-start(bf16[2048,640]{1,0:T(8,128)(2,1)} %get-tuple-element.391) | copy-start | bytes 7864324
  92.3 10.3 %copy-start.25 = (bf16[512,512]{1,0:T(8,128)(2,1)}, bf16[512,512]{1,0:T(8,128)(2,1)S(1)}, u32[]{:S(2)}) copy-start(bf16[512,512]{1,0:T(8,128)(2,1)S(1)} %get-tuple-element.395) | copy-start | bytes 1572868
  95.0 23.3 %copy-start = (bf16[256,2048]{1,0:T(8,128)(2,1)S(1)}, bf16[256,2048]{1,0:T(8,128)(2,1)}, u32[]{:S(2)}) copy-start(bf16[256,2048]{1,0:T(8,128)(2,1)} %refs_12_.1) | copy-start | bytes 3145732
  101.3 5.5 collective-permute-start.5
  102.6 4.1 collective-permute-start.6
  106.7 78.2 %collective-permute-start.10 = (bf16[256,4096]{1,0:T(8,128)(2,1)}, bf16[256,4096]{1,0:T(8,128)(2,1)}, u32[]{:S(2)}, u32[]{:S(2)}) collective-permute-start(bf16[256,4096]{1,0:T(8,128)(2,1)} %get-tuple-element.409.refs_5_), channel_id=1, source_target_pairs={{8,0},{10,2},{16,8},{18,10},{24,16},{26,18},{28,24},{30,26},{20,28... | collective-permute-start | bytes 6291464 | tf_op jit(solution)/shard_map/ppermute | solution.py:103
  112.2 72.7 %collective-permute-start.9 = (bf16[256,4096]{1,0:T(8,128)(2,1)}, bf16[256,4096]{1,0:T(8,128)(2,1)}, u32[]{:S(2)}, u32[]{:S(2)}) collective-permute-start(bf16[256,4096]{1,0:T(8,128)(2,1)} %get-tuple-element.409.refs_5_), channel_id=1, source_target_pairs={{0,8},{2,10},{8,16},{10,18},{16,24},{18,26},{24,28},{26,30},{28,20... | collective-permute-start | bytes 6291464 | tf_op jit(solution)/shard_map/ppermute | solution.py:100
  114.3 70.7 %collective-permute-start.7 = (bf16[256,2048]{1,0:T(8,128)(2,1)}, bf16[256,2048]{1,0:T(8,128)(2,1)}, u32[]{:S(2)}, u32[]{:S(2)}) collective-permute-start(bf16[256,2048]{1,0:T(8,128)(2,1)} %collective-permute-done.3.refs_1_), channel_id=1, source_target_pairs={{0,8},{2,10},{8,16},{10,18},{16,24},{18,26},{24,28},{26,30},{28,20... | collective-permute-start | bytes 3145736 | tf_op jit(solution)/shard_map/ppermute | solution.py:100
  116.3 68.6 %collective-permute-start.8 = (bf16[256,2048]{1,0:T(8,128)(2,1)}, bf16[256,2048]{1,0:T(8,128)(2,1)}, u32[]{:S(2)}, u32[]{:S(2)}) collective-permute-start(bf16[256,2048]{1,0:T(8,128)(2,1)} %collective-permute-done.4.refs_2_), channel_id=1, source_target_pairs={{8,0},{10,2},{16,8},{18,10},{24,16},{26,18},{28,24},{30,26},{20,28... | collective-permute-start | bytes 3145736 | tf_op jit(solution)/shard_map/ppermute | solution.py:103
  136.2 25.8 %collective-permute-start = (bf16[256,2048]{1,0:T(8,128)(2,1)S(1)}, bf16[256,2048]{1,0:T(8,128)(2,1)}, u32[]{:S(2)}, u32[]{:S(2)}) collective-permute-start(bf16[256,2048]{1,0:T(8,128)(2,1)S(1)} %slice.241), channel_id=1, source_target_pairs={{0,1},{1,0},{2,3},{3,2},{4,5},{5,4},{6,7},{7,6},{8,9},{9,8},{10,11... | collective-permute-start | bytes 3145736 | tf_op jit(solution)/shard_map/cond/branch_1_fun/ppermute | solution.py:110
  138.2 23.8 %copy-start.31 = (f32[512,2048]{1,0:T(8,128)S(1)}, f32[512,2048]{1,0:T(8,128)}, u32[]{:S(2)}) copy-start(f32[512,2048]{1,0:T(8,128)} %copy-done.30) | copy-start | bytes 12582916 | tf_op jit(solution)/shard_map/cond
  138.7 26.1 %copy-start.43 = (bf16[256,64]{0,1:T(8,128)(2,1)}, bf16[256,64]{0,1:T(8,128)(2,1)S(1)}, u32[]{:S(2)}) copy-start(bf16[256,64]{0,1:T(8,128)(2,1)S(1)} %convolution_convert_fusion) | copy-start | bytes 98308 | tf_op jit(solution)/shard_map/cond
  356.5 3.6 copy-start.6
  482.9 14.4 %copy-start.3 = (f32[256,2048]{1,0:T(8,128)S(1)}, f32[256,2048]{1,0:T(8,128)}, u32[]{:S(2)}) copy-start(f32[256,2048]{1,0:T(8,128)} %copy-done.2) | copy-start | bytes 6291460
  482.9 14.4 %copy-start.12 = (f32[256,2048]{1,0:T(8,128)S(1)}, f32[256,2048]{1,0:T(8,128)}, u32[]{:S(2)}) copy-start(f32[256,2048]{1,0:T(8,128)} %get-tuple-element.427) | copy-start | bytes 6291460
  482.9 14.4 %copy-start.55 = (f32[16,1,128]{2,1,0:T(1,128)S(1)}, f32[16,1,128]{2,1,0:T(1,128)}, u32[]{:S(2)}) copy-start(f32[16,1,128]{2,1,0:T(1,128)} %copy-done.54) | copy-start | bytes 24580
  493.2 69.1 %collective-permute-start.13 = (bf16[256,4096]{1,0:T(8,128)(2,1)}, bf16[256,4096]{1,0:T(8,128)(2,1)}, u32[]{:S(2)}, u32[]{:S(2)}) collective-permute-start(bf16[256,4096]{1,0:T(8,128)(2,1)} %get-tuple-element.425), channel_id=1, source_target_pairs={{0,8},{2,10},{8,16},{10,18},{16,24},{18,26},{24,28},{26,30},{28,20... | collective-permute-start | bytes 6291464 | tf_op jit(solution)/shard_map/ppermute | solution.py:100
  494.8 67.6 %collective-permute-start.14 = (bf16[256,4096]{1,0:T(8,128)(2,1)}, bf16[256,4096]{1,0:T(8,128)(2,1)}, u32[]{:S(2)}, u32[]{:S(2)}) collective-permute-start(bf16[256,4096]{1,0:T(8,128)(2,1)} %get-tuple-element.426), channel_id=1, source_target_pairs={{8,0},{10,2},{16,8},{18,10},{24,16},{26,18},{28,24},{30,26},{20,28... | collective-permute-start | bytes 6291464 | tf_op jit(solution)/shard_map/ppermute | solution.py:103
  495.3 66.1 %collective-permute-start.11 = (bf16[256,2048]{1,0:T(8,128)(2,1)}, bf16[256,2048]{1,0:T(8,128)(2,1)}, u32[]{:S(2)}, u32[]{:S(2)}) collective-permute-start(bf16[256,2048]{1,0:T(8,128)(2,1)} %get-tuple-element.420), channel_id=1, source_target_pairs={{0,8},{2,10},{8,16},{10,18},{16,24},{18,26},{24,28},{26,30},{28,20... | collective-permute-start | bytes 3145736 | tf_op jit(solution)/shard_map/ppermute | solution.py:100
  496.8 65.5 %collective-permute-start.12 = (bf16[256,2048]{1,0:T(8,128)(2,1)}, bf16[256,2048]{1,0:T(8,128)(2,1)}, u32[]{:S(2)}, u32[]{:S(2)}) collective-permute-start(bf16[256,2048]{1,0:T(8,128)(2,1)} %get-tuple-element.421), channel_id=1, source_target_pairs={{8,0},{10,2},{16,8},{18,10},{24,16},{26,18},{28,24},{30,26},{20,28... | collective-permute-start | bytes 3145736 | tf_op jit(solution)/shard_map/ppermute | solution.py:103
  507.1 21.8 %collective-permute-start.1 = (bf16[256,2048]{1,0:T(8,128)(2,1)S(1)}, bf16[256,2048]{1,0:T(8,128)(2,1)S(1)}, u32[]{:S(2)}, u32[]{:S(2)}) collective-permute-start(bf16[256,2048]{1,0:T(8,128)(2,1)S(1)} %fusion.25), channel_id=1, source_target_pairs={{0,1},{1,0},{2,3},{3,2},{4,5},{5,4},{6,7},{7,6},{8,9},{9,8},{10,11... | collective-permute-start | bytes 3145736 | tf_op jit(solution)/shard_map/cond/branch_1_fun/ppermute | solution.py:110
  509.0 9.4 %copy-start.57 = (s32[1280]{0:T(1024)S(1)}, s32[1280]{0:T(1024)}, u32[]{:S(2)}) copy-start(s32[1280]{0:T(1024)} %get-tuple-element.194) | copy-start | bytes 15364 | tf_op jit(solution)/shard_map/cond
  509.0 9.4 %copy-start.59 = (s32[512]{0:T(512)S(1)}, s32[512]{0:T(512)}, u32[]{:S(2)}) copy-start(s32[512]{0:T(512)} %get-tuple-element.193) | copy-start | bytes 6148 | tf_op jit(solution)/shard_map/cond
  509.0 9.4 %copy-start.64 = (s32[512]{0:T(512)S(1)}, s32[512]{0:T(512)}, u32[]{:S(2)}) copy-start(s32[512]{0:T(512)} %get-tuple-element.195) | copy-start | bytes 6148 | tf_op jit(solution)/shard_map/cond
  509.0 9.9 %copy-start.15 = (bf16[2048,256]{1,0:T(8,128)(2,1)S(1)}, bf16[2048,256]{1,0:T(8,128)(2,1)}, u32[]{:S(2)}) copy-start(bf16[2048,256]{1,0:T(8,128)(2,1)} %get-tuple-element.196) | copy-start | bytes 3145732 | tf_op jit(solution)/shard_map/cond
  509.0 9.9 %copy-start.27 = (bf16[1280,512]{1,0:T(8,128)(2,1)S(1)}, bf16[1280,512]{1,0:T(8,128)(2,1)}, u32[]{:S(2)}) copy-start(bf16[1280,512]{1,0:T(8,128)(2,1)} %get-tuple-element.197) | copy-start | bytes 3932164 | tf_op jit(solution)/shard_map/cond
  536.8 10.6 %slice-start = ((s8[10485760]{0:T(1024)(128)(4,1)}), s8[2097152]{0:T(1024)(128)(4,1)S(1)}, s32[]{:S(2)}) async-start(s8[10485760]{0:T(1024)(128)(4,1)} %bitcast.117), calls=%async_computation | async-start | bytes 4194304 | tf_op jit(solution)/shard_map/cond
  539.2 8.2 %slice-start.1 = ((s8[10485760]{0:T(1024)(128)(4,1)}), s8[4194304]{0:T(1024)(128)(4,1)S(1)}, s32[]{:S(2)}) async-start(s8[10485760]{0:T(1024)(128)(4,1)} %bitcast.117), calls=%async_computation.1 | async-start | bytes 8388608 | tf_op jit(solution)/shard_map/cond
  539.2 8.2 %slice-start.2 = ((s8[10485760]{0:T(1024)(128)(4,1)}), s8[4194304]{0:T(1024)(128)(4,1)S(1)}, s32[]{:S(2)}) async-start(s8[10485760]{0:T(1024)(128)(4,1)} %bitcast.117), calls=%async_computation.2 | async-start | bytes 8388608 | tf_op jit(solution)/shard_map/cond
  539.2 8.2 %copy-start.21 = (bf16[512,1024]{0,1:T(8,128)(2,1)S(1)}, bf16[512,1024]{0,1:T(8,128)(2,1)}, u32[]{:S(2)}) copy-start(bf16[512,1024]{0,1:T(8,128)(2,1)} %copy.119) | copy-start | bytes 3145732 | tf_op jit(solution)/shard_map/cond
  563.4 12.0 %collective-permute-start.15 = (bf16[512,512]{1,0:T(8,128)(2,1)}, bf16[512,512]{1,0:T(8,128)(2,1)}, u32[]{:S(2)}, u32[]{:S(2)}) collective-permute-start(bf16[512,512]{1,0:T(8,128)(2,1)} %copy.108), channel_id=1, source_target_pairs={{2,0},{4,2},{6,4},{8,6},{10,8},{12,10},{14,12},{16,14},{18,16},{20... | collective-permute-start | bytes 1572872 | tf_op jit(solution)/shard_map/ppermute | solution.py:1952
  565.5 12.3 %copy-start.10 = (f32[512,1536]{1,0:T(8,128)S(1)}, f32[512,1536]{1,0:T(8,128)}, u32[]{:S(2)}) copy-start(f32[512,1536]{1,0:T(8,128)} %get-tuple-element.450) | copy-start | bytes 9437188
  565.5 12.3 %copy-start.41 = (f32[512,128]{1,0:T(8,128)S(1)}, f32[512,128]{1,0:T(8,128)}, u32[]{:S(2)}) copy-start(f32[512,128]{1,0:T(8,128)} %copy-done.40) | copy-start | bytes 786436
  565.5 12.3 %copy-start.61 = (f32[8,256]{1,0:T(8,128)S(1)}, f32[8,256]{1,0:T(8,128)}, u32[]{:S(2)}) copy-start(f32[8,256]{1,0:T(8,128)} %copy-done.60) | copy-start | bytes 24580
  565.5 9.9 %collective-permute-start.16 = (bf16[256,512]{1,0:T(8,128)(2,1)}, bf16[256,512]{1,0:T(8,128)(2,1)}, u32[]{:S(2)}, u32[]{:S(2)}) collective-permute-start(bf16[256,512]{1,0:T(8,128)(2,1)} %copy.109), channel_id=1, source_target_pairs={{0,2},{2,4},{4,6},{6,8},{8,10},{10,12},{12,14},{14,16},{16,18},{18... | collective-permute-start | bytes 786440 | tf_op jit(solution)/shard_map/ppermute | solution.py:1953
  575.4 47.9 %collective-permute-start.17 = (bf16[256,4096]{1,0:T(8,128)(2,1)}, bf16[256,4096]{1,0:T(8,128)(2,1)}, u32[]{:S(2)}, u32[]{:S(2)}) collective-permute-start(bf16[256,4096]{1,0:T(8,128)(2,1)} %get-tuple-element.448), channel_id=1, source_target_pairs={{0,8},{2,10},{8,16},{10,18},{16,24},{18,26},{24,28},{26,30},{28,20... | collective-permute-start | bytes 6291464 | tf_op jit(solution)/shard_map/ppermute | solution.py:100
  576.2 48.8 %collective-permute-start.18 = (bf16[256,4096]{1,0:T(8,128)(2,1)}, bf16[256,4096]{1,0:T(8,128)(2,1)}, u32[]{:S(2)}, u32[]{:S(2)}) collective-permute-start(bf16[256,4096]{1,0:T(8,128)(2,1)} %get-tuple-element.449), channel_id=1, source_target_pairs={{8,0},{10,2},{16,8},{18,10},{24,16},{26,18},{28,24},{30,26},{20,28... | collective-permute-start | bytes 6291464 | tf_op jit(solution)/shard_map/ppermute | solution.py:103
  594.5 24.5 %collective-permute-start.2 = (bf16[256,2048]{1,0:T(8,128)(2,1)S(1)}, bf16[256,2048]{1,0:T(8,128)(2,1)S(1)}, u32[]{:S(2)}, u32[]{:S(2)}) collective-permute-start(bf16[256,2048]{1,0:T(8,128)(2,1)S(1)} %slice.242), channel_id=1, source_target_pairs={{0,1},{1,0},{2,3},{3,2},{4,5},{5,4},{6,7},{7,6},{8,9},{9,8},{10,11... | collective-permute-start | bytes 3145736 | tf_op jit(solution)/shard_map/cond/branch_1_fun/ppermute | solution.py:110
  605.5 6.3 copy-start.19
  625.0 9.0 %copy-start.9 = (bf16[256,2048]{1,0:T(8,128)(2,1)S(1)}, bf16[256,2048]{1,0:T(8,128)(2,1)}, u32[]{:S(2)}) copy-start(bf16[256,2048]{1,0:T(8,128)(2,1)} %param.57) | copy-start | bytes 3145732
  625.0 9.3 %copy-start.7 = (f32[256,2048]{1,0:T(8,128)S(1)}, f32[256,2048]{1,0:T(8,128)}, u32[]{:S(2)}) copy-start(f32[256,2048]{1,0:T(8,128)} %copy-done.6) | copy-start | bytes 6291460
  625.0 9.3 %copy-start.13 = (f32[256,2048]{1,0:T(8,128)S(1)}, f32[256,2048]{1,0:T(8,128)}, u32[]{:S(2)}) copy-start(f32[256,2048]{1,0:T(8,128)} %get-tuple-element.892) | copy-start | bytes 6291460
  625.0 9.3 %copy-start.17 = (bf16[2048,64]{1,0:T(8,128)(2,1)S(1)}, bf16[2048,64]{1,0:T(8,128)(2,1)}, u32[]{:S(2)}) copy-start(bf16[2048,64]{1,0:T(8,128)(2,1)} %get-tuple-element.540) | copy-start | bytes 786436
  625.1 9.3 %copy-start.44 = (bf16[256,64]{0,1:T(8,128)(2,1)S(1)}, bf16[256,64]{0,1:T(8,128)(2,1)}, u32[]{:S(2)}) copy-start(bf16[256,64]{0,1:T(8,128)(2,1)} %get-tuple-element.560) | copy-start | bytes 98308
  625.1 9.3 %copy-start.49 = (f32[16,1,128]{2,1,0:T(1,128)S(1)}, f32[16,1,128]{2,1,0:T(1,128)}, u32[]{:S(2)}) copy-start(f32[16,1,128]{2,1,0:T(1,128)} %copy-done.48) | copy-start | bytes 24580
  625.1 9.3 %copy-start.51 = (bf16[256,256]{1,0:T(8,128)(2,1)S(1)}, bf16[256,256]{1,0:T(8,128)(2,1)}, u32[]{:S(2)}) copy-start(bf16[256,256]{1,0:T(8,128)(2,1)} %copy-done.50) | copy-start | bytes 393220
  625.1 9.3 %copy-start.53 = (bf16[256,256]{1,0:T(8,128)(2,1)S(1)}, bf16[256,256]{1,0:T(8,128)(2,1)}, u32[]{:S(2)}) copy-start(bf16[256,256]{1,0:T(8,128)(2,1)} %copy-done.52) | copy-start | bytes 393220
  632.0 48.0 %collective-permute-start.19 = (bf16[256,4096]{1,0:T(8,128)(2,1)}, bf16[256,4096]{1,0:T(8,128)(2,1)}, u32[]{:S(2)}, u32[]{:S(2)}) collective-permute-start(bf16[256,4096]{1,0:T(8,128)(2,1)} %get-tuple-element.468), channel_id=1, source_target_pairs={{0,8},{2,10},{8,16},{10,18},{16,24},{18,26},{24,28},{26,30},{28,20... | collective-permute-start | bytes 6291464 | tf_op jit(solution)/shard_map/ppermute | solution.py:100
  632.7 47.3 %collective-permute-start.20 = (bf16[256,4096]{1,0:T(8,128)(2,1)}, bf16[256,4096]{1,0:T(8,128)(2,1)}, u32[]{:S(2)}, u32[]{:S(2)}) collective-permute-start(bf16[256,4096]{1,0:T(8,128)(2,1)} %get-tuple-element.469), channel_id=1, source_target_pairs={{8,0},{10,2},{16,8},{18,10},{24,16},{26,18},{28,24},{30,26},{20,28... | collective-permute-start | bytes 6291464 | tf_op jit(solution)/shard_map/ppermute | solution.py:103
  641.9 5.9 copy-start.20
  642.3 5.4 copy-start.45
  651.9 16.3 %copy-start.65 = (f32[256]{0:T(256)S(1)}, f32[256]{0:T(256)}, u32[]{:S(2)}) copy-start(f32[256]{0:T(256)} %get-tuple-element.871) | copy-start | bytes 3076 | tf_op jit(solution)/shard_map/cond
  651.9 16.4 %copy-start.11 = (f32[256,2048]{1,0:T(8,128)S(1)}, f32[256,2048]{1,0:T(8,128)}, u32[]{:S(2)}) copy-start(f32[256,2048]{1,0:T(8,128)} %get-tuple-element.898) | copy-start | bytes 6291460 | tf_op jit(solution)/shard_map/cond
  748.5 3.8 copy-start.36
  754.6 6.2 copy-start.33
  (33 other events, 65.5 us)

commit v7 on v6

--- a/solution.py
+++ b/solution.py
@@ -604,7 +604,7 @@
         out[...] = low(to_float(term[...]) + to_float(got[...]))
 
 
-def add_blocks(terms, gots, tile=1024):
+def add_blocks(terms, gots, tile=2048):
     tall, wide = terms[0].shape
     tile = min(tile, wide)
     count = len(terms)
@@ -1173,7 +1173,7 @@
     size, ff = held_up.shape
     cut = size // 2
     m = x.shape[0]
-    cols = min(512, ff)
+    cols = min(1024, ff)
     greet([hops.above, hops.below, hops.partner, hops.across])
     started, saved = [], []
 

time: 772 us -> 770 us (level)
  transfers between devices with their start and end apart: 21 -> 21, of which waited for: 13 -> 13; matrix products, arithmetic and copies ran while one was open for 15% -> 15% of each run, Pallas kernels for 9% -> 8%
where the time goes in v7:
time: 770 us; the launch traced here: 762 us
  Pallas kernels  504 us (65%)
  waiting for transfers between devices  66.7 us (9%)
  other arithmetic  54.6 us (7%)
  local copies, waits for them, and re-layouts  52.5 us (7%)
  matrix products  50.4 us (7%)
  starting transfers between devices  32.9 us (4%)
    pallas_call x1, Pallas kernels, forward(): pl.pallas_call(functools.partial(forward_kernel, hops_done, tile), out_sh...  169 us
    pallas_call x1, Pallas kernels, backward(): pl.pallas_call(backward_kernel, out_shape=[jax.ShapeDtypeStruct((m, width...  116 us
    pallas_call x10, Pallas kernels, grid_call(): pl.pallas_call(kernel, grid_spec=pltpu.PrefetchScalarGridSpec(num_scalar_...  80.3 us
    pallas_call x1, Pallas kernels, comm_call(): pl.pallas_call(kernel, out_shape=shapes, in_specs=[ANY] * len(operands),...  69.9 us
    pallas_call x1, Pallas kernels, last_reduce(): pl.pallas_call(functools.partial(last_kernel, large), out_shape=[jax.Shap...  68.4 us
    dot_general x9, matrix products, product_t(): lax.dot_general(left_in, right_in, (((1,), (1,)), ((), ())), preferred_el...  33.5 us
    ppermute x7, waiting for transfers between devices, up(): return lax.ppermute(values, 'dp', self.cw)  30.7 us
    ppermute x3, waiting for transfers between devices, across(): return lax.ppermute(values, 'tensor', [(0, 1), (1, 0)])  29.1 us
  transfers between devices with their start and end apart: 21, of which 13 were waited for; matrix products, arithmetic and copies ran while one was open for 15% of the time, Pallas kernels for 8%

profile of v7, /device:TPU:0, one launch (start us, length us, event | category | flops | bytes accessed | tf_op | source)
XLA Modules:
  0.0 762.5 jit_solution(7590165171579545600)
XLA Ops:
  4.1 69.9 %first_gather.1 = (bf16[2048,1536]{1,0:T(8,128)(2,1)}, bf16[2048,1024]{1,0:T(8,128)(2,1)}, bf16[2048,640]{1,0:T(8,128)(2,1)}, f32[256,128]{1,0:T(8,128)}, bf16[2...) custom-call(bf16[128,1024]{1,0:T(8,128)(2,1)} %refs_0_.1, bf16[128,256]{1,0:T(8,128)(2,1)} %refs_1_.1, ...), custom_call_target="tpu_custom_call" | custom-call | bytes 147324928 | tf_op jit(solution)/shard_map/first_gather/pallas_call | solution.py:314
  74.1 1.6 collective-permute-start.3
  82.3 10.0 %conditional.5 = (bf16[512,2048]{1,0:T(8,128)(2,1)}, f32[512,1536]{1,0:T(8,128)}, bf16[512,512]{1,0:T(8,128)(2,1)S(1)}, bf16[2048,256]{1,0:T(8,128)(2,1)}) conditional(s32[]{:T(128)} %convert_element_type.112, () %tuple.60, (s32[]{:T(128)}, f32[16,1,128]{2,1,0:T(1,128)S(1)}, bf16[512,2048]{1,0:T(8,128)(2,1)}, bf16[2048,1536]{1,0:T(8,128)(2,1)}, ...), branch_computations={%region_0.1_spmd, %region_1.2_spmd} | conditional | flops 3221225472 | bytes 15745068 | solution.py:1629
  82.8 9.5 %prepare.1 = (bf16[512,2048]{1,0:T(8,128)(2,1)}, f32[512,1536]{1,0:T(8,128)}, bf16[4,512,256]{2,1,0:T(8,128)(2,1)}, bf16[512,512]{1,0:T(8,128)(2,1)S(1)}) custom-call(s32[2]{0:T(128)} %compare_select_fusion.spots, bf16[512,2048]{1,0:T(8,128)(2,1)} %get-tuple-element.157.x, f32[1,2048]{1,0:T(1,128)S(1)} %bitcast.136, ...), custom_call_target="tpu_custom_call" | custom-call | flops 3221225472 | bytes 15745024 | tf_op jit(solution)/shard_map/cond/branch_1_fun/prepare/pallas_call | solution.py:484
  95.0 5.0 collective-permute-done.3.refs_1_
  103.9 2.8 collective-permute-done.6
  106.7 5.5 collective-permute-start.10
  112.2 2.1 collective-permute-start.9
  114.3 2.0 collective-permute-start.7
  119.4 50.0 %conditional.6 = (f32[4,512,1]{1,0,2:T(4,128)S(1)}, bf16[512,1024]{1,0:T(8,128)(2,1)}, f32[256,2048]{1,0:T(8,128)}, bf16[256,64]{0,1:T(8,128)(2,1)}, f32[256,204...) conditional(s32[]{:T(128)} %convert_element_type.112, () %tuple.59, (s32[512]{0:T(512)S(1)}, ...), branch_computations={%region_4.5_spmd, %region_5.12_spmd} | conditional | flops 5002117120 | bytes 144001344 | solution.py:1629
  119.9 2.6 broadcast_in_dim.55
  127.2 2.1 fusion.3
  130.4 3.6 fusion.77
  134.0 2.0 copy-done.30
  136.2 1.7 collective-permute-start
  138.7 1.8 multiply_reduce_fusion.1
  140.5 21.4 %collective-permute-done = bf16[256,2048]{1,0:T(8,128)(2,1)} collective-permute-done((bf16[256,2048]{1,0:T(8,128)(2,1)S(1)}, bf16[256,2048]{1,0:T(8,128)(2,1)}, u32[]{:S(2)}, u32[]{:S(2)}) %collective-permute-start) | collective-permute-done | bytes 1048608 | tf_op jit(solution)/shard_map/cond/branch_1_fun/ppermute | solution.py:110
  162.0 2.8 multiply_reduce_fusion.2
  164.8 3.3 multiply_reduce_fusion
  169.4 15.6 %collective-permute-done.7.refs_3_ = bf16[256,2048]{1,0:T(8,128)(2,1)} collective-permute-done((bf16[256,2048]{1,0:T(8,128)(2,1)}, bf16[256,2048]{1,0:T(8,128)(2,1)}, u32[]{:S(2)}, u32[]{:S(2)}) %collective-permute-start.7) | collective-permute-done | bytes 1048608 | tf_op jit(solution)/shard_map/ppermute | solution.py:100
  185.0 168.9 %forward.1 = (bf16[1024,2048]{1,0:T(8,128)(2,1)}, bf16[2,2048,2048]{2,1,0:T(8,128)(2,1)}, bf16[2,2048,2048]{2,1,0:T(8,128)(2,1)}, bf16[2048,2048]{1,0:T(8,128)(2...) custom-call(bf16[256,2048]{1,0:T(8,128)(2,1)} %get-tuple-element.411.x_own, ...), custom_call_target="tpu_custom_call" | custom-call | flops 25769803776 | tf_op jit(solution)/shard_map/forward/pallas_call | solution.py:1121
  353.9 2.0 multiply_reduce_fusion.18
  360.1 3.0 add_convert_fusion
  366.7 115.9 %backward.1 = (bf16[1024,2048]{1,0:T(8,128)(2,1)}, bf16[2,1024,2048]{2,1,0:T(8,128)(2,1)}, bf16[256,2048]{1,0:T(8,128)(2,1)}, bf16[256,2048]{1,0:T(8,128)(2,1)},...) custom-call(bf16[256,2048]{1,0:T(8,128)(2,1)} %fusion.51.d_own, ...), custom_call_target="tpu_custom_call" | custom-call | flops 25769803776 | tf_op jit(solution)/shard_map/backward/pallas_call | solution.py:1365
  482.6 10.3 %block_grads.9 = (bf16[256,4096]{1,0:T(8,128)(2,1)}, bf16[256,4096]{1,0:T(8,128)(2,1)}) custom-call(s32[2]{0:T(128)} %pad_add_fusion.4.spots, bf16[1024,2048]{1,0:T(8,128)(2,1)} %get-tuple-element.419.rows_in.refs_0_.refs_1_, bf16[1024,2048]{1,0:T(8,128)(2,1)} %get-tuple-element.419.rows_in.refs_0_.refs_1_, ...), custom_call_target="tpu_custom_call" | custom-call | tf_op jit(solution)/shard_map/block_grads/pallas_call | solution.py:484
  497.0 62.9 %conditional.7 = (bf16[256,4096]{1,0:T(8,128)(2,1)}, bf16[256,4096]{1,0:T(8,128)(2,1)}, bf16[512,512]{0,1:T(8,128)(2,1)S(1)}, bf16[256,512]{0,1:T(8,128)(2,1)S(1...) conditional(s32[]{:T(128)} %convert_element_type.112, () %tuple.66, ...), branch_computations={%region_16.17_spmd, %region_17.25_spmd} | conditional | flops 8914598912 | bytes 216835824 | solution.py:1629
  497.2 2.9 multiply_reduce_fusion.5
  500.1 4.6 multiply_reduce_fusion.4
  504.7 2.0 fusion.25
  508.5 9.4 %block_grads.5 = (bf16[256,4096]{1,0:T(8,128)(2,1)}, bf16[256,4096]{1,0:T(8,128)(2,1)}) custom-call(s32[2]{0:T(128)} %pad_add_fusion.spots, bf16[1024,2048]{1,0:T(8,128)(2,1)} %get-tuple-element.187.refs_0_.refs_1_, bf16[1024,2048]{1,0:T(8,128)(2,1)} %get-tuple-element.187.refs_0_.refs_1_, bf16[2,1024,2048]{2,1,0:T(8,128)(2,1)} %get-tuple-element.188.refs_2_), custom_call_target="tpu_custom_call" | custom-call | tf_op jit(solution)/shard_map/cond/branch_1_fun/block_grads/pallas_call | solution.py:484
  518.5 5.6 fusion.33
  524.1 4.4 collective-permute-done.1
  531.4 5.0 convolution_convert_fusion.1
  536.3 2.4 copy.119
  538.8 8.1 %multiply_reduce_fusion.3 = (f32[4,512]{1,0:T(4,128)S(1)}, f32[4,512,1280]{2,1,0:T(8,128)S(1)}) fusion(f32[4,512,1280]{2,1,0:T(8,128)} %bitcast.116, f32[4,512]{1,0:T(4,128)S(1)} %bitcast.144, pred[512,1280]{1,0:T(8,128)(4,1)S(1)} %compare_or_fusion.1, bf16[4,512,256]{1,2,0:T(8,128)(2,1)} %bitcast.124, bf16[1280,512]{1,0:T(8,128)(2,1)} %get-tuple-element.197), kind=kOutput, calls=%fused_computation.36 | convolution fusion | flops 1352660992 | bytes 23347200 | tf_op jit(solution)/shard_map/cond/branch_1_fun/dot_general | solution.py:65
  547.0 2.5 fusion.20
  549.5 3.2 multiply_convert_fusion.1
  552.7 1.6 fusion.78
  556.8 3.0 fusion.27
  565.3 4.0 collective-permute-start.16
  569.3 5.1 add_blocks.2
  577.3 44.7 %conditional.8 = (f32[256,2048]{1,0:T(8,128)}, bf16[256,2048]{1,0:T(8,128)(2,1)}, bf16[256,4096]{1,0:T(8,128)(2,1)}, bf16[256,4096]{1,0:T(8,128)(2,1)}, bf16[256...) conditional(s32[]{:T(128)} %convert_element_type.112, () %tuple.70, ...), branch_computations={%region_25.26_spmd, %region_26.27_spmd} | conditional | flops 3230138368 | bytes 68440800 | solution.py:1629
  577.3 2.5 copy.110.d_kv
  580.5 5.4 prepare_back.1
  585.9 6.0 fusion.76
  591.9 2.0 copy-done.29
  595.9 9.3 %block_grads.8 = (bf16[256,4096]{1,0:T(8,128)(2,1)}, bf16[256,4096]{1,0:T(8,128)(2,1)}) custom-call(s32[2]{0:T(128)} %pad_add_fusion.2.spots, bf16[1024,2048]{1,0:T(8,128)(2,1)} %get-tuple-element.215.refs_0_.refs_1_, bf16[1024,2048]{1,0:T(8,128)(2,1)} %get-tuple-element.215.refs_0_.refs_1_, bf16[2,1024,2048]{2,1,0:T(8,128)(2,1)} %get-tuple-element.216.refs_1_.refs_2_), custom_call_target="tpu_custom_call" | custom-call | tf_op jit(solution)/shard_map/cond/branch_1_fun/block_grads/pallas_call | solution.py:484
  605.1 6.3 block_grads.7
  611.4 3.3 block_grads.6
  615.5 3.3 collective-permute-done.2
  618.8 3.3 slice_add_fusion.1
  624.4 5.4 add_blocks.3
  632.2 37.4 %conditional.9 = (f32[256,2048]{1,0:T(8,128)}, f32[1024,3328]{1,0:T(8,128)}, bf16[1024,3328]{1,0:T(8,128)(2,1)}) conditional(s32[]{:T(128)} %convert_element_type.112, () %tuple.73, (f32[16,1,128]{2,1,0:T(1,128)S(1)}, f32[256,2048]{1,0:T(8,128)}, f32[256,2048]{1,0:T(8,128)}, bf16[2048,64]{1,0:T(8,128)(2,1)S(1)}, bf16[2048,64]{1,0:T(8,128)(2,1)}, ...), branch_computations={%region_29.30_spmd, %region_30.37_spmd.clone} | conditional | flops 6194473984 | bytes 90691848 | solution.py:1629
  632.2 1.8 multiply_reduce_fusion.14
  634.0 2.7 multiply_reduce_fusion.12
  636.8 2.9 fusion.44
  640.2 5.4 fusion.43
  649.8 16.3 %row_grads.1 = (f32[1024,3328]{1,0:T(8,128)}, bf16[1024,3328]{1,0:T(8,128)(2,1)}) custom-call(s32[1]{0:T(128)} %bitcast.53.spots, bf16[512,2048]{1,0:T(8,128)(2,1)} %get-tuple-element.516.refs_0_, bf16[512,2048]{1,0:T(8,128)(2,1)} %get-tuple-element.517.refs_1_, bf16[256,2048]{1,0:T(8,128)(2,1)S(1)} %copy-done.38, ...), custom_call_target="tpu_custom_call" | custom-call | flops 6039797760 | bytes 32833536 | tf_op jit(solution)/shard_map/cond/branch_1_fun/row_grads/pallas_call | solution.py:484
  666.1 3.5 fusion.45
  669.6 8.2 %collective-permute-done.19.refs_3_ = bf16[256,4096]{1,0:T(8,128)(2,1)} collective-permute-done((bf16[256,4096]{1,0:T(8,128)(2,1)}, bf16[256,4096]{1,0:T(8,128)(2,1)}, u32[]{:S(2)}, u32[]{:S(2)}) %collective-permute-start.19) | collective-permute-done | bytes 2097184 | tf_op jit(solution)/shard_map/ppermute | solution.py:100
  677.9 68.4 %last_reduce.1 = (f32[128,2560]{1,0:T(8,128)}, f32[128,768]{1,0:T(8,128)}, f32[128,4096]{1,0:T(8,128)}, f32[128,4096]{1,0:T(8,128)}, f32[128,4096]{1,0:T(8,128)}) custom-call(f32[1024,3328]{1,0:T(8,128)} %get-tuple-element.486.refs_0_, bf16[1024,3328]{1,0:T(8,128)(2,1)} %get-tuple-element.487.refs_1_, bf16[256,4096]{1,0:T(8,128)(2,1)} %get-tuple-element.488.refs_2_, ...), custom_call_target="tpu_custom_call" | custom-call | bytes 272629760 | tf_op jit(solution)/shard_map/last_reduce/pallas_call | solution.py:879
  746.3 2.1 slice_bitcast_fusion
  748.5 1.7 fusion.74
  752.4 3.0 copy.115
  (277 shorter events, 78.3 us)
Async XLA Ops:
  4.1 74.2 %copy-start.62 = (s32[1,64,64]{2,1,0:T(8,128)S(1)}, s32[1,64,64]{2,1,0:T(8,128)}, u32[]{:S(2)}) copy-start(s32[1,64,64]{2,1,0:T(8,128)} %param.37) | copy-start | bytes 49156
  74.1 25.9 %collective-permute-start.3 = (bf16[256,2048]{1,0:T(8,128)(2,1)}, bf16[256,2048]{1,0:T(8,128)(2,1)}, u32[]{:S(2)}, u32[]{:S(2)}) collective-permute-start(bf16[256,2048]{1,0:T(8,128)(2,1)} %get-tuple-element.386.refs_0_), channel_id=1, source_target_pairs={{0,8},{2,10},{8,16},{10,18},{16,24},{18,26},{24,28},{26,30},{28,20... | collective-permute-start | bytes 3145736 | tf_op jit(solution)/shard_map/ppermute | solution.py:100
  75.7 25.6 %collective-permute-start.4 = (bf16[256,2048]{1,0:T(8,128)(2,1)}, bf16[256,2048]{1,0:T(8,128)(2,1)}, u32[]{:S(2)}, u32[]{:S(2)}) collective-permute-start(bf16[256,2048]{1,0:T(8,128)(2,1)} %get-tuple-element.386.refs_0_), channel_id=1, source_target_pairs={{8,0},{10,2},{16,8},{18,10},{24,16},{26,18},{28,24},{30,26},{20,28... | collective-permute-start | bytes 3145736 | tf_op jit(solution)/shard_map/ppermute | solution.py:103
  78.3 40.0 %copy-start.46 = (f32[16,1,128]{2,1,0:T(1,128)}, f32[16,1,128]{2,1,0:T(1,128)S(1)}, u32[]{:S(2)}) copy-start(f32[16,1,128]{2,1,0:T(1,128)S(1)} %get-tuple-element.927) | copy-start | bytes 24580
  78.3 40.0 %copy-start.48 = (f32[16,1,128]{2,1,0:T(1,128)}, f32[16,1,128]{2,1,0:T(1,128)S(1)}, u32[]{:S(2)}) copy-start(f32[16,1,128]{2,1,0:T(1,128)S(1)} %get-tuple-element.930) | copy-start | bytes 24580
  78.3 40.0 %copy-start.54 = (f32[16,1,128]{2,1,0:T(1,128)}, f32[16,1,128]{2,1,0:T(1,128)S(1)}, u32[]{:S(2)}) copy-start(f32[16,1,128]{2,1,0:T(1,128)S(1)} %get-tuple-element.928) | copy-start | bytes 24580
  80.2 38.2 %copy-start.58 = (s32[512]{0:T(512)}, s32[512]{0:T(512)S(1)}, u32[]{:S(2)}) copy-start(s32[512]{0:T(512)S(1)} %add_select_fusion.1) | copy-start | bytes 6148
  80.3 38.1 %copy-start.63 = (s32[512]{0:T(512)}, s32[512]{0:T(512)S(1)}, u32[]{:S(2)}) copy-start(s32[512]{0:T(512)S(1)} %add_select_fusion) | copy-start | bytes 6148
  80.5 37.9 %copy-start.56 = (s32[1280]{0:T(1024)}, s32[1280]{0:T(1024)S(1)}, u32[]{:S(2)}) copy-start(s32[1280]{0:T(1024)S(1)} %pad_add_fusion.3) | copy-start | bytes 15364
  81.5 10.8 %copy-start.24 = (bf16[2048,640]{1,0:T(8,128)(2,1)S(1)}, bf16[2048,640]{1,0:T(8,128)(2,1)}, u32[]{:S(2)}) copy-start(bf16[2048,640]{1,0:T(8,128)(2,1)} %get-tuple-element.391) | copy-start | bytes 7864324
  92.3 10.3 %copy-start.25 = (bf16[512,512]{1,0:T(8,128)(2,1)}, bf16[512,512]{1,0:T(8,128)(2,1)S(1)}, u32[]{:S(2)}) copy-start(bf16[512,512]{1,0:T(8,128)(2,1)S(1)} %get-tuple-element.395) | copy-start | bytes 1572868
  95.0 23.3 %copy-start = (bf16[256,2048]{1,0:T(8,128)(2,1)S(1)}, bf16[256,2048]{1,0:T(8,128)(2,1)}, u32[]{:S(2)}) copy-start(bf16[256,2048]{1,0:T(8,128)(2,1)} %refs_12_.1) | copy-start | bytes 3145732
  101.3 5.5 collective-permute-start.5
  102.6 4.1 collective-permute-start.6
  106.7 78.2 %collective-permute-start.10 = (bf16[256,4096]{1,0:T(8,128)(2,1)}, bf16[256,4096]{1,0:T(8,128)(2,1)}, u32[]{:S(2)}, u32[]{:S(2)}) collective-permute-start(bf16[256,4096]{1,0:T(8,128)(2,1)} %get-tuple-element.409.refs_5_), channel_id=1, source_target_pairs={{8,0},{10,2},{16,8},{18,10},{24,16},{26,18},{28,24},{30,26},{20,28... | collective-permute-start | bytes 6291464 | tf_op jit(solution)/shard_map/ppermute | solution.py:103
  112.2 72.7 %collective-permute-start.9 = (bf16[256,4096]{1,0:T(8,128)(2,1)}, bf16[256,4096]{1,0:T(8,128)(2,1)}, u32[]{:S(2)}, u32[]{:S(2)}) collective-permute-start(bf16[256,4096]{1,0:T(8,128)(2,1)} %get-tuple-element.409.refs_5_), channel_id=1, source_target_pairs={{0,8},{2,10},{8,16},{10,18},{16,24},{18,26},{24,28},{26,30},{28,20... | collective-permute-start | bytes 6291464 | tf_op jit(solution)/shard_map/ppermute | solution.py:100
  114.3 70.7 %collective-permute-start.7 = (bf16[256,2048]{1,0:T(8,128)(2,1)}, bf16[256,2048]{1,0:T(8,128)(2,1)}, u32[]{:S(2)}, u32[]{:S(2)}) collective-permute-start(bf16[256,2048]{1,0:T(8,128)(2,1)} %collective-permute-done.3.refs_1_), channel_id=1, source_target_pairs={{0,8},{2,10},{8,16},{10,18},{16,24},{18,26},{24,28},{26,30},{28,20... | collective-permute-start | bytes 3145736 | tf_op jit(solution)/shard_map/ppermute | solution.py:100
  116.3 68.6 %collective-permute-start.8 = (bf16[256,2048]{1,0:T(8,128)(2,1)}, bf16[256,2048]{1,0:T(8,128)(2,1)}, u32[]{:S(2)}, u32[]{:S(2)}) collective-permute-start(bf16[256,2048]{1,0:T(8,128)(2,1)} %collective-permute-done.4.refs_2_), channel_id=1, source_target_pairs={{8,0},{10,2},{16,8},{18,10},{24,16},{26,18},{28,24},{30,26},{20,28... | collective-permute-start | bytes 3145736 | tf_op jit(solution)/shard_map/ppermute | solution.py:103
  136.2 25.8 %collective-permute-start = (bf16[256,2048]{1,0:T(8,128)(2,1)S(1)}, bf16[256,2048]{1,0:T(8,128)(2,1)}, u32[]{:S(2)}, u32[]{:S(2)}) collective-permute-start(bf16[256,2048]{1,0:T(8,128)(2,1)S(1)} %slice.241), channel_id=1, source_target_pairs={{0,1},{1,0},{2,3},{3,2},{4,5},{5,4},{6,7},{7,6},{8,9},{9,8},{10,11... | collective-permute-start | bytes 3145736 | tf_op jit(solution)/shard_map/cond/branch_1_fun/ppermute | solution.py:110
  138.2 23.8 %copy-start.31 = (f32[512,2048]{1,0:T(8,128)S(1)}, f32[512,2048]{1,0:T(8,128)}, u32[]{:S(2)}) copy-start(f32[512,2048]{1,0:T(8,128)} %copy-done.30) | copy-start | bytes 12582916 | tf_op jit(solution)/shard_map/cond
  138.7 26.1 %copy-start.43 = (bf16[256,64]{0,1:T(8,128)(2,1)}, bf16[256,64]{0,1:T(8,128)(2,1)S(1)}, u32[]{:S(2)}) copy-start(bf16[256,64]{0,1:T(8,128)(2,1)S(1)} %convolution_convert_fusion) | copy-start | bytes 98308 | tf_op jit(solution)/shard_map/cond
  356.5 3.6 copy-start.6
  482.6 14.4 %copy-start.3 = (f32[256,2048]{1,0:T(8,128)S(1)}, f32[256,2048]{1,0:T(8,128)}, u32[]{:S(2)}) copy-start(f32[256,2048]{1,0:T(8,128)} %copy-done.2) | copy-start | bytes 6291460
  482.6 14.4 %copy-start.12 = (f32[256,2048]{1,0:T(8,128)S(1)}, f32[256,2048]{1,0:T(8,128)}, u32[]{:S(2)}) copy-start(f32[256,2048]{1,0:T(8,128)} %get-tuple-element.427) | copy-start | bytes 6291460
  482.6 14.4 %copy-start.55 = (f32[16,1,128]{2,1,0:T(1,128)S(1)}, f32[16,1,128]{2,1,0:T(1,128)}, u32[]{:S(2)}) copy-start(f32[16,1,128]{2,1,0:T(1,128)} %copy-done.54) | copy-start | bytes 24580
  492.9 69.3 %collective-permute-start.13 = (bf16[256,4096]{1,0:T(8,128)(2,1)}, bf16[256,4096]{1,0:T(8,128)(2,1)}, u32[]{:S(2)}, u32[]{:S(2)}) collective-permute-start(bf16[256,4096]{1,0:T(8,128)(2,1)} %get-tuple-element.425), channel_id=1, source_target_pairs={{0,8},{2,10},{8,16},{10,18},{16,24},{18,26},{24,28},{26,30},{28,20... | collective-permute-start | bytes 6291464 | tf_op jit(solution)/shard_map/ppermute | solution.py:100
  494.3 67.9 %collective-permute-start.14 = (bf16[256,4096]{1,0:T(8,128)(2,1)}, bf16[256,4096]{1,0:T(8,128)(2,1)}, u32[]{:S(2)}, u32[]{:S(2)}) collective-permute-start(bf16[256,4096]{1,0:T(8,128)(2,1)} %get-tuple-element.426), channel_id=1, source_target_pairs={{8,0},{10,2},{16,8},{18,10},{24,16},{26,18},{28,24},{30,26},{20,28... | collective-permute-start | bytes 6291464 | tf_op jit(solution)/shard_map/ppermute | solution.py:103
  494.9 66.0 %collective-permute-start.11 = (bf16[256,2048]{1,0:T(8,128)(2,1)}, bf16[256,2048]{1,0:T(8,128)(2,1)}, u32[]{:S(2)}, u32[]{:S(2)}) collective-permute-start(bf16[256,2048]{1,0:T(8,128)(2,1)} %get-tuple-element.420), channel_id=1, source_target_pairs={{0,8},{2,10},{8,16},{10,18},{16,24},{18,26},{24,28},{26,30},{28,20... | collective-permute-start | bytes 3145736 | tf_op jit(solution)/shard_map/ppermute | solution.py:100
  496.3 65.8 %collective-permute-start.12 = (bf16[256,2048]{1,0:T(8,128)(2,1)}, bf16[256,2048]{1,0:T(8,128)(2,1)}, u32[]{:S(2)}, u32[]{:S(2)}) collective-permute-start(bf16[256,2048]{1,0:T(8,128)(2,1)} %get-tuple-element.421), channel_id=1, source_target_pairs={{8,0},{10,2},{16,8},{18,10},{24,16},{26,18},{28,24},{30,26},{20,28... | collective-permute-start | bytes 3145736 | tf_op jit(solution)/shard_map/ppermute | solution.py:103
  506.7 21.7 %collective-permute-start.1 = (bf16[256,2048]{1,0:T(8,128)(2,1)S(1)}, bf16[256,2048]{1,0:T(8,128)(2,1)S(1)}, u32[]{:S(2)}, u32[]{:S(2)}) collective-permute-start(bf16[256,2048]{1,0:T(8,128)(2,1)S(1)} %fusion.25), channel_id=1, source_target_pairs={{0,1},{1,0},{2,3},{3,2},{4,5},{5,4},{6,7},{7,6},{8,9},{9,8},{10,11... | collective-permute-start | bytes 3145736 | tf_op jit(solution)/shard_map/cond/branch_1_fun/ppermute | solution.py:110
  508.5 9.4 %copy-start.57 = (s32[1280]{0:T(1024)S(1)}, s32[1280]{0:T(1024)}, u32[]{:S(2)}) copy-start(s32[1280]{0:T(1024)} %get-tuple-element.194) | copy-start | bytes 15364 | tf_op jit(solution)/shard_map/cond
  508.5 9.4 %copy-start.59 = (s32[512]{0:T(512)S(1)}, s32[512]{0:T(512)}, u32[]{:S(2)}) copy-start(s32[512]{0:T(512)} %get-tuple-element.193) | copy-start | bytes 6148 | tf_op jit(solution)/shard_map/cond
  508.5 9.4 %copy-start.64 = (s32[512]{0:T(512)S(1)}, s32[512]{0:T(512)}, u32[]{:S(2)}) copy-start(s32[512]{0:T(512)} %get-tuple-element.195) | copy-start | bytes 6148 | tf_op jit(solution)/shard_map/cond
  508.5 10.0 %copy-start.15 = (bf16[2048,256]{1,0:T(8,128)(2,1)S(1)}, bf16[2048,256]{1,0:T(8,128)(2,1)}, u32[]{:S(2)}) copy-start(bf16[2048,256]{1,0:T(8,128)(2,1)} %get-tuple-element.196) | copy-start | bytes 3145732 | tf_op jit(solution)/shard_map/cond
  508.5 10.0 %copy-start.27 = (bf16[1280,512]{1,0:T(8,128)(2,1)S(1)}, bf16[1280,512]{1,0:T(8,128)(2,1)}, u32[]{:S(2)}) copy-start(bf16[1280,512]{1,0:T(8,128)(2,1)} %get-tuple-element.197) | copy-start | bytes 3932164 | tf_op jit(solution)/shard_map/cond
  536.3 10.6 %slice-start = ((s8[10485760]{0:T(1024)(128)(4,1)}), s8[2097152]{0:T(1024)(128)(4,1)S(1)}, s32[]{:S(2)}) async-start(s8[10485760]{0:T(1024)(128)(4,1)} %bitcast.117), calls=%async_computation | async-start | bytes 4194304 | tf_op jit(solution)/shard_map/cond
  538.8 8.2 %slice-start.1 = ((s8[10485760]{0:T(1024)(128)(4,1)}), s8[4194304]{0:T(1024)(128)(4,1)S(1)}, s32[]{:S(2)}) async-start(s8[10485760]{0:T(1024)(128)(4,1)} %bitcast.117), calls=%async_computation.1 | async-start | bytes 8388608 | tf_op jit(solution)/shard_map/cond
  538.8 8.2 %slice-start.2 = ((s8[10485760]{0:T(1024)(128)(4,1)}), s8[4194304]{0:T(1024)(128)(4,1)S(1)}, s32[]{:S(2)}) async-start(s8[10485760]{0:T(1024)(128)(4,1)} %bitcast.117), calls=%async_computation.2 | async-start | bytes 8388608 | tf_op jit(solution)/shard_map/cond
  538.8 8.2 %copy-start.21 = (bf16[512,1024]{0,1:T(8,128)(2,1)S(1)}, bf16[512,1024]{0,1:T(8,128)(2,1)}, u32[]{:S(2)}) copy-start(bf16[512,1024]{0,1:T(8,128)(2,1)} %copy.119) | copy-start | bytes 3145732 | tf_op jit(solution)/shard_map/cond
  563.2 11.3 %collective-permute-start.15 = (bf16[512,512]{1,0:T(8,128)(2,1)}, bf16[512,512]{1,0:T(8,128)(2,1)}, u32[]{:S(2)}, u32[]{:S(2)}) collective-permute-start(bf16[512,512]{1,0:T(8,128)(2,1)} %copy.108), channel_id=1, source_target_pairs={{2,0},{4,2},{6,4},{8,6},{10,8},{12,10},{14,12},{16,14},{18,16},{20... | collective-permute-start | bytes 1572872 | tf_op jit(solution)/shard_map/ppermute | solution.py:1952
  565.3 12.0 %copy-start.10 = (f32[512,1536]{1,0:T(8,128)S(1)}, f32[512,1536]{1,0:T(8,128)}, u32[]{:S(2)}) copy-start(f32[512,1536]{1,0:T(8,128)} %get-tuple-element.450) | copy-start | bytes 9437188
  565.3 12.0 %copy-start.41 = (f32[512,128]{1,0:T(8,128)S(1)}, f32[512,128]{1,0:T(8,128)}, u32[]{:S(2)}) copy-start(f32[512,128]{1,0:T(8,128)} %copy-done.40) | copy-start | bytes 786436
  565.3 12.0 %copy-start.61 = (f32[8,256]{1,0:T(8,128)S(1)}, f32[8,256]{1,0:T(8,128)}, u32[]{:S(2)}) copy-start(f32[8,256]{1,0:T(8,128)} %copy-done.60) | copy-start | bytes 24580
  565.3 9.2 %collective-permute-start.16 = (bf16[256,512]{1,0:T(8,128)(2,1)}, bf16[256,512]{1,0:T(8,128)(2,1)}, u32[]{:S(2)}, u32[]{:S(2)}) collective-permute-start(bf16[256,512]{1,0:T(8,128)(2,1)} %copy.109), channel_id=1, source_target_pairs={{0,2},{2,4},{4,6},{6,8},{8,10},{10,12},{12,14},{14,16},{16,18},{18... | collective-permute-start | bytes 786440 | tf_op jit(solution)/shard_map/ppermute | solution.py:1953
  574.5 48.3 %collective-permute-start.17 = (bf16[256,4096]{1,0:T(8,128)(2,1)}, bf16[256,4096]{1,0:T(8,128)(2,1)}, u32[]{:S(2)}, u32[]{:S(2)}) collective-permute-start(bf16[256,4096]{1,0:T(8,128)(2,1)} %get-tuple-element.448), channel_id=1, source_target_pairs={{0,8},{2,10},{8,16},{10,18},{16,24},{18,26},{24,28},{26,30},{28,20... | collective-permute-start | bytes 6291464 | tf_op jit(solution)/shard_map/ppermute | solution.py:100
  575.7 48.6 %collective-permute-start.18 = (bf16[256,4096]{1,0:T(8,128)(2,1)}, bf16[256,4096]{1,0:T(8,128)(2,1)}, u32[]{:S(2)}, u32[]{:S(2)}) collective-permute-start(bf16[256,4096]{1,0:T(8,128)(2,1)} %get-tuple-element.449), channel_id=1, source_target_pairs={{8,0},{10,2},{16,8},{18,10},{24,16},{26,18},{28,24},{30,26},{20,28... | collective-permute-start | bytes 6291464 | tf_op jit(solution)/shard_map/ppermute | solution.py:103
  594.1 24.7 %collective-permute-start.2 = (bf16[256,2048]{1,0:T(8,128)(2,1)S(1)}, bf16[256,2048]{1,0:T(8,128)(2,1)S(1)}, u32[]{:S(2)}, u32[]{:S(2)}) collective-permute-start(bf16[256,2048]{1,0:T(8,128)(2,1)S(1)} %slice.242), channel_id=1, source_target_pairs={{0,1},{1,0},{2,3},{3,2},{4,5},{5,4},{6,7},{7,6},{8,9},{9,8},{10,11... | collective-permute-start | bytes 3145736 | tf_op jit(solution)/shard_map/cond/branch_1_fun/ppermute | solution.py:110
  605.1 6.3 copy-start.19
  624.3 7.6 copy-start.9
  624.3 7.8 %copy-start.7 = (f32[256,2048]{1,0:T(8,128)S(1)}, f32[256,2048]{1,0:T(8,128)}, u32[]{:S(2)}) copy-start(f32[256,2048]{1,0:T(8,128)} %copy-done.6) | copy-start | bytes 6291460
  624.3 7.8 %copy-start.13 = (f32[256,2048]{1,0:T(8,128)S(1)}, f32[256,2048]{1,0:T(8,128)}, u32[]{:S(2)}) copy-start(f32[256,2048]{1,0:T(8,128)} %get-tuple-element.892) | copy-start | bytes 6291460
  624.3 7.8 %copy-start.17 = (bf16[2048,64]{1,0:T(8,128)(2,1)S(1)}, bf16[2048,64]{1,0:T(8,128)(2,1)}, u32[]{:S(2)}) copy-start(bf16[2048,64]{1,0:T(8,128)(2,1)} %get-tuple-element.540) | copy-start | bytes 786436
  624.4 7.8 %copy-start.44 = (bf16[256,64]{0,1:T(8,128)(2,1)S(1)}, bf16[256,64]{0,1:T(8,128)(2,1)}, u32[]{:S(2)}) copy-start(bf16[256,64]{0,1:T(8,128)(2,1)} %get-tuple-element.560) | copy-start | bytes 98308
  624.4 7.8 %copy-start.49 = (f32[16,1,128]{2,1,0:T(1,128)S(1)}, f32[16,1,128]{2,1,0:T(1,128)}, u32[]{:S(2)}) copy-start(f32[16,1,128]{2,1,0:T(1,128)} %copy-done.48) | copy-start | bytes 24580
  624.4 7.8 %copy-start.51 = (bf16[256,256]{1,0:T(8,128)(2,1)S(1)}, bf16[256,256]{1,0:T(8,128)(2,1)}, u32[]{:S(2)}) copy-start(bf16[256,256]{1,0:T(8,128)(2,1)} %copy-done.50) | copy-start | bytes 393220
  624.4 7.8 %copy-start.53 = (bf16[256,256]{1,0:T(8,128)(2,1)S(1)}, bf16[256,256]{1,0:T(8,128)(2,1)}, u32[]{:S(2)}) copy-start(bf16[256,256]{1,0:T(8,128)(2,1)} %copy-done.52) | copy-start | bytes 393220
  629.8 48.0 %collective-permute-start.19 = (bf16[256,4096]{1,0:T(8,128)(2,1)}, bf16[256,4096]{1,0:T(8,128)(2,1)}, u32[]{:S(2)}, u32[]{:S(2)}) collective-permute-start(bf16[256,4096]{1,0:T(8,128)(2,1)} %get-tuple-element.468), channel_id=1, source_target_pairs={{0,8},{2,10},{8,16},{10,18},{16,24},{18,26},{24,28},{26,30},{28,20... | collective-permute-start | bytes 6291464 | tf_op jit(solution)/shard_map/ppermute | solution.py:100
  630.8 47.1 %collective-permute-start.20 = (bf16[256,4096]{1,0:T(8,128)(2,1)}, bf16[256,4096]{1,0:T(8,128)(2,1)}, u32[]{:S(2)}, u32[]{:S(2)}) collective-permute-start(bf16[256,4096]{1,0:T(8,128)(2,1)} %get-tuple-element.469), channel_id=1, source_target_pairs={{8,0},{10,2},{16,8},{18,10},{24,16},{26,18},{28,24},{30,26},{20,28... | collective-permute-start | bytes 6291464 | tf_op jit(solution)/shard_map/ppermute | solution.py:103
  639.7 5.8 copy-start.20
  640.2 5.4 copy-start.45
  649.8 16.3 %copy-start.65 = (f32[256]{0:T(256)S(1)}, f32[256]{0:T(256)}, u32[]{:S(2)}) copy-start(f32[256]{0:T(256)} %get-tuple-element.871) | copy-start | bytes 3076 | tf_op jit(solution)/shard_map/cond
  649.8 16.4 %copy-start.11 = (f32[256,2048]{1,0:T(8,128)S(1)}, f32[256,2048]{1,0:T(8,128)}, u32[]{:S(2)}) copy-start(f32[256,2048]{1,0:T(8,128)} %get-tuple-element.898) | copy-start | bytes 6291460 | tf_op jit(solution)/shard_map/cond
  746.3 3.8 copy-start.36
  752.4 6.2 copy-start.33
  (33 other events, 64.6 us)
